TPU v7x, 256 devices: a whole 4x4x8 slice. The times are simulated.
256 devices in a mesh: dp: 16 (over z, x_hi), shard: 16 (over x_lo, y, core).
Axes of the slice: x: 4 (x_hi: 2, x_lo: 2; x = x_hi * 2 + x_lo), y: 4, z: 8, core: 2. Of those that a mesh axis runs over, the one named last changes fastest.
Arguments:
- tokens: bfloat16 [16384, 2048], P(('dp', 'shard')), may hold values from -6 to 6
- router_probs: float32 [16384, 8], P(('dp', 'shard')), may hold values from 0.05 to 1
- expert_ids: int32 [16384, 8], P(('dp', 'shard')), may hold values from 0 to 31, all different within a row; in each aligned block of 64 rows (0 to 63, 64 to 127, ...) at most 32 rows name the same one
- old_place: int32 [32], replicated, may hold values from 0 to 31, as said below
- new_place: int32 [32], replicated, may hold values from 0 to 31, as said below
- w_gate: bfloat16 [32, 2048, 1024], P('dp', 'shard'), may hold values from -0.125 to 0.125
- w_up: bfloat16 [32, 2048, 1024], P('dp', 'shard'), may hold values from -0.125 to 0.125
- w_down: bfloat16 [32, 2048, 1024], P('dp', 'shard'), may hold values from -0.1875 to 0.1875
Outputs:
- moe_output: bfloat16 [16384, 2048], P(('dp', 'shard'))
- new_gate: bfloat16 [32, 2048, 1024], P('dp', 'shard')
- new_up: bfloat16 [32, 2048, 1024], P('dp', 'shard')
- new_down: bfloat16 [32, 2048, 1024], P('dp', 'shard')
Inputs may be any that keep to these rules, and one draw needn't show every extreme that they name: `expert_ids`: each token names 8 different experts; among the tokens of one device no expert is named by more than 32 tokens, a bound that some block reaches. `old_place`: a permutation of the 32 experts over the 32 slots. `new_place`: equal to old_place except at exactly one of the slots 2 k and 2 k + 1 for each k; the expert leaving the refilled slot of k moves to the refilled slot of (k + 1) mod (16), so that new_place is again a permutation.
All inputs are finite; a program needn't handle non-finite values.
Results may differ from a plain program's by a relative error of at most 0.0064.
Values may be sent and summed in bfloat16 or wider, within the bound.
A program may use at most 128 MiB of HBM per device.

v0:
```python
import jax
import jax.numpy as jnp
from jax import lax
from jax.sharding import PartitionSpec as P


def partner_2(x, axis, apart):
    return lax.ppermute(x, axis, [(i, i ^ 1 << apart) for i in range(lax.axis_size(axis))])


def passed_along(x, axis, by):
    size = lax.axis_size(axis)
    return lax.ppermute(x, axis, [(i, (i + by) % size) for i in range(size)])


def lookup(lookup_keys, lookup_table, entry_count):
    matches = lookup_keys[..., None] == jnp.arange(entry_count, dtype=jnp.int32)
    return jnp.sum(jnp.where(matches, lookup_table, 0), axis=-1)


def widen(pieces, half_count):
    return jnp.repeat(pieces, half_count, axis=0)


def pair_halves(upper_half, own_rows, other_rows):
    return jnp.where(
        upper_half,
        jnp.stack([other_rows, own_rows], axis=1),
        jnp.stack([own_rows, other_rows], axis=1),
    )


def local(tokens, router_probs, expert_ids, old_place, new_place, w_gate, w_up, w_down):
    slot_count = old_place.shape[0]
    tok_count, top_count = expert_ids.shape
    model_width = tokens.shape[1]
    n_shard = lax.axis_size("shard")
    half_count = n_shard // 2
    partner_bit = n_shard.bit_length() - 2
    column = lax.axis_index("shard")
    row_id = lax.axis_index("dp")
    n_rows = lax.axis_size("dp")
    upper_half = column >= half_count
    capacity = max(2, 2 * tok_count * top_count // slot_count)
    places = slot_count * capacity
    full_gate, full_up, full_down = (
        lax.all_to_all(widen(w_gate, half_count), "shard", split_axis=0, concat_axis=1, tiled=True),
        lax.all_to_all(widen(w_up, half_count), "shard", split_axis=0, concat_axis=1, tiled=True),
        lax.all_to_all(widen(w_down, half_count), "shard", split_axis=0, concat_axis=1, tiled=True),
    )
    full_gate = full_gate[0]
    full_up = full_up[0]
    full_down = full_down[0]
    slot_index = jnp.arange(slot_count, dtype=jnp.int32)
    owner_slot = jnp.sum(
        jnp.where(old_place[None, :] == slot_index[:, None], slot_index[None, :], 0), axis=1
    )
    slot_ids = lookup(expert_ids, owner_slot, slot_count)
    gate_weights = (router_probs / jnp.sum(router_probs, axis=1, keepdims=True)).astype(
        jnp.bfloat16
    )
    flat_slots = slot_ids.reshape(-1)
    members = (flat_slots[:, None] == slot_index[None, :]).astype(jnp.int32)
    earlier = jnp.cumsum(members, axis=0) - members
    slot_rank = jnp.sum(earlier * members, axis=1)
    position = (flat_slots * capacity + slot_rank).reshape(tok_count, top_count)
    matches = position[:, :, None] == jnp.arange(places, dtype=jnp.int32)[None, None, :]
    chosen = jnp.any(matches, axis=1).astype(jnp.bfloat16)
    outgoing = lax.dot_general(
        chosen, tokens, (((0,), (0,)), ((), ())), preferred_element_type=jnp.float32
    ).astype(jnp.bfloat16)
    outgoing = outgoing.reshape(n_rows, 2, capacity, model_width)
    arrived = lax.all_to_all(outgoing, "dp", split_axis=0, concat_axis=0, tiled=True)
    own_rows = jnp.where(upper_half, arrived[:, 1], arrived[:, 0])
    other_rows = jnp.where(upper_half, arrived[:, 0], arrived[:, 1])
    partner = partner_2(other_rows, "shard", partner_bit)
    work_rows = jnp.stack([own_rows, partner], axis=0)
    flat_rows = work_rows.reshape(-1, model_width)
    gate_part = jnp.dot(flat_rows, full_gate, preferred_element_type=jnp.float32)
    up_part = jnp.dot(flat_rows, full_up, preferred_element_type=jnp.float32)
    hidden = (jax.nn.silu(gate_part) * up_part).astype(jnp.bfloat16)
    result = lax.dot_general(
        hidden, full_down, (((1,), (1,)), ((), ())), preferred_element_type=jnp.float32
    ).astype(jnp.bfloat16)
    result = result.reshape(2, n_rows, capacity, model_width)
    returned_other = partner_2(result[1], "shard", partner_bit)
    returned = lax.all_to_all(
        pair_halves(upper_half, result[0], returned_other),
        "dp",
        split_axis=0,
        concat_axis=0,
        tiled=True,
    )
    combine = jnp.sum(
        jnp.where(matches, gate_weights[:, :, None], jnp.zeros((), jnp.bfloat16)), axis=1
    )
    moe_output = jnp.dot(
        combine, returned.reshape(places, model_width), preferred_element_type=jnp.float32
    ).astype(jnp.bfloat16)
    base_slot = 2 * row_id
    second_old = lax.dynamic_index_in_dim(old_place, base_slot + 1, 0, keepdims=False)
    second_new = lax.dynamic_index_in_dim(new_place, base_slot + 1, 0, keepdims=False)
    second_moved = second_new != second_old
    leave_gate = jnp.where(second_moved, w_gate[1], w_gate[0])
    leave_up = jnp.where(second_moved, w_up[1], w_up[0])
    leave_down = jnp.where(second_moved, w_down[1], w_down[0])
    arrive_gate, arrive_up, arrive_down = passed_along((leave_gate, leave_up, leave_down), "dp", 1)
    new_gate = jnp.stack(
        [
            jnp.where(second_moved, w_gate[0], arrive_gate),
            jnp.where(second_moved, arrive_gate, w_gate[1]),
        ],
        axis=0,
    )
    new_up = jnp.stack(
        [jnp.where(second_moved, w_up[0], arrive_up), jnp.where(second_moved, arrive_up, w_up[1])],
        axis=0,
    )
    new_down = jnp.stack(
        [
            jnp.where(second_moved, w_down[0], arrive_down),
            jnp.where(second_moved, arrive_down, w_down[1]),
        ],
        axis=0,
    )
    return (moe_output, new_gate, new_up, new_down)


def solution(mesh):
    in_specs = (
        P(("dp", "shard"), None),
        P(("dp", "shard"), None),
        P(("dp", "shard"), None),
        P(),
        P(),
        P("dp", "shard", None),
        P("dp", "shard", None),
        P("dp", "shard", None),
    )
    out_specs = (
        P(("dp", "shard"), None),
        P("dp", "shard", None),
        P("dp", "shard", None),
        P("dp", "shard", None),
    )
    return jax.shard_map(local, mesh=mesh, in_specs=in_specs, out_specs=out_specs, check_vma=False)
```

profile of v0, /device:TPU:8, one launch (start us, length us, event | category | flops | bytes accessed | tf_op | source)
XLA Modules:
  0.0 552.8 jit_solution(8231416247993723823)
XLA Ops:
  0.6 1.6 broadcast_in_dim.56
  2.3 52.6 %all_to_all.37 = bf16[16,128,1024]{2,1,0:T(8,128)(2,1)} all-to-all(bf16[16,128,1024]{2,1,0:T(8,128)(2,1)S(1)} %bitcast.106), channel_id=1, replica_groups=mesh['dp'=16,'shard'=16] {'shard'}, dimensions={0} | all-to-all | bytes 8388608 | tf_op jit(solution)/shard_map/all_to_all | solution.py:47
  54.9 2.5 broadcast_in_dim.57
  57.4 7.9 %all-to-all-start.2 = ((bf16[16,128,1024]{2,1,0:T(8,128)(2,1)}), bf16[16,128,1024]{2,1,0:T(8,128)(2,1)}, u32[]{:S(2)}, u32[]{:S(2)}) async-start(bf16[16,128,1024]{2,1,0:T(8,128)(2,1)} %bitcast.103), calls=%async_computation.2 | async-start | bytes 8388608 | tf_op jit(solution)/shard_map/all_to_all | solution.py:48
  65.4 0.1 select_reduce_fusion.1
  65.5 0.1 select_reduce_fusion
  65.7 0.1 eq.74
  65.8 0.1 eq.70
  65.9 1.2 reduce-window.6
  67.0 0.2 slice_reduce_fusion
  67.3 0.1 fusion.13
  67.4 0.1 reduce_sum.53
  67.6 0.1 copy.31
  67.7 0.7 fusion.2
  68.4 3.3 convolution_convert_fusion
  71.6 53.1 %all-to-all-done.2 = bf16[16,128,1024]{2,1,0:T(8,128)(2,1)} async-done(((bf16[16,128,1024]{2,1,0:T(8,128)(2,1)}), bf16[16,128,1024]{2,1,0:T(8,128)(2,1)}, u32[]{:S(2)}, u32[]{:S(2)}) %all-to-all-start.2) | async-done | bytes 4194336 | tf_op jit(solution)/shard_map/all_to_all | solution.py:48
  124.7 10.9 %all-to-all-start = ((bf16[16,2,32,2048]{3,2,1,0:T(8,128)(2,1)}), bf16[16,2,32,2048]{3,2,1,0:T(8,128)(2,1)}, u32[]{:S(2)}, u32[]{:S(2)}) async-start(bf16[16,2,32,2048]{3,2,1,0:T(8,128)(2,1)} %bitcast.105), calls=%async_computation | async-start | bytes 8388608 | tf_op jit(solution)/shard_map/all_to_all | solution.py:73
  135.7 98.7 %all-to-all-done = bf16[16,2,32,2048]{3,2,1,0:T(8,128)(2,1)} async-done(((bf16[16,2,32,2048]{3,2,1,0:T(8,128)(2,1)}), bf16[16,2,32,2048]{3,2,1,0:T(8,128)(2,1)}, u32[]{:S(2)}, u32[]{:S(2)}) %all-to-all-start) | async-done | bytes 4194336 | tf_op jit(solution)/shard_map/all_to_all | solution.py:73
  234.3 2.5 broadcast_in_dim.58
  236.8 7.9 %all-to-all-start.3 = ((bf16[16,128,1024]{2,1,0:T(8,128)(2,1)}), bf16[16,128,1024]{2,1,0:T(8,128)(2,1)}, u32[]{:S(2)}, u32[]{:S(2)}) async-start(bf16[16,128,1024]{2,1,0:T(8,128)(2,1)} %bitcast.104), calls=%async_computation.3 | async-start | bytes 8388608 | tf_op jit(solution)/shard_map/all_to_all | solution.py:49
  244.7 2.4 fusion
  247.1 1.6 collective-permute-start
  248.7 2.4 fusion.1
  251.1 99.3 %collective-permute-done = bf16[16,32,2048]{2,1,0:T(8,128)(2,1)S(1)} collective-permute-done((bf16[16,32,2048]{2,1,0:T(8,128)(2,1)S(1)}, bf16[16,32,2048]{2,1,0:T(8,128)(2,1)S(1)}, u32[]{:S(2)}, u32[]{:S(2)}) %collective-permute-start) | collective-permute-done | bytes 2097184 | tf_op jit(solution)/shard_map/ppermute | solution.py:8
  350.5 0.4 pad_maximum_fusion
  350.9 2.1 copy-done.6
  353.0 1.2 copy-done.5
  354.2 6.1 %fusion.17 = f32[1024,1024]{1,0:T(8,128)} fusion(bf16[1024,2048]{1,0:T(8,128)(2,1)S(1)} %bitcast.109, bf16[2048,1024]{1,0:T(8,128)(2,1)S(1)} %bitcast.108), kind=kOutput, calls=%fused_computation.49 | convolution fusion | flops 4294967296 | bytes 12582912 | tf_op jit(solution)/shard_map/dot_general | solution.py:79
  360.3 15.1 %convolution_convert_fusion.1 = bf16[1024,2048]{1,0:T(8,128)(2,1)} fusion(bf16[2048,1024]{1,0:T(8,128)(2,1)} %bitcast.14, f32[1024,1024]{1,0:T(8,128)} %fusion.17, bf16[1024,2048]{1,0:T(8,128)(2,1)} %bitcast.110, bf16[2048,1024]{1,0:T(8,128)(2,1)} %bitcast.12), kind=kOutput, calls=%fused_computation.5 | convolution fusion | flops 8598323200 | bytes 20971520 | tf_op jit(solution)/shard_map/dot_general | solution.py:82
  375.4 2.7 fusion.16
  378.1 1.9 collective-permute-start.1
  380.0 45.5 %collective-permute-done.1 = bf16[16,32,2048]{2,1,0:T(8,128)(2,1)S(1)} collective-permute-done((bf16[16,32,2048]{2,1,0:T(8,128)(2,1)S(1)}, bf16[16,32,2048]{2,1,0:T(8,128)(2,1)S(1)}, u32[]{:S(2)}, u32[]{:S(2)}) %collective-permute-start.1) | collective-permute-done | bytes 2097184 | tf_op jit(solution)/shard_map/ppermute | solution.py:8
  425.5 2.2 maximum_select_fusion
  427.7 6.5 %all-to-all-start.4 = ((bf16[16,2,32,2048]{3,2,1,0:T(8,128)(2,1)}), bf16[16,2,32,2048]{3,2,1,0:T(8,128)(2,1)}, u32[]{:S(2)}, u32[]{:S(2)}) async-start(bf16[16,2,32,2048]{3,2,1,0:T(8,128)(2,1)} %maximum_select_fusion), calls=%async_computation.4 | async-start | bytes 8388608 | tf_op jit(solution)/shard_map/all_to_all | solution.py:87
  434.2 0.6 dynamic_slice.8
  434.8 0.6 dynamic_slice.7
  436.8 3.4 collective-permute-start.2
  440.2 1.5 collective-permute-start.3
  441.8 3.0 collective-permute-start.4
  444.9 0.1 copy.32
  445.0 0.7 fusion.4
  445.7 92.7 %collective-permute-done.2 = bf16[128,1024]{1,0:T(8,128)(2,1)S(1)} collective-permute-done((bf16[128,1024]{1,0:T(8,128)(2,1)S(1)}, bf16[128,1024]{1,0:T(8,128)(2,1)S(1)}, u32[]{:S(2)}, u32[]{:S(2)}) %collective-permute-start.2) | collective-permute-done | bytes 262176 | tf_op jit(solution)/shard_map/ppermute | solution.py:13
  538.5 5.6 %collective-permute-done.3 = bf16[128,1024]{1,0:T(8,128)(2,1)S(1)} collective-permute-done((bf16[128,1024]{1,0:T(8,128)(2,1)S(1)}, bf16[128,1024]{1,0:T(8,128)(2,1)S(1)}, u32[]{:S(2)}, u32[]{:S(2)}) %collective-permute-start.3) | collective-permute-done | bytes 262176 | tf_op jit(solution)/shard_map/ppermute | solution.py:13
  544.1 0.8 pad_maximum_fusion.1
  545.0 0.8 pad_maximum_fusion.2
  545.8 2.3 collective-permute-done.4
  548.2 0.8 pad_maximum_fusion.3
  549.0 3.7 convolution_convert_fusion.2
  (36 shorter events, 0.5 us)
Async XLA Ops:
  0.6 67.7 %copy-start = (bf16[64,2048]{1,0:T(8,128)(2,1)S(1)}, bf16[64,2048]{1,0:T(8,128)(2,1)}, u32[]{:S(2)}) copy-start(bf16[64,2048]{1,0:T(8,128)(2,1)} %param.8) | copy-start | bytes 786436
  2.3 52.7 %copy-start.3 = (bf16[2,128,1024]{2,1,0:T(8,128)(2,1)S(1)}, bf16[2,128,1024]{2,1,0:T(8,128)(2,1)}, u32[]{:S(2)}) copy-start(bf16[2,128,1024]{2,1,0:T(8,128)(2,1)} %param.14) | copy-start | bytes 1572868
  57.4 7.9 %copy-start.9 = (s32[32]{0:T(128)S(1)}, s32[32]{0:T(128)}, u32[]{:S(2)}) copy-start(s32[32]{0:T(128)} %param.11) | copy-start | bytes 388
  57.4 8.0 %copy-start.8 = (s32[64,8]{0,1:T(8,128)S(1)}, s32[64,8]{0,1:T(8,128)}, u32[]{:S(2)}) copy-start(s32[64,8]{0,1:T(8,128)} %param.10) | copy-start | bytes 6148
  57.4 67.3 %all-to-all-start.2 = ((bf16[16,128,1024]{2,1,0:T(8,128)(2,1)}), bf16[16,128,1024]{2,1,0:T(8,128)(2,1)}, u32[]{:S(2)}, u32[]{:S(2)}) async-start(bf16[16,128,1024]{2,1,0:T(8,128)(2,1)} %bitcast.103), calls=%async_computation.2 | async-start | bytes 8388608 | tf_op jit(solution)/shard_map/all_to_all | solution.py:48
  124.7 109.6 %copy-start.4 = (bf16[2,128,1024]{2,1,0:T(8,128)(2,1)S(1)}, bf16[2,128,1024]{2,1,0:T(8,128)(2,1)}, u32[]{:S(2)}) copy-start(bf16[2,128,1024]{2,1,0:T(8,128)(2,1)} %param.15) | copy-start | bytes 1572868
  124.7 109.6 %all-to-all-start = ((bf16[16,2,32,2048]{3,2,1,0:T(8,128)(2,1)}), bf16[16,2,32,2048]{3,2,1,0:T(8,128)(2,1)}, u32[]{:S(2)}, u32[]{:S(2)}) async-start(bf16[16,2,32,2048]{3,2,1,0:T(8,128)(2,1)} %bitcast.105), calls=%async_computation | async-start | bytes 8388608 | tf_op jit(solution)/shard_map/all_to_all | solution.py:73
  236.8 123.5 %all-to-all-start.3 = ((bf16[16,128,1024]{2,1,0:T(8,128)(2,1)}), bf16[16,128,1024]{2,1,0:T(8,128)(2,1)}, u32[]{:S(2)}, u32[]{:S(2)}) async-start(bf16[16,128,1024]{2,1,0:T(8,128)(2,1)} %bitcast.104), calls=%async_computation.3 | async-start | bytes 8388608 | tf_op jit(solution)/shard_map/all_to_all | solution.py:49
  247.1 103.3 %collective-permute-start = (bf16[16,32,2048]{2,1,0:T(8,128)(2,1)S(1)}, bf16[16,32,2048]{2,1,0:T(8,128)(2,1)S(1)}, u32[]{:S(2)}, u32[]{:S(2)}) collective-permute-start(bf16[16,32,2048]{2,1,0:T(8,128)(2,1)S(1)} %fusion), channel_id=1, source_target_pairs={{0,8},{1,9},{2,10},{3,11},{4,12},{5,13},{6,14},{7,15},{8,0},{9,1},... | collective-permute-start | bytes 6291464 | tf_op jit(solution)/shard_map/ppermute | solution.py:8
  350.5 3.7 copy-start.5
  350.9 2.1 copy-start.6
  378.1 47.4 %collective-permute-start.1 = (bf16[16,32,2048]{2,1,0:T(8,128)(2,1)S(1)}, bf16[16,32,2048]{2,1,0:T(8,128)(2,1)S(1)}, u32[]{:S(2)}, u32[]{:S(2)}) collective-permute-start(bf16[16,32,2048]{2,1,0:T(8,128)(2,1)S(1)} %bitcast.113), channel_id=1, source_target_pairs={{0,8},{1,9},{2,10},{3,11},{4,12},{5,13},{6,14},{7,15},{8,0},{9,1},... | collective-permute-start | bytes 6291464 | tf_op jit(solution)/shard_map/ppermute | solution.py:8
  427.7 7.1 %copy-start.10 = (s32[32]{0:T(128)S(1)}, s32[32]{0:T(128)}, u32[]{:S(2)}) copy-start(s32[32]{0:T(128)} %param.12) | copy-start | bytes 388
  427.7 9.0 %copy-start.2 = (bf16[2,128,1024]{2,1,0:T(8,128)(2,1)S(1)}, bf16[2,128,1024]{2,1,0:T(8,128)(2,1)}, u32[]{:S(2)}) copy-start(bf16[2,128,1024]{2,1,0:T(8,128)(2,1)} %param.13) | copy-start | bytes 1572868
  427.7 17.2 %copy-start.7 = (f32[64,8]{0,1:T(8,128)S(1)}, f32[64,8]{0,1:T(8,128)}, u32[]{:S(2)}) copy-start(f32[64,8]{0,1:T(8,128)} %param.9) | copy-start | bytes 6148
  427.7 121.3 %all-to-all-start.4 = ((bf16[16,2,32,2048]{3,2,1,0:T(8,128)(2,1)}), bf16[16,2,32,2048]{3,2,1,0:T(8,128)(2,1)}, u32[]{:S(2)}, u32[]{:S(2)}) async-start(bf16[16,2,32,2048]{3,2,1,0:T(8,128)(2,1)} %maximum_select_fusion), calls=%async_computation.4 | async-start | bytes 8388608 | tf_op jit(solution)/shard_map/all_to_all | solution.py:87
  436.8 101.7 %collective-permute-start.2 = (bf16[128,1024]{1,0:T(8,128)(2,1)S(1)}, bf16[128,1024]{1,0:T(8,128)(2,1)S(1)}, u32[]{:S(2)}, u32[]{:S(2)}) collective-permute-start(bf16[128,1024]{1,0:T(8,128)(2,1)S(1)} %bitcast_select_fusion.9), channel_id=1, source_target_pairs={{0,16},{16,32},{32,48},{48,64},{64,80},{80,96},{96,112},{112,128},... | collective-permute-start | bytes 786440 | tf_op jit(solution)/shard_map/ppermute | solution.py:13
  440.2 103.8 %collective-permute-start.3 = (bf16[128,1024]{1,0:T(8,128)(2,1)S(1)}, bf16[128,1024]{1,0:T(8,128)(2,1)S(1)}, u32[]{:S(2)}, u32[]{:S(2)}) collective-permute-start(bf16[128,1024]{1,0:T(8,128)(2,1)S(1)} %bitcast_select_fusion.6), channel_id=1, source_target_pairs={{0,16},{16,32},{32,48},{48,64},{64,80},{80,96},{96,112},{112,128},... | collective-permute-start | bytes 786440 | tf_op jit(solution)/shard_map/ppermute | solution.py:13
  441.8 106.3 %collective-permute-start.4 = (bf16[128,1024]{1,0:T(8,128)(2,1)S(1)}, bf16[128,1024]{1,0:T(8,128)(2,1)S(1)}, u32[]{:S(2)}, u32[]{:S(2)}) collective-permute-start(bf16[128,1024]{1,0:T(8,128)(2,1)S(1)} %bitcast_select_fusion.3), channel_id=1, source_target_pairs={{0,16},{16,32},{32,48},{48,64},{64,80},{80,96},{96,112},{112,128},... | collective-permute-start | bytes 786440 | tf_op jit(solution)/shard_map/ppermute | solution.py:13
  544.1 8.6 %copy-start.1 = (bf16[64,2048]{1,0:T(8,128)(2,1)S(1)}, bf16[64,2048]{1,0:T(8,128)(2,1)}, u32[]{:S(2)}) copy-start(bf16[64,2048]{1,0:T(8,128)(2,1)} %param.8) | copy-start | bytes 786436
where the time goes:
time: 553 us
  waiting for transfers between devices  397 us (72%)
  blocking collectives  52.6 us (10%)
  starting transfers between devices  44.8 us (8%)
  matrix products  28.2 us (5%)
  local copies, waits for them, and re-layouts  14.6 us (3%)
  other arithmetic  13.2 us (2%)
    ppermute x2, waiting for transfers between devices, partner_2(): lax.ppermute(x, axis, [(i, i ^ 1 << apart) for i in range(lax.axis_size(a...  145 us
    ppermute x3, waiting for transfers between devices, passed_along(): return lax.ppermute(x, axis, [(i, (i + by) % size) for i in range(size)])  101 us
    all_to_all x1, waiting for transfers between devices, local(): lax.all_to_all(outgoing, 'dp', split_axis=0, concat_axis=0, tiled=True)  98.7 us
    all_to_all x1, waiting for transfers between devices, local(): lax.all_to_all(widen(w_up, half_count), 'shard', split_axis=0, concat_axi...  53.1 us
    all_to_all x1, blocking collectives, local(): lax.all_to_all(widen(w_gate, half_count), 'shard', split_axis=0, concat_a...  52.6 us
    dot_general x1, matrix products, local(): lax.dot_general(hidden, full_down, (((1,), (1,)), ((), ())), preferred_el...  15.1 us
  transfers between devices with their start and end apart: 9, of which 7 were waited for; matrix products, arithmetic and copies ran while one was open for 4% of the time, Pallas kernels for 0%

commit v1 on v0

--- a/solution.py
+++ b/solution.py
@@ -65,12 +65,22 @@
     slot_rank = jnp.sum(earlier * members, axis=1)
     position = (flat_slots * capacity + slot_rank).reshape(tok_count, top_count)
     matches = position[:, :, None] == jnp.arange(places, dtype=jnp.int32)[None, None, :]
-    chosen = jnp.any(matches, axis=1).astype(jnp.bfloat16)
-    outgoing = lax.dot_general(
-        chosen, tokens, (((0,), (0,)), ((), ())), preferred_element_type=jnp.float32
+    gathered_tokens = lax.all_gather(tokens, "dp", axis=0, tiled=False)
+    gathered_ids = lax.all_gather(expert_ids, "dp", axis=0, tiled=False)
+    gathered_slots = lookup(gathered_ids, owner_slot, slot_count).reshape(n_rows, -1)
+    row_slots = 2 * row_id + jnp.arange(2, dtype=jnp.int32)
+    in_row = (gathered_slots[:, :, None] == row_slots[None, None, :]).astype(jnp.int32)
+    row_rank = jnp.cumsum(in_row, axis=1) - in_row
+    picks = (in_row[..., None] == 1) & (
+        row_rank[..., None] == jnp.arange(capacity, dtype=jnp.int32)
+    )
+    picks = jnp.any(picks.reshape(n_rows, tok_count, top_count, 2, capacity), axis=2)
+    arrived = jnp.einsum(
+        "stcr,std->scrd",
+        picks.astype(jnp.bfloat16),
+        gathered_tokens,
+        preferred_element_type=jnp.float32,
     ).astype(jnp.bfloat16)
-    outgoing = outgoing.reshape(n_rows, 2, capacity, model_width)
-    arrived = lax.all_to_all(outgoing, "dp", split_axis=0, concat_axis=0, tiled=True)
     own_rows = jnp.where(upper_half, arrived[:, 1], arrived[:, 0])
     other_rows = jnp.where(upper_half, arrived[:, 0], arrived[:, 1])
     partner = partner_2(other_rows, "shard", partner_bit)

time: 553 us -> 512 us (0.926)
  waiting for transfers between devices: 397 us -> 247 us
  blocking collectives: 52.6 us -> 160 us
  starting transfers between devices: 44.8 us -> 26.4 us
  between operations: 2.13 us -> 15.6 us
    all_gather x0 -> x1, blocking collectives: none -> 105 us  [local(): gathered_ids = lax.all_gather(expert_ids, 'dp', axis=0, tiled=False)]
    all_to_all x1 -> x0, waiting for transfers between devices: 98.7 us -> none  [local(): lax.all_to_all(outgoing, 'dp', split_axis=0, concat_axis=0, tiled=True)]
    all_to_all x1, waiting for transfers between devices: 53.1 us -> 0.01 us  [local(): lax.all_to_all(widen(w_up, half_count), 'shard', split_axis=0, concat_axi...]
    all_to_all x1 -> x0, starting transfers between devices: 10.9 us -> none  [local(): lax.all_to_all(outgoing, 'dp', split_axis=0, concat_axis=0, tiled=True)]
  transfers between devices with their start and end apart: 9 -> 9, of which waited for: 7 -> 5; matrix products, arithmetic and copies ran while one was open for 4% -> 6% of each run, Pallas kernels for 0% -> 0%
where the time goes in v1:
time: 512 us; the launch traced here: 510 us
  waiting for transfers between devices  247 us (48%)
  blocking collectives  160 us (31%)
  matrix products  30.3 us (6%)
  starting transfers between devices  26.4 us (5%)
  local copies, waits for them, and re-layouts  15.8 us (3%)
  between operations  15.6 us (3%)
  other arithmetic  14.8 us (3%)
    ppermute x2, waiting for transfers between devices, partner_2(): lax.ppermute(x, axis, [(i, i ^ 1 << apart) for i in range(lax.axis_size(a...  148 us
    all_gather x1, blocking collectives, local(): gathered_ids = lax.all_gather(expert_ids, 'dp', axis=0, tiled=False)  105 us
    ppermute x3, waiting for transfers between devices, passed_along(): return lax.ppermute(x, axis, [(i, (i + by) % size) for i in range(size)])  98.2 us
    all_to_all x1, blocking collectives, local(): lax.all_to_all(widen(w_gate, half_count), 'shard', split_axis=0, concat_a...  55.3 us
    dot_general x1, matrix products, local(): lax.dot_general(hidden, full_down, (((1,), (1,)), ((), ())), preferred_el...  15.1 us
  transfers between devices with their start and end apart: 9, of which 5 were waited for; matrix products, arithmetic and copies ran while one was open for 6% of the time, Pallas kernels for 0%

profile of v1, /device:TPU:8, one launch (start us, length us, event | category | flops | bytes accessed | tf_op | source)
XLA Modules:
  0.0 510.0 jit_solution(15251958741874217629)
XLA Ops:
  7.2 0.7 all-gather.5.cloned.1.call-update
  7.9 1.6 broadcast_in_dim.72
  9.5 55.3 %all_to_all.32 = bf16[16,128,1024]{2,1,0:T(8,128)(2,1)} all-to-all(bf16[16,128,1024]{2,1,0:T(8,128)(2,1)S(1)} %bitcast.125), channel_id=1, replica_groups=mesh['dp'=16,'shard'=16] {'shard'}, dimensions={0} | all-to-all | bytes 8388608 | tf_op jit(solution)/shard_map/all_to_all | solution.py:47
  64.8 2.5 broadcast_in_dim.73
  67.3 8.1 %all-to-all-start.1 = ((bf16[16,128,1024]{2,1,0:T(8,128)(2,1)}), bf16[16,128,1024]{2,1,0:T(8,128)(2,1)}, u32[]{:S(2)}, u32[]{:S(2)}) async-start(bf16[16,128,1024]{2,1,0:T(8,128)(2,1)} %bitcast.123), calls=%async_computation.1 | async-start | bytes 8388608 | tf_op jit(solution)/shard_map/all_to_all | solution.py:48
  75.4 104.7 %all-gather.2 = s32[16,64,8]{1,2,0:T(8,128)S(1)} all-gather(s32[1,64,8]{1,2,0:T(8,128)S(1)} %bitcast.138), channel_id=2, replica_groups=mesh['dp'=16,'shard'=16] {'dp'}, dimensions={0}, use_global_device_ids=true | all-gather | bytes 34816 | tf_op jit(solution)/shard_map/all_gather | solution.py:69
  180.0 0.1 select_reduce_fusion.2
  180.2 0.7 select_reduce_fusion
  180.9 0.2 copy.80
  181.3 2.3 reduce-window.16
  183.6 0.1 copy.82
  184.0 0.2 copy.87
  184.2 0.2 copy.88
  184.4 0.1 fusion.12
  184.6 1.0 fusion.1
  185.6 5.4 %convolution_convert_fusion = bf16[16,2,32,2048]{3,2,1,0:T(8,128)(2,1)} fusion(pred[16,64,2,32]{1,3,2,0:T(8,128)(4,1)S(1)} %fusion.1, bf16[16,64,2048,1]{2,1,3,0:T(8,128)(2,1)} %bitcast.128), kind=kOutput, calls=%fused_computation.7 | convolution fusion | flops 270532608 | bytes 8454144 | tf_op jit(solution)/shard_map/stcr,std->scrd/dot_general | solution.py:78
  191.1 2.5 broadcast_in_dim.74
  193.5 4.5 all-to-all-start.2
  198.0 2.6 fusion.2
  200.6 0.6 collective-permute-start
  201.2 0.3 copy-done
  201.5 0.2 fusion.3
  201.7 101.0 %collective-permute-done = bf16[16,32,2048]{2,1,0:T(8,128)(2,1)S(1)} collective-permute-done((bf16[16,32,2048]{2,1,0:T(8,128)(2,1)S(1)}, bf16[16,32,2048]{2,1,0:T(8,128)(2,1)S(1)}, u32[]{:S(2)}, u32[]{:S(2)}) %collective-permute-start) | collective-permute-done | bytes 2097184 | tf_op jit(solution)/shard_map/ppermute | solution.py:8
  302.6 0.4 pad_maximum_fusion
  303.0 2.1 copy-done.5
  305.2 1.2 copy-done.4
  306.3 6.0 %fusion.20 = f32[1024,1024]{1,0:T(8,128)} fusion(bf16[1024,2048]{1,0:T(8,128)(2,1)S(1)} %bitcast.129, bf16[2048,1024]{1,0:T(8,128)(2,1)S(1)} %bitcast.127), kind=kOutput, calls=%fused_computation.60 | convolution fusion | flops 4294967296 | bytes 12582912 | tf_op jit(solution)/shard_map/dot_general | solution.py:89
  312.4 15.1 %convolution_convert_fusion.1 = bf16[1024,2048]{1,0:T(8,128)(2,1)} fusion(bf16[2048,1024]{1,0:T(8,128)(2,1)} %bitcast.22, f32[1024,1024]{1,0:T(8,128)} %fusion.20, bf16[1024,2048]{1,0:T(8,128)(2,1)} %bitcast.130, bf16[2048,1024]{1,0:T(8,128)(2,1)} %bitcast.20), kind=kOutput, calls=%fused_computation.8 | convolution fusion | flops 8598323200 | bytes 20971520 | tf_op jit(solution)/shard_map/dot_general | solution.py:92
  327.5 2.7 fusion.19
  330.3 47.2 %collective-permute-done.1 = bf16[16,32,2048]{2,1,0:T(8,128)(2,1)S(1)} collective-permute-done((bf16[16,32,2048]{2,1,0:T(8,128)(2,1)S(1)}, bf16[16,32,2048]{2,1,0:T(8,128)(2,1)S(1)}, u32[]{:S(2)}, u32[]{:S(2)}) %collective-permute-start.1) | collective-permute-done | bytes 2097184 | tf_op jit(solution)/shard_map/ppermute | solution.py:8
  377.5 2.2 maximum_select_fusion
  379.7 5.2 %all-to-all-start.3 = ((bf16[16,2,32,2048]{3,2,1,0:T(8,128)(2,1)}), bf16[16,2,32,2048]{3,2,1,0:T(8,128)(2,1)}, u32[]{:S(2)}, u32[]{:S(2)}) async-start(bf16[16,2,32,2048]{3,2,1,0:T(8,128)(2,1)} %maximum_select_fusion), calls=%async_computation.3 | async-start | bytes 8388608 | tf_op jit(solution)/shard_map/all_to_all | solution.py:97
  384.8 0.6 dynamic_slice.8
  385.4 0.6 dynamic_slice.7
  387.4 3.5 collective-permute-start.2
  390.8 1.5 collective-permute-start.3
  392.4 3.0 collective-permute-start.4
  395.9 1.2 reduce-window.14
  397.0 0.2 slice_reduce_fusion
  397.3 0.1 fusion.16
  397.8 0.7 fusion.5
  398.5 90.4 %collective-permute-done.2 = bf16[128,1024]{1,0:T(8,128)(2,1)S(1)} collective-permute-done((bf16[128,1024]{1,0:T(8,128)(2,1)S(1)}, bf16[128,1024]{1,0:T(8,128)(2,1)S(1)}, u32[]{:S(2)}, u32[]{:S(2)}) %collective-permute-start.2) | collective-permute-done | bytes 262176 | tf_op jit(solution)/shard_map/ppermute | solution.py:13
  489.0 5.6 %collective-permute-done.3 = bf16[128,1024]{1,0:T(8,128)(2,1)S(1)} collective-permute-done((bf16[128,1024]{1,0:T(8,128)(2,1)S(1)}, bf16[128,1024]{1,0:T(8,128)(2,1)S(1)}, u32[]{:S(2)}, u32[]{:S(2)}) %collective-permute-start.3) | collective-permute-done | bytes 262176 | tf_op jit(solution)/shard_map/ppermute | solution.py:13
  494.6 0.8 pad_maximum_fusion.1
  495.5 0.8 pad_maximum_fusion.2
  496.3 2.2 collective-permute-done.4
  498.5 0.8 pad_maximum_fusion.3
  499.4 3.7 convolution_convert_fusion.2
  (52 shorter events, 1.7 us)
Async XLA Ops:
  7.2 178.4 %all-gather.5.cloned.1.call-start = ((), (), s32[]{:S(2)}) async-start(), calls=%async_computation.4 | async-start | bytes 4456448 | tf_op jit(solution)/shard_map/all_gather | solution.py:68
  9.5 55.3 %copy-start.2 = (bf16[2,128,1024]{2,1,0:T(8,128)(2,1)S(1)}, bf16[2,128,1024]{2,1,0:T(8,128)(2,1)}, u32[]{:S(2)}) copy-start(bf16[2,128,1024]{2,1,0:T(8,128)(2,1)} %param.14) | copy-start | bytes 1572868
  67.3 8.1 %copy-start.6 = (s32[64,8]{0,1:T(8,128)S(1)}, s32[64,8]{0,1:T(8,128)}, u32[]{:S(2)}) copy-start(s32[64,8]{0,1:T(8,128)} %param.10) | copy-start | bytes 6148
  67.3 112.8 %copy-start.8 = (s32[32]{0:T(128)S(1)}, s32[32]{0:T(128)}, u32[]{:S(2)}) copy-start(s32[32]{0:T(128)} %param.11) | copy-start | bytes 388
  67.3 123.8 %all-to-all-start.1 = ((bf16[16,128,1024]{2,1,0:T(8,128)(2,1)}), bf16[16,128,1024]{2,1,0:T(8,128)(2,1)}, u32[]{:S(2)}, u32[]{:S(2)}) async-start(bf16[16,128,1024]{2,1,0:T(8,128)(2,1)} %bitcast.123), calls=%async_computation.1 | async-start | bytes 8388608 | tf_op jit(solution)/shard_map/all_to_all | solution.py:48
  185.6 5.5 %copy-start.3 = (bf16[2,128,1024]{2,1,0:T(8,128)(2,1)S(1)}, bf16[2,128,1024]{2,1,0:T(8,128)(2,1)}, u32[]{:S(2)}) copy-start(bf16[2,128,1024]{2,1,0:T(8,128)(2,1)} %param.15) | copy-start | bytes 1572868
  193.5 118.9 %all-to-all-start.2 = ((bf16[16,128,1024]{2,1,0:T(8,128)(2,1)}), bf16[16,128,1024]{2,1,0:T(8,128)(2,1)}, u32[]{:S(2)}, u32[]{:S(2)}) async-start(bf16[16,128,1024]{2,1,0:T(8,128)(2,1)} %bitcast.124), calls=%async_computation.2 | async-start | bytes 8388608 | tf_op jit(solution)/shard_map/all_to_all | solution.py:49
  198.0 3.5 copy-start
  200.6 102.0 %collective-permute-start = (bf16[16,32,2048]{2,1,0:T(8,128)(2,1)S(1)}, bf16[16,32,2048]{2,1,0:T(8,128)(2,1)S(1)}, u32[]{:S(2)}, u32[]{:S(2)}) collective-permute-start(bf16[16,32,2048]{2,1,0:T(8,128)(2,1)S(1)} %fusion.2), channel_id=1, source_target_pairs={{0,8},{1,9},{2,10},{3,11},{4,12},{5,13},{6,14},{7,15},{8,0},{9,1},... | collective-permute-start | bytes 6291464 | tf_op jit(solution)/shard_map/ppermute | solution.py:8
  302.6 3.7 copy-start.4
  303.0 2.1 copy-start.5
  330.2 47.3 %collective-permute-start.1 = (bf16[16,32,2048]{2,1,0:T(8,128)(2,1)S(1)}, bf16[16,32,2048]{2,1,0:T(8,128)(2,1)S(1)}, u32[]{:S(2)}, u32[]{:S(2)}) collective-permute-start(bf16[16,32,2048]{2,1,0:T(8,128)(2,1)S(1)} %bitcast.136), channel_id=1, source_target_pairs={{0,8},{1,9},{2,10},{3,11},{4,12},{5,13},{6,14},{7,15},{8,0},{9,1},... | collective-permute-start | bytes 6291464 | tf_op jit(solution)/shard_map/ppermute | solution.py:8
  379.7 5.8 %copy-start.9 = (s32[32]{0:T(128)S(1)}, s32[32]{0:T(128)}, u32[]{:S(2)}) copy-start(s32[32]{0:T(128)} %param.12) | copy-start | bytes 388
  379.7 7.7 %copy-start.1 = (bf16[2,128,1024]{2,1,0:T(8,128)(2,1)S(1)}, bf16[2,128,1024]{2,1,0:T(8,128)(2,1)}, u32[]{:S(2)}) copy-start(bf16[2,128,1024]{2,1,0:T(8,128)(2,1)} %param.13) | copy-start | bytes 1572868
  379.7 17.9 %copy-start.7 = (f32[64,8]{0,1:T(8,128)S(1)}, f32[64,8]{0,1:T(8,128)}, u32[]{:S(2)}) copy-start(f32[64,8]{0,1:T(8,128)} %param.9) | copy-start | bytes 6148
  379.7 119.7 %all-to-all-start.3 = ((bf16[16,2,32,2048]{3,2,1,0:T(8,128)(2,1)}), bf16[16,2,32,2048]{3,2,1,0:T(8,128)(2,1)}, u32[]{:S(2)}, u32[]{:S(2)}) async-start(bf16[16,2,32,2048]{3,2,1,0:T(8,128)(2,1)} %maximum_select_fusion), calls=%async_computation.3 | async-start | bytes 8388608 | tf_op jit(solution)/shard_map/all_to_all | solution.py:97
  387.4 101.6 %collective-permute-start.2 = (bf16[128,1024]{1,0:T(8,128)(2,1)S(1)}, bf16[128,1024]{1,0:T(8,128)(2,1)S(1)}, u32[]{:S(2)}, u32[]{:S(2)}) collective-permute-start(bf16[128,1024]{1,0:T(8,128)(2,1)S(1)} %bitcast_select_fusion.9), channel_id=1, source_target_pairs={{0,16},{16,32},{32,48},{48,64},{64,80},{80,96},{96,112},{112,128},... | collective-permute-start | bytes 786440 | tf_op jit(solution)/shard_map/ppermute | solution.py:13
  390.8 103.7 %collective-permute-start.3 = (bf16[128,1024]{1,0:T(8,128)(2,1)S(1)}, bf16[128,1024]{1,0:T(8,128)(2,1)S(1)}, u32[]{:S(2)}, u32[]{:S(2)}) collective-permute-start(bf16[128,1024]{1,0:T(8,128)(2,1)S(1)} %bitcast_select_fusion.6), channel_id=1, source_target_pairs={{0,16},{16,32},{32,48},{48,64},{64,80},{80,96},{96,112},{112,128},... | collective-permute-start | bytes 786440 | tf_op jit(solution)/shard_map/ppermute | solution.py:13
  392.4 106.1 %collective-permute-start.4 = (bf16[128,1024]{1,0:T(8,128)(2,1)S(1)}, bf16[128,1024]{1,0:T(8,128)(2,1)S(1)}, u32[]{:S(2)}, u32[]{:S(2)}) collective-permute-start(bf16[128,1024]{1,0:T(8,128)(2,1)S(1)} %bitcast_select_fusion.3), channel_id=1, source_target_pairs={{0,16},{16,32},{32,48},{48,64},{64,80},{80,96},{96,112},{112,128},... | collective-permute-start | bytes 786440 | tf_op jit(solution)/shard_map/ppermute | solution.py:13
Sparse Core Ops, SparseCore 0:
  10.6 114.7 all-gather.4

commit v2 on v1

--- a/solution.py
+++ b/solution.py
@@ -19,7 +19,7 @@
 
 
 def widen(pieces, half_count):
-    return jnp.repeat(pieces, half_count, axis=0)
+    return jnp.tile(pieces, (half_count, 1, 1))
 
 
 def pair_halves(upper_half, own_rows, other_rows):
@@ -36,11 +36,10 @@
     model_width = tokens.shape[1]
     n_shard = lax.axis_size("shard")
     half_count = n_shard // 2
-    partner_bit = n_shard.bit_length() - 2
     column = lax.axis_index("shard")
     row_id = lax.axis_index("dp")
     n_rows = lax.axis_size("dp")
-    upper_half = column >= half_count
+    upper_half = column % 2 == 1
     capacity = max(2, 2 * tok_count * top_count // slot_count)
     places = slot_count * capacity
     full_gate, full_up, full_down = (
@@ -83,7 +82,7 @@
     ).astype(jnp.bfloat16)
     own_rows = jnp.where(upper_half, arrived[:, 1], arrived[:, 0])
     other_rows = jnp.where(upper_half, arrived[:, 0], arrived[:, 1])
-    partner = partner_2(other_rows, "shard", partner_bit)
+    partner = partner_2(other_rows, "shard", 0)
     work_rows = jnp.stack([own_rows, partner], axis=0)
     flat_rows = work_rows.reshape(-1, model_width)
     gate_part = jnp.dot(flat_rows, full_gate, preferred_element_type=jnp.float32)
@@ -93,7 +92,7 @@
         hidden, full_down, (((1,), (1,)), ((), ())), preferred_element_type=jnp.float32
     ).astype(jnp.bfloat16)
     result = result.reshape(2, n_rows, capacity, model_width)
-    returned_other = partner_2(result[1], "shard", partner_bit)
+    returned_other = partner_2(result[1], "shard", 0)
     returned = lax.all_to_all(
         pair_halves(upper_half, result[0], returned_other),
         "dp",

time: 512 us -> 417 us (0.81)
  waiting for transfers between devices: 247 us -> 143 us
  starting transfers between devices: 26.4 us -> 32.3 us
    ppermute x2, waiting for transfers between devices: 148 us -> 7.51 us  [partner_2(): lax.ppermute(x, axis, [(i, i ^ 1 << apart) for i in range(lax.axis_size(a...]
    all_to_all x1, waiting for transfers between devices: 0.01 us -> 34.1 us  [local(): lax.all_to_all(widen(w_down, half_count), 'shard', split_axis=0, concat_a...]
    broadcast_in_dim x3 -> x0, local copies, waits for them, and re-layouts: 6.49 us -> none  [widen(): return jnp.repeat(pieces, half_count, axis=0)]
    another operation x5 -> x8, local copies, waits for them, and re-layouts: 0.22 us -> 6.71 us  [the longest x3 6.49 us: widen(): return jnp.tile(pieces, (half_count, 1, 1))]
    all_to_all x1, starting transfers between devices: 5.18 us -> 11.3 us  [local(): lax.all_to_all(pair_halves(upper_half, result[0], returned_other), 'dp',...]
  transfers between devices with their start and end apart: 9 -> 9, of which waited for: 5 -> 6; matrix products, arithmetic and copies ran while one was open for 6% -> 8% of each run, Pallas kernels for 0% -> 0%
where the time goes in v2:
time: 417 us; the launch traced here: 412 us
  blocking collectives  160 us (38%)
  waiting for transfers between devices  143 us (34%)
  starting transfers between devices  32.3 us (8%)
  matrix products  30.3 us (7%)
  local copies, waits for them, and re-layouts  16.1 us (4%)
  between operations  15.6 us (4%)
  other arithmetic  14.8 us (4%)
    all_gather x1, blocking collectives, local(): gathered_ids = lax.all_gather(expert_ids, 'dp', axis=0, tiled=False)  105 us
    ppermute x3, waiting for transfers between devices, passed_along(): return lax.ppermute(x, axis, [(i, (i + by) % size) for i in range(size)])  101 us
    all_to_all x1, blocking collectives, local(): lax.all_to_all(widen(w_gate, half_count), 'shard', split_axis=0, concat_a...  55.3 us
    all_to_all x1, waiting for transfers between devices, local(): lax.all_to_all(widen(w_down, half_count), 'shard', split_axis=0, concat_a...  34.1 us
    dot_general x1, matrix products, local(): lax.dot_general(hidden, full_down, (((1,), (1,)), ((), ())), preferred_el...  15.1 us
    all_to_all x1, starting transfers between devices, local(): lax.all_to_all(pair_halves(upper_half, result[0], returned_other), 'dp',...  11.3 us
  transfers between devices with their start and end apart: 9, of which 6 were waited for; matrix products, arithmetic and copies ran while one was open for 8% of the time, Pallas kernels for 0%

profile of v2, /device:TPU:8, one launch (start us, length us, event | category | flops | bytes accessed | tf_op | source)
XLA Modules:
  0.0 412.3 jit_solution(6118269516517855737)
XLA Ops:
  7.2 0.7 all-gather.5.cloned.1.call-update
  7.9 1.6 tile.12
  9.5 55.3 %all_to_all.32 = bf16[16,128,1024]{2,1,0:T(8,128)(2,1)} all-to-all(bf16[16,128,1024]{2,1,0:T(8,128)(2,1)S(1)} %bitcast.125), channel_id=1, replica_groups=mesh['dp'=16,'shard'=16] {'shard'}, dimensions={0} | all-to-all | bytes 8388608 | tf_op jit(solution)/shard_map/all_to_all | solution.py:46
  64.8 2.5 tile.14
  67.3 8.1 %all-to-all-start.1 = ((bf16[16,128,1024]{2,1,0:T(8,128)(2,1)}), bf16[16,128,1024]{2,1,0:T(8,128)(2,1)}, u32[]{:S(2)}, u32[]{:S(2)}) async-start(bf16[16,128,1024]{2,1,0:T(8,128)(2,1)} %bitcast.123), calls=%async_computation.1 | async-start | bytes 8388608 | tf_op jit(solution)/shard_map/all_to_all | solution.py:47
  75.4 104.7 %all-gather.2 = s32[16,64,8]{1,2,0:T(8,128)S(1)} all-gather(s32[1,64,8]{1,2,0:T(8,128)S(1)} %bitcast.138), channel_id=2, replica_groups=mesh['dp'=16,'shard'=16] {'dp'}, dimensions={0}, use_global_device_ids=true | all-gather | bytes 34816 | tf_op jit(solution)/shard_map/all_gather | solution.py:68
  180.0 0.1 select_reduce_fusion.2
  180.2 0.7 select_reduce_fusion
  180.9 0.2 copy.80
  181.3 2.3 reduce-window.16
  183.6 0.1 copy.82
  184.0 0.2 copy.87
  184.2 0.2 copy.88
  184.4 0.1 fusion.12
  184.6 1.0 fusion.1
  185.6 5.4 %convolution_convert_fusion = bf16[16,2,32,2048]{3,2,1,0:T(8,128)(2,1)} fusion(pred[16,64,2,32]{1,3,2,0:T(8,128)(4,1)S(1)} %fusion.1, bf16[16,64,2048,1]{2,1,3,0:T(8,128)(2,1)} %bitcast.128), kind=kOutput, calls=%fused_computation.7 | convolution fusion | flops 270532608 | bytes 8454144 | tf_op jit(solution)/shard_map/stcr,std->scrd/dot_general | solution.py:77
  191.1 2.5 tile.31
  193.5 4.5 %all-to-all-start.2 = ((bf16[16,128,1024]{2,1,0:T(8,128)(2,1)}), bf16[16,128,1024]{2,1,0:T(8,128)(2,1)}, u32[]{:S(2)}, u32[]{:S(2)}) async-start(bf16[16,128,1024]{2,1,0:T(8,128)(2,1)} %bitcast.124), calls=%async_computation.2 | async-start | bytes 8388608 | tf_op jit(solution)/shard_map/all_to_all | solution.py:48
  198.0 2.6 fusion.2
  200.6 0.3 collective-permute-start
  200.9 0.6 copy-done
  201.4 0.2 fusion.3
  201.7 3.4 collective-permute-done
  205.0 0.4 pad_maximum_fusion
  205.4 2.1 copy-done.5
  207.6 1.2 copy-done.4
  208.7 6.0 %fusion.20 = f32[1024,1024]{1,0:T(8,128)} fusion(bf16[1024,2048]{1,0:T(8,128)(2,1)S(1)} %bitcast.129, bf16[2048,1024]{1,0:T(8,128)(2,1)S(1)} %bitcast.127), kind=kOutput, calls=%fused_computation.60 | convolution fusion | flops 4294967296 | bytes 12582912 | tf_op jit(solution)/shard_map/dot_general | solution.py:88
  214.8 34.1 %all-to-all-done.2 = bf16[16,128,1024]{2,1,0:T(8,128)(2,1)} async-done(((bf16[16,128,1024]{2,1,0:T(8,128)(2,1)}), bf16[16,128,1024]{2,1,0:T(8,128)(2,1)}, u32[]{:S(2)}, u32[]{:S(2)}) %all-to-all-start.2) | async-done | bytes 4194336 | tf_op jit(solution)/shard_map/all_to_all | solution.py:48
  248.9 15.1 %convolution_convert_fusion.1 = bf16[1024,2048]{1,0:T(8,128)(2,1)} fusion(bf16[2048,1024]{1,0:T(8,128)(2,1)} %bitcast.22, f32[1024,1024]{1,0:T(8,128)} %fusion.20, bf16[1024,2048]{1,0:T(8,128)(2,1)} %bitcast.130, bf16[2048,1024]{1,0:T(8,128)(2,1)} %bitcast.20), kind=kOutput, calls=%fused_computation.8 | convolution fusion | flops 8598323200 | bytes 20971520 | tf_op jit(solution)/shard_map/dot_general | solution.py:91
  264.0 2.7 fusion.19
  266.8 4.1 %collective-permute-done.1 = bf16[16,32,2048]{2,1,0:T(8,128)(2,1)S(1)} collective-permute-done((bf16[16,32,2048]{2,1,0:T(8,128)(2,1)S(1)}, bf16[16,32,2048]{2,1,0:T(8,128)(2,1)S(1)}, u32[]{:S(2)}, u32[]{:S(2)}) %collective-permute-start.1) | collective-permute-done | bytes 2097184 | tf_op jit(solution)/shard_map/ppermute | solution.py:8
  271.0 2.2 maximum_select_fusion
  273.1 11.3 %all-to-all-start.3 = ((bf16[16,2,32,2048]{3,2,1,0:T(8,128)(2,1)}), bf16[16,2,32,2048]{3,2,1,0:T(8,128)(2,1)}, u32[]{:S(2)}, u32[]{:S(2)}) async-start(bf16[16,2,32,2048]{3,2,1,0:T(8,128)(2,1)} %maximum_select_fusion), calls=%async_computation.3 | async-start | bytes 8388608 | tf_op jit(solution)/shard_map/all_to_all | solution.py:96
  284.5 0.6 dynamic_slice.8
  285.1 0.6 dynamic_slice.7
  287.0 3.5 collective-permute-start.2
  290.5 1.5 collective-permute-start.3
  292.1 3.0 collective-permute-start.4
  295.5 1.2 reduce-window.14
  296.7 0.2 slice_reduce_fusion
  297.4 0.7 fusion.5
  298.2 92.4 %collective-permute-done.2 = bf16[128,1024]{1,0:T(8,128)(2,1)S(1)} collective-permute-done((bf16[128,1024]{1,0:T(8,128)(2,1)S(1)}, bf16[128,1024]{1,0:T(8,128)(2,1)S(1)}, u32[]{:S(2)}, u32[]{:S(2)}) %collective-permute-start.2) | collective-permute-done | bytes 262176 | tf_op jit(solution)/shard_map/ppermute | solution.py:13
  390.6 5.6 %collective-permute-done.3 = bf16[128,1024]{1,0:T(8,128)(2,1)S(1)} collective-permute-done((bf16[128,1024]{1,0:T(8,128)(2,1)S(1)}, bf16[128,1024]{1,0:T(8,128)(2,1)S(1)}, u32[]{:S(2)}, u32[]{:S(2)}) %collective-permute-start.3) | collective-permute-done | bytes 262176 | tf_op jit(solution)/shard_map/ppermute | solution.py:13
  396.3 0.8 pad_maximum_fusion.1
  397.1 0.8 pad_maximum_fusion.2
  397.9 2.9 collective-permute-done.4
  400.9 0.8 pad_maximum_fusion.3
  401.7 3.7 convolution_convert_fusion.2
  (52 shorter events, 1.8 us)
Async XLA Ops:
  7.2 178.4 %all-gather.5.cloned.1.call-start = ((), (), s32[]{:S(2)}) async-start(), calls=%async_computation.4 | async-start | bytes 4456448 | tf_op jit(solution)/shard_map/all_gather | solution.py:67
  9.5 55.3 %copy-start.2 = (bf16[2,128,1024]{2,1,0:T(8,128)(2,1)S(1)}, bf16[2,128,1024]{2,1,0:T(8,128)(2,1)}, u32[]{:S(2)}) copy-start(bf16[2,128,1024]{2,1,0:T(8,128)(2,1)} %param.14) | copy-start | bytes 1572868
  67.3 8.1 %copy-start.6 = (s32[64,8]{0,1:T(8,128)S(1)}, s32[64,8]{0,1:T(8,128)}, u32[]{:S(2)}) copy-start(s32[64,8]{0,1:T(8,128)} %param.10) | copy-start | bytes 6148
  67.3 112.8 %copy-start.8 = (s32[32]{0:T(128)S(1)}, s32[32]{0:T(128)}, u32[]{:S(2)}) copy-start(s32[32]{0:T(128)} %param.11) | copy-start | bytes 388
  67.3 123.8 %all-to-all-start.1 = ((bf16[16,128,1024]{2,1,0:T(8,128)(2,1)}), bf16[16,128,1024]{2,1,0:T(8,128)(2,1)}, u32[]{:S(2)}, u32[]{:S(2)}) async-start(bf16[16,128,1024]{2,1,0:T(8,128)(2,1)} %bitcast.123), calls=%async_computation.1 | async-start | bytes 8388608 | tf_op jit(solution)/shard_map/all_to_all | solution.py:47
  185.6 5.5 %copy-start.3 = (bf16[2,128,1024]{2,1,0:T(8,128)(2,1)S(1)}, bf16[2,128,1024]{2,1,0:T(8,128)(2,1)}, u32[]{:S(2)}) copy-start(bf16[2,128,1024]{2,1,0:T(8,128)(2,1)} %param.15) | copy-start | bytes 1572868
  193.5 55.4 %all-to-all-start.2 = ((bf16[16,128,1024]{2,1,0:T(8,128)(2,1)}), bf16[16,128,1024]{2,1,0:T(8,128)(2,1)}, u32[]{:S(2)}, u32[]{:S(2)}) async-start(bf16[16,128,1024]{2,1,0:T(8,128)(2,1)} %bitcast.124), calls=%async_computation.2 | async-start | bytes 8388608 | tf_op jit(solution)/shard_map/all_to_all | solution.py:48
  198.0 3.5 copy-start
  200.6 4.4 %collective-permute-start = (bf16[16,32,2048]{2,1,0:T(8,128)(2,1)S(1)}, bf16[16,32,2048]{2,1,0:T(8,128)(2,1)S(1)}, u32[]{:S(2)}, u32[]{:S(2)}) collective-permute-start(bf16[16,32,2048]{2,1,0:T(8,128)(2,1)S(1)} %fusion.2), channel_id=1, source_target_pairs={{0,1},{1,0},{2,3},{3,2},{4,5},{5,4},{6,7},{7,6},{8,9},{9,8},{10,11... | collective-permute-start | bytes 6291464 | tf_op jit(solution)/shard_map/ppermute | solution.py:8
  205.0 3.7 copy-start.4
  205.4 2.1 copy-start.5
  266.7 4.2 %collective-permute-start.1 = (bf16[16,32,2048]{2,1,0:T(8,128)(2,1)S(1)}, bf16[16,32,2048]{2,1,0:T(8,128)(2,1)S(1)}, u32[]{:S(2)}, u32[]{:S(2)}) collective-permute-start(bf16[16,32,2048]{2,1,0:T(8,128)(2,1)S(1)} %bitcast.136), channel_id=1, source_target_pairs={{0,1},{1,0},{2,3},{3,2},{4,5},{5,4},{6,7},{7,6},{8,9},{9,8},{10,11... | collective-permute-start | bytes 6291464 | tf_op jit(solution)/shard_map/ppermute | solution.py:8
  273.1 11.9 %copy-start.9 = (s32[32]{0:T(128)S(1)}, s32[32]{0:T(128)}, u32[]{:S(2)}) copy-start(s32[32]{0:T(128)} %param.12) | copy-start | bytes 388
  273.1 13.8 %copy-start.1 = (bf16[2,128,1024]{2,1,0:T(8,128)(2,1)S(1)}, bf16[2,128,1024]{2,1,0:T(8,128)(2,1)}, u32[]{:S(2)}) copy-start(bf16[2,128,1024]{2,1,0:T(8,128)(2,1)} %param.13) | copy-start | bytes 1572868
  273.1 24.1 %copy-start.7 = (f32[64,8]{0,1:T(8,128)S(1)}, f32[64,8]{0,1:T(8,128)}, u32[]{:S(2)}) copy-start(f32[64,8]{0,1:T(8,128)} %param.9) | copy-start | bytes 6148
  273.1 128.6 %all-to-all-start.3 = ((bf16[16,2,32,2048]{3,2,1,0:T(8,128)(2,1)}), bf16[16,2,32,2048]{3,2,1,0:T(8,128)(2,1)}, u32[]{:S(2)}, u32[]{:S(2)}) async-start(bf16[16,2,32,2048]{3,2,1,0:T(8,128)(2,1)} %maximum_select_fusion), calls=%async_computation.3 | async-start | bytes 8388608 | tf_op jit(solution)/shard_map/all_to_all | solution.py:96
  287.0 103.6 %collective-permute-start.2 = (bf16[128,1024]{1,0:T(8,128)(2,1)S(1)}, bf16[128,1024]{1,0:T(8,128)(2,1)S(1)}, u32[]{:S(2)}, u32[]{:S(2)}) collective-permute-start(bf16[128,1024]{1,0:T(8,128)(2,1)S(1)} %bitcast_select_fusion.9), channel_id=1, source_target_pairs={{0,16},{16,32},{32,48},{48,64},{64,80},{80,96},{96,112},{112,128},... | collective-permute-start | bytes 786440 | tf_op jit(solution)/shard_map/ppermute | solution.py:13
  290.5 105.7 %collective-permute-start.3 = (bf16[128,1024]{1,0:T(8,128)(2,1)S(1)}, bf16[128,1024]{1,0:T(8,128)(2,1)S(1)}, u32[]{:S(2)}, u32[]{:S(2)}) collective-permute-start(bf16[128,1024]{1,0:T(8,128)(2,1)S(1)} %bitcast_select_fusion.6), channel_id=1, source_target_pairs={{0,16},{16,32},{32,48},{48,64},{64,80},{80,96},{96,112},{112,128},... | collective-permute-start | bytes 786440 | tf_op jit(solution)/shard_map/ppermute | solution.py:13
  292.1 108.8 %collective-permute-start.4 = (bf16[128,1024]{1,0:T(8,128)(2,1)S(1)}, bf16[128,1024]{1,0:T(8,128)(2,1)S(1)}, u32[]{:S(2)}, u32[]{:S(2)}) collective-permute-start(bf16[128,1024]{1,0:T(8,128)(2,1)S(1)} %bitcast_select_fusion.3), channel_id=1, source_target_pairs={{0,16},{16,32},{32,48},{48,64},{64,80},{80,96},{96,112},{112,128},... | collective-permute-start | bytes 786440 | tf_op jit(solution)/shard_map/ppermute | solution.py:13
Sparse Core Ops, SparseCore 0:
  10.6 114.7 all-gather.4

commit v3 on v2

--- a/solution.py
+++ b/solution.py
@@ -58,22 +58,31 @@
     gate_weights = (router_probs / jnp.sum(router_probs, axis=1, keepdims=True)).astype(
         jnp.bfloat16
     )
-    flat_slots = slot_ids.reshape(-1)
-    members = (flat_slots[:, None] == slot_index[None, :]).astype(jnp.int32)
-    earlier = jnp.cumsum(members, axis=0) - members
-    slot_rank = jnp.sum(earlier * members, axis=1)
-    position = (flat_slots * capacity + slot_rank).reshape(tok_count, top_count)
-    matches = position[:, :, None] == jnp.arange(places, dtype=jnp.int32)[None, None, :]
-    gathered_tokens = lax.all_gather(tokens, "dp", axis=0, tiled=False)
-    gathered_ids = lax.all_gather(expert_ids, "dp", axis=0, tiled=False)
-    gathered_slots = lookup(gathered_ids, owner_slot, slot_count).reshape(n_rows, -1)
+    side = jnp.concatenate(
+        [
+            slot_ids.astype(jnp.bfloat16),
+            gate_weights,
+            jnp.zeros((tok_count, 128 - 2 * top_count), jnp.bfloat16),
+        ],
+        axis=1,
+    )
+    gathered = lax.all_gather(jnp.concatenate([tokens, side], axis=1), "dp", axis=0, tiled=False)
+    gathered_tokens = gathered[..., :model_width]
+    gathered_slots = (
+        gathered[..., model_width : model_width + top_count].astype(jnp.int32).reshape(n_rows, -1)
+    )
+    gathered_gates = gathered[..., model_width + top_count : model_width + 2 * top_count]
     row_slots = 2 * row_id + jnp.arange(2, dtype=jnp.int32)
     in_row = (gathered_slots[:, :, None] == row_slots[None, None, :]).astype(jnp.int32)
     row_rank = jnp.cumsum(in_row, axis=1) - in_row
     picks = (in_row[..., None] == 1) & (
         row_rank[..., None] == jnp.arange(capacity, dtype=jnp.int32)
     )
-    picks = jnp.any(picks.reshape(n_rows, tok_count, top_count, 2, capacity), axis=2)
+    picks = picks.reshape(n_rows, tok_count, top_count, 2, capacity)
+    weights = jnp.sum(
+        jnp.where(picks, gathered_gates[..., None, None], jnp.zeros((), jnp.bfloat16)), axis=2
+    )
+    picks = jnp.any(picks, axis=2)
     arrived = jnp.einsum(
         "stcr,std->scrd",
         picks.astype(jnp.bfloat16),
@@ -93,19 +102,13 @@
     ).astype(jnp.bfloat16)
     result = result.reshape(2, n_rows, capacity, model_width)
     returned_other = partner_2(result[1], "shard", 0)
-    returned = lax.all_to_all(
+    partial = jnp.einsum(
+        "stcr,scrd->std",
+        weights,
         pair_halves(upper_half, result[0], returned_other),
-        "dp",
-        split_axis=0,
-        concat_axis=0,
-        tiled=True,
-    )
-    combine = jnp.sum(
-        jnp.where(matches, gate_weights[:, :, None], jnp.zeros((), jnp.bfloat16)), axis=1
-    )
-    moe_output = jnp.dot(
-        combine, returned.reshape(places, model_width), preferred_element_type=jnp.float32
+        preferred_element_type=jnp.float32,
     ).astype(jnp.bfloat16)
+    moe_output = lax.psum_scatter(partial, "dp", scatter_dimension=0, tiled=True)[0]
     base_slot = 2 * row_id
     second_old = lax.dynamic_index_in_dim(old_place, base_slot + 1, 0, keepdims=False)
     second_new = lax.dynamic_index_in_dim(new_place, base_slot + 1, 0, keepdims=False)

time: 417 us -> 477 us (1.14)
  waiting for transfers between devices: 143 us -> 311 us
  blocking collectives: 160 us -> 55.5 us
  starting transfers between devices: 32.3 us -> 24.3 us
    reduce_scatter x0 -> x1, waiting for transfers between devices: none -> 188 us  [local(): lax.psum_scatter(partial, 'dp', scatter_dimension=0, tiled=True)[0]]
    all_gather x1 -> x0, blocking collectives: 105 us -> none  [local(): gathered_ids = lax.all_gather(expert_ids, 'dp', axis=0, tiled=False)]
    ppermute x3, waiting for transfers between devices: 101 us -> 20.2 us  [passed_along(): return lax.ppermute(x, axis, [(i, (i + by) % size) for i in range(size)])]
    all_gather x1, waiting for transfers between devices: 0.02 us -> 49.8 us  [local(): lax.all_gather(jnp.concatenate([tokens, side], axis=1), 'dp', axis=0, til...]
    all_to_all x1, waiting for transfers between devices: 0.01 us -> 42.5 us  [local(): lax.all_to_all(widen(w_up, half_count), 'shard', split_axis=0, concat_axi...]
    all_to_all x2 -> x1, waiting for transfers between devices: 34.1 us -> 6.24 us  [local(): lax.all_to_all(widen(w_gate, half_count), 'shard', split_axis=0, concat_a...]
    all_to_all x2 -> x1, starting transfers between devices: 15.8 us -> 8.65 us  [local(): lax.all_to_all(widen(w_gate, half_count), 'shard', split_axis=0, concat_a...]
  transfers between devices with their start and end apart: 9 -> 9, of which waited for: 6 -> 9; matrix products, arithmetic and copies ran while one was open for 8% -> 7% of each run, Pallas kernels for 0% -> 0%
where the time goes in v3:
time: 477 us; the launch traced here: 476 us
  waiting for transfers between devices  311 us (65%)
  blocking collectives  55.5 us (12%)
  matrix products  34.2 us (7%)
  starting transfers between devices  24.3 us (5%)
  local copies, waits for them, and re-layouts  20.4 us (4%)
  between operations  15.5 us (3%)
  other arithmetic  14.8 us (3%)
    reduce_scatter x1, waiting for transfers between devices, local(): lax.psum_scatter(partial, 'dp', scatter_dimension=0, tiled=True)[0]  188 us
    all_to_all x1, blocking collectives, local(): lax.all_to_all(widen(w_down, half_count), 'shard', split_axis=0, concat_a...  55.5 us
    all_gather x1, waiting for transfers between devices, local(): lax.all_gather(jnp.concatenate([tokens, side], axis=1), 'dp', axis=0, til...  49.8 us
    all_to_all x1, waiting for transfers between devices, local(): lax.all_to_all(widen(w_up, half_count), 'shard', split_axis=0, concat_axi...  42.5 us
    ppermute x3, waiting for transfers between devices, passed_along(): return lax.ppermute(x, axis, [(i, (i + by) % size) for i in range(size)])  20.2 us
    dot_general x1, matrix products, local(): lax.dot_general(hidden, full_down, (((1,), (1,)), ((), ())), preferred_el...  15.2 us
  transfers between devices with their start and end apart: 9, of which 9 were waited for; matrix products, arithmetic and copies ran while one was open for 7% of the time, Pallas kernels for 0%

profile of v3, /device:TPU:8, one launch (start us, length us, event | category | flops | bytes accessed | tf_op | source)
XLA Modules:
  0.0 476.2 jit_solution(18302798292876203175)
XLA Ops:
  7.2 0.8 select_reduce_fusion.1
  8.0 0.8 select_reduce_fusion
  8.9 0.7 reduce_sum.41
  9.6 0.7 divide_convert_fusion
  10.4 1.8 concatenate.3
  12.2 1.6 tile.31
  13.8 55.5 %all_to_all.12 = bf16[16,128,1024]{2,1,0:T(8,128)(2,1)} all-to-all(bf16[16,128,1024]{2,1,0:T(8,128)(2,1)S(1)} %bitcast.109), channel_id=1, replica_groups=mesh['dp'=16,'shard'=16] {'shard'}, dimensions={0} | all-to-all | bytes 8388608 | tf_op jit(solution)/shard_map/all_to_all | solution.py:48
  69.3 2.5 tile.12
  71.7 8.7 %all-to-all-start = ((bf16[16,128,1024]{2,1,0:T(8,128)(2,1)}), bf16[16,128,1024]{2,1,0:T(8,128)(2,1)}, u32[]{:S(2)}, u32[]{:S(2)}) async-start(bf16[16,128,1024]{2,1,0:T(8,128)(2,1)} %bitcast.107), calls=%async_computation | async-start | bytes 8388608 | tf_op jit(solution)/shard_map/all_to_all | solution.py:46
  80.4 49.8 %all-gather.3.cloned.1.call-done = bf16[1024,2176]{1,0:T(8,128)(2,1)} async-done(((bf16[64,2176]{1,0:T(8,128)(2,1)}), bf16[1024,2176]{1,0:T(8,128)(2,1)}) %all-gather.3.cloned.1.call-update) | async-done | bytes 4456464 | tf_op jit(solution)/shard_map/all_gather | solution.py:69
  130.2 1.2 fusion.24
  132.0 2.3 reduce-window.6
  134.6 0.2 copy.104
  134.8 0.2 copy.105
  135.3 0.6 copy-done.5
  135.9 1.0 fusion.7
  136.9 5.4 %fusion.10 = bf16[16,2,32,2048]{3,2,1,0:T(8,128)(2,1)} fusion(pred[16,64,2,32]{1,3,2,0:T(8,128)(4,1)S(1)} %fusion.7, bf16[16,64,2176]{2,1,0:T(8,128)(2,1)} %bitcast.111), kind=kOutput, calls=%fused_computation.17 | convolution fusion | flops 270532608 | bytes 8454144 | tf_op jit(solution)/shard_map/stcr,std->scrd/dot_general | solution.py:86
  142.3 6.2 %all-to-all-done = bf16[16,128,1024]{2,1,0:T(8,128)(2,1)} async-done(((bf16[16,128,1024]{2,1,0:T(8,128)(2,1)}), bf16[16,128,1024]{2,1,0:T(8,128)(2,1)}, u32[]{:S(2)}, u32[]{:S(2)}) %all-to-all-start) | async-done | bytes 4194336 | tf_op jit(solution)/shard_map/all_to_all | solution.py:46
  148.5 2.5 tile.14
  151.0 7.3 %all-to-all-start.1 = ((bf16[16,128,1024]{2,1,0:T(8,128)(2,1)}), bf16[16,128,1024]{2,1,0:T(8,128)(2,1)}, u32[]{:S(2)}, u32[]{:S(2)}) async-start(bf16[16,128,1024]{2,1,0:T(8,128)(2,1)} %bitcast.108), calls=%async_computation.1 | async-start | bytes 8388608 | tf_op jit(solution)/shard_map/all_to_all | solution.py:47
  158.3 2.6 fusion.11
  161.0 0.4 collective-permute-start
  161.4 0.4 copy-done
  161.8 0.2 fusion.13
  162.0 3.4 collective-permute-done
  165.4 0.4 pad_maximum_fusion
  165.8 1.9 copy-done.4
  167.7 8.2 %fusion.26 = f32[1024,1024]{1,0:T(8,128)} fusion(bf16[1024,2048]{1,0:T(8,128)(2,1)S(1)} %bitcast.113, bf16[2048,1024]{1,0:T(8,128)(2,1)} %bitcast.16), kind=kOutput, calls=%fused_computation.57 | convolution fusion | flops 4294967296 | bytes 12582912 | tf_op jit(solution)/shard_map/dot_general | solution.py:97
  175.9 42.5 %all-to-all-done.1 = bf16[16,128,1024]{2,1,0:T(8,128)(2,1)} async-done(((bf16[16,128,1024]{2,1,0:T(8,128)(2,1)}), bf16[16,128,1024]{2,1,0:T(8,128)(2,1)}, u32[]{:S(2)}, u32[]{:S(2)}) %all-to-all-start.1) | async-done | bytes 4194336 | tf_op jit(solution)/shard_map/all_to_all | solution.py:47
  218.4 15.2 %convolution_convert_fusion = bf16[1024,2048]{1,0:T(8,128)(2,1)} fusion(bf16[2048,1024]{1,0:T(8,128)(2,1)} %bitcast.112, f32[1024,1024]{1,0:T(8,128)} %fusion.26, bf16[1024,2048]{1,0:T(8,128)(2,1)} %bitcast.114, bf16[2048,1024]{1,0:T(8,128)(2,1)} %bitcast.18), kind=kOutput, calls=%fused_computation.18 | convolution fusion | flops 8598323200 | bytes 20971520 | tf_op jit(solution)/shard_map/dot_general | solution.py:100
  233.6 4.0 fusion.25
  237.6 0.7 copy.106
  238.3 2.2 fusion.12
  240.6 1.5 collective-permute-done.1
  242.1 5.5 %bitcast_convert_fusion = bf16[16,64,2048]{2,1,0:T(8,128)(2,1)} fusion(bf16[16,64,2,32]{1,3,2,0:T(8,128)(2,1)S(1)} %fusion.12, bf16[16,1,32,2048]{3,2,1,0:T(8,128)(2,1)S(1)} %bitcast.118, bf16[16,1,32,2048]{3,2,1,0:T(8,128)(2,1)} %bitcast.22, pred[]{:T(512)S(6)} %eq.116), kind=kOutput, calls=%fused_computation | convolution fusion | flops 276824064 | bytes 8519681 | tf_op jit(solution)/shard_map/stcr,scrd->std/dot_general | solution.py:105
  247.6 0.6 copy-done.6
  248.2 0.6 dynamic_slice.8
  248.8 0.6 dynamic_slice.7
  250.7 2.9 collective-permute-start.2
  253.6 2.2 collective-permute-start.3
  255.9 2.8 collective-permute-start.4
  258.7 7.2 %collective-permute-done.2 = bf16[128,1024]{1,0:T(8,128)(2,1)S(1)} collective-permute-done((bf16[128,1024]{1,0:T(8,128)(2,1)S(1)}, bf16[128,1024]{1,0:T(8,128)(2,1)S(1)}, u32[]{:S(2)}, u32[]{:S(2)}) %collective-permute-start.2) | collective-permute-done | bytes 262176 | tf_op jit(solution)/shard_map/ppermute | solution.py:13
  265.9 7.1 %collective-permute-done.3 = bf16[128,1024]{1,0:T(8,128)(2,1)S(1)} collective-permute-done((bf16[128,1024]{1,0:T(8,128)(2,1)S(1)}, bf16[128,1024]{1,0:T(8,128)(2,1)S(1)}, u32[]{:S(2)}, u32[]{:S(2)}) %collective-permute-start.3) | collective-permute-done | bytes 262176 | tf_op jit(solution)/shard_map/ppermute | solution.py:13
  273.1 0.8 pad_maximum_fusion.1
  273.9 0.8 pad_maximum_fusion.2
  274.7 6.0 %collective-permute-done.4 = bf16[128,1024]{1,0:T(8,128)(2,1)S(1)} collective-permute-done((bf16[128,1024]{1,0:T(8,128)(2,1)S(1)}, bf16[128,1024]{1,0:T(8,128)(2,1)S(1)}, u32[]{:S(2)}, u32[]{:S(2)}) %collective-permute-start.4) | collective-permute-done | bytes 262176 | tf_op jit(solution)/shard_map/ppermute | solution.py:13
  280.8 0.8 pad_maximum_fusion.3
  281.6 187.7 %reduce-scatter.2.cloned.1.call-done = bf16[1,64,2048]{2,1,0:T(8,128)(2,1)} async-done(((bf16[16,64,2048]{2,1,0:T(8,128)(2,1)}), bf16[1,64,2048]{2,1,0:T(8,128)(2,1)}) %reduce-scatter.2.cloned.1.call-update) | async-done | bytes 262160 | tf_op jit(solution)/shard_map/reduce_scatter | solution.py:111
  (41 shorter events, 1.7 us)
Async XLA Ops:
  7.2 123.0 %all-gather.3.cloned.1.call-start = ((), (), s32[]{:S(2)}) async-start(), calls=%async_computation.5 | async-start | bytes 4734976 | tf_op jit(solution)/shard_map/all_gather | solution.py:69
  13.7 55.5 %copy-start.1 = (bf16[2,128,1024]{2,1,0:T(8,128)(2,1)S(1)}, bf16[2,128,1024]{2,1,0:T(8,128)(2,1)}, u32[]{:S(2)}) copy-start(bf16[2,128,1024]{2,1,0:T(8,128)(2,1)} %param.13) | copy-start | bytes 1572868
  71.7 76.8 %all-to-all-start = ((bf16[16,128,1024]{2,1,0:T(8,128)(2,1)}), bf16[16,128,1024]{2,1,0:T(8,128)(2,1)}, u32[]{:S(2)}, u32[]{:S(2)}) async-start(bf16[16,128,1024]{2,1,0:T(8,128)(2,1)} %bitcast.107), calls=%async_computation | async-start | bytes 8388608 | tf_op jit(solution)/shard_map/all_to_all | solution.py:46
  135.2 0.6 copy-start.5
  136.9 11.7 %copy-start.2 = (bf16[2,128,1024]{2,1,0:T(8,128)(2,1)S(1)}, bf16[2,128,1024]{2,1,0:T(8,128)(2,1)}, u32[]{:S(2)}) copy-start(bf16[2,128,1024]{2,1,0:T(8,128)(2,1)} %param.14) | copy-start | bytes 1572868
  151.0 67.4 %all-to-all-start.1 = ((bf16[16,128,1024]{2,1,0:T(8,128)(2,1)}), bf16[16,128,1024]{2,1,0:T(8,128)(2,1)}, u32[]{:S(2)}, u32[]{:S(2)}) async-start(bf16[16,128,1024]{2,1,0:T(8,128)(2,1)} %bitcast.108), calls=%async_computation.1 | async-start | bytes 8388608 | tf_op jit(solution)/shard_map/all_to_all | solution.py:47
  158.3 311.0 %reduce-scatter.2.cloned.1.call-start = ((), (), s32[]{:S(2)}) async-start(), calls=%async_computation.4 | async-start | bytes 4456448 | tf_op jit(solution)/shard_map/reduce_scatter | solution.py:111
  158.3 3.5 copy-start
  161.0 4.4 collective-permute-start
  165.8 1.9 copy-start.4
  237.6 4.5 collective-permute-start.1
  247.5 0.7 copy-start.6
  247.5 1.2 copy-start.7
  247.6 8.3 %copy-start.3 = (bf16[2,128,1024]{2,1,0:T(8,128)(2,1)S(1)}, bf16[2,128,1024]{2,1,0:T(8,128)(2,1)}, u32[]{:S(2)}) copy-start(bf16[2,128,1024]{2,1,0:T(8,128)(2,1)} %param.15) | copy-start | bytes 1572868
  250.7 15.2 %collective-permute-start.2 = (bf16[128,1024]{1,0:T(8,128)(2,1)S(1)}, bf16[128,1024]{1,0:T(8,128)(2,1)S(1)}, u32[]{:S(2)}, u32[]{:S(2)}) collective-permute-start(bf16[128,1024]{1,0:T(8,128)(2,1)S(1)} %bitcast_select_fusion.9), channel_id=1, source_target_pairs={{0,16},{16,32},{32,48},{48,64},{64,80},{80,96},{96,112},{112,128},... | collective-permute-start | bytes 786440 | tf_op jit(solution)/shard_map/ppermute | solution.py:13
  253.6 19.4 %collective-permute-start.3 = (bf16[128,1024]{1,0:T(8,128)(2,1)S(1)}, bf16[128,1024]{1,0:T(8,128)(2,1)S(1)}, u32[]{:S(2)}, u32[]{:S(2)}) collective-permute-start(bf16[128,1024]{1,0:T(8,128)(2,1)S(1)} %bitcast_select_fusion.6), channel_id=1, source_target_pairs={{0,16},{16,32},{32,48},{48,64},{64,80},{80,96},{96,112},{112,128},... | collective-permute-start | bytes 786440 | tf_op jit(solution)/shard_map/ppermute | solution.py:13
  255.9 24.8 %collective-permute-start.4 = (bf16[128,1024]{1,0:T(8,128)(2,1)S(1)}, bf16[128,1024]{1,0:T(8,128)(2,1)S(1)}, u32[]{:S(2)}, u32[]{:S(2)}) collective-permute-start(bf16[128,1024]{1,0:T(8,128)(2,1)S(1)} %bitcast_select_fusion.3), channel_id=1, source_target_pairs={{0,16},{16,32},{32,48},{48,64},{64,80},{80,96},{96,112},{112,128},... | collective-permute-start | bytes 786440 | tf_op jit(solution)/shard_map/ppermute | solution.py:13
Sparse Core Ops, SparseCore 0:
  12.3 117.8 all-gather.2
  247.7 221.5 reduce-scatter.1

commit v4 on v3

--- a/solution.py
+++ b/solution.py
@@ -61,8 +61,7 @@
     side = jnp.concatenate(
         [
             slot_ids.astype(jnp.bfloat16),
-            gate_weights,
-            jnp.zeros((tok_count, 128 - 2 * top_count), jnp.bfloat16),
+            jnp.zeros((tok_count, 128 - top_count), jnp.bfloat16),
         ],
         axis=1,
     )
@@ -71,7 +70,6 @@
     gathered_slots = (
         gathered[..., model_width : model_width + top_count].astype(jnp.int32).reshape(n_rows, -1)
     )
-    gathered_gates = gathered[..., model_width + top_count : model_width + 2 * top_count]
     row_slots = 2 * row_id + jnp.arange(2, dtype=jnp.int32)
     in_row = (gathered_slots[:, :, None] == row_slots[None, None, :]).astype(jnp.int32)
     row_rank = jnp.cumsum(in_row, axis=1) - in_row
@@ -79,9 +77,6 @@
         row_rank[..., None] == jnp.arange(capacity, dtype=jnp.int32)
     )
     picks = picks.reshape(n_rows, tok_count, top_count, 2, capacity)
-    weights = jnp.sum(
-        jnp.where(picks, gathered_gates[..., None, None], jnp.zeros((), jnp.bfloat16)), axis=2
-    )
     picks = jnp.any(picks, axis=2)
     arrived = jnp.einsum(
         "stcr,std->scrd",
@@ -102,13 +97,25 @@
     ).astype(jnp.bfloat16)
     result = result.reshape(2, n_rows, capacity, model_width)
     returned_other = partner_2(result[1], "shard", 0)
-    partial = jnp.einsum(
-        "stcr,scrd->std",
-        weights,
+    returned = lax.all_to_all(
         pair_halves(upper_half, result[0], returned_other),
-        preferred_element_type=jnp.float32,
+        "dp",
+        split_axis=0,
+        concat_axis=0,
+        tiled=True,
+    )
+    flat_slots = slot_ids.reshape(-1)
+    members = (flat_slots[:, None] == slot_index[None, :]).astype(jnp.int32)
+    earlier = jnp.cumsum(members, axis=0) - members
+    slot_rank = jnp.sum(earlier * members, axis=1)
+    position = (flat_slots * capacity + slot_rank).reshape(tok_count, top_count)
+    matches = position[:, :, None] == jnp.arange(places, dtype=jnp.int32)[None, None, :]
+    combine = jnp.sum(
+        jnp.where(matches, gate_weights[:, :, None], jnp.zeros((), jnp.bfloat16)), axis=1
+    )
+    moe_output = jnp.dot(
+        combine, returned.reshape(places, model_width), preferred_element_type=jnp.float32
     ).astype(jnp.bfloat16)
-    moe_output = lax.psum_scatter(partial, "dp", scatter_dimension=0, tiled=True)[0]
     base_slot = 2 * row_id
     second_old = lax.dynamic_index_in_dim(old_place, base_slot + 1, 0, keepdims=False)
     second_new = lax.dynamic_index_in_dim(new_place, base_slot + 1, 0, keepdims=False)

time: 477 us -> 384 us (0.81)
  waiting for transfers between devices: 311 us -> 211 us
  starting transfers between devices: 24.3 us -> 35.3 us
    reduce_scatter x1 -> x0, waiting for transfers between devices: 188 us -> none  [local(): lax.psum_scatter(partial, 'dp', scatter_dimension=0, tiled=True)[0]]
    ppermute x3, waiting for transfers between devices: 20.2 us -> 103 us  [passed_along(): return lax.ppermute(x, axis, [(i, (i + by) % size) for i in range(size)])]
    all_to_all x1 -> x2, waiting for transfers between devices: 6.24 us -> 43.3 us  [the longest x1 43.3 us: local(): lax.all_to_all(widen(w_down, half_count), 'shard', split_axis=0, concat_a...]
    all_to_all x1, waiting for transfers between devices: 42.5 us -> 7.13 us  [local(): lax.all_to_all(widen(w_up, half_count), 'shard', split_axis=0, concat_axi...]
    all_to_all x1 -> x2, starting transfers between devices: 8.65 us -> 18 us  [the longest x1 10.8 us: local(): lax.all_to_all(pair_halves(upper_half, result[0], returned_other), 'dp',...]
  transfers between devices with their start and end apart: 9 -> 9, of which waited for: 9 -> 8; matrix products, arithmetic and copies ran while one was open for 7% -> 8% of each run, Pallas kernels for 0% -> 0%
where the time goes in v4:
time: 384 us; the launch traced here: 382 us
  waiting for transfers between devices  211 us (55%)
  blocking collectives  55.5 us (14%)
  starting transfers between devices  35.3 us (9%)
  matrix products  30.3 us (8%)
  local copies, waits for them, and re-layouts  19 us (5%)
  between operations  15.6 us (4%)
  other arithmetic  15.4 us (4%)
    ppermute x3, waiting for transfers between devices, passed_along(): return lax.ppermute(x, axis, [(i, (i + by) % size) for i in range(size)])  103 us
    all_to_all x1, blocking collectives, local(): lax.all_to_all(widen(w_gate, half_count), 'shard', split_axis=0, concat_a...  55.5 us
    all_gather x1, waiting for transfers between devices, local(): lax.all_gather(jnp.concatenate([tokens, side], axis=1), 'dp', axis=0, til...  49.8 us
    all_to_all x1, waiting for transfers between devices, local(): lax.all_to_all(widen(w_down, half_count), 'shard', split_axis=0, concat_a...  43.3 us
    dot_general x1, matrix products, local(): lax.dot_general(hidden, full_down, (((1,), (1,)), ((), ())), preferred_el...  15.1 us
    all_to_all x1, starting transfers between devices, local(): lax.all_to_all(pair_halves(upper_half, result[0], returned_other), 'dp',...  10.8 us
    all_to_all x1, starting transfers between devices, local(): lax.all_to_all(widen(w_up, half_count), 'shard', split_axis=0, concat_axi...  8.65 us
    ppermute x3, starting transfers between devices, passed_along(): return lax.ppermute(x, axis, [(i, (i + by) % size) for i in range(size)])  8.04 us
  transfers between devices with their start and end apart: 9, of which 8 were waited for; matrix products, arithmetic and copies ran while one was open for 8% of the time, Pallas kernels for 0%

profile of v4, /device:TPU:8, one launch (start us, length us, event | category | flops | bytes accessed | tf_op | source)
XLA Modules:
  0.0 381.7 jit_solution(670369694472279847)
XLA Ops:
  7.2 0.8 select_reduce_fusion.1
  8.0 0.8 select_reduce_fusion
  9.1 1.2 reduce-window.14
  10.2 0.2 slice_reduce_fusion
  10.9 1.7 concatenate.3
  12.7 1.6 tile.12
  14.2 55.5 %all_to_all.32 = bf16[16,128,1024]{2,1,0:T(8,128)(2,1)} all-to-all(bf16[16,128,1024]{2,1,0:T(8,128)(2,1)S(1)} %bitcast.126), channel_id=1, replica_groups=mesh['dp'=16,'shard'=16] {'shard'}, dimensions={0} | all-to-all | bytes 8388608 | tf_op jit(solution)/shard_map/all_to_all | solution.py:46
  69.7 2.5 tile.14
  72.2 8.7 %all-to-all-start.1 = ((bf16[16,128,1024]{2,1,0:T(8,128)(2,1)}), bf16[16,128,1024]{2,1,0:T(8,128)(2,1)}, u32[]{:S(2)}, u32[]{:S(2)}) async-start(bf16[16,128,1024]{2,1,0:T(8,128)(2,1)} %bitcast.124), calls=%async_computation.1 | async-start | bytes 8388608 | tf_op jit(solution)/shard_map/all_to_all | solution.py:47
  80.9 49.8 %all-gather.3.cloned.1.call-done = bf16[1024,2176]{1,0:T(8,128)(2,1)} async-done(((bf16[64,2176]{1,0:T(8,128)(2,1)}), bf16[1024,2176]{1,0:T(8,128)(2,1)}) %all-gather.3.cloned.1.call-update) | async-done | bytes 4456464 | tf_op jit(solution)/shard_map/all_gather | solution.py:68
  130.7 1.0 slice.75
  131.8 0.2 copy.110
  132.1 2.3 reduce-window.16
  134.9 0.2 copy.117
  135.1 0.2 copy.118
  135.5 1.0 fusion.2
  136.5 5.4 %fusion.3 = bf16[16,2,32,2048]{3,2,1,0:T(8,128)(2,1)} fusion(pred[16,64,2,32]{1,3,2,0:T(8,128)(4,1)S(1)} %fusion.2, bf16[16,64,2176]{2,1,0:T(8,128)(2,1)} %bitcast.129), kind=kOutput, calls=%fused_computation.9 | convolution fusion | flops 270532608 | bytes 8454144 | tf_op jit(solution)/shard_map/stcr,std->scrd/dot_general | solution.py:81
  141.9 7.1 %all-to-all-done.1 = bf16[16,128,1024]{2,1,0:T(8,128)(2,1)} async-done(((bf16[16,128,1024]{2,1,0:T(8,128)(2,1)}), bf16[16,128,1024]{2,1,0:T(8,128)(2,1)}, u32[]{:S(2)}, u32[]{:S(2)}) %all-to-all-start.1) | async-done | bytes 4194336 | tf_op jit(solution)/shard_map/all_to_all | solution.py:47
  149.0 2.5 tile.31
  151.5 7.3 %all-to-all-start.2 = ((bf16[16,128,1024]{2,1,0:T(8,128)(2,1)}), bf16[16,128,1024]{2,1,0:T(8,128)(2,1)}, u32[]{:S(2)}, u32[]{:S(2)}) async-start(bf16[16,128,1024]{2,1,0:T(8,128)(2,1)} %bitcast.125), calls=%async_computation.2 | async-start | bytes 8388608 | tf_op jit(solution)/shard_map/all_to_all | solution.py:48
  158.8 2.6 fusion.4
  161.4 0.4 collective-permute-start
  161.8 0.4 copy-done
  162.2 0.2 fusion.5
  162.4 3.4 collective-permute-done
  165.8 0.4 pad_maximum_fusion
  166.2 2.1 copy-done.5
  168.3 1.2 copy-done.4
  169.5 6.0 %fusion.23 = f32[1024,1024]{1,0:T(8,128)} fusion(bf16[1024,2048]{1,0:T(8,128)(2,1)S(1)} %bitcast.131, bf16[2048,1024]{1,0:T(8,128)(2,1)S(1)} %bitcast.130), kind=kOutput, calls=%fused_computation.61 | convolution fusion | flops 4294967296 | bytes 12582912 | tf_op jit(solution)/shard_map/dot_general | solution.py:92
  175.5 43.3 %all-to-all-done.2 = bf16[16,128,1024]{2,1,0:T(8,128)(2,1)} async-done(((bf16[16,128,1024]{2,1,0:T(8,128)(2,1)}), bf16[16,128,1024]{2,1,0:T(8,128)(2,1)}, u32[]{:S(2)}, u32[]{:S(2)}) %all-to-all-start.2) | async-done | bytes 4194336 | tf_op jit(solution)/shard_map/all_to_all | solution.py:48
  218.9 15.1 %convolution_convert_fusion = bf16[1024,2048]{1,0:T(8,128)(2,1)} fusion(bf16[2048,1024]{1,0:T(8,128)(2,1)} %bitcast.21, f32[1024,1024]{1,0:T(8,128)} %fusion.23, bf16[1024,2048]{1,0:T(8,128)(2,1)} %bitcast.132, bf16[2048,1024]{1,0:T(8,128)(2,1)} %bitcast.19), kind=kOutput, calls=%fused_computation.10 | convolution fusion | flops 8598323200 | bytes 20971520 | tf_op jit(solution)/shard_map/dot_general | solution.py:95
  234.0 2.7 fusion.21
  236.8 4.1 %collective-permute-done.1 = bf16[16,32,2048]{2,1,0:T(8,128)(2,1)S(1)} collective-permute-done((bf16[16,32,2048]{2,1,0:T(8,128)(2,1)S(1)}, bf16[16,32,2048]{2,1,0:T(8,128)(2,1)S(1)}, u32[]{:S(2)}, u32[]{:S(2)}) %collective-permute-start.1) | collective-permute-done | bytes 2097184 | tf_op jit(solution)/shard_map/ppermute | solution.py:8
  241.0 2.2 maximum_select_fusion
  243.2 10.8 %all-to-all-start.3 = ((bf16[16,2,32,2048]{3,2,1,0:T(8,128)(2,1)}), bf16[16,2,32,2048]{3,2,1,0:T(8,128)(2,1)}, u32[]{:S(2)}, u32[]{:S(2)}) async-start(bf16[16,2,32,2048]{3,2,1,0:T(8,128)(2,1)} %maximum_select_fusion), calls=%async_computation.3 | async-start | bytes 8388608 | tf_op jit(solution)/shard_map/all_to_all | solution.py:100
  253.9 0.6 dynamic_slice.8
  254.5 0.6 dynamic_slice.7
  256.5 3.5 collective-permute-start.2
  259.9 1.5 collective-permute-start.3
  261.5 3.0 collective-permute-start.4
  264.8 0.7 fusion.7
  265.5 94.5 %collective-permute-done.2 = bf16[128,1024]{1,0:T(8,128)(2,1)S(1)} collective-permute-done((bf16[128,1024]{1,0:T(8,128)(2,1)S(1)}, bf16[128,1024]{1,0:T(8,128)(2,1)S(1)}, u32[]{:S(2)}, u32[]{:S(2)}) %collective-permute-start.2) | collective-permute-done | bytes 262176 | tf_op jit(solution)/shard_map/ppermute | solution.py:13
  360.1 5.6 %collective-permute-done.3 = bf16[128,1024]{1,0:T(8,128)(2,1)S(1)} collective-permute-done((bf16[128,1024]{1,0:T(8,128)(2,1)S(1)}, bf16[128,1024]{1,0:T(8,128)(2,1)S(1)}, u32[]{:S(2)}, u32[]{:S(2)}) %collective-permute-start.3) | collective-permute-done | bytes 262176 | tf_op jit(solution)/shard_map/ppermute | solution.py:13
  365.7 0.8 pad_maximum_fusion.1
  366.5 0.8 pad_maximum_fusion.2
  367.4 2.9 collective-permute-done.4
  370.3 0.8 pad_maximum_fusion.3
  371.2 3.7 convolution_convert_fusion.1
  (54 shorter events, 2.2 us)
Async XLA Ops:
  7.2 123.5 %all-gather.3.cloned.1.call-start = ((), (), s32[]{:S(2)}) async-start(), calls=%async_computation.4 | async-start | bytes 4734976 | tf_op jit(solution)/shard_map/all_gather | solution.py:68
  14.2 55.5 %copy-start.2 = (bf16[2,128,1024]{2,1,0:T(8,128)(2,1)S(1)}, bf16[2,128,1024]{2,1,0:T(8,128)(2,1)}, u32[]{:S(2)}) copy-start(bf16[2,128,1024]{2,1,0:T(8,128)(2,1)} %param.14) | copy-start | bytes 1572868
  72.2 76.8 %all-to-all-start.1 = ((bf16[16,128,1024]{2,1,0:T(8,128)(2,1)}), bf16[16,128,1024]{2,1,0:T(8,128)(2,1)}, u32[]{:S(2)}, u32[]{:S(2)}) async-start(bf16[16,128,1024]{2,1,0:T(8,128)(2,1)} %bitcast.124), calls=%async_computation.1 | async-start | bytes 8388608 | tf_op jit(solution)/shard_map/all_to_all | solution.py:47
  136.5 12.5 %copy-start.3 = (bf16[2,128,1024]{2,1,0:T(8,128)(2,1)S(1)}, bf16[2,128,1024]{2,1,0:T(8,128)(2,1)}, u32[]{:S(2)}) copy-start(bf16[2,128,1024]{2,1,0:T(8,128)(2,1)} %param.15) | copy-start | bytes 1572868
  151.5 67.4 %all-to-all-start.2 = ((bf16[16,128,1024]{2,1,0:T(8,128)(2,1)}), bf16[16,128,1024]{2,1,0:T(8,128)(2,1)}, u32[]{:S(2)}, u32[]{:S(2)}) async-start(bf16[16,128,1024]{2,1,0:T(8,128)(2,1)} %bitcast.125), calls=%async_computation.2 | async-start | bytes 8388608 | tf_op jit(solution)/shard_map/all_to_all | solution.py:48
  158.8 3.5 copy-start
  161.4 4.4 %collective-permute-start = (bf16[16,32,2048]{2,1,0:T(8,128)(2,1)S(1)}, bf16[16,32,2048]{2,1,0:T(8,128)(2,1)S(1)}, u32[]{:S(2)}, u32[]{:S(2)}) collective-permute-start(bf16[16,32,2048]{2,1,0:T(8,128)(2,1)S(1)} %fusion.4), channel_id=1, source_target_pairs={{0,1},{1,0},{2,3},{3,2},{4,5},{5,4},{6,7},{7,6},{8,9},{9,8},{10,11... | collective-permute-start | bytes 6291464 | tf_op jit(solution)/shard_map/ppermute | solution.py:8
  165.8 3.7 copy-start.4
  166.2 2.1 copy-start.5
  236.7 4.2 %collective-permute-start.1 = (bf16[16,32,2048]{2,1,0:T(8,128)(2,1)S(1)}, bf16[16,32,2048]{2,1,0:T(8,128)(2,1)S(1)}, u32[]{:S(2)}, u32[]{:S(2)}) collective-permute-start(bf16[16,32,2048]{2,1,0:T(8,128)(2,1)S(1)} %bitcast.138), channel_id=1, source_target_pairs={{0,1},{1,0},{2,3},{3,2},{4,5},{5,4},{6,7},{7,6},{8,9},{9,8},{10,11... | collective-permute-start | bytes 6291464 | tf_op jit(solution)/shard_map/ppermute | solution.py:8
  243.2 10.8 %copy-start.7 = (s32[32]{0:T(128)S(1)}, s32[32]{0:T(128)}, u32[]{:S(2)}) copy-start(s32[32]{0:T(128)} %param.11) | copy-start | bytes 388
  243.2 11.4 %copy-start.8 = (s32[32]{0:T(128)S(1)}, s32[32]{0:T(128)}, u32[]{:S(2)}) copy-start(s32[32]{0:T(128)} %param.12) | copy-start | bytes 388
  243.2 13.3 %copy-start.1 = (bf16[2,128,1024]{2,1,0:T(8,128)(2,1)S(1)}, bf16[2,128,1024]{2,1,0:T(8,128)(2,1)}, u32[]{:S(2)}) copy-start(bf16[2,128,1024]{2,1,0:T(8,128)(2,1)} %param.13) | copy-start | bytes 1572868
  243.2 21.4 %copy-start.6 = (f32[64,8]{0,1:T(8,128)S(1)}, f32[64,8]{0,1:T(8,128)}, u32[]{:S(2)}) copy-start(f32[64,8]{0,1:T(8,128)} %param.9) | copy-start | bytes 6148
  243.2 128.0 %all-to-all-start.3 = ((bf16[16,2,32,2048]{3,2,1,0:T(8,128)(2,1)}), bf16[16,2,32,2048]{3,2,1,0:T(8,128)(2,1)}, u32[]{:S(2)}, u32[]{:S(2)}) async-start(bf16[16,2,32,2048]{3,2,1,0:T(8,128)(2,1)} %maximum_select_fusion), calls=%async_computation.3 | async-start | bytes 8388608 | tf_op jit(solution)/shard_map/all_to_all | solution.py:100
  256.5 103.6 %collective-permute-start.2 = (bf16[128,1024]{1,0:T(8,128)(2,1)S(1)}, bf16[128,1024]{1,0:T(8,128)(2,1)S(1)}, u32[]{:S(2)}, u32[]{:S(2)}) collective-permute-start(bf16[128,1024]{1,0:T(8,128)(2,1)S(1)} %bitcast_select_fusion.9), channel_id=1, source_target_pairs={{0,16},{16,32},{32,48},{48,64},{64,80},{80,96},{96,112},{112,128},... | collective-permute-start | bytes 786440 | tf_op jit(solution)/shard_map/ppermute | solution.py:13
  259.9 105.7 %collective-permute-start.3 = (bf16[128,1024]{1,0:T(8,128)(2,1)S(1)}, bf16[128,1024]{1,0:T(8,128)(2,1)S(1)}, u32[]{:S(2)}, u32[]{:S(2)}) collective-permute-start(bf16[128,1024]{1,0:T(8,128)(2,1)S(1)} %bitcast_select_fusion.6), channel_id=1, source_target_pairs={{0,16},{16,32},{32,48},{48,64},{64,80},{80,96},{96,112},{112,128},... | collective-permute-start | bytes 786440 | tf_op jit(solution)/shard_map/ppermute | solution.py:13
  261.5 108.7 %collective-permute-start.4 = (bf16[128,1024]{1,0:T(8,128)(2,1)S(1)}, bf16[128,1024]{1,0:T(8,128)(2,1)S(1)}, u32[]{:S(2)}, u32[]{:S(2)}) collective-permute-start(bf16[128,1024]{1,0:T(8,128)(2,1)S(1)} %bitcast_select_fusion.3), channel_id=1, source_target_pairs={{0,16},{16,32},{32,48},{48,64},{64,80},{80,96},{96,112},{112,128},... | collective-permute-start | bytes 786440 | tf_op jit(solution)/shard_map/ppermute | solution.py:13
Sparse Core Ops, SparseCore 0:
  12.8 117.8 all-gather.2

commit v5 on v4

--- a/solution.py
+++ b/solution.py
@@ -19,7 +19,7 @@
 
 
 def widen(pieces, half_count):
-    return jnp.tile(pieces, (half_count, 1, 1))
+    return jnp.tile(pieces, (half_count,) + (1,) * (pieces.ndim - 1))
 
 
 def pair_halves(upper_half, own_rows, other_rows):
@@ -42,14 +42,11 @@
     upper_half = column % 2 == 1
     capacity = max(2, 2 * tok_count * top_count // slot_count)
     places = slot_count * capacity
-    full_gate, full_up, full_down = (
-        lax.all_to_all(widen(w_gate, half_count), "shard", split_axis=0, concat_axis=1, tiled=True),
-        lax.all_to_all(widen(w_up, half_count), "shard", split_axis=0, concat_axis=1, tiled=True),
-        lax.all_to_all(widen(w_down, half_count), "shard", split_axis=0, concat_axis=1, tiled=True),
-    )
-    full_gate = full_gate[0]
-    full_up = full_up[0]
-    full_down = full_down[0]
+    stacked = jnp.stack([w_gate, w_up, w_down], axis=1)
+    full = lax.all_to_all(widen(stacked, half_count), "shard", split_axis=0, concat_axis=2, tiled=True)
+    full_gate = full[0, 0]
+    full_up = full[0, 1]
+    full_down = full[0, 2]
     slot_index = jnp.arange(slot_count, dtype=jnp.int32)
     owner_slot = jnp.sum(
         jnp.where(old_place[None, :] == slot_index[:, None], slot_index[None, :], 0), axis=1

time: 384 us -> 407 us (1.060)
  waiting for transfers between devices: 211 us -> 291 us
  blocking collectives: 55.5 us -> 0 us
  starting transfers between devices: 35.3 us -> 25.5 us
  local copies, waits for them, and re-layouts: 19 us -> 26.1 us
    all_gather x1, waiting for transfers between devices: 49.8 us -> 117 us  [local(): lax.all_gather(jnp.concatenate([tokens, side], axis=1), 'dp', axis=0, til...]
    all_to_all x1 -> x0, blocking collectives: 55.5 us -> none  [local(): lax.all_to_all(widen(w_gate, half_count), 'shard', split_axis=0, concat_a...]
    all_to_all x2 -> x1, waiting for transfers between devices: 50.5 us -> 62.6 us  [local(): lax.all_to_all(widen(stacked, half_count), 'shard', split_axis=0, concat_...]
    all_to_all x2 -> x1, starting transfers between devices: 15.9 us -> 6.85 us  [local(): lax.all_to_all(widen(stacked, half_count), 'shard', split_axis=0, concat_...]
    all_to_all x0 -> x1, local copies, waits for them, and re-layouts: none -> 6.54 us  [local(): lax.all_to_all(widen(stacked, half_count), 'shard', split_axis=0, concat_...]
  transfers between devices with their start and end apart: 9 -> 8, of which waited for: 8 -> 7; matrix products, arithmetic and copies ran while one was open for 8% -> 6% of each run, Pallas kernels for 0% -> 0%
where the time goes in v5:
time: 407 us; the launch traced here: 403 us
  waiting for transfers between devices  291 us (71%)
  matrix products  28.3 us (7%)
  local copies, waits for them, and re-layouts  26.1 us (6%)
  starting transfers between devices  25.5 us (6%)
  other arithmetic  16.5 us (4%)
  between operations  15.6 us (4%)
    all_gather x1, waiting for transfers between devices, local(): lax.all_gather(jnp.concatenate([tokens, side], axis=1), 'dp', axis=0, til...  117 us
    ppermute x3, waiting for transfers between devices, passed_along(): return lax.ppermute(x, axis, [(i, (i + by) % size) for i in range(size)])  103 us
    all_to_all x1, waiting for transfers between devices, local(): lax.all_to_all(widen(stacked, half_count), 'shard', split_axis=0, concat_...  62.6 us
    dot_general x1, matrix products, local(): lax.dot_general(hidden, full_down, (((1,), (1,)), ((), ())), preferred_el...  15.1 us
    all_to_all x1, starting transfers between devices, local(): lax.all_to_all(pair_halves(upper_half, result[0], returned_other), 'dp',...  10.2 us
  transfers between devices with their start and end apart: 8, of which 7 were waited for; matrix products, arithmetic and copies ran while one was open for 6% of the time, Pallas kernels for 0%

profile of v5, /device:TPU:8, one launch (start us, length us, event | category | flops | bytes accessed | tf_op | source)
XLA Modules:
  0.0 403.1 jit_solution(1880118928578186012)
XLA Ops:
  7.2 0.8 select_reduce_fusion.1
  8.0 0.8 select_reduce_fusion
  9.1 1.2 reduce-window.14
  10.2 0.2 slice_reduce_fusion
  10.5 0.1 fusion.22
  10.9 1.7 concatenate.3
  12.7 1.5 pad_maximum_fusion.1
  14.2 0.2 copy.148
  14.4 6.1 %tile.4 = bf16[8,2,3,128,1024]{4,3,2,1,0:T(8,128)(2,1)} broadcast(bf16[2,3,128,1024]{3,2,1,0:T(8,128)(2,1)S(1)} %copy.148), dimensions={1,2,3,4} | broadcast | bytes 14155776 | tf_op jit(solution)/shard_map/tile | solution.py:22
  20.5 6.9 %all-to-all-start = ((bf16[16,3,128,1024]{3,2,1,0:T(8,128)(2,1)}), bf16[16,3,128,1024]{3,2,1,0:T(8,128)(2,1)}, u32[]{:S(2)}, u32[]{:S(2)}) async-start(bf16[16,3,128,1024]{3,2,1,0:T(8,128)(2,1)} %bitcast.139), calls=%async_computation | async-start | bytes 25165824 | tf_op jit(solution)/shard_map/all_to_all | solution.py:46
  27.4 117.5 %all-gather.3.cloned.1.call-done = bf16[1024,2176]{1,0:T(8,128)(2,1)} async-done(((bf16[64,2176]{1,0:T(8,128)(2,1)}), bf16[1024,2176]{1,0:T(8,128)(2,1)}) %all-gather.3.cloned.1.call-update) | async-done | bytes 4456464 | tf_op jit(solution)/shard_map/all_gather | solution.py:65
  144.8 1.0 slice.87
  145.8 0.1 copy.153
  146.0 0.2 copy.135
  146.4 2.3 reduce-window.16
  148.8 0.1 copy.137
  149.0 0.2 copy.142
  149.2 0.2 copy.143
  149.5 0.1 fusion.18
  149.6 1.0 fusion.5
  150.6 3.4 fusion.6
  154.1 0.2 fusion.8
  154.3 0.3 collective-permute-start
  154.6 0.2 fusion.9
  154.8 3.9 collective-permute-done
  158.7 2.3 pad_maximum_fusion
  161.1 62.6 %all-to-all-done = bf16[16,3,128,1024]{3,2,1,0:T(8,128)(2,1)} async-done(((bf16[16,3,128,1024]{3,2,1,0:T(8,128)(2,1)}), bf16[16,3,128,1024]{3,2,1,0:T(8,128)(2,1)}, u32[]{:S(2)}, u32[]{:S(2)}) %all-to-all-start) | async-done | bytes 12582944 | tf_op jit(solution)/shard_map/all_to_all | solution.py:46
  223.6 6.5 %copy.149 = bf16[16,3,128,1024]{3,2,0,1:T(8,128)(2,1)S(1)} copy(bf16[16,3,128,1024]{3,2,1,0:T(8,128)(2,1)} %all-to-all-done) | data formatting | bytes 25165824 | tf_op jit(solution)/shard_map/all_to_all | solution.py:46
  230.2 4.6 %copy-done = bf16[16,3,128,1024]{3,2,0,1:T(8,128)(2,1)} copy-done((bf16[16,3,128,1024]{3,2,0,1:T(8,128)(2,1)}, bf16[16,3,128,1024]{3,2,0,1:T(8,128)(2,1)S(1)}, u32[]{:S(2)}) %copy-start) | copy-done | bytes 12582936
  234.8 6.0 %fusion.2 = f32[1024,1024]{1,0:T(8,128)} fusion(bf16[1024,2048]{1,0:T(8,128)(2,1)S(1)} %bitcast.149, bf16[1,3,2048,1024]{3,2,1,0:T(8,128)(2,1)S(1)} %bitcast.140), kind=kOutput, calls=%fused_computation.5 | convolution fusion | flops 4294967296 | bytes 12582912 | tf_op jit(solution)/shard_map/dot_general | solution.py:89
  240.8 15.1 %fusion.7 = bf16[1024,2048]{1,0:T(8,128)(2,1)} fusion(bf16[1,3,2048,1024]{3,2,1,0:T(8,128)(2,1)} %bitcast.141, f32[1024,1024]{1,0:T(8,128)} %fusion.2, bf16[1024,2048]{1,0:T(8,128)(2,1)} %bitcast.148), kind=kOutput, calls=%fused_computation.16 | convolution fusion | flops 8598323200 | bytes 20971520 | tf_op jit(solution)/shard_map/dot_general | solution.py:92
  255.9 2.7 fusion.25
  258.7 4.1 %collective-permute-done.1 = bf16[16,32,2048]{2,1,0:T(8,128)(2,1)S(1)} collective-permute-done((bf16[16,32,2048]{2,1,0:T(8,128)(2,1)S(1)}, bf16[16,32,2048]{2,1,0:T(8,128)(2,1)S(1)}, u32[]{:S(2)}, u32[]{:S(2)}) %collective-permute-start.1) | collective-permute-done | bytes 2097184 | tf_op jit(solution)/shard_map/ppermute | solution.py:8
  262.9 2.2 maximum_select_fusion
  265.1 10.2 %all-to-all-start.1 = ((bf16[16,2,32,2048]{3,2,1,0:T(8,128)(2,1)}), bf16[16,2,32,2048]{3,2,1,0:T(8,128)(2,1)}, u32[]{:S(2)}, u32[]{:S(2)}) async-start(bf16[16,2,32,2048]{3,2,1,0:T(8,128)(2,1)} %maximum_select_fusion), calls=%async_computation.1 | async-start | bytes 8388608 | tf_op jit(solution)/shard_map/all_to_all | solution.py:97
  275.3 0.6 dynamic_slice.8
  275.9 0.6 dynamic_slice.7
  277.8 3.5 collective-permute-start.2
  281.3 1.5 collective-permute-start.3
  282.9 3.0 collective-permute-start.4
  286.1 0.7 fusion.11
  286.9 94.5 %collective-permute-done.2 = bf16[128,1024]{1,0:T(8,128)(2,1)S(1)} collective-permute-done((bf16[128,1024]{1,0:T(8,128)(2,1)S(1)}, bf16[128,1024]{1,0:T(8,128)(2,1)S(1)}, u32[]{:S(2)}, u32[]{:S(2)}) %collective-permute-start.2) | collective-permute-done | bytes 262176 | tf_op jit(solution)/shard_map/ppermute | solution.py:13
  381.4 5.6 %collective-permute-done.3 = bf16[128,1024]{1,0:T(8,128)(2,1)S(1)} collective-permute-done((bf16[128,1024]{1,0:T(8,128)(2,1)S(1)}, bf16[128,1024]{1,0:T(8,128)(2,1)S(1)}, u32[]{:S(2)}, u32[]{:S(2)}) %collective-permute-start.3) | collective-permute-done | bytes 262176 | tf_op jit(solution)/shard_map/ppermute | solution.py:13
  387.0 0.8 pad_maximum_fusion.2
  387.9 0.8 pad_maximum_fusion.3
  388.7 2.9 collective-permute-done.4
  391.6 0.8 pad_maximum_fusion.4
  392.5 3.7 convolution_convert_fusion
  (50 shorter events, 1.7 us)
Async XLA Ops:
  7.2 137.7 %all-gather.3.cloned.1.call-start = ((), (), s32[]{:S(2)}) async-start(), calls=%async_computation.2 | async-start | bytes 4734976 | tf_op jit(solution)/shard_map/all_gather | solution.py:65
  20.5 203.1 %all-to-all-start = ((bf16[16,3,128,1024]{3,2,1,0:T(8,128)(2,1)}), bf16[16,3,128,1024]{3,2,1,0:T(8,128)(2,1)}, u32[]{:S(2)}, u32[]{:S(2)}) async-start(bf16[16,3,128,1024]{3,2,1,0:T(8,128)(2,1)} %bitcast.139), calls=%async_computation | async-start | bytes 25165824 | tf_op jit(solution)/shard_map/all_to_all | solution.py:46
  154.3 4.4 %collective-permute-start = (bf16[16,32,2048]{2,1,0:T(8,128)(2,1)S(1)}, bf16[16,32,2048]{2,1,0:T(8,128)(2,1)S(1)}, u32[]{:S(2)}, u32[]{:S(2)}) collective-permute-start(bf16[16,32,2048]{2,1,0:T(8,128)(2,1)S(1)} %fusion.8), channel_id=1, source_target_pairs={{0,1},{1,0},{2,3},{3,2},{4,5},{5,4},{6,7},{7,6},{8,9},{9,8},{10,11... | collective-permute-start | bytes 6291464 | tf_op jit(solution)/shard_map/ppermute | solution.py:8
  223.6 11.1 %copy-start.4 = (bf16[2,16,32,2048]{3,2,1,0:T(8,128)(2,1)S(1)}, bf16[2,16,32,2048]{3,2,1,0:T(8,128)(2,1)}, u32[]{:S(2)}) copy-start(bf16[2,16,32,2048]{3,2,1,0:T(8,128)(2,1)} %pad_maximum_fusion) | copy-start | bytes 12582916
  230.2 4.6 %copy-start = (bf16[16,3,128,1024]{3,2,0,1:T(8,128)(2,1)}, bf16[16,3,128,1024]{3,2,0,1:T(8,128)(2,1)S(1)}, u32[]{:S(2)}) copy-start(bf16[16,3,128,1024]{3,2,0,1:T(8,128)(2,1)S(1)} %copy.149) | copy-start | bytes 37748740
  258.6 4.2 %collective-permute-start.1 = (bf16[16,32,2048]{2,1,0:T(8,128)(2,1)S(1)}, bf16[16,32,2048]{2,1,0:T(8,128)(2,1)S(1)}, u32[]{:S(2)}, u32[]{:S(2)}) collective-permute-start(bf16[16,32,2048]{2,1,0:T(8,128)(2,1)S(1)} %bitcast.155), channel_id=1, source_target_pairs={{0,1},{1,0},{2,3},{3,2},{4,5},{5,4},{6,7},{7,6},{8,9},{9,8},{10,11... | collective-permute-start | bytes 6291464 | tf_op jit(solution)/shard_map/ppermute | solution.py:8
  265.1 10.2 %copy-start.6 = (s32[32]{0:T(128)S(1)}, s32[32]{0:T(128)}, u32[]{:S(2)}) copy-start(s32[32]{0:T(128)} %param.11) | copy-start | bytes 388
  265.1 10.8 %copy-start.7 = (s32[32]{0:T(128)S(1)}, s32[32]{0:T(128)}, u32[]{:S(2)}) copy-start(s32[32]{0:T(128)} %param.12) | copy-start | bytes 388
  265.1 12.7 %copy-start.1 = (bf16[2,128,1024]{2,1,0:T(8,128)(2,1)S(1)}, bf16[2,128,1024]{2,1,0:T(8,128)(2,1)}, u32[]{:S(2)}) copy-start(bf16[2,128,1024]{2,1,0:T(8,128)(2,1)} %param.13) | copy-start | bytes 1572868
  265.1 16.2 %copy-start.2 = (bf16[2,128,1024]{2,1,0:T(8,128)(2,1)S(1)}, bf16[2,128,1024]{2,1,0:T(8,128)(2,1)}, u32[]{:S(2)}) copy-start(bf16[2,128,1024]{2,1,0:T(8,128)(2,1)} %param.14) | copy-start | bytes 1572868
  265.1 17.8 %copy-start.3 = (bf16[2,128,1024]{2,1,0:T(8,128)(2,1)S(1)}, bf16[2,128,1024]{2,1,0:T(8,128)(2,1)}, u32[]{:S(2)}) copy-start(bf16[2,128,1024]{2,1,0:T(8,128)(2,1)} %param.15) | copy-start | bytes 1572868
  265.1 20.8 %copy-start.5 = (f32[64,8]{0,1:T(8,128)S(1)}, f32[64,8]{0,1:T(8,128)}, u32[]{:S(2)}) copy-start(f32[64,8]{0,1:T(8,128)} %param.9) | copy-start | bytes 6148
  265.1 127.4 %all-to-all-start.1 = ((bf16[16,2,32,2048]{3,2,1,0:T(8,128)(2,1)}), bf16[16,2,32,2048]{3,2,1,0:T(8,128)(2,1)}, u32[]{:S(2)}, u32[]{:S(2)}) async-start(bf16[16,2,32,2048]{3,2,1,0:T(8,128)(2,1)} %maximum_select_fusion), calls=%async_computation.1 | async-start | bytes 8388608 | tf_op jit(solution)/shard_map/all_to_all | solution.py:97
  277.8 103.6 %collective-permute-start.2 = (bf16[128,1024]{1,0:T(8,128)(2,1)S(1)}, bf16[128,1024]{1,0:T(8,128)(2,1)S(1)}, u32[]{:S(2)}, u32[]{:S(2)}) collective-permute-start(bf16[128,1024]{1,0:T(8,128)(2,1)S(1)} %bitcast_select_fusion.9), channel_id=1, source_target_pairs={{0,16},{16,32},{32,48},{48,64},{64,80},{80,96},{96,112},{112,128},... | collective-permute-start | bytes 786440 | tf_op jit(solution)/shard_map/ppermute | solution.py:13
  281.3 105.7 %collective-permute-start.3 = (bf16[128,1024]{1,0:T(8,128)(2,1)S(1)}, bf16[128,1024]{1,0:T(8,128)(2,1)S(1)}, u32[]{:S(2)}, u32[]{:S(2)}) collective-permute-start(bf16[128,1024]{1,0:T(8,128)(2,1)S(1)} %bitcast_select_fusion.6), channel_id=1, source_target_pairs={{0,16},{16,32},{32,48},{48,64},{64,80},{80,96},{96,112},{112,128},... | collective-permute-start | bytes 786440 | tf_op jit(solution)/shard_map/ppermute | solution.py:13
  282.9 108.7 %collective-permute-start.4 = (bf16[128,1024]{1,0:T(8,128)(2,1)S(1)}, bf16[128,1024]{1,0:T(8,128)(2,1)S(1)}, u32[]{:S(2)}, u32[]{:S(2)}) collective-permute-start(bf16[128,1024]{1,0:T(8,128)(2,1)S(1)} %bitcast_select_fusion.3), channel_id=1, source_target_pairs={{0,16},{16,32},{32,48},{48,64},{64,80},{80,96},{96,112},{112,128},... | collective-permute-start | bytes 786440 | tf_op jit(solution)/shard_map/ppermute | solution.py:13
Sparse Core Ops, SparseCore 0:
  12.8 132.0 all-gather.2

commit v6 on v5

--- a/solution.py
+++ b/solution.py
@@ -1,7 +1,68 @@
 import jax
 import jax.numpy as jnp
 from jax import lax
+from jax.experimental import pallas as pl
+from jax.experimental.pallas import tpu as pltpu
 from jax.sharding import PartitionSpec as P
+
+
+def gather_kernel(n_shard, *refs):
+    sources, outputs = refs[0:3], refs[3:6]
+    send_sem, recv_sem, local_sem = refs[6:9]
+    me = lax.axis_index("shard")
+    row = lax.axis_index("dp")
+
+    def remote(w, peer, sender, target):
+        return pltpu.make_async_remote_copy(
+            src_ref=sources[w].at[peer % 2],
+            dst_ref=outputs[w].at[sender],
+            send_sem=send_sem.at[w, peer],
+            recv_sem=recv_sem.at[w, sender],
+            device_id=(row, target),
+            device_id_type=pl.DeviceIdType.MESH,
+        )
+
+    def local(w):
+        return pltpu.make_async_copy(
+            sources[w].at[me % 2], outputs[w].at[me], local_sem.at[w]
+        )
+
+    for w in range(3):
+        for peer in range(n_shard):
+
+            @pl.when(peer != me)
+            def _():
+                remote(w, peer, me, peer).start()
+
+        local(w).start()
+    for w in range(3):
+        local(w).wait()
+        for peer in range(n_shard):
+
+            @pl.when(peer != me)
+            def _():
+                remote(w, peer, me, peer).wait_send()
+                remote(w, peer, peer, peer).wait_recv()
+
+
+def gather_slots(w_gate, w_up, w_down, n_shard):
+    piece = jax.ShapeDtypeStruct((n_shard,) + w_gate.shape[1:], w_gate.dtype)
+    anywhere = pl.BlockSpec(memory_space=pl.ANY)
+    return pl.pallas_call(
+        lambda *refs: gather_kernel(n_shard, *refs),
+        out_shape=(piece, piece, piece),
+        in_specs=[anywhere] * 3,
+        out_specs=(anywhere, anywhere, anywhere),
+        scratch_shapes=[
+            pltpu.SemaphoreType.DMA((3, n_shard)),
+            pltpu.SemaphoreType.DMA((3, n_shard)),
+            pltpu.SemaphoreType.DMA((3,)),
+        ],
+        compiler_params=pltpu.CompilerParams(has_side_effects=True),
+        cost_estimate=pl.CostEstimate(
+            flops=0, bytes_accessed=6 * n_shard * w_gate[0].size * 2, transcendentals=0
+        ),
+    )(w_gate, w_up, w_down)
 
 
 def partner_2(x, axis, apart):
@@ -19,7 +80,7 @@
 
 
 def widen(pieces, half_count):
-    return jnp.tile(pieces, (half_count,) + (1,) * (pieces.ndim - 1))
+    return jnp.tile(pieces, (half_count, 1, 1))
 
 
 def pair_halves(upper_half, own_rows, other_rows):
@@ -42,11 +103,6 @@
     upper_half = column % 2 == 1
     capacity = max(2, 2 * tok_count * top_count // slot_count)
     places = slot_count * capacity
-    stacked = jnp.stack([w_gate, w_up, w_down], axis=1)
-    full = lax.all_to_all(widen(stacked, half_count), "shard", split_axis=0, concat_axis=2, tiled=True)
-    full_gate = full[0, 0]
-    full_up = full[0, 1]
-    full_down = full[0, 2]
     slot_index = jnp.arange(slot_count, dtype=jnp.int32)
     owner_slot = jnp.sum(
         jnp.where(old_place[None, :] == slot_index[:, None], slot_index[None, :], 0), axis=1
@@ -63,6 +119,9 @@
         axis=1,
     )
     gathered = lax.all_gather(jnp.concatenate([tokens, side], axis=1), "dp", axis=0, tiled=False)
+    full_slots = gather_slots(w_gate, w_up, w_down, n_shard)
+    gathered, full_slots = lax.optimization_barrier((gathered, full_slots))
+    full_gate, full_up, full_down = (piece.reshape(model_width, -1) for piece in full_slots)
     gathered_tokens = gathered[..., :model_width]
     gathered_slots = (
         gathered[..., model_width : model_width + top_count].astype(jnp.int32).reshape(n_rows, -1)

time: 407 us -> 414 us (1.017)
  Pallas kernels: 0 us -> 196 us
  waiting for transfers between devices: 291 us -> 111 us
  local copies, waits for them, and re-layouts: 26.1 us -> 20.1 us
    pallas_call x0 -> x1, Pallas kernels: none -> 196 us  [gather_slots(): pl.pallas_call(lambda *refs: gather_kernel(n_shard, *refs), out_shape=(pi...]
    all_gather x1, waiting for transfers between devices: 117 us -> 0.02 us  [local(): lax.all_gather(jnp.concatenate([tokens, side], axis=1), 'dp', axis=0, til...]
    all_to_all x1 -> x0, waiting for transfers between devices: 62.6 us -> none  [local(): lax.all_to_all(widen(stacked, half_count), 'shard', split_axis=0, concat_...]
    optimization_barrier x0 -> x1, local copies, waits for them, and re-layouts: none -> 9.2 us  [local(): gathered, full_slots = lax.optimization_barrier((gathered, full_slots))]
    all_to_all x1 -> x0, starting transfers between devices: 6.85 us -> none  [local(): lax.all_to_all(widen(stacked, half_count), 'shard', split_axis=0, concat_...]
    all_to_all x1 -> x0, local copies, waits for them, and re-layouts: 6.54 us -> none  [local(): lax.all_to_all(widen(stacked, half_count), 'shard', split_axis=0, concat_...]
    another operation x7 -> x5, local copies, waits for them, and re-layouts: 6.53 us -> 0.22 us  [the longest x1 6.14 us: widen(): return jnp.tile(pieces, (half_count,) + (1,) * (pieces.ndim - 1))]
    all_to_all x1, starting transfers between devices: 10.2 us -> 15.1 us  [local(): lax.all_to_all(pair_halves(upper_half, result[0], returned_other), 'dp',...]
  transfers between devices with their start and end apart: 8 -> 7, of which waited for: 7 -> 5; matrix products, arithmetic and copies ran while one was open for 6% -> 1% of each run, Pallas kernels for 0% -> 48%
where the time goes in v6:
time: 414 us; the launch traced here: 408 us
  Pallas kernels  196 us (47%)
  waiting for transfers between devices  111 us (27%)
  matrix products  28.3 us (7%)
  starting transfers between devices  23.7 us (6%)
  local copies, waits for them, and re-layouts  20.1 us (5%)
  between operations  15.6 us (4%)
  other arithmetic  13.8 us (3%)
    pallas_call x1, Pallas kernels, gather_slots(): pl.pallas_call(lambda *refs: gather_kernel(n_shard, *refs), out_shape=(pi...  196 us
    ppermute x3, waiting for transfers between devices, passed_along(): return lax.ppermute(x, axis, [(i, (i + by) % size) for i in range(size)])  103 us
    dot_general x1, matrix products, local(): lax.dot_general(hidden, full_down, (((1,), (1,)), ((), ())), preferred_el...  15.1 us
    all_to_all x1, starting transfers between devices, local(): lax.all_to_all(pair_halves(upper_half, result[0], returned_other), 'dp',...  15.1 us
    optimization_barrier x1, local copies, waits for them, and re-layouts, local(): gathered, full_slots = lax.optimization_barrier((gathered, full_slots))  9.2 us
  transfers between devices with their start and end apart: 7, of which 5 were waited for; matrix products, arithmetic and copies ran while one was open for 1% of the time, Pallas kernels for 48%

profile of v6, /device:TPU:8, one launch (start us, length us, event | category | flops | bytes accessed | tf_op | source)
XLA Modules:
  0.0 408.2 jit_solution(5937668464107816846)
XLA Ops:
  7.2 0.8 select_reduce_fusion.1
  8.0 0.8 select_reduce_fusion
  9.1 1.2 reduce-window.14
  10.2 0.2 slice_reduce_fusion
  10.5 0.1 fusion.22
  10.8 0.1 copy.108
  10.9 1.7 concatenate.3
  12.7 195.8 %shard_map.111 = (bf16[16,128,1024]{2,1,0:T(8,128)(2,1)}, bf16[16,128,1024]{2,1,0:T(8,128)(2,1)}, bf16[16,128,1024]{2,1,0:T(8,128)(2,1)}) custom-call(bf16[2,128,1024]{2,1,0:T(8,128)(2,1)} %refs_0_.1, bf16[2,128,1024]{2,1,0:T(8,128)(2,1)} %refs_1_.1, bf16[2,128,1024]{2,1,0:T(8,128)(2,1)} %refs_2_.1), custom_call_target="tpu_custom_call" | custom-call | bytes 25165824 | tf_op jit(solution)/shard_map/pallas_call | solution.py:51
  208.5 9.2 %copy.109 = bf16[16,64,2176]{1,2,0:T(8,128)(2,1)} copy(bf16[16,64,2176]{2,1,0:T(8,128)(2,1)} %bitcast.121) | data formatting | bytes 8912896 | tf_op jit(solution)/shard_map/optimization_barrier | solution.py:123
  217.7 0.8 slice_convert_fusion
  218.5 0.2 copy.110
  218.7 0.1 copy.111
  218.8 0.2 fusion.18
  219.0 2.3 reduce-window.16
  221.3 0.1 copy.112
  221.5 0.1 copy.116
  221.6 0.1 fusion.19
  221.7 0.2 copy.117
  221.9 0.2 copy.118
  222.2 1.0 fusion.4
  223.2 3.4 fusion.5
  226.6 0.2 fusion.8
  226.8 0.3 collective-permute-start
  227.1 0.2 fusion.9
  227.3 3.9 collective-permute-done
  231.2 0.4 pad_maximum_fusion
  231.6 3.3 copy-done.5
  234.9 6.0 %fusion.27 = f32[1024,1024]{1,0:T(8,128)} fusion(bf16[1024,2048]{1,0:T(8,128)(2,1)S(1)} %bitcast.124, bf16[2048,1024]{1,0:T(8,128)(2,1)S(1)} %bitcast.135), kind=kOutput, calls=%fused_computation.63 | convolution fusion | flops 4294967296 | bytes 12582912 | tf_op jit(solution)/shard_map/dot_general | solution.py:148
  241.0 15.1 %convolution_convert_fusion = bf16[1024,2048]{1,0:T(8,128)(2,1)} fusion(bf16[2048,1024]{1,0:T(8,128)(2,1)} %bitcast.134, f32[1024,1024]{1,0:T(8,128)} %fusion.27, bf16[1024,2048]{1,0:T(8,128)(2,1)} %bitcast.125, bf16[2048,1024]{1,0:T(8,128)(2,1)} %bitcast.133), kind=kOutput, calls=%fused_computation.11 | convolution fusion | flops 8598323200 | bytes 20971520 | tf_op jit(solution)/shard_map/dot_general | solution.py:151
  256.1 2.7 fusion.25
  258.8 0.2 collective-permute-start.1
  259.1 4.0 collective-permute-done.1
  263.1 2.2 maximum_select_fusion
  265.3 15.1 %all-to-all-start = ((bf16[16,2,32,2048]{3,2,1,0:T(8,128)(2,1)}), bf16[16,2,32,2048]{3,2,1,0:T(8,128)(2,1)}, u32[]{:S(2)}, u32[]{:S(2)}) async-start(bf16[16,2,32,2048]{3,2,1,0:T(8,128)(2,1)} %maximum_select_fusion), calls=%async_computation | async-start | bytes 8388608 | tf_op jit(solution)/shard_map/all_to_all | solution.py:156
  280.4 0.6 dynamic_slice.8
  281.0 0.6 dynamic_slice.7
  282.9 3.5 collective-permute-start.2
  286.4 1.5 collective-permute-start.3
  288.0 3.0 collective-permute-start.4
  291.1 0.1 copy.107
  291.2 0.7 fusion.11
  292.0 94.5 %collective-permute-done.2 = bf16[128,1024]{1,0:T(8,128)(2,1)S(1)} collective-permute-done((bf16[128,1024]{1,0:T(8,128)(2,1)S(1)}, bf16[128,1024]{1,0:T(8,128)(2,1)S(1)}, u32[]{:S(2)}, u32[]{:S(2)}) %collective-permute-start.2) | collective-permute-done | bytes 262176 | tf_op jit(solution)/shard_map/ppermute | solution.py:74
  386.5 5.6 %collective-permute-done.3 = bf16[128,1024]{1,0:T(8,128)(2,1)S(1)} collective-permute-done((bf16[128,1024]{1,0:T(8,128)(2,1)S(1)}, bf16[128,1024]{1,0:T(8,128)(2,1)S(1)}, u32[]{:S(2)}, u32[]{:S(2)}) %collective-permute-start.3) | collective-permute-done | bytes 262176 | tf_op jit(solution)/shard_map/ppermute | solution.py:74
  392.2 0.8 pad_maximum_fusion.1
  393.0 0.8 pad_maximum_fusion.2
  393.8 2.9 collective-permute-done.4
  396.8 0.8 pad_maximum_fusion.3
  397.6 3.7 convolution_convert_fusion.1
  (44 shorter events, 1.1 us)
Async XLA Ops:
  7.2 201.4 %all-gather.3.cloned.1.call-start = ((), (), s32[]{:S(2)}) async-start(), calls=%async_computation.1 | async-start | bytes 4734976 | tf_op jit(solution)/shard_map/all_gather | solution.py:121
  226.8 4.4 %collective-permute-start = (bf16[16,32,2048]{2,1,0:T(8,128)(2,1)S(1)}, bf16[16,32,2048]{2,1,0:T(8,128)(2,1)S(1)}, u32[]{:S(2)}, u32[]{:S(2)}) collective-permute-start(bf16[16,32,2048]{2,1,0:T(8,128)(2,1)S(1)} %fusion.8), channel_id=1, source_target_pairs={{0,1},{1,0},{2,3},{3,2},{4,5},{5,4},{6,7},{7,6},{8,9},{9,8},{10,11... | collective-permute-start | bytes 6291464 | tf_op jit(solution)/shard_map/ppermute | solution.py:69
  231.2 3.7 copy-start.5
  231.6 9.4 %copy-start.3 = (bf16[2,16,32,2048]{3,2,1,0:T(8,128)(2,1)}, bf16[2,16,32,2048]{3,2,1,0:T(8,128)(2,1)S(1)}, u32[]{:S(2)}) copy-start(bf16[2,16,32,2048]{3,2,1,0:T(8,128)(2,1)S(1)} %pad_maximum_fusion) | copy-start | bytes 12582916
  258.8 4.2 %collective-permute-start.1 = (bf16[16,32,2048]{2,1,0:T(8,128)(2,1)S(1)}, bf16[16,32,2048]{2,1,0:T(8,128)(2,1)S(1)}, u32[]{:S(2)}, u32[]{:S(2)}) collective-permute-start(bf16[16,32,2048]{2,1,0:T(8,128)(2,1)S(1)} %bitcast.131), channel_id=1, source_target_pairs={{0,1},{1,0},{2,3},{3,2},{4,5},{5,4},{6,7},{7,6},{8,9},{9,8},{10,11... | collective-permute-start | bytes 6291464 | tf_op jit(solution)/shard_map/ppermute | solution.py:69
  265.2 15.1 %copy-start.6 = (s32[32]{0:T(128)S(1)}, s32[32]{0:T(128)}, u32[]{:S(2)}) copy-start(s32[32]{0:T(128)} %param.11) | copy-start | bytes 388
  265.2 15.7 %copy-start.7 = (s32[32]{0:T(128)S(1)}, s32[32]{0:T(128)}, u32[]{:S(2)}) copy-start(s32[32]{0:T(128)} %param.12) | copy-start | bytes 388
  265.2 17.6 %copy-start = (bf16[2,128,1024]{2,1,0:T(8,128)(2,1)S(1)}, bf16[2,128,1024]{2,1,0:T(8,128)(2,1)}, u32[]{:S(2)}) copy-start(bf16[2,128,1024]{2,1,0:T(8,128)(2,1)} %refs_0_.1) | copy-start | bytes 1572868
  265.2 21.1 %copy-start.1 = (bf16[2,128,1024]{2,1,0:T(8,128)(2,1)S(1)}, bf16[2,128,1024]{2,1,0:T(8,128)(2,1)}, u32[]{:S(2)}) copy-start(bf16[2,128,1024]{2,1,0:T(8,128)(2,1)} %refs_1_.1) | copy-start | bytes 1572868
  265.3 22.7 %copy-start.2 = (bf16[2,128,1024]{2,1,0:T(8,128)(2,1)S(1)}, bf16[2,128,1024]{2,1,0:T(8,128)(2,1)}, u32[]{:S(2)}) copy-start(bf16[2,128,1024]{2,1,0:T(8,128)(2,1)} %refs_2_.1) | copy-start | bytes 1572868
  265.3 25.8 %copy-start.4 = (f32[64,8]{0,1:T(8,128)S(1)}, f32[64,8]{0,1:T(8,128)}, u32[]{:S(2)}) copy-start(f32[64,8]{0,1:T(8,128)} %param.9) | copy-start | bytes 6148
  265.3 132.3 %all-to-all-start = ((bf16[16,2,32,2048]{3,2,1,0:T(8,128)(2,1)}), bf16[16,2,32,2048]{3,2,1,0:T(8,128)(2,1)}, u32[]{:S(2)}, u32[]{:S(2)}) async-start(bf16[16,2,32,2048]{3,2,1,0:T(8,128)(2,1)} %maximum_select_fusion), calls=%async_computation | async-start | bytes 8388608 | tf_op jit(solution)/shard_map/all_to_all | solution.py:156
  282.9 103.6 %collective-permute-start.2 = (bf16[128,1024]{1,0:T(8,128)(2,1)S(1)}, bf16[128,1024]{1,0:T(8,128)(2,1)S(1)}, u32[]{:S(2)}, u32[]{:S(2)}) collective-permute-start(bf16[128,1024]{1,0:T(8,128)(2,1)S(1)} %bitcast_select_fusion.9), channel_id=1, source_target_pairs={{0,16},{16,32},{32,48},{48,64},{64,80},{80,96},{96,112},{112,128},... | collective-permute-start | bytes 786440 | tf_op jit(solution)/shard_map/ppermute | solution.py:74
  286.4 105.7 %collective-permute-start.3 = (bf16[128,1024]{1,0:T(8,128)(2,1)S(1)}, bf16[128,1024]{1,0:T(8,128)(2,1)S(1)}, u32[]{:S(2)}, u32[]{:S(2)}) collective-permute-start(bf16[128,1024]{1,0:T(8,128)(2,1)S(1)} %bitcast_select_fusion.6), channel_id=1, source_target_pairs={{0,16},{16,32},{32,48},{48,64},{64,80},{80,96},{96,112},{112,128},... | collective-permute-start | bytes 786440 | tf_op jit(solution)/shard_map/ppermute | solution.py:74
  288.0 108.8 %collective-permute-start.4 = (bf16[128,1024]{1,0:T(8,128)(2,1)S(1)}, bf16[128,1024]{1,0:T(8,128)(2,1)S(1)}, u32[]{:S(2)}, u32[]{:S(2)}) collective-permute-start(bf16[128,1024]{1,0:T(8,128)(2,1)S(1)} %bitcast_select_fusion.3), channel_id=1, source_target_pairs={{0,16},{16,32},{32,48},{48,64},{64,80},{80,96},{96,112},{112,128},... | collective-permute-start | bytes 786440 | tf_op jit(solution)/shard_map/ppermute | solution.py:74
Sparse Core Ops, SparseCore 0:
  12.8 131.8 all-gather.2

commit v7 on v4

--- a/solution.py
+++ b/solution.py
@@ -65,7 +65,12 @@
         ],
         axis=1,
     )
-    gathered = lax.all_gather(jnp.concatenate([tokens, side], axis=1), "dp", axis=0, tiled=False)
+    ext = jnp.concatenate([tokens, side], axis=1)
+    pair = jnp.stack([ext, partner_2(ext, "dp", 0)], axis=0)
+    pair = jnp.where(row_id % 2 == 1, pair[::-1], pair)
+    groups = [list(range(g, n_rows, 2)) for g in range(2)]
+    gathered = lax.all_gather(pair, "dp", axis=0, tiled=True, axis_index_groups=groups)
+    gathered = gathered.reshape(n_rows, tok_count, -1)
     gathered_tokens = gathered[..., :model_width]
     gathered_slots = (
         gathered[..., model_width : model_width + top_count].astype(jnp.int32).reshape(n_rows, -1)

time: 384 us -> 381 us (level)
    all_gather x1, waiting for transfers between devices: 49.8 us -> 0.02 us  [local(): lax.all_gather(pair, 'dp', axis=0, tiled=True, axis_index_groups=groups)]
    all_to_all x1, waiting for transfers between devices: 7.13 us -> 48.1 us  [local(): lax.all_to_all(widen(w_up, half_count), 'shard', split_axis=0, concat_axi...]
    ppermute x2 -> x3, waiting for transfers between devices: 7.51 us -> 14.4 us  [partner_2(): lax.ppermute(x, axis, [(i, i ^ 1 << apart) for i in range(lax.axis_size(a...]
  transfers between devices with their start and end apart: 9 -> 10, of which waited for: 8 -> 8; matrix products, arithmetic and copies ran while one was open for 8% -> 7% of each run, Pallas kernels for 0% -> 0%
where the time goes in v7:
time: 381 us; the launch traced here: 378 us
  waiting for transfers between devices  209 us (55%)
  blocking collectives  52.6 us (14%)
  starting transfers between devices  37.4 us (10%)
  matrix products  30.3 us (8%)
  local copies, waits for them, and re-layouts  17.2 us (5%)
  other arithmetic  16.4 us (4%)
  between operations  15.6 us (4%)
    ppermute x3, waiting for transfers between devices, passed_along(): return lax.ppermute(x, axis, [(i, (i + by) % size) for i in range(size)])  103 us
    all_to_all x1, blocking collectives, local(): lax.all_to_all(widen(w_gate, half_count), 'shard', split_axis=0, concat_a...  52.6 us
    all_to_all x1, waiting for transfers between devices, local(): lax.all_to_all(widen(w_up, half_count), 'shard', split_axis=0, concat_axi...  48.1 us
    all_to_all x1, waiting for transfers between devices, local(): lax.all_to_all(widen(w_down, half_count), 'shard', split_axis=0, concat_a...  43.3 us
    dot_general x1, matrix products, local(): lax.dot_general(hidden, full_down, (((1,), (1,)), ((), ())), preferred_el...  15.1 us
    ppermute x3, waiting for transfers between devices, partner_2(): lax.ppermute(x, axis, [(i, i ^ 1 << apart) for i in range(lax.axis_size(a...  14.4 us
    all_to_all x1, starting transfers between devices, local(): lax.all_to_all(pair_halves(upper_half, result[0], returned_other), 'dp',...  10.9 us
    ppermute x3, starting transfers between devices, passed_along(): return lax.ppermute(x, axis, [(i, (i + by) % size) for i in range(size)])  8.03 us
  transfers between devices with their start and end apart: 10, of which 8 were waited for; matrix products, arithmetic and copies ran while one was open for 7% of the time, Pallas kernels for 0%

profile of v7, /device:TPU:8, one launch (start us, length us, event | category | flops | bytes accessed | tf_op | source)
XLA Modules:
  0.0 378.5 jit_solution(15810444522356864750)
XLA Ops:
  7.2 0.8 select_reduce_fusion.1
  8.0 0.8 select_reduce_fusion
  9.1 1.2 reduce-window.14
  10.3 0.2 slice_reduce_fusion
  10.9 1.0 concatenate.3
  12.0 3.1 collective-permute-start
  15.1 6.9 %collective-permute-done = bf16[64,2176]{1,0:T(8,128)(2,1)S(1)} collective-permute-done((bf16[64,2176]{1,0:T(8,128)(2,1)S(1)}, bf16[64,2176]{1,0:T(8,128)(2,1)S(1)}, u32[]{:S(2)}, u32[]{:S(2)}) %collective-permute-start) | collective-permute-done | bytes 278560 | tf_op jit(solution)/shard_map/ppermute | solution.py:8
  22.0 0.9 reverse_select_fusion
  23.0 0.5 tile.12
  23.6 52.6 %all_to_all.32 = bf16[16,128,1024]{2,1,0:T(8,128)(2,1)} all-to-all(bf16[16,128,1024]{2,1,0:T(8,128)(2,1)S(1)} %bitcast.127), channel_id=1, replica_groups=mesh['dp'=16,'shard'=16] {'shard'}, dimensions={0} | all-to-all | bytes 8388608 | tf_op jit(solution)/shard_map/all_to_all | solution.py:46
  76.2 2.5 tile.14
  78.7 7.8 %all-to-all-start.1 = ((bf16[16,128,1024]{2,1,0:T(8,128)(2,1)}), bf16[16,128,1024]{2,1,0:T(8,128)(2,1)}, u32[]{:S(2)}, u32[]{:S(2)}) async-start(bf16[16,128,1024]{2,1,0:T(8,128)(2,1)} %bitcast.125), calls=%async_computation.1 | async-start | bytes 8388608 | tf_op jit(solution)/shard_map/all_to_all | solution.py:47
  86.5 1.0 slice.75
  88.0 2.3 reduce-window.16
  90.9 0.2 copy.113
  91.3 1.0 fusion.2
  92.3 5.4 %fusion.3 = bf16[16,2,32,2048]{3,2,1,0:T(8,128)(2,1)} fusion(pred[16,64,2,32]{1,3,2,0:T(8,128)(4,1)S(1)} %fusion.2, bf16[16,64,2176]{2,1,0:T(8,128)(2,1)} %all-gather.2.cloned.1.call-done), kind=kOutput, calls=%fused_computation.9 | convolution fusion | flops 270532608 | bytes 8454144 | tf_op jit(solution)/shard_map/stcr,std->scrd/dot_general | solution.py:86
  97.7 48.1 %all-to-all-done.1 = bf16[16,128,1024]{2,1,0:T(8,128)(2,1)} async-done(((bf16[16,128,1024]{2,1,0:T(8,128)(2,1)}), bf16[16,128,1024]{2,1,0:T(8,128)(2,1)}, u32[]{:S(2)}, u32[]{:S(2)}) %all-to-all-start.1) | async-done | bytes 4194336 | tf_op jit(solution)/shard_map/all_to_all | solution.py:47
  145.9 2.5 tile.31
  148.4 7.0 %all-to-all-start.2 = ((bf16[16,128,1024]{2,1,0:T(8,128)(2,1)}), bf16[16,128,1024]{2,1,0:T(8,128)(2,1)}, u32[]{:S(2)}, u32[]{:S(2)}) async-start(bf16[16,128,1024]{2,1,0:T(8,128)(2,1)} %bitcast.126), calls=%async_computation.2 | async-start | bytes 8388608 | tf_op jit(solution)/shard_map/all_to_all | solution.py:48
  155.4 2.6 fusion.4
  158.0 0.4 collective-permute-start.1
  158.4 0.4 copy-done
  158.8 0.2 fusion.5
  159.0 3.4 collective-permute-done.1
  162.4 0.4 pad_maximum_fusion
  162.8 2.1 copy-done.5
  164.9 1.2 copy-done.4
  166.1 6.0 %fusion.23 = f32[1024,1024]{1,0:T(8,128)} fusion(bf16[1024,2048]{1,0:T(8,128)(2,1)S(1)} %bitcast.130, bf16[2048,1024]{1,0:T(8,128)(2,1)S(1)} %bitcast.129), kind=kOutput, calls=%fused_computation.63 | convolution fusion | flops 4294967296 | bytes 12582912 | tf_op jit(solution)/shard_map/dot_general | solution.py:97
  172.1 43.3 %all-to-all-done.2 = bf16[16,128,1024]{2,1,0:T(8,128)(2,1)} async-done(((bf16[16,128,1024]{2,1,0:T(8,128)(2,1)}), bf16[16,128,1024]{2,1,0:T(8,128)(2,1)}, u32[]{:S(2)}, u32[]{:S(2)}) %all-to-all-start.2) | async-done | bytes 4194336 | tf_op jit(solution)/shard_map/all_to_all | solution.py:48
  215.5 15.1 %convolution_convert_fusion = bf16[1024,2048]{1,0:T(8,128)(2,1)} fusion(bf16[2048,1024]{1,0:T(8,128)(2,1)} %bitcast.22, f32[1024,1024]{1,0:T(8,128)} %fusion.23, bf16[1024,2048]{1,0:T(8,128)(2,1)} %bitcast.131, bf16[2048,1024]{1,0:T(8,128)(2,1)} %bitcast.20), kind=kOutput, calls=%fused_computation.10 | convolution fusion | flops 8598323200 | bytes 20971520 | tf_op jit(solution)/shard_map/dot_general | solution.py:100
  230.6 2.7 fusion.21
  233.4 4.1 %collective-permute-done.2 = bf16[16,32,2048]{2,1,0:T(8,128)(2,1)S(1)} collective-permute-done((bf16[16,32,2048]{2,1,0:T(8,128)(2,1)S(1)}, bf16[16,32,2048]{2,1,0:T(8,128)(2,1)S(1)}, u32[]{:S(2)}, u32[]{:S(2)}) %collective-permute-start.2) | collective-permute-done | bytes 2097184 | tf_op jit(solution)/shard_map/ppermute | solution.py:8
  237.6 2.2 maximum_select_fusion
  239.8 10.9 %all-to-all-start.3 = ((bf16[16,2,32,2048]{3,2,1,0:T(8,128)(2,1)}), bf16[16,2,32,2048]{3,2,1,0:T(8,128)(2,1)}, u32[]{:S(2)}, u32[]{:S(2)}) async-start(bf16[16,2,32,2048]{3,2,1,0:T(8,128)(2,1)} %maximum_select_fusion), calls=%async_computation.3 | async-start | bytes 8388608 | tf_op jit(solution)/shard_map/all_to_all | solution.py:105
  250.7 0.6 dynamic_slice.8
  251.3 0.6 dynamic_slice.7
  253.2 3.4 collective-permute-start.3
  256.7 1.5 collective-permute-start.4
  258.3 3.0 collective-permute-start.5
  261.5 0.7 fusion.7
  262.3 94.5 %collective-permute-done.3 = bf16[128,1024]{1,0:T(8,128)(2,1)S(1)} collective-permute-done((bf16[128,1024]{1,0:T(8,128)(2,1)S(1)}, bf16[128,1024]{1,0:T(8,128)(2,1)S(1)}, u32[]{:S(2)}, u32[]{:S(2)}) %collective-permute-start.3) | collective-permute-done | bytes 262176 | tf_op jit(solution)/shard_map/ppermute | solution.py:13
  356.8 5.6 %collective-permute-done.4 = bf16[128,1024]{1,0:T(8,128)(2,1)S(1)} collective-permute-done((bf16[128,1024]{1,0:T(8,128)(2,1)S(1)}, bf16[128,1024]{1,0:T(8,128)(2,1)S(1)}, u32[]{:S(2)}, u32[]{:S(2)}) %collective-permute-start.4) | collective-permute-done | bytes 262176 | tf_op jit(solution)/shard_map/ppermute | solution.py:13
  362.5 0.8 pad_maximum_fusion.2
  363.3 0.8 pad_maximum_fusion.3
  364.1 2.9 collective-permute-done.5
  367.1 0.8 pad_maximum_fusion.4
  367.9 3.7 convolution_convert_fusion.1
  (58 shorter events, 2.7 us)
Async XLA Ops:
  7.2 15.8 %copy-start.1 = (bf16[2,128,1024]{2,1,0:T(8,128)(2,1)S(1)}, bf16[2,128,1024]{2,1,0:T(8,128)(2,1)}, u32[]{:S(2)}) copy-start(bf16[2,128,1024]{2,1,0:T(8,128)(2,1)} %param.13) | copy-start | bytes 1572868
  7.2 79.4 %all-gather.2.cloned.1.call-start = ((), (), s32[]{:S(2)}) async-start(), calls=%async_computation.4 | async-start | bytes 5013504 | tf_op jit(solution)/shard_map/all_gather | solution.py:72
  12.0 10.0 %collective-permute-start = (bf16[64,2176]{1,0:T(8,128)(2,1)S(1)}, bf16[64,2176]{1,0:T(8,128)(2,1)S(1)}, u32[]{:S(2)}, u32[]{:S(2)}) collective-permute-start(bf16[64,2176]{1,0:T(8,128)(2,1)S(1)} %concatenate.3), channel_id=1, source_target_pairs={{0,16},{16,0},{32,48},{48,32},{64,80},{80,64},{96,112},{112,96},{1... | collective-permute-start | bytes 835592 | tf_op jit(solution)/shard_map/ppermute | solution.py:8
  23.6 52.7 %copy-start.2 = (bf16[2,128,1024]{2,1,0:T(8,128)(2,1)S(1)}, bf16[2,128,1024]{2,1,0:T(8,128)(2,1)}, u32[]{:S(2)}) copy-start(bf16[2,128,1024]{2,1,0:T(8,128)(2,1)} %param.14) | copy-start | bytes 1572868
  78.7 67.2 %all-to-all-start.1 = ((bf16[16,128,1024]{2,1,0:T(8,128)(2,1)}), bf16[16,128,1024]{2,1,0:T(8,128)(2,1)}, u32[]{:S(2)}, u32[]{:S(2)}) async-start(bf16[16,128,1024]{2,1,0:T(8,128)(2,1)} %bitcast.125), calls=%async_computation.1 | async-start | bytes 8388608 | tf_op jit(solution)/shard_map/all_to_all | solution.py:47
  92.3 53.6 %copy-start.3 = (bf16[2,128,1024]{2,1,0:T(8,128)(2,1)S(1)}, bf16[2,128,1024]{2,1,0:T(8,128)(2,1)}, u32[]{:S(2)}) copy-start(bf16[2,128,1024]{2,1,0:T(8,128)(2,1)} %param.15) | copy-start | bytes 1572868
  148.4 67.1 %all-to-all-start.2 = ((bf16[16,128,1024]{2,1,0:T(8,128)(2,1)}), bf16[16,128,1024]{2,1,0:T(8,128)(2,1)}, u32[]{:S(2)}, u32[]{:S(2)}) async-start(bf16[16,128,1024]{2,1,0:T(8,128)(2,1)} %bitcast.126), calls=%async_computation.2 | async-start | bytes 8388608 | tf_op jit(solution)/shard_map/all_to_all | solution.py:48
  155.4 3.5 copy-start
  158.0 4.4 %collective-permute-start.1 = (bf16[16,32,2048]{2,1,0:T(8,128)(2,1)S(1)}, bf16[16,32,2048]{2,1,0:T(8,128)(2,1)S(1)}, u32[]{:S(2)}, u32[]{:S(2)}) collective-permute-start(bf16[16,32,2048]{2,1,0:T(8,128)(2,1)S(1)} %fusion.4), channel_id=1, source_target_pairs={{0,1},{1,0},{2,3},{3,2},{4,5},{5,4},{6,7},{7,6},{8,9},{9,8},{10,11... | collective-permute-start | bytes 6291464 | tf_op jit(solution)/shard_map/ppermute | solution.py:8
  162.4 3.7 copy-start.4
  162.8 2.1 copy-start.5
  233.3 4.2 %collective-permute-start.2 = (bf16[16,32,2048]{2,1,0:T(8,128)(2,1)S(1)}, bf16[16,32,2048]{2,1,0:T(8,128)(2,1)S(1)}, u32[]{:S(2)}, u32[]{:S(2)}) collective-permute-start(bf16[16,32,2048]{2,1,0:T(8,128)(2,1)S(1)} %bitcast.137), channel_id=1, source_target_pairs={{0,1},{1,0},{2,3},{3,2},{4,5},{5,4},{6,7},{7,6},{8,9},{9,8},{10,11... | collective-permute-start | bytes 6291464 | tf_op jit(solution)/shard_map/ppermute | solution.py:8
  239.8 10.9 %copy-start.7 = (s32[32]{0:T(128)S(1)}, s32[32]{0:T(128)}, u32[]{:S(2)}) copy-start(s32[32]{0:T(128)} %param.11) | copy-start | bytes 388
  239.8 11.5 %copy-start.8 = (s32[32]{0:T(128)S(1)}, s32[32]{0:T(128)}, u32[]{:S(2)}) copy-start(s32[32]{0:T(128)} %param.12) | copy-start | bytes 388
  239.8 21.6 %copy-start.6 = (f32[64,8]{0,1:T(8,128)S(1)}, f32[64,8]{0,1:T(8,128)}, u32[]{:S(2)}) copy-start(f32[64,8]{0,1:T(8,128)} %param.9) | copy-start | bytes 6148
  239.8 128.2 %all-to-all-start.3 = ((bf16[16,2,32,2048]{3,2,1,0:T(8,128)(2,1)}), bf16[16,2,32,2048]{3,2,1,0:T(8,128)(2,1)}, u32[]{:S(2)}, u32[]{:S(2)}) async-start(bf16[16,2,32,2048]{3,2,1,0:T(8,128)(2,1)} %maximum_select_fusion), calls=%async_computation.3 | async-start | bytes 8388608 | tf_op jit(solution)/shard_map/all_to_all | solution.py:105
  253.2 103.6 %collective-permute-start.3 = (bf16[128,1024]{1,0:T(8,128)(2,1)S(1)}, bf16[128,1024]{1,0:T(8,128)(2,1)S(1)}, u32[]{:S(2)}, u32[]{:S(2)}) collective-permute-start(bf16[128,1024]{1,0:T(8,128)(2,1)S(1)} %bitcast_select_fusion.9), channel_id=1, source_target_pairs={{0,16},{16,32},{32,48},{48,64},{64,80},{80,96},{96,112},{112,128},... | collective-permute-start | bytes 786440 | tf_op jit(solution)/shard_map/ppermute | solution.py:13
  256.7 105.7 %collective-permute-start.4 = (bf16[128,1024]{1,0:T(8,128)(2,1)S(1)}, bf16[128,1024]{1,0:T(8,128)(2,1)S(1)}, u32[]{:S(2)}, u32[]{:S(2)}) collective-permute-start(bf16[128,1024]{1,0:T(8,128)(2,1)S(1)} %bitcast_select_fusion.6), channel_id=1, source_target_pairs={{0,16},{16,32},{32,48},{48,64},{64,80},{80,96},{96,112},{112,128},... | collective-permute-start | bytes 786440 | tf_op jit(solution)/shard_map/ppermute | solution.py:13
  258.3 108.8 %collective-permute-start.5 = (bf16[128,1024]{1,0:T(8,128)(2,1)S(1)}, bf16[128,1024]{1,0:T(8,128)(2,1)S(1)}, u32[]{:S(2)}, u32[]{:S(2)}) collective-permute-start(bf16[128,1024]{1,0:T(8,128)(2,1)S(1)} %bitcast_select_fusion.3), channel_id=1, source_target_pairs={{0,16},{16,32},{32,48},{48,64},{64,80},{80,96},{96,112},{112,128},... | collective-permute-start | bytes 786440 | tf_op jit(solution)/shard_map/ppermute | solution.py:13
Sparse Core Ops, SparseCore 0:
  23.1 60.1 all-gather.1

commit v8 on v6

--- a/solution.py
+++ b/solution.py
@@ -118,7 +118,12 @@
         ],
         axis=1,
     )
-    gathered = lax.all_gather(jnp.concatenate([tokens, side], axis=1), "dp", axis=0, tiled=False)
+    ext = jnp.concatenate([tokens, side], axis=1)
+    pair = jnp.stack([ext, partner_2(ext, "dp", 0)], axis=0)
+    pair = jnp.where(row_id % 2 == 1, pair[::-1], pair)
+    groups = [list(range(g, n_rows, 2)) for g in range(2)]
+    gathered = lax.all_gather(pair, "dp", axis=0, tiled=True, axis_index_groups=groups)
+    gathered = gathered.reshape(n_rows, tok_count, -1)
     full_slots = gather_slots(w_gate, w_up, w_down, n_shard)
     gathered, full_slots = lax.optimization_barrier((gathered, full_slots))
     full_gate, full_up, full_down = (piece.reshape(model_width, -1) for piece in full_slots)

time: 414 us -> 414 us (level)
  Pallas kernels: 196 us -> 177 us
  starting transfers between devices: 23.7 us -> 37.6 us
  waiting for transfers between devices: 111 us -> 118 us
    pallas_call x1, Pallas kernels: 196 us -> 177 us  [gather_slots(): pl.pallas_call(lambda *refs: gather_kernel(n_shard, *refs), out_shape=(pi...]
    all_to_all x1, starting transfers between devices: 15.1 us -> 25.9 us  [local(): lax.all_to_all(pair_halves(upper_half, result[0], returned_other), 'dp',...]
    ppermute x2 -> x3, waiting for transfers between devices: 7.94 us -> 14.8 us  [partner_2(): lax.ppermute(x, axis, [(i, i ^ 1 << apart) for i in range(lax.axis_size(a...]
  transfers between devices with their start and end apart: 7 -> 8, of which waited for: 5 -> 6; matrix products, arithmetic and copies ran while one was open for 1% -> 1% of each run, Pallas kernels for 48% -> 43%
where the time goes in v8:
time: 414 us; the launch traced here: 411 us
  Pallas kernels  177 us (43%)
  waiting for transfers between devices  118 us (29%)
  starting transfers between devices  37.6 us (9%)
  matrix products  28.3 us (7%)
  local copies, waits for them, and re-layouts  19.4 us (5%)
  between operations  15.6 us (4%)
  other arithmetic  14.7 us (4%)
    pallas_call x1, Pallas kernels, gather_slots(): pl.pallas_call(lambda *refs: gather_kernel(n_shard, *refs), out_shape=(pi...  177 us
    ppermute x3, waiting for transfers between devices, passed_along(): return lax.ppermute(x, axis, [(i, (i + by) % size) for i in range(size)])  103 us
    all_to_all x1, starting transfers between devices, local(): lax.all_to_all(pair_halves(upper_half, result[0], returned_other), 'dp',...  25.9 us
    dot_general x1, matrix products, local(): lax.dot_general(hidden, full_down, (((1,), (1,)), ((), ())), preferred_el...  15.1 us
    ppermute x3, waiting for transfers between devices, partner_2(): lax.ppermute(x, axis, [(i, i ^ 1 << apart) for i in range(lax.axis_size(a...  14.8 us
    optimization_barrier x1, local copies, waits for them, and re-layouts, local(): gathered, full_slots = lax.optimization_barrier((gathered, full_slots))  9.2 us
  transfers between devices with their start and end apart: 8, of which 6 were waited for; matrix products, arithmetic and copies ran while one was open for 1% of the time, Pallas kernels for 43%

profile of v8, /device:TPU:8, one launch (start us, length us, event | category | flops | bytes accessed | tf_op | source)
XLA Modules:
  0.0 410.6 jit_solution(4306214697555537413)
XLA Ops:
  7.2 0.8 select_reduce_fusion.1
  8.0 0.8 select_reduce_fusion
  9.1 1.2 reduce-window.14
  10.2 0.2 slice_reduce_fusion
  10.5 0.1 fusion.22
  10.8 0.1 copy.103
  10.9 1.0 concatenate.3
  11.9 3.1 collective-permute-start
  15.0 6.9 %collective-permute-done = bf16[64,2176]{1,0:T(8,128)(2,1)S(1)} collective-permute-done((bf16[64,2176]{1,0:T(8,128)(2,1)S(1)}, bf16[64,2176]{1,0:T(8,128)(2,1)S(1)}, u32[]{:S(2)}, u32[]{:S(2)}) %collective-permute-start) | collective-permute-done | bytes 278560 | tf_op jit(solution)/shard_map/ppermute | solution.py:69
  22.0 0.9 reverse_select_fusion
  22.9 177.2 %shard_map.111 = (bf16[16,128,1024]{2,1,0:T(8,128)(2,1)}, bf16[16,128,1024]{2,1,0:T(8,128)(2,1)}, bf16[16,128,1024]{2,1,0:T(8,128)(2,1)}) custom-call(bf16[2,128,1024]{2,1,0:T(8,128)(2,1)} %refs_0_.1, bf16[2,128,1024]{2,1,0:T(8,128)(2,1)} %refs_1_.1, bf16[2,128,1024]{2,1,0:T(8,128)(2,1)} %refs_2_.1), custom_call_target="tpu_custom_call" | custom-call | bytes 25165824 | tf_op jit(solution)/shard_map/pallas_call | solution.py:51
  200.1 9.2 %copy.104 = bf16[16,64,2176]{1,2,0:T(8,128)(2,1)} copy(bf16[16,64,2176]{2,1,0:T(8,128)(2,1)} %all-gather.2.cloned.1.call-done) | data formatting | bytes 8912896 | tf_op jit(solution)/shard_map/optimization_barrier | solution.py:128
  209.3 0.8 slice_convert_fusion
  210.1 0.2 copy.105
  210.3 0.2 fusion.18
  210.6 2.3 reduce-window.16
  212.9 0.1 copy.107
  213.1 0.1 copy.111
  213.3 0.2 copy.112
  213.5 0.2 copy.113
  213.8 1.0 fusion.4
  214.8 3.4 fusion.5
  218.2 0.2 fusion.8
  218.4 0.3 collective-permute-start.1
  218.7 0.2 fusion.9
  218.9 3.9 collective-permute-done.1
  222.8 0.4 pad_maximum_fusion
  223.2 3.3 copy-done.5
  226.5 6.0 %fusion.27 = f32[1024,1024]{1,0:T(8,128)} fusion(bf16[1024,2048]{1,0:T(8,128)(2,1)S(1)} %bitcast.123, bf16[2048,1024]{1,0:T(8,128)(2,1)S(1)} %bitcast.136), kind=kOutput, calls=%fused_computation.65 | convolution fusion | flops 4294967296 | bytes 12582912 | tf_op jit(solution)/shard_map/dot_general | solution.py:153
  232.6 15.1 %convolution_convert_fusion = bf16[1024,2048]{1,0:T(8,128)(2,1)} fusion(bf16[2048,1024]{1,0:T(8,128)(2,1)} %bitcast.135, f32[1024,1024]{1,0:T(8,128)} %fusion.27, bf16[1024,2048]{1,0:T(8,128)(2,1)} %bitcast.124, bf16[2048,1024]{1,0:T(8,128)(2,1)} %bitcast.134), kind=kOutput, calls=%fused_computation.11 | convolution fusion | flops 8598323200 | bytes 20971520 | tf_op jit(solution)/shard_map/dot_general | solution.py:156
  247.7 2.7 fusion.25
  250.4 0.2 collective-permute-start.2
  250.7 4.0 collective-permute-done.2
  254.7 2.2 maximum_select_fusion
  256.9 25.9 %all-to-all-start = ((bf16[16,2,32,2048]{3,2,1,0:T(8,128)(2,1)}), bf16[16,2,32,2048]{3,2,1,0:T(8,128)(2,1)}, u32[]{:S(2)}, u32[]{:S(2)}) async-start(bf16[16,2,32,2048]{3,2,1,0:T(8,128)(2,1)} %maximum_select_fusion), calls=%async_computation | async-start | bytes 8388608 | tf_op jit(solution)/shard_map/all_to_all | solution.py:161
  282.8 0.6 dynamic_slice.8
  283.4 0.6 dynamic_slice.7
  285.4 3.4 collective-permute-start.3
  288.8 1.5 collective-permute-start.4
  290.4 3.0 collective-permute-start.5
  293.7 0.7 fusion.11
  294.4 94.5 %collective-permute-done.3 = bf16[128,1024]{1,0:T(8,128)(2,1)S(1)} collective-permute-done((bf16[128,1024]{1,0:T(8,128)(2,1)S(1)}, bf16[128,1024]{1,0:T(8,128)(2,1)S(1)}, u32[]{:S(2)}, u32[]{:S(2)}) %collective-permute-start.3) | collective-permute-done | bytes 262176 | tf_op jit(solution)/shard_map/ppermute | solution.py:74
  389.0 5.6 %collective-permute-done.4 = bf16[128,1024]{1,0:T(8,128)(2,1)S(1)} collective-permute-done((bf16[128,1024]{1,0:T(8,128)(2,1)S(1)}, bf16[128,1024]{1,0:T(8,128)(2,1)S(1)}, u32[]{:S(2)}, u32[]{:S(2)}) %collective-permute-start.4) | collective-permute-done | bytes 262176 | tf_op jit(solution)/shard_map/ppermute | solution.py:74
  394.6 0.8 pad_maximum_fusion.2
  395.4 0.8 pad_maximum_fusion.3
  396.3 2.9 collective-permute-done.5
  399.2 0.8 pad_maximum_fusion.4
  400.1 3.7 convolution_convert_fusion.1
  (48 shorter events, 1.5 us)
Async XLA Ops:
  7.2 193.0 %all-gather.2.cloned.1.call-start = ((), (), s32[]{:S(2)}) async-start(), calls=%async_computation.1 | async-start | bytes 5013504 | tf_op jit(solution)/shard_map/all_gather | solution.py:125
  11.9 10.0 %collective-permute-start = (bf16[64,2176]{1,0:T(8,128)(2,1)S(1)}, bf16[64,2176]{1,0:T(8,128)(2,1)S(1)}, u32[]{:S(2)}, u32[]{:S(2)}) collective-permute-start(bf16[64,2176]{1,0:T(8,128)(2,1)S(1)} %concatenate.3), channel_id=1, source_target_pairs={{0,16},{16,0},{32,48},{48,32},{64,80},{80,64},{96,112},{112,96},{1... | collective-permute-start | bytes 835592 | tf_op jit(solution)/shard_map/ppermute | solution.py:69
  218.4 4.4 %collective-permute-start.1 = (bf16[16,32,2048]{2,1,0:T(8,128)(2,1)S(1)}, bf16[16,32,2048]{2,1,0:T(8,128)(2,1)S(1)}, u32[]{:S(2)}, u32[]{:S(2)}) collective-permute-start(bf16[16,32,2048]{2,1,0:T(8,128)(2,1)S(1)} %fusion.8), channel_id=1, source_target_pairs={{0,1},{1,0},{2,3},{3,2},{4,5},{5,4},{6,7},{7,6},{8,9},{9,8},{10,11... | collective-permute-start | bytes 6291464 | tf_op jit(solution)/shard_map/ppermute | solution.py:69
  222.8 3.7 copy-start.5
  223.2 9.4 %copy-start.3 = (bf16[2,16,32,2048]{3,2,1,0:T(8,128)(2,1)}, bf16[2,16,32,2048]{3,2,1,0:T(8,128)(2,1)S(1)}, u32[]{:S(2)}) copy-start(bf16[2,16,32,2048]{3,2,1,0:T(8,128)(2,1)S(1)} %pad_maximum_fusion) | copy-start | bytes 12582916
  250.4 4.2 %collective-permute-start.2 = (bf16[16,32,2048]{2,1,0:T(8,128)(2,1)S(1)}, bf16[16,32,2048]{2,1,0:T(8,128)(2,1)S(1)}, u32[]{:S(2)}, u32[]{:S(2)}) collective-permute-start(bf16[16,32,2048]{2,1,0:T(8,128)(2,1)S(1)} %bitcast.130), channel_id=1, source_target_pairs={{0,1},{1,0},{2,3},{3,2},{4,5},{5,4},{6,7},{7,6},{8,9},{9,8},{10,11... | collective-permute-start | bytes 6291464 | tf_op jit(solution)/shard_map/ppermute | solution.py:69
  256.8 26.0 %copy-start.6 = (s32[32]{0:T(128)S(1)}, s32[32]{0:T(128)}, u32[]{:S(2)}) copy-start(s32[32]{0:T(128)} %param.11) | copy-start | bytes 388
  256.8 26.6 %copy-start.7 = (s32[32]{0:T(128)S(1)}, s32[32]{0:T(128)}, u32[]{:S(2)}) copy-start(s32[32]{0:T(128)} %param.12) | copy-start | bytes 388
  256.8 28.5 %copy-start = (bf16[2,128,1024]{2,1,0:T(8,128)(2,1)S(1)}, bf16[2,128,1024]{2,1,0:T(8,128)(2,1)}, u32[]{:S(2)}) copy-start(bf16[2,128,1024]{2,1,0:T(8,128)(2,1)} %refs_0_.1) | copy-start | bytes 1572868
  256.8 32.0 %copy-start.1 = (bf16[2,128,1024]{2,1,0:T(8,128)(2,1)S(1)}, bf16[2,128,1024]{2,1,0:T(8,128)(2,1)}, u32[]{:S(2)}) copy-start(bf16[2,128,1024]{2,1,0:T(8,128)(2,1)} %refs_1_.1) | copy-start | bytes 1572868
  256.8 33.5 %copy-start.2 = (bf16[2,128,1024]{2,1,0:T(8,128)(2,1)S(1)}, bf16[2,128,1024]{2,1,0:T(8,128)(2,1)}, u32[]{:S(2)}) copy-start(bf16[2,128,1024]{2,1,0:T(8,128)(2,1)} %refs_2_.1) | copy-start | bytes 1572868
  256.9 36.6 %copy-start.4 = (f32[64,8]{0,1:T(8,128)S(1)}, f32[64,8]{0,1:T(8,128)}, u32[]{:S(2)}) copy-start(f32[64,8]{0,1:T(8,128)} %param.9) | copy-start | bytes 6148
  256.9 143.2 %all-to-all-start = ((bf16[16,2,32,2048]{3,2,1,0:T(8,128)(2,1)}), bf16[16,2,32,2048]{3,2,1,0:T(8,128)(2,1)}, u32[]{:S(2)}, u32[]{:S(2)}) async-start(bf16[16,2,32,2048]{3,2,1,0:T(8,128)(2,1)} %maximum_select_fusion), calls=%async_computation | async-start | bytes 8388608 | tf_op jit(solution)/shard_map/all_to_all | solution.py:161
  285.4 103.6 %collective-permute-start.3 = (bf16[128,1024]{1,0:T(8,128)(2,1)S(1)}, bf16[128,1024]{1,0:T(8,128)(2,1)S(1)}, u32[]{:S(2)}, u32[]{:S(2)}) collective-permute-start(bf16[128,1024]{1,0:T(8,128)(2,1)S(1)} %bitcast_select_fusion.9), channel_id=1, source_target_pairs={{0,16},{16,32},{32,48},{48,64},{64,80},{80,96},{96,112},{112,128},... | collective-permute-start | bytes 786440 | tf_op jit(solution)/shard_map/ppermute | solution.py:74
  288.8 105.7 %collective-permute-start.4 = (bf16[128,1024]{1,0:T(8,128)(2,1)S(1)}, bf16[128,1024]{1,0:T(8,128)(2,1)S(1)}, u32[]{:S(2)}, u32[]{:S(2)}) collective-permute-start(bf16[128,1024]{1,0:T(8,128)(2,1)S(1)} %bitcast_select_fusion.6), channel_id=1, source_target_pairs={{0,16},{16,32},{32,48},{48,64},{64,80},{80,96},{96,112},{112,128},... | collective-permute-start | bytes 786440 | tf_op jit(solution)/shard_map/ppermute | solution.py:74
  290.4 108.8 %collective-permute-start.5 = (bf16[128,1024]{1,0:T(8,128)(2,1)S(1)}, bf16[128,1024]{1,0:T(8,128)(2,1)S(1)}, u32[]{:S(2)}, u32[]{:S(2)}) collective-permute-start(bf16[128,1024]{1,0:T(8,128)(2,1)S(1)} %bitcast_select_fusion.3), channel_id=1, source_target_pairs={{0,16},{16,32},{32,48},{48,64},{64,80},{80,96},{96,112},{112,128},... | collective-permute-start | bytes 786440 | tf_op jit(solution)/shard_map/ppermute | solution.py:74
Sparse Core Ops, SparseCore 0:
  23.0 60.1 all-gather.1

commit v9 on v7

--- a/solution.py
+++ b/solution.py
@@ -93,6 +93,17 @@
     other_rows = jnp.where(upper_half, arrived[:, 0], arrived[:, 1])
     partner = partner_2(other_rows, "shard", 0)
     work_rows = jnp.stack([own_rows, partner], axis=0)
+    base_slot = 2 * row_id
+    second_old = lax.dynamic_index_in_dim(old_place, base_slot + 1, 0, keepdims=False)
+    second_new = lax.dynamic_index_in_dim(new_place, base_slot + 1, 0, keepdims=False)
+    second_moved = second_new != second_old
+    leave_gate = jnp.where(second_moved, w_gate[1], w_gate[0])
+    leave_up = jnp.where(second_moved, w_up[1], w_up[0])
+    leave_down = jnp.where(second_moved, w_down[1], w_down[0])
+    arrive_gate, arrive_up, arrive_down = passed_along((leave_gate, leave_up, leave_down), "dp", 1)
+    work_rows, arrive_gate, arrive_up, arrive_down = lax.optimization_barrier(
+        (work_rows, arrive_gate, arrive_up, arrive_down)
+    )
     flat_rows = work_rows.reshape(-1, model_width)
     gate_part = jnp.dot(flat_rows, full_gate, preferred_element_type=jnp.float32)
     up_part = jnp.dot(flat_rows, full_up, preferred_element_type=jnp.float32)
@@ -121,14 +132,6 @@
     moe_output = jnp.dot(
         combine, returned.reshape(places, model_width), preferred_element_type=jnp.float32
     ).astype(jnp.bfloat16)
-    base_slot = 2 * row_id
-    second_old = lax.dynamic_index_in_dim(old_place, base_slot + 1, 0, keepdims=False)
-    second_new = lax.dynamic_index_in_dim(new_place, base_slot + 1, 0, keepdims=False)
-    second_moved = second_new != second_old
-    leave_gate = jnp.where(second_moved, w_gate[1], w_gate[0])
-    leave_up = jnp.where(second_moved, w_up[1], w_up[0])
-    leave_down = jnp.where(second_moved, w_down[1], w_down[0])
-    arrive_gate, arrive_up, arrive_down = passed_along((leave_gate, leave_up, leave_down), "dp", 1)
     new_gate = jnp.stack(
         [
             jnp.where(second_moved, w_gate[0], arrive_gate),

time: 381 us -> 388 us (1.018)
  waiting for transfers between devices: 209 us -> 214 us
  other arithmetic: 16.4 us -> 20.8 us
    all_to_all x1, waiting for transfers between devices: 0.01 us -> 96.6 us  [local(): lax.all_to_all(pair_halves(upper_half, result[0], returned_other), 'dp',...]
    all_to_all x1, waiting for transfers between devices: 48.1 us -> 0.01 us  [local(): lax.all_to_all(widen(w_up, half_count), 'shard', split_axis=0, concat_axi...]
    ppermute x3, waiting for transfers between devices: 103 us -> 57.8 us  [passed_along(): return lax.ppermute(x, axis, [(i, (i + by) % size) for i in range(size)])]
    all_to_all x1, waiting for transfers between devices: 43.3 us -> 48.1 us  [local(): lax.all_to_all(widen(w_gate, half_count), 'shard', split_axis=0, concat_a...]
  transfers between devices with their start and end apart: 10 -> 10, of which waited for: 8 -> 7; matrix products, arithmetic and copies ran while one was open for 7% -> 9% of each run, Pallas kernels for 0% -> 0%
where the time goes in v9:
time: 388 us; the launch traced here: 387 us
  waiting for transfers between devices  214 us (55%)
  blocking collectives  52.6 us (14%)
  starting transfers between devices  38.4 us (10%)
  matrix products  32.5 us (8%)
  other arithmetic  20.8 us (5%)
  between operations  15.6 us (4%)
  local copies, waits for them, and re-layouts  13.5 us (3%)
    all_to_all x1, waiting for transfers between devices, local(): lax.all_to_all(pair_halves(upper_half, result[0], returned_other), 'dp',...  96.6 us
    ppermute x3, waiting for transfers between devices, passed_along(): return lax.ppermute(x, axis, [(i, (i + by) % size) for i in range(size)])  57.8 us
    all_to_all x1, blocking collectives, local(): lax.all_to_all(widen(w_down, half_count), 'shard', split_axis=0, concat_a...  52.6 us
    all_to_all x1, waiting for transfers between devices, local(): lax.all_to_all(widen(w_gate, half_count), 'shard', split_axis=0, concat_a...  48.1 us
    dot_general x1, matrix products, local(): lax.dot_general(hidden, full_down, (((1,), (1,)), ((), ())), preferred_el...  15.2 us
    all_to_all x1, starting transfers between devices, local(): lax.all_to_all(pair_halves(upper_half, result[0], returned_other), 'dp',...  12.2 us
    ppermute x3, waiting for transfers between devices, partner_2(): lax.ppermute(x, axis, [(i, i ^ 1 << apart) for i in range(lax.axis_size(a...  11 us
    dot_general x1, matrix products, local(): jnp.dot(flat_rows, full_gate, preferred_element_type=jnp.float32)  8.2 us
  transfers between devices with their start and end apart: 10, of which 7 were waited for; matrix products, arithmetic and copies ran while one was open for 9% of the time, Pallas kernels for 0%

profile of v9, /device:TPU:8, one launch (start us, length us, event | category | flops | bytes accessed | tf_op | source)
XLA Modules:
  0.0 387.1 jit_solution(9944659460060622984)
XLA Ops:
  7.2 0.8 select_reduce_fusion.1
  8.0 0.8 select_reduce_fusion
  9.1 1.2 reduce-window.14
  10.3 0.2 slice_reduce_fusion
  10.9 1.0 concatenate.3
  12.0 3.1 collective-permute-start
  15.1 6.9 %collective-permute-done = bf16[64,2176]{1,0:T(8,128)(2,1)S(1)} collective-permute-done((bf16[64,2176]{1,0:T(8,128)(2,1)S(1)}, bf16[64,2176]{1,0:T(8,128)(2,1)S(1)}, u32[]{:S(2)}, u32[]{:S(2)}) %collective-permute-start) | collective-permute-done | bytes 278560 | tf_op jit(solution)/shard_map/ppermute | solution.py:8
  22.0 0.9 reverse_select_fusion
  23.0 0.5 tile.31
  23.6 52.6 %all_to_all.32 = bf16[16,128,1024]{2,1,0:T(8,128)(2,1)} all-to-all(bf16[16,128,1024]{2,1,0:T(8,128)(2,1)S(1)} %bitcast.127), channel_id=1, replica_groups=mesh['dp'=16,'shard'=16] {'shard'}, dimensions={0} | all-to-all | bytes 8388608 | tf_op jit(solution)/shard_map/all_to_all | solution.py:48
  76.2 2.5 tile.12
  78.7 7.8 %all-to-all-start = ((bf16[16,128,1024]{2,1,0:T(8,128)(2,1)}), bf16[16,128,1024]{2,1,0:T(8,128)(2,1)}, u32[]{:S(2)}, u32[]{:S(2)}) async-start(bf16[16,128,1024]{2,1,0:T(8,128)(2,1)} %bitcast.125), calls=%async_computation | async-start | bytes 8388608 | tf_op jit(solution)/shard_map/all_to_all | solution.py:46
  86.6 1.0 slice.75
  87.5 0.1 copy.121
  87.7 0.2 copy.105
  88.1 2.3 reduce-window.16
  90.5 0.1 copy.107
  90.8 0.2 copy.112
  91.0 0.2 copy.113
  91.2 0.1 fusion.14
  91.4 1.0 fusion.2
  92.4 5.4 %fusion.3 = bf16[16,2,32,2048]{3,2,1,0:T(8,128)(2,1)} fusion(pred[16,64,2,32]{1,3,2,0:T(8,128)(4,1)S(1)} %fusion.2, bf16[16,64,2176]{2,1,0:T(8,128)(2,1)} %all-gather.2.cloned.1.call-done), kind=kOutput, calls=%fused_computation.9 | convolution fusion | flops 270532608 | bytes 8454144 | tf_op jit(solution)/shard_map/stcr,std->scrd/dot_general | solution.py:86
  97.8 48.1 %all-to-all-done = bf16[16,128,1024]{2,1,0:T(8,128)(2,1)} async-done(((bf16[16,128,1024]{2,1,0:T(8,128)(2,1)}), bf16[16,128,1024]{2,1,0:T(8,128)(2,1)}, u32[]{:S(2)}, u32[]{:S(2)}) %all-to-all-start) | async-done | bytes 4194336 | tf_op jit(solution)/shard_map/all_to_all | solution.py:46
  145.9 2.5 tile.14
  148.4 7.0 %all-to-all-start.1 = ((bf16[16,128,1024]{2,1,0:T(8,128)(2,1)}), bf16[16,128,1024]{2,1,0:T(8,128)(2,1)}, u32[]{:S(2)}, u32[]{:S(2)}) async-start(bf16[16,128,1024]{2,1,0:T(8,128)(2,1)} %bitcast.126), calls=%async_computation.1 | async-start | bytes 8388608 | tf_op jit(solution)/shard_map/all_to_all | solution.py:47
  155.4 3.8 fusion.4
  159.2 0.1 collective-permute-start.1
  159.3 0.6 dynamic_slice.8
  159.9 0.6 dynamic_slice.7
  161.8 2.8 collective-permute-start.2
  164.7 2.2 collective-permute-start.3
  167.0 3.0 collective-permute-start.4
  169.9 2.4 fusion.5
  172.4 2.0 pad_maximum_fusion
  174.4 47.1 %collective-permute-done.2 = bf16[128,1024]{1,0:T(8,128)(2,1)S(1)} collective-permute-done((bf16[128,1024]{1,0:T(8,128)(2,1)S(1)}, bf16[128,1024]{1,0:T(8,128)(2,1)S(1)}, u32[]{:S(2)}, u32[]{:S(2)}) %collective-permute-start.2) | collective-permute-done | bytes 262176 | tf_op jit(solution)/shard_map/ppermute | solution.py:13
  221.5 5.6 %collective-permute-done.3 = bf16[128,1024]{1,0:T(8,128)(2,1)S(1)} collective-permute-done((bf16[128,1024]{1,0:T(8,128)(2,1)S(1)}, bf16[128,1024]{1,0:T(8,128)(2,1)S(1)}, u32[]{:S(2)}, u32[]{:S(2)}) %collective-permute-start.3) | collective-permute-done | bytes 262176 | tf_op jit(solution)/shard_map/ppermute | solution.py:13
  227.1 5.1 %collective-permute-done.4 = bf16[128,1024]{1,0:T(8,128)(2,1)S(1)} collective-permute-done((bf16[128,1024]{1,0:T(8,128)(2,1)S(1)}, bf16[128,1024]{1,0:T(8,128)(2,1)S(1)}, u32[]{:S(2)}, u32[]{:S(2)}) %collective-permute-start.4) | collective-permute-done | bytes 262176 | tf_op jit(solution)/shard_map/ppermute | solution.py:13
  232.2 8.2 %fusion.23 = f32[1024,1024]{1,0:T(8,128)} fusion(bf16[1024,2048]{1,0:T(8,128)(2,1)S(1)} %bitcast.130, bf16[2048,1024]{1,0:T(8,128)(2,1)} %bitcast.25), kind=kOutput, calls=%fused_computation.63 | convolution fusion | flops 4294967296 | bytes 12582912 | tf_op jit(solution)/shard_map/dot_general | solution.py:108
  240.4 15.2 %convolution_convert_fusion = bf16[1024,2048]{1,0:T(8,128)(2,1)} fusion(bf16[2048,1024]{1,0:T(8,128)(2,1)} %bitcast.129, f32[1024,1024]{1,0:T(8,128)} %fusion.23, bf16[1024,2048]{1,0:T(8,128)(2,1)} %bitcast.131, bf16[2048,1024]{1,0:T(8,128)(2,1)} %bitcast.27), kind=kOutput, calls=%fused_computation.10 | convolution fusion | flops 8598323200 | bytes 20971520 | tf_op jit(solution)/shard_map/dot_general | solution.py:111
  255.6 2.7 fusion.21
  258.4 4.1 %collective-permute-done.5 = bf16[16,32,2048]{2,1,0:T(8,128)(2,1)S(1)} collective-permute-done((bf16[16,32,2048]{2,1,0:T(8,128)(2,1)S(1)}, bf16[16,32,2048]{2,1,0:T(8,128)(2,1)S(1)}, u32[]{:S(2)}, u32[]{:S(2)}) %collective-permute-start.5) | collective-permute-done | bytes 2097184 | tf_op jit(solution)/shard_map/ppermute | solution.py:8
  262.6 2.2 maximum_select_fusion
  264.8 12.2 %all-to-all-start.3 = ((bf16[16,2,32,2048]{3,2,1,0:T(8,128)(2,1)}), bf16[16,2,32,2048]{3,2,1,0:T(8,128)(2,1)}, u32[]{:S(2)}, u32[]{:S(2)}) async-start(bf16[16,2,32,2048]{3,2,1,0:T(8,128)(2,1)} %maximum_select_fusion), calls=%async_computation.3 | async-start | bytes 8388608 | tf_op jit(solution)/shard_map/all_to_all | solution.py:116
  277.2 0.7 fusion.7
  278.0 0.8 pad_maximum_fusion.4
  278.9 1.1 pad_maximum_fusion.2
  280.0 96.6 %all-to-all-done.3 = bf16[16,2,32,2048]{3,2,1,0:T(8,128)(2,1)} async-done(((bf16[16,2,32,2048]{3,2,1,0:T(8,128)(2,1)}), bf16[16,2,32,2048]{3,2,1,0:T(8,128)(2,1)}, u32[]{:S(2)}, u32[]{:S(2)}) %all-to-all-start.3) | async-done | bytes 4194336 | tf_op jit(solution)/shard_map/all_to_all | solution.py:116
  376.5 3.7 convolution_convert_fusion.1
  (53 shorter events, 1.9 us)
Async XLA Ops:
  7.2 15.8 %copy-start = (bf16[2,128,1024]{2,1,0:T(8,128)(2,1)S(1)}, bf16[2,128,1024]{2,1,0:T(8,128)(2,1)}, u32[]{:S(2)}) copy-start(bf16[2,128,1024]{2,1,0:T(8,128)(2,1)} %param.15) | copy-start | bytes 1572868
  7.2 79.4 %all-gather.2.cloned.1.call-start = ((), (), s32[]{:S(2)}) async-start(), calls=%async_computation.4 | async-start | bytes 5013504 | tf_op jit(solution)/shard_map/all_gather | solution.py:72
  12.0 10.0 %collective-permute-start = (bf16[64,2176]{1,0:T(8,128)(2,1)S(1)}, bf16[64,2176]{1,0:T(8,128)(2,1)S(1)}, u32[]{:S(2)}, u32[]{:S(2)}) collective-permute-start(bf16[64,2176]{1,0:T(8,128)(2,1)S(1)} %concatenate.3), channel_id=1, source_target_pairs={{0,16},{16,0},{32,48},{48,32},{64,80},{80,64},{96,112},{112,96},{1... | collective-permute-start | bytes 835592 | tf_op jit(solution)/shard_map/ppermute | solution.py:8
  23.6 52.7 %copy-start.1 = (bf16[2,128,1024]{2,1,0:T(8,128)(2,1)S(1)}, bf16[2,128,1024]{2,1,0:T(8,128)(2,1)}, u32[]{:S(2)}) copy-start(bf16[2,128,1024]{2,1,0:T(8,128)(2,1)} %param.13) | copy-start | bytes 1572868
  78.7 67.2 %all-to-all-start = ((bf16[16,128,1024]{2,1,0:T(8,128)(2,1)}), bf16[16,128,1024]{2,1,0:T(8,128)(2,1)}, u32[]{:S(2)}, u32[]{:S(2)}) async-start(bf16[16,128,1024]{2,1,0:T(8,128)(2,1)} %bitcast.125), calls=%async_computation | async-start | bytes 8388608 | tf_op jit(solution)/shard_map/all_to_all | solution.py:46
  92.3 53.6 %copy-start.2 = (bf16[2,128,1024]{2,1,0:T(8,128)(2,1)S(1)}, bf16[2,128,1024]{2,1,0:T(8,128)(2,1)}, u32[]{:S(2)}) copy-start(bf16[2,128,1024]{2,1,0:T(8,128)(2,1)} %param.14) | copy-start | bytes 1572868
  148.4 92.0 %all-to-all-start.1 = ((bf16[16,128,1024]{2,1,0:T(8,128)(2,1)}), bf16[16,128,1024]{2,1,0:T(8,128)(2,1)}, u32[]{:S(2)}, u32[]{:S(2)}) async-start(bf16[16,128,1024]{2,1,0:T(8,128)(2,1)} %bitcast.126), calls=%async_computation.1 | async-start | bytes 8388608 | tf_op jit(solution)/shard_map/all_to_all | solution.py:47
  155.4 4.0 %copy-start.5 = (s32[32]{0:T(128)S(1)}, s32[32]{0:T(128)}, u32[]{:S(2)}) copy-start(s32[32]{0:T(128)} %param.11) | copy-start | bytes 388
  155.4 4.5 %copy-start.6 = (s32[32]{0:T(128)S(1)}, s32[32]{0:T(128)}, u32[]{:S(2)}) copy-start(s32[32]{0:T(128)} %param.12) | copy-start | bytes 388
  159.2 13.2 %collective-permute-start.1 = (bf16[16,32,2048]{2,1,0:T(8,128)(2,1)}, bf16[16,32,2048]{2,1,0:T(8,128)(2,1)}, u32[]{:S(2)}, u32[]{:S(2)}) collective-permute-start(bf16[16,32,2048]{2,1,0:T(8,128)(2,1)} %fusion.4), channel_id=1, source_target_pairs={{0,1},{1,0},{2,3},{3,2},{4,5},{5,4},{6,7},{7,6},{8,9},{9,8},{10,11... | collective-permute-start | bytes 6291464 | tf_op jit(solution)/shard_map/ppermute | solution.py:8
  161.8 59.6 %collective-permute-start.2 = (bf16[128,1024]{1,0:T(8,128)(2,1)S(1)}, bf16[128,1024]{1,0:T(8,128)(2,1)S(1)}, u32[]{:S(2)}, u32[]{:S(2)}) collective-permute-start(bf16[128,1024]{1,0:T(8,128)(2,1)S(1)} %bitcast_select_fusion.9), channel_id=1, source_target_pairs={{0,16},{16,32},{32,48},{48,64},{64,80},{80,96},{96,112},{112,128},... | collective-permute-start | bytes 786440 | tf_op jit(solution)/shard_map/ppermute | solution.py:13
  164.7 62.4 %collective-permute-start.3 = (bf16[128,1024]{1,0:T(8,128)(2,1)S(1)}, bf16[128,1024]{1,0:T(8,128)(2,1)S(1)}, u32[]{:S(2)}, u32[]{:S(2)}) collective-permute-start(bf16[128,1024]{1,0:T(8,128)(2,1)S(1)} %bitcast_select_fusion.6), channel_id=1, source_target_pairs={{0,16},{16,32},{32,48},{48,64},{64,80},{80,96},{96,112},{112,128},... | collective-permute-start | bytes 786440 | tf_op jit(solution)/shard_map/ppermute | solution.py:13
  167.0 65.3 %collective-permute-start.4 = (bf16[128,1024]{1,0:T(8,128)(2,1)S(1)}, bf16[128,1024]{1,0:T(8,128)(2,1)S(1)}, u32[]{:S(2)}, u32[]{:S(2)}) collective-permute-start(bf16[128,1024]{1,0:T(8,128)(2,1)S(1)} %bitcast_select_fusion.3), channel_id=1, source_target_pairs={{0,16},{16,32},{32,48},{48,64},{64,80},{80,96},{96,112},{112,128},... | collective-permute-start | bytes 786440 | tf_op jit(solution)/shard_map/ppermute | solution.py:13
  174.4 57.9 %copy-start.3 = (bf16[2,16,32,2048]{3,2,1,0:T(8,128)(2,1)}, bf16[2,16,32,2048]{3,2,1,0:T(8,128)(2,1)S(1)}, u32[]{:S(2)}) copy-start(bf16[2,16,32,2048]{3,2,1,0:T(8,128)(2,1)S(1)} %pad_maximum_fusion) | copy-start | bytes 12582916
  258.3 4.2 %collective-permute-start.5 = (bf16[16,32,2048]{2,1,0:T(8,128)(2,1)S(1)}, bf16[16,32,2048]{2,1,0:T(8,128)(2,1)S(1)}, u32[]{:S(2)}, u32[]{:S(2)}) collective-permute-start(bf16[16,32,2048]{2,1,0:T(8,128)(2,1)S(1)} %bitcast.136), channel_id=1, source_target_pairs={{0,1},{1,0},{2,3},{3,2},{4,5},{5,4},{6,7},{7,6},{8,9},{9,8},{10,11... | collective-permute-start | bytes 6291464 | tf_op jit(solution)/shard_map/ppermute | solution.py:8
  264.8 12.3 %copy-start.4 = (f32[64,8]{0,1:T(8,128)S(1)}, f32[64,8]{0,1:T(8,128)}, u32[]{:S(2)}) copy-start(f32[64,8]{0,1:T(8,128)} %param.9) | copy-start | bytes 6148
  264.8 111.8 %all-to-all-start.3 = ((bf16[16,2,32,2048]{3,2,1,0:T(8,128)(2,1)}), bf16[16,2,32,2048]{3,2,1,0:T(8,128)(2,1)}, u32[]{:S(2)}, u32[]{:S(2)}) async-start(bf16[16,2,32,2048]{3,2,1,0:T(8,128)(2,1)} %maximum_select_fusion), calls=%async_computation.3 | async-start | bytes 8388608 | tf_op jit(solution)/shard_map/all_to_all | solution.py:116
Sparse Core Ops, SparseCore 0:
  23.1 60.1 all-gather.1

commit v10 on v7

--- a/solution.py
+++ b/solution.py
@@ -42,14 +42,21 @@
     upper_half = column % 2 == 1
     capacity = max(2, 2 * tok_count * top_count // slot_count)
     places = slot_count * capacity
-    full_gate, full_up, full_down = (
-        lax.all_to_all(widen(w_gate, half_count), "shard", split_axis=0, concat_axis=1, tiled=True),
-        lax.all_to_all(widen(w_up, half_count), "shard", split_axis=0, concat_axis=1, tiled=True),
-        lax.all_to_all(widen(w_down, half_count), "shard", split_axis=0, concat_axis=1, tiled=True),
+    core = column % 2
+    own = jnp.stack([w_gate, w_up, w_down], axis=1)
+    across = partner_2(own, "shard", n_shard.bit_length() - 2)
+    first_plane = column < half_count
+    by_plane = jnp.where(first_plane, jnp.stack([own, across]), jnp.stack([across, own]))
+    kept = jnp.where(core == 0, by_plane[:, 0], by_plane[:, 1])
+    handed = jnp.where(core == 0, by_plane[:, 1], by_plane[:, 0])
+    received = partner_2(handed, "shard", 0)
+    block = jnp.where(
+        core == 0, jnp.stack([kept, received], axis=1), jnp.stack([received, kept], axis=1)
     )
-    full_gate = full_gate[0]
-    full_up = full_up[0]
-    full_down = full_down[0]
+    groups = [list(range(g % 2 + (g // 2) * half_count, (g // 2 + 1) * half_count, 2)) for g in range(4)]
+    ring = lax.all_gather(block, "shard", axis=0, tiled=False, axis_index_groups=groups)
+    full = jnp.transpose(ring, (3, 1, 0, 2, 4, 5)).reshape(3, model_width, -1)
+    full_gate, full_up, full_down = full[0], full[1], full[2]
     slot_index = jnp.arange(slot_count, dtype=jnp.int32)
     owner_slot = jnp.sum(
         jnp.where(old_place[None, :] == slot_index[:, None], slot_index[None, :], 0), axis=1

time: 381 us -> 381 us (level)
  waiting for transfers between devices: 209 us -> 276 us
  blocking collectives: 52.6 us -> 0 us
  starting transfers between devices: 37.4 us -> 22.9 us
  other arithmetic: 16.4 us -> 22 us
    all_gather x0 -> x1, waiting for transfers between devices: none -> 105 us  [local(): lax.all_gather(block, 'shard', axis=0, tiled=False, axis_index_groups=gro...]
    all_to_all x2 -> x0, waiting for transfers between devices: 91.5 us -> none  [the longest x1 48.1 us: local(): lax.all_to_all(widen(w_up, half_count), 'shard', split_axis=0, concat_axi...]
    all_to_all x1 -> x0, blocking collectives: 52.6 us -> none  [local(): lax.all_to_all(widen(w_gate, half_count), 'shard', split_axis=0, concat_a...]
    ppermute x3 -> x5, waiting for transfers between devices: 14.4 us -> 52.4 us  [partner_2(): lax.ppermute(x, axis, [(i, i ^ 1 << apart) for i in range(lax.axis_size(a...]
    all_gather x1, waiting for transfers between devices: 0.02 us -> 15.3 us  [local(): lax.all_gather(pair, 'dp', axis=0, tiled=True, axis_index_groups=groups)]
    all_to_all x2 -> x0, starting transfers between devices: 14.8 us -> none  [the longest x1 7.81 us: local(): lax.all_to_all(widen(w_up, half_count), 'shard', split_axis=0, concat_axi...]
    slice x1 -> x2, local copies, waits for them, and re-layouts: 0.22 us -> 8.07 us  [the longest x1 7.85 us: local(): full_gate, full_up, full_down = (full[0], full[1], full[2])]
    another operation x8 -> x5, local copies, waits for them, and re-layouts: 5.72 us -> 0.22 us  [the longest x3 5.5 us: widen(): return jnp.tile(pieces, (half_count, 1, 1))]
  transfers between devices with their start and end apart: 10 -> 11, of which waited for: 8 -> 10; matrix products, arithmetic and copies ran while one was open for 7% -> 6% of each run, Pallas kernels for 0% -> 0%
where the time goes in v10:
time: 381 us
  waiting for transfers between devices  276 us (72%)
  matrix products  28.3 us (7%)
  starting transfers between devices  22.9 us (6%)
  other arithmetic  22 us (6%)
  local copies, waits for them, and re-layouts  15.9 us (4%)
  between operations  15.6 us (4%)
    all_gather x1, waiting for transfers between devices, local(): lax.all_gather(block, 'shard', axis=0, tiled=False, axis_index_groups=gro...  105 us
    ppermute x3, waiting for transfers between devices, passed_along(): return lax.ppermute(x, axis, [(i, (i + by) % size) for i in range(size)])  103 us
    ppermute x5, waiting for transfers between devices, partner_2(): lax.ppermute(x, axis, [(i, i ^ 1 << apart) for i in range(lax.axis_size(a...  52.4 us
    all_gather x1, waiting for transfers between devices, local(): lax.all_gather(pair, 'dp', axis=0, tiled=True, axis_index_groups=groups)  15.3 us
    dot_general x1, matrix products, local(): lax.dot_general(hidden, full_down, (((1,), (1,)), ((), ())), preferred_el...  15.2 us
    all_to_all x1, starting transfers between devices, local(): lax.all_to_all(pair_halves(upper_half, result[0], returned_other), 'dp',...  9.71 us
    ppermute x3, starting transfers between devices, passed_along(): return lax.ppermute(x, axis, [(i, (i + by) % size) for i in range(size)])  8.03 us
    slice x1, local copies, waits for them, and re-layouts, local(): full_gate, full_up, full_down = (full[0], full[1], full[2])  7.85 us
  transfers between devices with their start and end apart: 11, of which 10 were waited for; matrix products, arithmetic and copies ran while one was open for 6% of the time, Pallas kernels for 0%

profile of v10, /device:TPU:8, one launch (start us, length us, event | category | flops | bytes accessed | tf_op | source)
XLA Modules:
  0.0 380.7 jit_solution(12730518975673931493)
XLA Ops:
  7.2 0.9 select_reduce_fusion.1
  8.1 0.8 select_reduce_fusion
  9.2 1.2 reduce-window.14
  10.4 0.2 slice_reduce_fusion
  11.0 1.0 concatenate.17
  12.1 3.1 collective-permute-start
  15.2 6.9 %collective-permute-done = bf16[64,2176]{1,0:T(8,128)(2,1)S(1)} collective-permute-done((bf16[64,2176]{1,0:T(8,128)(2,1)S(1)}, bf16[64,2176]{1,0:T(8,128)(2,1)S(1)}, u32[]{:S(2)}, u32[]{:S(2)}) %collective-permute-start) | collective-permute-done | bytes 278560 | tf_op jit(solution)/shard_map/ppermute | solution.py:8
  22.1 0.9 reverse_select_fusion
  23.1 1.4 fusion.21
  24.5 1.5 collective-permute-start.2
  26.0 34.1 %collective-permute-done.2 = bf16[2,3,128,1024]{3,2,1,0:T(8,128)(2,1)} collective-permute-done((bf16[2,3,128,1024]{3,2,1,0:T(8,128)(2,1)}, bf16[2,3,128,1024]{3,2,1,0:T(8,128)(2,1)}, u32[]{:S(2)}, u32[]{:S(2)}) %collective-permute-start.2) | collective-permute-done | bytes 1572896 | tf_op jit(solution)/shard_map/ppermute | solution.py:8
  60.1 2.3 maximum_select_fusion.1
  62.4 0.2 select_bitcast_fusion.1
  62.7 3.4 collective-permute-done.3
  66.1 1.9 maximum_select_fusion.2
  68.1 15.3 %all-gather.3.cloned.1.call-done = bf16[16,64,2176]{2,1,0:T(8,128)(2,1)} async-done(((bf16[2,64,2176]{2,1,0:T(8,128)(2,1)}), bf16[16,64,2176]{2,1,0:T(8,128)(2,1)}) %all-gather.3.cloned.1.call-update) | async-done | bytes 4456464 | tf_op jit(solution)/shard_map/all_gather | solution.py:79
  83.4 1.0 slice.100
  84.9 2.3 reduce-window.16
  87.6 0.2 copy.116
  87.8 0.2 copy.117
  88.2 1.0 fusion.2
  89.2 3.4 fusion.3
  92.6 0.2 fusion.4
  92.8 0.3 collective-permute-start.1
  93.1 0.2 fusion.5
  93.3 3.9 %collective-permute-done.1 = bf16[16,32,2048]{2,1,0:T(8,128)(2,1)S(1)} collective-permute-done((bf16[16,32,2048]{2,1,0:T(8,128)(2,1)S(1)}, bf16[16,32,2048]{2,1,0:T(8,128)(2,1)S(1)}, u32[]{:S(2)}, u32[]{:S(2)}) %collective-permute-start.1) | collective-permute-done | bytes 2097184 | tf_op jit(solution)/shard_map/ppermute | solution.py:8
  97.2 2.5 pad_maximum_fusion
  99.7 105.3 %all-gather.5.cloned.1.call-done = bf16[4,2,2,3,128,1024]{5,4,2,0,1,3:T(8,128)(2,1)} async-done(((bf16[1,2,2,3,128,1024]{5,4,2,0,1,3:T(8,128)(2,1)}), bf16[4,2,2,3,128,1024]{5,4,2,0,1,3:T(8,128)(2,1)}) %all-gather.5.cloned.1.call-update) | async-done | bytes 12582928 | tf_op jit(solution)/shard_map/all_gather | solution.py:57
  205.0 7.9 %fusion.22 = (bf16[1,2,4,2,128,1024]{5,4,3,2,1,0:T(8,128)(2,1)}, bf16[1,2,4,2,128,1024]{5,4,3,2,1,0:T(8,128)(2,1)}, bf16[1,2,4,2,128,1024]{5,4,3,2,1,0:T(8,128)(2,1)S(1)}) fusion(bf16[3,2,4,2,128,1024]{5,4,3,2,1,0:T(8,128)(2,1)} %bitcast.134), kind=kLoop, calls=%fused_computation.67 | loop fusion | bytes 25165824 | tf_op jit(solution)/shard_map/slice | solution.py:59
  212.8 6.0 %fusion.25 = f32[1024,1024]{1,0:T(8,128)} fusion(bf16[1024,2048]{1,0:T(8,128)(2,1)S(1)} %bitcast.140, bf16[2048,1024]{1,0:T(8,128)(2,1)S(1)} %bitcast.143), kind=kOutput, calls=%fused_computation.70 | convolution fusion | flops 4294967296 | bytes 12582912 | tf_op jit(solution)/shard_map/dot_general | solution.py:104
  218.8 15.2 %convolution_convert_fusion = bf16[1024,2048]{1,0:T(8,128)(2,1)} fusion(bf16[2048,1024]{1,0:T(8,128)(2,1)} %bitcast.142, f32[1024,1024]{1,0:T(8,128)} %fusion.25, bf16[1024,2048]{1,0:T(8,128)(2,1)} %bitcast.139, bf16[2048,1024]{1,0:T(8,128)(2,1)} %bitcast.141), kind=kOutput, calls=%fused_computation.10 | convolution fusion | flops 8598323200 | bytes 20971520 | tf_op jit(solution)/shard_map/dot_general | solution.py:107
  234.0 2.7 fusion.23
  236.8 4.1 %collective-permute-done.4 = bf16[16,32,2048]{2,1,0:T(8,128)(2,1)S(1)} collective-permute-done((bf16[16,32,2048]{2,1,0:T(8,128)(2,1)S(1)}, bf16[16,32,2048]{2,1,0:T(8,128)(2,1)S(1)}, u32[]{:S(2)}, u32[]{:S(2)}) %collective-permute-start.4) | collective-permute-done | bytes 2097184 | tf_op jit(solution)/shard_map/ppermute | solution.py:8
  241.0 2.2 maximum_select_fusion
  243.2 9.7 %all-to-all-start = ((bf16[16,2,32,2048]{3,2,1,0:T(8,128)(2,1)}), bf16[16,2,32,2048]{3,2,1,0:T(8,128)(2,1)}, u32[]{:S(2)}, u32[]{:S(2)}) async-start(bf16[16,2,32,2048]{3,2,1,0:T(8,128)(2,1)} %maximum_select_fusion), calls=%async_computation | async-start | bytes 8388608 | tf_op jit(solution)/shard_map/all_to_all | solution.py:112
  252.9 0.6 dynamic_slice.8
  253.5 0.6 dynamic_slice.7
  255.4 3.4 collective-permute-start.5
  258.9 1.5 collective-permute-start.6
  260.5 3.0 collective-permute-start.7
  263.7 0.7 fusion.7
  264.5 94.5 %collective-permute-done.5 = bf16[128,1024]{1,0:T(8,128)(2,1)S(1)} collective-permute-done((bf16[128,1024]{1,0:T(8,128)(2,1)S(1)}, bf16[128,1024]{1,0:T(8,128)(2,1)S(1)}, u32[]{:S(2)}, u32[]{:S(2)}) %collective-permute-start.5) | collective-permute-done | bytes 262176 | tf_op jit(solution)/shard_map/ppermute | solution.py:13
  359.0 5.6 %collective-permute-done.6 = bf16[128,1024]{1,0:T(8,128)(2,1)S(1)} collective-permute-done((bf16[128,1024]{1,0:T(8,128)(2,1)S(1)}, bf16[128,1024]{1,0:T(8,128)(2,1)S(1)}, u32[]{:S(2)}, u32[]{:S(2)}) %collective-permute-start.6) | collective-permute-done | bytes 262176 | tf_op jit(solution)/shard_map/ppermute | solution.py:13
  364.6 0.8 pad_maximum_fusion.3
  365.5 0.8 pad_maximum_fusion.4
  366.3 2.9 collective-permute-done.7
  369.3 0.8 pad_maximum_fusion.5
  370.1 3.7 convolution_convert_fusion.1
  (58 shorter events, 2.6 us)
Async XLA Ops:
  7.2 15.9 %copy-start.2 = (bf16[2,128,1024]{2,1,0:T(8,128)(2,1)S(1)}, bf16[2,128,1024]{2,1,0:T(8,128)(2,1)}, u32[]{:S(2)}) copy-start(bf16[2,128,1024]{2,1,0:T(8,128)(2,1)} %param.15) | copy-start | bytes 1572868
  7.2 15.9 %copy-start.1 = (bf16[2,128,1024]{2,1,0:T(8,128)(2,1)S(1)}, bf16[2,128,1024]{2,1,0:T(8,128)(2,1)}, u32[]{:S(2)}) copy-start(bf16[2,128,1024]{2,1,0:T(8,128)(2,1)} %param.14) | copy-start | bytes 1572868
  7.2 15.9 %copy-start = (bf16[2,128,1024]{2,1,0:T(8,128)(2,1)S(1)}, bf16[2,128,1024]{2,1,0:T(8,128)(2,1)}, u32[]{:S(2)}) copy-start(bf16[2,128,1024]{2,1,0:T(8,128)(2,1)} %param.13) | copy-start | bytes 1572868
  7.2 76.2 %all-gather.3.cloned.1.call-start = ((), (), s32[]{:S(2)}) async-start(), calls=%async_computation.1 | async-start | bytes 5013504 | tf_op jit(solution)/shard_map/all_gather | solution.py:79
  12.1 10.0 %collective-permute-start = (bf16[64,2176]{1,0:T(8,128)(2,1)S(1)}, bf16[64,2176]{1,0:T(8,128)(2,1)S(1)}, u32[]{:S(2)}, u32[]{:S(2)}) collective-permute-start(bf16[64,2176]{1,0:T(8,128)(2,1)S(1)} %concatenate.17), channel_id=1, source_target_pairs={{0,16},{16,0},{32,48},{48,32},{64,80},{80,64},{96,112},{112,96},{1... | collective-permute-start | bytes 835592 | tf_op jit(solution)/shard_map/ppermute | solution.py:8
  23.0 181.9 %all-gather.5.cloned.1.call-start = ((), (), s32[]{:S(2)}) async-start(), calls=%async_computation.2 | async-start | bytes 15728640 | tf_op jit(solution)/shard_map/all_gather | solution.py:57
  24.5 35.6 %collective-permute-start.2 = (bf16[2,3,128,1024]{3,2,1,0:T(8,128)(2,1)}, bf16[2,3,128,1024]{3,2,1,0:T(8,128)(2,1)}, u32[]{:S(2)}, u32[]{:S(2)}) collective-permute-start(bf16[2,3,128,1024]{3,2,1,0:T(8,128)(2,1)} %get-tuple-element.12), channel_id=1, source_target_pairs={{0,8},{1,9},{2,10},{3,11},{4,12},{5,13},{6,14},{7,15},{8,0},{9,1},... | collective-permute-start | bytes 4718600 | tf_op jit(solution)/shard_map/ppermute | solution.py:8
  62.6 3.5 collective-permute-start.3
  92.8 4.4 %collective-permute-start.1 = (bf16[16,32,2048]{2,1,0:T(8,128)(2,1)S(1)}, bf16[16,32,2048]{2,1,0:T(8,128)(2,1)S(1)}, u32[]{:S(2)}, u32[]{:S(2)}) collective-permute-start(bf16[16,32,2048]{2,1,0:T(8,128)(2,1)S(1)} %fusion.4), channel_id=1, source_target_pairs={{0,1},{1,0},{2,3},{3,2},{4,5},{5,4},{6,7},{7,6},{8,9},{9,8},{10,11... | collective-permute-start | bytes 6291464 | tf_op jit(solution)/shard_map/ppermute | solution.py:8
  205.0 7.9 %copy-start.3 = (bf16[2,16,32,2048]{3,2,1,0:T(8,128)(2,1)S(1)}, bf16[2,16,32,2048]{3,2,1,0:T(8,128)(2,1)}, u32[]{:S(2)}) copy-start(bf16[2,16,32,2048]{3,2,1,0:T(8,128)(2,1)} %pad_maximum_fusion) | copy-start | bytes 12582916
  236.7 4.2 %collective-permute-start.4 = (bf16[16,32,2048]{2,1,0:T(8,128)(2,1)S(1)}, bf16[16,32,2048]{2,1,0:T(8,128)(2,1)S(1)}, u32[]{:S(2)}, u32[]{:S(2)}) collective-permute-start(bf16[16,32,2048]{2,1,0:T(8,128)(2,1)S(1)} %bitcast.149), channel_id=1, source_target_pairs={{0,1},{1,0},{2,3},{3,2},{4,5},{5,4},{6,7},{7,6},{8,9},{9,8},{10,11... | collective-permute-start | bytes 6291464 | tf_op jit(solution)/shard_map/ppermute | solution.py:8
  243.2 9.7 %copy-start.5 = (s32[32]{0:T(128)S(1)}, s32[32]{0:T(128)}, u32[]{:S(2)}) copy-start(s32[32]{0:T(128)} %param.11) | copy-start | bytes 388
  243.2 10.3 %copy-start.6 = (s32[32]{0:T(128)S(1)}, s32[32]{0:T(128)}, u32[]{:S(2)}) copy-start(s32[32]{0:T(128)} %param.12) | copy-start | bytes 388
  243.2 20.4 %copy-start.4 = (f32[64,8]{0,1:T(8,128)S(1)}, f32[64,8]{0,1:T(8,128)}, u32[]{:S(2)}) copy-start(f32[64,8]{0,1:T(8,128)} %param.9) | copy-start | bytes 6148
  243.2 126.9 %all-to-all-start = ((bf16[16,2,32,2048]{3,2,1,0:T(8,128)(2,1)}), bf16[16,2,32,2048]{3,2,1,0:T(8,128)(2,1)}, u32[]{:S(2)}, u32[]{:S(2)}) async-start(bf16[16,2,32,2048]{3,2,1,0:T(8,128)(2,1)} %maximum_select_fusion), calls=%async_computation | async-start | bytes 8388608 | tf_op jit(solution)/shard_map/all_to_all | solution.py:112
  255.4 103.6 %collective-permute-start.5 = (bf16[128,1024]{1,0:T(8,128)(2,1)S(1)}, bf16[128,1024]{1,0:T(8,128)(2,1)S(1)}, u32[]{:S(2)}, u32[]{:S(2)}) collective-permute-start(bf16[128,1024]{1,0:T(8,128)(2,1)S(1)} %bitcast_select_fusion.9), channel_id=1, source_target_pairs={{0,16},{16,32},{32,48},{48,64},{64,80},{80,96},{96,112},{112,128},... | collective-permute-start | bytes 786440 | tf_op jit(solution)/shard_map/ppermute | solution.py:13
  258.9 105.7 %collective-permute-start.6 = (bf16[128,1024]{1,0:T(8,128)(2,1)S(1)}, bf16[128,1024]{1,0:T(8,128)(2,1)S(1)}, u32[]{:S(2)}, u32[]{:S(2)}) collective-permute-start(bf16[128,1024]{1,0:T(8,128)(2,1)S(1)} %bitcast_select_fusion.6), channel_id=1, source_target_pairs={{0,16},{16,32},{32,48},{48,64},{64,80},{80,96},{96,112},{112,128},... | collective-permute-start | bytes 786440 | tf_op jit(solution)/shard_map/ppermute | solution.py:13
  260.5 108.8 %collective-permute-start.7 = (bf16[128,1024]{1,0:T(8,128)(2,1)S(1)}, bf16[128,1024]{1,0:T(8,128)(2,1)S(1)}, u32[]{:S(2)}, u32[]{:S(2)}) collective-permute-start(bf16[128,1024]{1,0:T(8,128)(2,1)S(1)} %bitcast_select_fusion.3), channel_id=1, source_target_pairs={{0,16},{16,32},{32,48},{48,64},{64,80},{80,96},{96,112},{112,128},... | collective-permute-start | bytes 786440 | tf_op jit(solution)/shard_map/ppermute | solution.py:13
Sparse Core Ops, SparseCore 0:
  23.2 60.1 all-gather.2
  85.2 119.7 all-gather.4

commit v11 on v10

--- a/solution.py
+++ b/solution.py
@@ -75,9 +75,15 @@
     ext = jnp.concatenate([tokens, side], axis=1)
     pair = jnp.stack([ext, partner_2(ext, "dp", 0)], axis=0)
     pair = jnp.where(row_id % 2 == 1, pair[::-1], pair)
-    groups = [list(range(g, n_rows, 2)) for g in range(2)]
-    gathered = lax.all_gather(pair, "dp", axis=0, tiled=True, axis_index_groups=groups)
-    gathered = gathered.reshape(n_rows, tok_count, -1)
+    z_count = n_rows // 2
+    ahead = [pair]
+    behind = [pair]
+    for hop in range(1, z_count // 2 + 1):
+        ahead.append(passed_along(ahead[-1], "dp", -2))
+        if hop < z_count // 2:
+            behind.append(passed_along(behind[-1], "dp", 2))
+    by_offset = jnp.stack(ahead + behind[:0:-1], axis=0)
+    gathered = jnp.roll(by_offset, row_id // 2, axis=0).reshape(n_rows, tok_count, -1)
     gathered_tokens = gathered[..., :model_width]
     gathered_slots = (
         gathered[..., model_width : model_width + top_count].astype(jnp.int32).reshape(n_rows, -1)

time: 381 us -> 353 us (0.927)
  waiting for transfers between devices: 276 us -> 204 us
  local copies, waits for them, and re-layouts: 15.9 us -> 40.6 us
  starting transfers between devices: 22.9 us -> 39.8 us
    all_gather x1, waiting for transfers between devices: 105 us -> 10.6 us  [local(): lax.all_gather(block, 'shard', axis=0, tiled=False, axis_index_groups=gro...]
    ppermute x3 -> x10, waiting for transfers between devices: 103 us -> 140 us  [passed_along(): return lax.ppermute(x, axis, [(i, (i + by) % size) for i in range(size)])]
    ppermute x3 -> x10, starting transfers between devices: 8.03 us -> 25 us  [passed_along(): return lax.ppermute(x, axis, [(i, (i + by) % size) for i in range(size)])]
    all_gather x1 -> x0, waiting for transfers between devices: 15.3 us -> none  [local(): lax.all_gather(pair, 'dp', axis=0, tiled=True, axis_index_groups=groups)]
    dynamic_slice x0 -> x2, local copies, waits for them, and re-layouts: none -> 13.9 us  [local(): jnp.roll(by_offset, row_id // 2, axis=0).reshape(n_rows, tok_count, -1)]
    unnamed x15 -> x32, local copies, waits for them, and re-layouts: 0.15 us -> 12 us
  transfers between devices with their start and end apart: 11 -> 17, of which waited for: 10 -> 13; matrix products, arithmetic and copies ran while one was open for 6% -> 14% of each run, Pallas kernels for 0% -> 0%
where the time goes in v11:
time: 353 us; the launch traced here: 352 us
  waiting for transfers between devices  204 us (58%)
  local copies, waits for them, and re-layouts  40.6 us (12%)
  starting transfers between devices  39.8 us (11%)
  matrix products  31.3 us (9%)
  other arithmetic  20.6 us (6%)
  between operations  15.6 us (4%)
    ppermute x10, waiting for transfers between devices, passed_along(): return lax.ppermute(x, axis, [(i, (i + by) % size) for i in range(size)])  140 us
    ppermute x5, waiting for transfers between devices, partner_2(): lax.ppermute(x, axis, [(i, i ^ 1 << apart) for i in range(lax.axis_size(a...  53.5 us
    ppermute x10, starting transfers between devices, passed_along(): return lax.ppermute(x, axis, [(i, (i + by) % size) for i in range(size)])  25 us
    dot_general x1, matrix products, local(): lax.dot_general(hidden, full_down, (((1,), (1,)), ((), ())), preferred_el...  15.2 us
    dynamic_slice x2, local copies, waits for them, and re-layouts, local(): jnp.roll(by_offset, row_id // 2, axis=0).reshape(n_rows, tok_count, -1)  13.9 us
    unnamed x32, local copies, waits for them, and re-layouts  12 us
    all_gather x1, waiting for transfers between devices, local(): lax.all_gather(block, 'shard', axis=0, tiled=False, axis_index_groups=gro...  10.6 us
    all_to_all x1, starting transfers between devices, local(): lax.all_to_all(pair_halves(upper_half, result[0], returned_other), 'dp',...  9.73 us
  transfers between devices with their start and end apart: 17, of which 13 were waited for; matrix products, arithmetic and copies ran while one was open for 14% of the time, Pallas kernels for 0%

profile of v11, /device:TPU:8, one launch (start us, length us, event | category | flops | bytes accessed | tf_op | source)
XLA Modules:
  0.0 352.4 jit_solution(6258454415929151955)
XLA Ops:
  7.2 2.7 fusion.21
  10.0 1.5 collective-permute-start.9
  11.4 34.9 %collective-permute-done.9 = bf16[2,3,128,1024]{3,2,1,0:T(8,128)(2,1)S(1)} collective-permute-done((bf16[2,3,128,1024]{3,2,1,0:T(8,128)(2,1)}, bf16[2,3,128,1024]{3,2,1,0:T(8,128)(2,1)S(1)}, u32[]{:S(2)}, u32[]{:S(2)}) %collective-permute-start.9) | collective-permute-done | bytes 1572896 | tf_op jit(solution)/shard_map/ppermute | solution.py:8
  47.1 3.4 collective-permute-done.10
  50.5 1.9 maximum_select_fusion.2
  52.9 1.2 reduce-window.14
  54.8 3.1 collective-permute-start
  57.9 7.2 %collective-permute-done = bf16[64,2176]{1,0:T(8,128)(2,1)S(1)} collective-permute-done((bf16[64,2176]{1,0:T(8,128)(2,1)S(1)}, bf16[64,2176]{1,0:T(8,128)(2,1)S(1)}, u32[]{:S(2)}, u32[]{:S(2)}) %collective-permute-start) | collective-permute-done | bytes 278560 | tf_op jit(solution)/shard_map/ppermute | solution.py:8
  65.2 0.9 bitcast_dynamic-update-slice_fusion.14
  66.1 5.9 %collective-permute-start.1 = (bf16[2,64,2176]{2,1,0:T(8,128)(2,1)S(1)}, bf16[2,64,2176]{2,1,0:T(8,128)(2,1)S(1)}, u32[]{:S(2)}, u32[]{:S(2)}) collective-permute-start(bf16[2,64,2176]{2,1,0:T(8,128)(2,1)S(1)} %get-tuple-element.5), channel_id=1, source_target_pairs={{0,224},{16,240},{32,0},{48,16},{64,32},{80,48},{96,64},{112,80},{... | collective-permute-start | bytes 1671176 | tf_op jit(solution)/shard_map/ppermute | solution.py:13
  72.0 11.4 %collective-permute-done.1 = bf16[2,64,2176]{2,1,0:T(8,128)(2,1)S(1)} collective-permute-done((bf16[2,64,2176]{2,1,0:T(8,128)(2,1)S(1)}, bf16[2,64,2176]{2,1,0:T(8,128)(2,1)S(1)}, u32[]{:S(2)}, u32[]{:S(2)}) %collective-permute-start.1) | collective-permute-done | bytes 557088 | tf_op jit(solution)/shard_map/ppermute | solution.py:13
  83.3 3.7 %collective-permute-start.2 = (bf16[2,64,2176]{2,1,0:T(8,128)(2,1)S(1)}, bf16[2,64,2176]{2,1,0:T(8,128)(2,1)S(1)}, u32[]{:S(2)}, u32[]{:S(2)}) collective-permute-start(bf16[2,64,2176]{2,1,0:T(8,128)(2,1)S(1)} %collective-permute-done.1), channel_id=1, source_target_pairs={{0,224},{16,240},{32,0},{48,16},{64,32},{80,48},{96,64},{112,80},{... | collective-permute-start | bytes 1671176 | tf_op jit(solution)/shard_map/ppermute | solution.py:13
  87.0 0.9 bitcast_dynamic-update-slice_fusion.12
  87.9 9.6 %collective-permute-done.2 = bf16[2,64,2176]{2,1,0:T(8,128)(2,1)S(1)} collective-permute-done((bf16[2,64,2176]{2,1,0:T(8,128)(2,1)S(1)}, bf16[2,64,2176]{2,1,0:T(8,128)(2,1)S(1)}, u32[]{:S(2)}, u32[]{:S(2)}) %collective-permute-start.2) | collective-permute-done | bytes 557088 | tf_op jit(solution)/shard_map/ppermute | solution.py:13
  97.5 3.7 %collective-permute-start.3 = (bf16[2,64,2176]{2,1,0:T(8,128)(2,1)S(1)}, bf16[2,64,2176]{2,1,0:T(8,128)(2,1)S(1)}, u32[]{:S(2)}, u32[]{:S(2)}) collective-permute-start(bf16[2,64,2176]{2,1,0:T(8,128)(2,1)S(1)} %collective-permute-done.2), channel_id=1, source_target_pairs={{0,224},{16,240},{32,0},{48,16},{64,32},{80,48},{96,64},{112,80},{... | collective-permute-start | bytes 1671176 | tf_op jit(solution)/shard_map/ppermute | solution.py:13
  101.2 0.9 bitcast_dynamic-update-slice_fusion.10
  102.0 8.6 %collective-permute-done.3 = bf16[2,64,2176]{2,1,0:T(8,128)(2,1)S(1)} collective-permute-done((bf16[2,64,2176]{2,1,0:T(8,128)(2,1)S(1)}, bf16[2,64,2176]{2,1,0:T(8,128)(2,1)S(1)}, u32[]{:S(2)}, u32[]{:S(2)}) %collective-permute-start.3) | collective-permute-done | bytes 557088 | tf_op jit(solution)/shard_map/ppermute | solution.py:13
  110.7 3.7 %collective-permute-start.4 = (bf16[2,64,2176]{2,1,0:T(8,128)(2,1)S(1)}, bf16[2,64,2176]{2,1,0:T(8,128)(2,1)S(1)}, u32[]{:S(2)}, u32[]{:S(2)}) collective-permute-start(bf16[2,64,2176]{2,1,0:T(8,128)(2,1)S(1)} %collective-permute-done.3), channel_id=1, source_target_pairs={{0,224},{16,240},{32,0},{48,16},{64,32},{80,48},{96,64},{112,80},{... | collective-permute-start | bytes 1671176 | tf_op jit(solution)/shard_map/ppermute | solution.py:13
  115.2 7.8 %collective-permute-done.4 = bf16[2,64,2176]{2,1,0:T(8,128)(2,1)S(1)} collective-permute-done((bf16[2,64,2176]{2,1,0:T(8,128)(2,1)S(1)}, bf16[2,64,2176]{2,1,0:T(8,128)(2,1)S(1)}, u32[]{:S(2)}, u32[]{:S(2)}) %collective-permute-start.4) | collective-permute-done | bytes 557088 | tf_op jit(solution)/shard_map/ppermute | solution.py:13
  123.8 0.9 bitcast_dynamic-update-slice_fusion.4
  124.7 0.9 bitcast_dynamic-update-slice_fusion.2
  125.6 0.8 bitcast_dynamic-update-slice_fusion
  126.4 0.9 bitcast_dynamic-update-slice_fusion.15
  128.1 0.9 bitcast_dynamic-update-slice_fusion.11
  129.8 0.9 bitcast_dynamic-update-slice_fusion.7
  132.4 0.8 bitcast_dynamic-update-slice_fusion.1
  133.2 4.7 %constant_dynamic-slice_fusion = bf16[8,2,64,2176]{3,2,1,0:T(8,128)(2,1)} fusion(bf16[16,2,64,2176]{3,2,1,0:T(8,128)(2,1)} %bitcast_dynamic-update-slice_fusion.1, s32[]{:T(128)S(6)} %select_n.175), kind=kLoop, calls=%fused_computation.82 | loop fusion | bytes 8912900 | tf_op jit(solution)/shard_map/jit(_roll_dynamic)/dynamic_slice | solution.py:86
  137.9 9.2 %copy.90 = bf16[8,2,64,2176]{2,3,1,0:T(8,128)(2,1)} copy(bf16[8,2,64,2176]{3,2,1,0:T(8,128)(2,1)} %constant_dynamic-slice_fusion) | data formatting | bytes 8912896 | tf_op jit(solution)/shard_map/jit(_roll_dynamic)/dynamic_slice | solution.py:86
  148.3 2.3 reduce-window.16
  151.6 1.0 fusion.2
  152.6 6.4 %fusion.3 = bf16[16,2,32,2048]{3,2,1,0:T(8,128)(2,1)S(1)} fusion(pred[16,64,2,32]{1,3,2,0:T(8,128)(4,1)S(1)} %fusion.2, bf16[16,64,2176]{1,2,0:T(8,128)(2,1)} %bitcast.160), kind=kOutput, calls=%fused_computation.9 | convolution fusion | flops 270532608 | bytes 12648448 | tf_op jit(solution)/shard_map/stcr,std->scrd/dot_general | solution.py:99
  159.8 3.9 %collective-permute-done.8 = bf16[16,32,2048]{2,1,0:T(8,128)(2,1)S(1)} collective-permute-done((bf16[16,32,2048]{2,1,0:T(8,128)(2,1)S(1)}, bf16[16,32,2048]{2,1,0:T(8,128)(2,1)S(1)}, u32[]{:S(2)}, u32[]{:S(2)}) %collective-permute-start.8) | collective-permute-done | bytes 2097184 | tf_op jit(solution)/shard_map/ppermute | solution.py:8
  163.7 2.3 pad_maximum_fusion
  166.0 10.6 %all-gather.2.cloned.1.call-done = bf16[4,2,2,3,128,1024]{5,4,2,0,1,3:T(8,128)(2,1)} async-done(((bf16[1,2,2,3,128,1024]{5,4,2,0,1,3:T(8,128)(2,1)}), bf16[4,2,2,3,128,1024]{5,4,2,0,1,3:T(8,128)(2,1)}) %all-gather.2.cloned.1.call-update) | async-done | bytes 12582928 | tf_op jit(solution)/shard_map/all_gather | solution.py:57
  176.6 7.9 %fusion.22 = (bf16[1,2,4,2,128,1024]{5,4,3,2,1,0:T(8,128)(2,1)}, bf16[1,2,4,2,128,1024]{5,4,3,2,1,0:T(8,128)(2,1)}, bf16[1,2,4,2,128,1024]{5,4,3,2,1,0:T(8,128)(2,1)S(1)}) fusion(bf16[3,2,4,2,128,1024]{5,4,3,2,1,0:T(8,128)(2,1)} %bitcast.161), kind=kLoop, calls=%fused_computation.85 | loop fusion | bytes 25165824 | tf_op jit(solution)/shard_map/slice | solution.py:59
  184.5 6.0 %fusion.25 = f32[1024,1024]{1,0:T(8,128)} fusion(bf16[1024,2048]{1,0:T(8,128)(2,1)S(1)} %bitcast.167, bf16[2048,1024]{1,0:T(8,128)(2,1)S(1)} %bitcast.170), kind=kOutput, calls=%fused_computation.88 | convolution fusion | flops 4294967296 | bytes 12582912 | tf_op jit(solution)/shard_map/dot_general | solution.py:110
  190.5 15.2 %convolution_convert_fusion = bf16[1024,2048]{1,0:T(8,128)(2,1)} fusion(bf16[2048,1024]{1,0:T(8,128)(2,1)} %bitcast.169, f32[1024,1024]{1,0:T(8,128)} %fusion.25, bf16[1024,2048]{1,0:T(8,128)(2,1)} %bitcast.166, bf16[2048,1024]{1,0:T(8,128)(2,1)} %bitcast.168), kind=kOutput, calls=%fused_computation.10 | convolution fusion | flops 8598323200 | bytes 20971520 | tf_op jit(solution)/shard_map/dot_general | solution.py:113
  205.7 2.7 fusion.23
  208.5 4.1 %collective-permute-done.11 = bf16[16,32,2048]{2,1,0:T(8,128)(2,1)S(1)} collective-permute-done((bf16[16,32,2048]{2,1,0:T(8,128)(2,1)S(1)}, bf16[16,32,2048]{2,1,0:T(8,128)(2,1)S(1)}, u32[]{:S(2)}, u32[]{:S(2)}) %collective-permute-start.11) | collective-permute-done | bytes 2097184 | tf_op jit(solution)/shard_map/ppermute | solution.py:8
  212.7 2.2 maximum_select_fusion
  214.9 9.7 %all-to-all-start = ((bf16[16,2,32,2048]{3,2,1,0:T(8,128)(2,1)}), bf16[16,2,32,2048]{3,2,1,0:T(8,128)(2,1)}, u32[]{:S(2)}, u32[]{:S(2)}) async-start(bf16[16,2,32,2048]{3,2,1,0:T(8,128)(2,1)} %maximum_select_fusion), calls=%async_computation | async-start | bytes 8388608 | tf_op jit(solution)/shard_map/all_to_all | solution.py:118
  227.1 3.4 collective-permute-start.12
  230.6 1.5 collective-permute-start.13
  232.2 3.0 collective-permute-start.14
  236.2 94.5 %collective-permute-done.12 = bf16[128,1024]{1,0:T(8,128)(2,1)S(1)} collective-permute-done((bf16[128,1024]{1,0:T(8,128)(2,1)S(1)}, bf16[128,1024]{1,0:T(8,128)(2,1)S(1)}, u32[]{:S(2)}, u32[]{:S(2)}) %collective-permute-start.12) | collective-permute-done | bytes 262176 | tf_op jit(solution)/shard_map/ppermute | solution.py:13
  330.8 5.6 %collective-permute-done.13 = bf16[128,1024]{1,0:T(8,128)(2,1)S(1)} collective-permute-done((bf16[128,1024]{1,0:T(8,128)(2,1)S(1)}, bf16[128,1024]{1,0:T(8,128)(2,1)S(1)}, u32[]{:S(2)}, u32[]{:S(2)}) %collective-permute-start.13) | collective-permute-done | bytes 262176 | tf_op jit(solution)/shard_map/ppermute | solution.py:13
  338.1 2.9 collective-permute-done.14
  341.8 3.7 %convolution_convert_fusion.1 = bf16[64,2048]{1,0:T(8,128)(2,1)} fusion(bf16[64,1024]{1,0:T(8,128)(2,1)S(1)} %fusion.7, bf16[1024,2048]{1,0:T(8,128)(2,1)} %bitcast.42), kind=kOutput, calls=%fused_computation.13 | convolution fusion | flops 268566528 | bytes 4587520 | tf_op jit(solution)/shard_map/dot_general | solution.py:134
  (88 shorter events, 15.0 us)
Async XLA Ops:
  7.2 169.5 %all-gather.2.cloned.1.call-start = ((), (), s32[]{:S(2)}) async-start(), calls=%async_computation.1 | async-start | bytes 15728640 | tf_op jit(solution)/shard_map/all_gather | solution.py:57
  10.0 36.3 %collective-permute-start.9 = (bf16[2,3,128,1024]{3,2,1,0:T(8,128)(2,1)}, bf16[2,3,128,1024]{3,2,1,0:T(8,128)(2,1)S(1)}, u32[]{:S(2)}, u32[]{:S(2)}) collective-permute-start(bf16[2,3,128,1024]{3,2,1,0:T(8,128)(2,1)} %get-tuple-element.14), channel_id=1, source_target_pairs={{0,8},{1,9},{2,10},{3,11},{4,12},{5,13},{6,14},{7,15},{8,0},{9,1},... | collective-permute-start | bytes 4718600 | tf_op jit(solution)/shard_map/ppermute | solution.py:8
  47.0 3.5 collective-permute-start.10
  50.5 1.9 copy-start.7
  50.5 2.0 copy-start.6
  50.5 4.2 %copy-start.4 = (bf16[64,2048]{1,0:T(8,128)(2,1)S(1)}, bf16[64,2048]{1,0:T(8,128)(2,1)}, u32[]{:S(2)}) copy-start(bf16[64,2048]{1,0:T(8,128)(2,1)} %param.8) | copy-start | bytes 786436
  54.8 10.3 %collective-permute-start = (bf16[64,2176]{1,0:T(8,128)(2,1)S(1)}, bf16[64,2176]{1,0:T(8,128)(2,1)S(1)}, u32[]{:S(2)}, u32[]{:S(2)}) collective-permute-start(bf16[64,2176]{1,0:T(8,128)(2,1)S(1)} %concatenate.22), channel_id=1, source_target_pairs={{0,16},{16,0},{32,48},{48,32},{64,80},{80,64},{96,112},{112,96},{1... | collective-permute-start | bytes 835592 | tf_op jit(solution)/shard_map/ppermute | solution.py:8
  66.1 17.2 %collective-permute-start.1 = (bf16[2,64,2176]{2,1,0:T(8,128)(2,1)S(1)}, bf16[2,64,2176]{2,1,0:T(8,128)(2,1)S(1)}, u32[]{:S(2)}, u32[]{:S(2)}) collective-permute-start(bf16[2,64,2176]{2,1,0:T(8,128)(2,1)S(1)} %get-tuple-element.5), channel_id=1, source_target_pairs={{0,224},{16,240},{32,0},{48,16},{64,32},{80,48},{96,64},{112,80},{... | collective-permute-start | bytes 1671176 | tf_op jit(solution)/shard_map/ppermute | solution.py:13
  72.0 15.1 %collective-permute-start.5 = (bf16[2,64,2176]{2,1,0:T(8,128)(2,1)S(1)}, bf16[2,64,2176]{2,1,0:T(8,128)(2,1)S(1)}, u32[]{:S(2)}, u32[]{:S(2)}) collective-permute-start(bf16[2,64,2176]{2,1,0:T(8,128)(2,1)S(1)} %get-tuple-element.5), channel_id=1, source_target_pairs={{0,32},{16,48},{32,64},{48,80},{64,96},{80,112},{96,128},{112,144}... | collective-permute-start | bytes 1671176 | tf_op jit(solution)/shard_map/ppermute | solution.py:13
  83.3 14.1 %collective-permute-start.2 = (bf16[2,64,2176]{2,1,0:T(8,128)(2,1)S(1)}, bf16[2,64,2176]{2,1,0:T(8,128)(2,1)S(1)}, u32[]{:S(2)}, u32[]{:S(2)}) collective-permute-start(bf16[2,64,2176]{2,1,0:T(8,128)(2,1)S(1)} %collective-permute-done.1), channel_id=1, source_target_pairs={{0,224},{16,240},{32,0},{48,16},{64,32},{80,48},{96,64},{112,80},{... | collective-permute-start | bytes 1671176 | tf_op jit(solution)/shard_map/ppermute | solution.py:13
  87.0 14.1 %collective-permute-start.6 = (bf16[2,64,2176]{2,1,0:T(8,128)(2,1)S(1)}, bf16[2,64,2176]{2,1,0:T(8,128)(2,1)S(1)}, u32[]{:S(2)}, u32[]{:S(2)}) collective-permute-start(bf16[2,64,2176]{2,1,0:T(8,128)(2,1)S(1)} %collective-permute-done.5), channel_id=1, source_target_pairs={{0,32},{16,48},{32,64},{48,80},{64,96},{80,112},{96,128},{112,144}... | collective-permute-start | bytes 1671176 | tf_op jit(solution)/shard_map/ppermute | solution.py:13
  97.5 13.2 %collective-permute-start.3 = (bf16[2,64,2176]{2,1,0:T(8,128)(2,1)S(1)}, bf16[2,64,2176]{2,1,0:T(8,128)(2,1)S(1)}, u32[]{:S(2)}, u32[]{:S(2)}) collective-permute-start(bf16[2,64,2176]{2,1,0:T(8,128)(2,1)S(1)} %collective-permute-done.2), channel_id=1, source_target_pairs={{0,224},{16,240},{32,0},{48,16},{64,32},{80,48},{96,64},{112,80},{... | collective-permute-start | bytes 1671176 | tf_op jit(solution)/shard_map/ppermute | solution.py:13
  101.2 22.6 %collective-permute-start.7 = (bf16[2,64,2176]{2,1,0:T(8,128)(2,1)S(1)}, bf16[2,64,2176]{2,1,0:T(8,128)(2,1)S(1)}, u32[]{:S(2)}, u32[]{:S(2)}) collective-permute-start(bf16[2,64,2176]{2,1,0:T(8,128)(2,1)S(1)} %collective-permute-done.6), channel_id=1, source_target_pairs={{0,32},{16,48},{32,64},{48,80},{64,96},{80,112},{96,128},{112,144}... | collective-permute-start | bytes 1671176 | tf_op jit(solution)/shard_map/ppermute | solution.py:13
  110.7 12.3 %collective-permute-start.4 = (bf16[2,64,2176]{2,1,0:T(8,128)(2,1)S(1)}, bf16[2,64,2176]{2,1,0:T(8,128)(2,1)S(1)}, u32[]{:S(2)}, u32[]{:S(2)}) collective-permute-start(bf16[2,64,2176]{2,1,0:T(8,128)(2,1)S(1)} %collective-permute-done.3), channel_id=1, source_target_pairs={{0,224},{16,240},{32,0},{48,16},{64,32},{80,48},{96,64},{112,80},{... | collective-permute-start | bytes 1671176 | tf_op jit(solution)/shard_map/ppermute | solution.py:13
  159.2 4.5 %collective-permute-start.8 = (bf16[16,32,2048]{2,1,0:T(8,128)(2,1)S(1)}, bf16[16,32,2048]{2,1,0:T(8,128)(2,1)S(1)}, u32[]{:S(2)}, u32[]{:S(2)}) collective-permute-start(bf16[16,32,2048]{2,1,0:T(8,128)(2,1)S(1)} %fusion.4), channel_id=1, source_target_pairs={{0,1},{1,0},{2,3},{3,2},{4,5},{5,4},{6,7},{7,6},{8,9},{9,8},{10,11... | collective-permute-start | bytes 6291464 | tf_op jit(solution)/shard_map/ppermute | solution.py:8
  176.6 7.9 %copy-start.3 = (bf16[2,16,32,2048]{3,2,1,0:T(8,128)(2,1)S(1)}, bf16[2,16,32,2048]{3,2,1,0:T(8,128)(2,1)}, u32[]{:S(2)}) copy-start(bf16[2,16,32,2048]{3,2,1,0:T(8,128)(2,1)} %pad_maximum_fusion) | copy-start | bytes 12582916
  208.4 4.2 %collective-permute-start.11 = (bf16[16,32,2048]{2,1,0:T(8,128)(2,1)S(1)}, bf16[16,32,2048]{2,1,0:T(8,128)(2,1)S(1)}, u32[]{:S(2)}, u32[]{:S(2)}) collective-permute-start(bf16[16,32,2048]{2,1,0:T(8,128)(2,1)S(1)} %bitcast.176), channel_id=1, source_target_pairs={{0,1},{1,0},{2,3},{3,2},{4,5},{5,4},{6,7},{7,6},{8,9},{9,8},{10,11... | collective-permute-start | bytes 6291464 | tf_op jit(solution)/shard_map/ppermute | solution.py:8
  214.8 10.4 %copy-start.8 = (s32[32]{0:T(128)S(1)}, s32[32]{0:T(128)}, u32[]{:S(2)}) copy-start(s32[32]{0:T(128)} %param.12) | copy-start | bytes 388
  214.8 12.2 %copy-start = (bf16[2,128,1024]{2,1,0:T(8,128)(2,1)S(1)}, bf16[2,128,1024]{2,1,0:T(8,128)(2,1)}, u32[]{:S(2)}) copy-start(bf16[2,128,1024]{2,1,0:T(8,128)(2,1)} %param.13) | copy-start | bytes 1572868
  214.9 15.7 %copy-start.1 = (bf16[2,128,1024]{2,1,0:T(8,128)(2,1)S(1)}, bf16[2,128,1024]{2,1,0:T(8,128)(2,1)}, u32[]{:S(2)}) copy-start(bf16[2,128,1024]{2,1,0:T(8,128)(2,1)} %param.14) | copy-start | bytes 1572868
  214.9 17.3 %copy-start.2 = (bf16[2,128,1024]{2,1,0:T(8,128)(2,1)S(1)}, bf16[2,128,1024]{2,1,0:T(8,128)(2,1)}, u32[]{:S(2)}) copy-start(bf16[2,128,1024]{2,1,0:T(8,128)(2,1)} %param.15) | copy-start | bytes 1572868
  214.9 20.4 %copy-start.5 = (f32[64,8]{0,1:T(8,128)S(1)}, f32[64,8]{0,1:T(8,128)}, u32[]{:S(2)}) copy-start(f32[64,8]{0,1:T(8,128)} %param.9) | copy-start | bytes 6148
  214.9 127.0 %all-to-all-start = ((bf16[16,2,32,2048]{3,2,1,0:T(8,128)(2,1)}), bf16[16,2,32,2048]{3,2,1,0:T(8,128)(2,1)}, u32[]{:S(2)}, u32[]{:S(2)}) async-start(bf16[16,2,32,2048]{3,2,1,0:T(8,128)(2,1)} %maximum_select_fusion), calls=%async_computation | async-start | bytes 8388608 | tf_op jit(solution)/shard_map/all_to_all | solution.py:118
  227.1 103.6 %collective-permute-start.12 = (bf16[128,1024]{1,0:T(8,128)(2,1)S(1)}, bf16[128,1024]{1,0:T(8,128)(2,1)S(1)}, u32[]{:S(2)}, u32[]{:S(2)}) collective-permute-start(bf16[128,1024]{1,0:T(8,128)(2,1)S(1)} %bitcast_select_fusion.9), channel_id=1, source_target_pairs={{0,16},{16,32},{32,48},{48,64},{64,80},{80,96},{96,112},{112,128},... | collective-permute-start | bytes 786440 | tf_op jit(solution)/shard_map/ppermute | solution.py:13
  230.6 105.7 %collective-permute-start.13 = (bf16[128,1024]{1,0:T(8,128)(2,1)S(1)}, bf16[128,1024]{1,0:T(8,128)(2,1)S(1)}, u32[]{:S(2)}, u32[]{:S(2)}) collective-permute-start(bf16[128,1024]{1,0:T(8,128)(2,1)S(1)} %bitcast_select_fusion.6), channel_id=1, source_target_pairs={{0,16},{16,32},{32,48},{48,64},{64,80},{80,96},{96,112},{112,128},... | collective-permute-start | bytes 786440 | tf_op jit(solution)/shard_map/ppermute | solution.py:13
  232.2 108.7 %collective-permute-start.14 = (bf16[128,1024]{1,0:T(8,128)(2,1)S(1)}, bf16[128,1024]{1,0:T(8,128)(2,1)S(1)}, u32[]{:S(2)}, u32[]{:S(2)}) collective-permute-start(bf16[128,1024]{1,0:T(8,128)(2,1)S(1)} %bitcast_select_fusion.3), channel_id=1, source_target_pairs={{0,16},{16,32},{32,48},{48,64},{64,80},{80,96},{96,112},{112,128},... | collective-permute-start | bytes 786440 | tf_op jit(solution)/shard_map/ppermute | solution.py:13
Sparse Core Ops, SparseCore 0:
  52.5 124.0 all-gather.1

commit v12 on v11

--- a/solution.py
+++ b/solution.py
@@ -106,6 +106,17 @@
     other_rows = jnp.where(upper_half, arrived[:, 0], arrived[:, 1])
     partner = partner_2(other_rows, "shard", 0)
     work_rows = jnp.stack([own_rows, partner], axis=0)
+    base_slot = 2 * row_id
+    second_old = lax.dynamic_index_in_dim(old_place, base_slot + 1, 0, keepdims=False)
+    second_new = lax.dynamic_index_in_dim(new_place, base_slot + 1, 0, keepdims=False)
+    second_moved = second_new != second_old
+    leave_gate = jnp.where(second_moved, w_gate[1], w_gate[0])
+    leave_up = jnp.where(second_moved, w_up[1], w_up[0])
+    leave_down = jnp.where(second_moved, w_down[1], w_down[0])
+    arrive_gate, arrive_up, arrive_down = passed_along((leave_gate, leave_up, leave_down), "dp", 1)
+    work_rows, arrive_gate, arrive_up, arrive_down = lax.optimization_barrier(
+        (work_rows, arrive_gate, arrive_up, arrive_down)
+    )
     flat_rows = work_rows.reshape(-1, model_width)
     gate_part = jnp.dot(flat_rows, full_gate, preferred_element_type=jnp.float32)
     up_part = jnp.dot(flat_rows, full_up, preferred_element_type=jnp.float32)
@@ -134,14 +145,6 @@
     moe_output = jnp.dot(
         combine, returned.reshape(places, model_width), preferred_element_type=jnp.float32
     ).astype(jnp.bfloat16)
-    base_slot = 2 * row_id
-    second_old = lax.dynamic_index_in_dim(old_place, base_slot + 1, 0, keepdims=False)
-    second_new = lax.dynamic_index_in_dim(new_place, base_slot + 1, 0, keepdims=False)
-    second_moved = second_new != second_old
-    leave_gate = jnp.where(second_moved, w_gate[1], w_gate[0])
-    leave_up = jnp.where(second_moved, w_up[1], w_up[0])
-    leave_down = jnp.where(second_moved, w_down[1], w_down[0])
-    arrive_gate, arrive_up, arrive_down = passed_along((leave_gate, leave_up, leave_down), "dp", 1)
     new_gate = jnp.stack(
         [
             jnp.where(second_moved, w_gate[0], arrive_gate),

time: 353 us -> 344 us (0.975)
  waiting for transfers between devices: 204 us -> 196 us
  starting transfers between devices: 39.8 us -> 31.8 us
  other arithmetic: 20.6 us -> 25.8 us
    all_to_all x1, waiting for transfers between devices: 0.01 us -> 96.2 us  [local(): lax.all_to_all(pair_halves(upper_half, result[0], returned_other), 'dp',...]
    ppermute x10, waiting for transfers between devices: 140 us -> 50.1 us  [passed_along(): return lax.ppermute(x, axis, [(i, (i + by) % size) for i in range(size)])]
    all_gather x1, waiting for transfers between devices: 10.6 us -> 0.01 us  [local(): lax.all_gather(block, 'shard', axis=0, tiled=False, axis_index_groups=gro...]
    all_to_all x1, starting transfers between devices: 9.73 us -> 4.8 us  [local(): lax.all_to_all(pair_halves(upper_half, result[0], returned_other), 'dp',...]
    ppermute x5, waiting for transfers between devices: 53.5 us -> 49.6 us  [partner_2(): lax.ppermute(x, axis, [(i, i ^ 1 << apart) for i in range(lax.axis_size(a...]
    unnamed x32 -> x34, local copies, waits for them, and re-layouts: 12 us -> 13.9 us
  transfers between devices with their start and end apart: 17 -> 17, of which waited for: 13 -> 12; matrix products, arithmetic and copies ran while one was open for 14% -> 16% of each run, Pallas kernels for 0% -> 0%
where the time goes in v12:
time: 344 us; the launch traced here: 343 us
  waiting for transfers between devices  196 us (57%)
  local copies, waits for them, and re-layouts  42.5 us (12%)
  starting transfers between devices  31.8 us (9%)
  matrix products  31.3 us (9%)
  other arithmetic  25.8 us (8%)
  between operations  15.6 us (5%)
    all_to_all x1, waiting for transfers between devices, local(): lax.all_to_all(pair_halves(upper_half, result[0], returned_other), 'dp',...  96.2 us
    ppermute x10, waiting for transfers between devices, passed_along(): return lax.ppermute(x, axis, [(i, (i + by) % size) for i in range(size)])  50.1 us
    ppermute x5, waiting for transfers between devices, partner_2(): lax.ppermute(x, axis, [(i, i ^ 1 << apart) for i in range(lax.axis_size(a...  49.6 us
    ppermute x10, starting transfers between devices, passed_along(): return lax.ppermute(x, axis, [(i, (i + by) % size) for i in range(size)])  22.1 us
    dot_general x1, matrix products, local(): lax.dot_general(hidden, full_down, (((1,), (1,)), ((), ())), preferred_el...  15.2 us
    dynamic_slice x2, local copies, waits for them, and re-layouts, local(): jnp.roll(by_offset, row_id // 2, axis=0).reshape(n_rows, tok_count, -1)  13.9 us
    unnamed x34, local copies, waits for them, and re-layouts  13.9 us
    slice x1, local copies, waits for them, and re-layouts, local(): full_gate, full_up, full_down = (full[0], full[1], full[2])  7.86 us
  transfers between devices with their start and end apart: 17, of which 12 were waited for; matrix products, arithmetic and copies ran while one was open for 16% of the time, Pallas kernels for 0%

profile of v12, /device:TPU:8, one launch (start us, length us, event | category | flops | bytes accessed | tf_op | source)
XLA Modules:
  0.0 342.9 jit_solution(16167238119329433535)
XLA Ops:
  7.2 2.7 fusion.21
  10.0 1.5 collective-permute-start.12
  11.4 34.9 %collective-permute-done.12 = bf16[2,3,128,1024]{3,2,1,0:T(8,128)(2,1)S(1)} collective-permute-done((bf16[2,3,128,1024]{3,2,1,0:T(8,128)(2,1)}, bf16[2,3,128,1024]{3,2,1,0:T(8,128)(2,1)S(1)}, u32[]{:S(2)}, u32[]{:S(2)}) %collective-permute-start.12) | collective-permute-done | bytes 1572896 | tf_op jit(solution)/shard_map/ppermute | solution.py:8
  47.1 3.4 collective-permute-done.13
  50.5 1.9 maximum_select_fusion.2
  52.9 1.2 reduce-window.14
  54.8 3.1 collective-permute-start
  57.9 7.2 %collective-permute-done = bf16[64,2176]{1,0:T(8,128)(2,1)S(1)} collective-permute-done((bf16[64,2176]{1,0:T(8,128)(2,1)S(1)}, bf16[64,2176]{1,0:T(8,128)(2,1)S(1)}, u32[]{:S(2)}, u32[]{:S(2)}) %collective-permute-start) | collective-permute-done | bytes 278560 | tf_op jit(solution)/shard_map/ppermute | solution.py:8
  65.2 0.9 bitcast_dynamic-update-slice_fusion.14
  66.1 5.9 %collective-permute-start.1 = (bf16[2,64,2176]{2,1,0:T(8,128)(2,1)S(1)}, bf16[2,64,2176]{2,1,0:T(8,128)(2,1)S(1)}, u32[]{:S(2)}, u32[]{:S(2)}) collective-permute-start(bf16[2,64,2176]{2,1,0:T(8,128)(2,1)S(1)} %get-tuple-element.13), channel_id=1, source_target_pairs={{0,224},{16,240},{32,0},{48,16},{64,32},{80,48},{96,64},{112,80},{... | collective-permute-start | bytes 1671176 | tf_op jit(solution)/shard_map/ppermute | solution.py:13
  72.0 11.4 %collective-permute-done.1 = bf16[2,64,2176]{2,1,0:T(8,128)(2,1)S(1)} collective-permute-done((bf16[2,64,2176]{2,1,0:T(8,128)(2,1)S(1)}, bf16[2,64,2176]{2,1,0:T(8,128)(2,1)S(1)}, u32[]{:S(2)}, u32[]{:S(2)}) %collective-permute-start.1) | collective-permute-done | bytes 557088 | tf_op jit(solution)/shard_map/ppermute | solution.py:13
  83.3 3.7 %collective-permute-start.2 = (bf16[2,64,2176]{2,1,0:T(8,128)(2,1)S(1)}, bf16[2,64,2176]{2,1,0:T(8,128)(2,1)S(1)}, u32[]{:S(2)}, u32[]{:S(2)}) collective-permute-start(bf16[2,64,2176]{2,1,0:T(8,128)(2,1)S(1)} %collective-permute-done.1), channel_id=1, source_target_pairs={{0,224},{16,240},{32,0},{48,16},{64,32},{80,48},{96,64},{112,80},{... | collective-permute-start | bytes 1671176 | tf_op jit(solution)/shard_map/ppermute | solution.py:13
  87.0 0.9 bitcast_dynamic-update-slice_fusion.12
  87.9 9.6 %collective-permute-done.2 = bf16[2,64,2176]{2,1,0:T(8,128)(2,1)S(1)} collective-permute-done((bf16[2,64,2176]{2,1,0:T(8,128)(2,1)S(1)}, bf16[2,64,2176]{2,1,0:T(8,128)(2,1)S(1)}, u32[]{:S(2)}, u32[]{:S(2)}) %collective-permute-start.2) | collective-permute-done | bytes 557088 | tf_op jit(solution)/shard_map/ppermute | solution.py:13
  97.5 3.7 %collective-permute-start.3 = (bf16[2,64,2176]{2,1,0:T(8,128)(2,1)S(1)}, bf16[2,64,2176]{2,1,0:T(8,128)(2,1)S(1)}, u32[]{:S(2)}, u32[]{:S(2)}) collective-permute-start(bf16[2,64,2176]{2,1,0:T(8,128)(2,1)S(1)} %collective-permute-done.2), channel_id=1, source_target_pairs={{0,224},{16,240},{32,0},{48,16},{64,32},{80,48},{96,64},{112,80},{... | collective-permute-start | bytes 1671176 | tf_op jit(solution)/shard_map/ppermute | solution.py:13
  101.2 0.9 bitcast_dynamic-update-slice_fusion.10
  102.0 8.6 %collective-permute-done.3 = bf16[2,64,2176]{2,1,0:T(8,128)(2,1)S(1)} collective-permute-done((bf16[2,64,2176]{2,1,0:T(8,128)(2,1)S(1)}, bf16[2,64,2176]{2,1,0:T(8,128)(2,1)S(1)}, u32[]{:S(2)}, u32[]{:S(2)}) %collective-permute-start.3) | collective-permute-done | bytes 557088 | tf_op jit(solution)/shard_map/ppermute | solution.py:13
  110.7 3.7 %collective-permute-start.4 = (bf16[2,64,2176]{2,1,0:T(8,128)(2,1)S(1)}, bf16[2,64,2176]{2,1,0:T(8,128)(2,1)S(1)}, u32[]{:S(2)}, u32[]{:S(2)}) collective-permute-start(bf16[2,64,2176]{2,1,0:T(8,128)(2,1)S(1)} %collective-permute-done.3), channel_id=1, source_target_pairs={{0,224},{16,240},{32,0},{48,16},{64,32},{80,48},{96,64},{112,80},{... | collective-permute-start | bytes 1671176 | tf_op jit(solution)/shard_map/ppermute | solution.py:13
  115.2 7.8 %collective-permute-done.4 = bf16[2,64,2176]{2,1,0:T(8,128)(2,1)S(1)} collective-permute-done((bf16[2,64,2176]{2,1,0:T(8,128)(2,1)S(1)}, bf16[2,64,2176]{2,1,0:T(8,128)(2,1)S(1)}, u32[]{:S(2)}, u32[]{:S(2)}) %collective-permute-start.4) | collective-permute-done | bytes 557088 | tf_op jit(solution)/shard_map/ppermute | solution.py:13
  123.8 0.9 bitcast_dynamic-update-slice_fusion.4
  124.7 0.9 bitcast_dynamic-update-slice_fusion.2
  126.4 0.9 bitcast_dynamic-update-slice_fusion.15
  128.1 0.9 bitcast_dynamic-update-slice_fusion.11
  129.8 0.9 bitcast_dynamic-update-slice_fusion.7
  132.4 0.8 bitcast_dynamic-update-slice_fusion.1
  133.2 4.7 %constant_dynamic-slice_fusion = bf16[8,2,64,2176]{3,2,1,0:T(8,128)(2,1)} fusion(bf16[16,2,64,2176]{3,2,1,0:T(8,128)(2,1)} %bitcast_dynamic-update-slice_fusion.1, s32[]{:T(128)S(6)} %select_n.175), kind=kLoop, calls=%fused_computation.82 | loop fusion | bytes 8912900 | tf_op jit(solution)/shard_map/jit(_roll_dynamic)/dynamic_slice | solution.py:86
  137.9 9.2 %copy.90 = bf16[8,2,64,2176]{2,3,1,0:T(8,128)(2,1)} copy(bf16[8,2,64,2176]{3,2,1,0:T(8,128)(2,1)} %constant_dynamic-slice_fusion) | data formatting | bytes 8912896 | tf_op jit(solution)/shard_map/jit(_roll_dynamic)/dynamic_slice | solution.py:86
  148.3 2.3 reduce-window.16
  151.6 1.0 fusion.2
  152.6 6.4 %fusion.3 = bf16[16,2,32,2048]{3,2,1,0:T(8,128)(2,1)S(1)} fusion(pred[16,64,2,32]{1,3,2,0:T(8,128)(4,1)S(1)} %fusion.2, bf16[16,64,2176]{1,2,0:T(8,128)(2,1)} %bitcast.160), kind=kOutput, calls=%fused_computation.9 | convolution fusion | flops 270532608 | bytes 12648448 | tf_op jit(solution)/shard_map/stcr,std->scrd/dot_general | solution.py:99
  159.0 1.9 copy-done
  161.0 1.5 fusion.4
  165.0 3.1 collective-permute-start.10
  168.3 2.0 collective-permute-start.9
  170.3 2.4 fusion.5
  172.7 3.9 %pad_maximum_fusion = bf16[2,16,32,2048]{3,2,1,0:T(8,128)(2,1)} fusion(bf16[1,16,32,2048]{3,2,1,0:T(8,128)(2,1)} %bitcast.23, bf16[1,16,32,2048]{3,2,1,0:T(8,128)(2,1)S(1)} %fusion.5), kind=kLoop, calls=%fused_computation.2 | loop fusion | flops 2097152 | bytes 8388608 | tf_op jit(solution)/shard_map/stack | solution.py:108
  176.6 1.8 collective-permute-done.10
  178.4 5.6 %collective-permute-done.11 = bf16[128,1024]{1,0:T(8,128)(2,1)S(1)} collective-permute-done((bf16[128,1024]{1,0:T(8,128)(2,1)S(1)}, bf16[128,1024]{1,0:T(8,128)(2,1)S(1)}, u32[]{:S(2)}, u32[]{:S(2)}) %collective-permute-start.11) | collective-permute-done | bytes 262176 | tf_op jit(solution)/shard_map/ppermute | solution.py:13
  184.0 5.4 %collective-permute-done.9 = bf16[128,1024]{1,0:T(8,128)(2,1)S(1)} collective-permute-done((bf16[128,1024]{1,0:T(8,128)(2,1)S(1)}, bf16[128,1024]{1,0:T(8,128)(2,1)S(1)}, u32[]{:S(2)}, u32[]{:S(2)}) %collective-permute-start.9) | collective-permute-done | bytes 262176 | tf_op jit(solution)/shard_map/ppermute | solution.py:13
  189.5 7.9 %fusion.22 = (bf16[1,2,4,2,128,1024]{5,4,3,2,1,0:T(8,128)(2,1)}, bf16[1,2,4,2,128,1024]{5,4,3,2,1,0:T(8,128)(2,1)}, bf16[1,2,4,2,128,1024]{5,4,3,2,1,0:T(8,128)(2,1)S(1)}) fusion(bf16[3,2,4,2,128,1024]{5,4,3,2,1,0:T(8,128)(2,1)} %bitcast.161), kind=kLoop, calls=%fused_computation.85 | loop fusion | bytes 25165824 | tf_op jit(solution)/shard_map/slice | solution.py:59
  197.3 6.0 %fusion.25 = f32[1024,1024]{1,0:T(8,128)} fusion(bf16[1024,2048]{1,0:T(8,128)(2,1)S(1)} %bitcast.167, bf16[2048,1024]{1,0:T(8,128)(2,1)S(1)} %bitcast.170), kind=kOutput, calls=%fused_computation.88 | convolution fusion | flops 4294967296 | bytes 12582912 | tf_op jit(solution)/shard_map/dot_general | solution.py:121
  203.4 15.2 %convolution_convert_fusion = bf16[1024,2048]{1,0:T(8,128)(2,1)} fusion(bf16[2048,1024]{1,0:T(8,128)(2,1)} %bitcast.169, f32[1024,1024]{1,0:T(8,128)} %fusion.25, bf16[1024,2048]{1,0:T(8,128)(2,1)} %bitcast.166, bf16[2048,1024]{1,0:T(8,128)(2,1)} %bitcast.168), kind=kOutput, calls=%fused_computation.10 | convolution fusion | flops 8598323200 | bytes 20971520 | tf_op jit(solution)/shard_map/dot_general | solution.py:124
  218.5 2.7 fusion.23
  221.4 4.1 %collective-permute-done.14 = bf16[16,32,2048]{2,1,0:T(8,128)(2,1)S(1)} collective-permute-done((bf16[16,32,2048]{2,1,0:T(8,128)(2,1)S(1)}, bf16[16,32,2048]{2,1,0:T(8,128)(2,1)S(1)}, u32[]{:S(2)}, u32[]{:S(2)}) %collective-permute-start.14) | collective-permute-done | bytes 2097184 | tf_op jit(solution)/shard_map/ppermute | solution.py:8
  225.5 2.2 maximum_select_fusion
  227.7 4.8 %all-to-all-start = ((bf16[16,2,32,2048]{3,2,1,0:T(8,128)(2,1)}), bf16[16,2,32,2048]{3,2,1,0:T(8,128)(2,1)}, u32[]{:S(2)}, u32[]{:S(2)}) async-start(bf16[16,2,32,2048]{3,2,1,0:T(8,128)(2,1)} %maximum_select_fusion), calls=%async_computation | async-start | bytes 8388608 | tf_op jit(solution)/shard_map/all_to_all | solution.py:129
  236.1 96.2 %all-to-all-done = bf16[16,2,32,2048]{3,2,1,0:T(8,128)(2,1)} async-done(((bf16[16,2,32,2048]{3,2,1,0:T(8,128)(2,1)}), bf16[16,2,32,2048]{3,2,1,0:T(8,128)(2,1)}, u32[]{:S(2)}, u32[]{:S(2)}) %all-to-all-start) | async-done | bytes 4194336 | tf_op jit(solution)/shard_map/all_to_all | solution.py:129
  332.3 3.7 %convolution_convert_fusion.1 = bf16[64,2048]{1,0:T(8,128)(2,1)} fusion(bf16[64,1024]{1,0:T(8,128)(2,1)S(1)} %fusion.7, bf16[1024,2048]{1,0:T(8,128)(2,1)} %bitcast.49), kind=kOutput, calls=%fused_computation.13 | convolution fusion | flops 268566528 | bytes 4587520 | tf_op jit(solution)/shard_map/dot_general | solution.py:145
  (89 shorter events, 15.2 us)
Async XLA Ops:
  7.2 182.3 %all-gather.2.cloned.1.call-start = ((), (), s32[]{:S(2)}) async-start(), calls=%async_computation.1 | async-start | bytes 15728640 | tf_op jit(solution)/shard_map/all_gather | solution.py:57
  10.0 36.3 %collective-permute-start.12 = (bf16[2,3,128,1024]{3,2,1,0:T(8,128)(2,1)}, bf16[2,3,128,1024]{3,2,1,0:T(8,128)(2,1)S(1)}, u32[]{:S(2)}, u32[]{:S(2)}) collective-permute-start(bf16[2,3,128,1024]{3,2,1,0:T(8,128)(2,1)} %get-tuple-element.22), channel_id=1, source_target_pairs={{0,8},{1,9},{2,10},{3,11},{4,12},{5,13},{6,14},{7,15},{8,0},{9,1},... | collective-permute-start | bytes 4718600 | tf_op jit(solution)/shard_map/ppermute | solution.py:8
  47.0 3.5 %collective-permute-start.13 = (bf16[2,3,128,1024]{3,2,0,1:T(8,128)(2,1)S(1)}, bf16[2,3,128,1024]{3,2,0,1:T(8,128)(2,1)S(1)}, u32[]{:S(2)}, u32[]{:S(2)}) collective-permute-start(bf16[2,3,128,1024]{3,2,0,1:T(8,128)(2,1)S(1)} %get-tuple-element.20), channel_id=1, source_target_pairs={{0,1},{1,0},{2,3},{3,2},{4,5},{5,4},{6,7},{7,6},{8,9},{9,8},{10,11... | collective-permute-start | bytes 4718600 | tf_op jit(solution)/shard_map/ppermute | solution.py:8
  50.5 1.9 copy-start.8
  50.5 2.0 copy-start.7
  50.5 4.2 %copy-start.5 = (bf16[64,2048]{1,0:T(8,128)(2,1)S(1)}, bf16[64,2048]{1,0:T(8,128)(2,1)}, u32[]{:S(2)}) copy-start(bf16[64,2048]{1,0:T(8,128)(2,1)} %param.8) | copy-start | bytes 786436
  54.8 10.3 %collective-permute-start = (bf16[64,2176]{1,0:T(8,128)(2,1)S(1)}, bf16[64,2176]{1,0:T(8,128)(2,1)S(1)}, u32[]{:S(2)}, u32[]{:S(2)}) collective-permute-start(bf16[64,2176]{1,0:T(8,128)(2,1)S(1)} %concatenate.22), channel_id=1, source_target_pairs={{0,16},{16,0},{32,48},{48,32},{64,80},{80,64},{96,112},{112,96},{1... | collective-permute-start | bytes 835592 | tf_op jit(solution)/shard_map/ppermute | solution.py:8
  66.1 17.2 %collective-permute-start.1 = (bf16[2,64,2176]{2,1,0:T(8,128)(2,1)S(1)}, bf16[2,64,2176]{2,1,0:T(8,128)(2,1)S(1)}, u32[]{:S(2)}, u32[]{:S(2)}) collective-permute-start(bf16[2,64,2176]{2,1,0:T(8,128)(2,1)S(1)} %get-tuple-element.13), channel_id=1, source_target_pairs={{0,224},{16,240},{32,0},{48,16},{64,32},{80,48},{96,64},{112,80},{... | collective-permute-start | bytes 1671176 | tf_op jit(solution)/shard_map/ppermute | solution.py:13
  72.0 15.1 %collective-permute-start.5 = (bf16[2,64,2176]{2,1,0:T(8,128)(2,1)S(1)}, bf16[2,64,2176]{2,1,0:T(8,128)(2,1)S(1)}, u32[]{:S(2)}, u32[]{:S(2)}) collective-permute-start(bf16[2,64,2176]{2,1,0:T(8,128)(2,1)S(1)} %get-tuple-element.13), channel_id=1, source_target_pairs={{0,32},{16,48},{32,64},{48,80},{64,96},{80,112},{96,128},{112,144}... | collective-permute-start | bytes 1671176 | tf_op jit(solution)/shard_map/ppermute | solution.py:13
  83.3 14.1 %collective-permute-start.2 = (bf16[2,64,2176]{2,1,0:T(8,128)(2,1)S(1)}, bf16[2,64,2176]{2,1,0:T(8,128)(2,1)S(1)}, u32[]{:S(2)}, u32[]{:S(2)}) collective-permute-start(bf16[2,64,2176]{2,1,0:T(8,128)(2,1)S(1)} %collective-permute-done.1), channel_id=1, source_target_pairs={{0,224},{16,240},{32,0},{48,16},{64,32},{80,48},{96,64},{112,80},{... | collective-permute-start | bytes 1671176 | tf_op jit(solution)/shard_map/ppermute | solution.py:13
  87.0 14.1 %collective-permute-start.6 = (bf16[2,64,2176]{2,1,0:T(8,128)(2,1)S(1)}, bf16[2,64,2176]{2,1,0:T(8,128)(2,1)S(1)}, u32[]{:S(2)}, u32[]{:S(2)}) collective-permute-start(bf16[2,64,2176]{2,1,0:T(8,128)(2,1)S(1)} %collective-permute-done.5), channel_id=1, source_target_pairs={{0,32},{16,48},{32,64},{48,80},{64,96},{80,112},{96,128},{112,144}... | collective-permute-start | bytes 1671176 | tf_op jit(solution)/shard_map/ppermute | solution.py:13
  97.5 13.2 %collective-permute-start.3 = (bf16[2,64,2176]{2,1,0:T(8,128)(2,1)S(1)}, bf16[2,64,2176]{2,1,0:T(8,128)(2,1)S(1)}, u32[]{:S(2)}, u32[]{:S(2)}) collective-permute-start(bf16[2,64,2176]{2,1,0:T(8,128)(2,1)S(1)} %collective-permute-done.2), channel_id=1, source_target_pairs={{0,224},{16,240},{32,0},{48,16},{64,32},{80,48},{96,64},{112,80},{... | collective-permute-start | bytes 1671176 | tf_op jit(solution)/shard_map/ppermute | solution.py:13
  101.2 22.6 %collective-permute-start.7 = (bf16[2,64,2176]{2,1,0:T(8,128)(2,1)S(1)}, bf16[2,64,2176]{2,1,0:T(8,128)(2,1)S(1)}, u32[]{:S(2)}, u32[]{:S(2)}) collective-permute-start(bf16[2,64,2176]{2,1,0:T(8,128)(2,1)S(1)} %collective-permute-done.6), channel_id=1, source_target_pairs={{0,32},{16,48},{32,64},{48,80},{64,96},{80,112},{96,128},{112,144}... | collective-permute-start | bytes 1671176 | tf_op jit(solution)/shard_map/ppermute | solution.py:13
  110.7 12.3 %collective-permute-start.4 = (bf16[2,64,2176]{2,1,0:T(8,128)(2,1)S(1)}, bf16[2,64,2176]{2,1,0:T(8,128)(2,1)S(1)}, u32[]{:S(2)}, u32[]{:S(2)}) collective-permute-start(bf16[2,64,2176]{2,1,0:T(8,128)(2,1)S(1)} %collective-permute-done.3), channel_id=1, source_target_pairs={{0,224},{16,240},{32,0},{48,16},{64,32},{80,48},{96,64},{112,80},{... | collective-permute-start | bytes 1671176 | tf_op jit(solution)/shard_map/ppermute | solution.py:13
  159.0 1.9 copy-start
  161.0 2.1 copy-start.9
  161.0 4.0 %copy-start.3 = (bf16[2,128,1024]{2,1,0:T(8,128)(2,1)S(1)}, bf16[2,128,1024]{2,1,0:T(8,128)(2,1)}, u32[]{:S(2)}) copy-start(bf16[2,128,1024]{2,1,0:T(8,128)(2,1)} %param.14) | copy-start | bytes 1572868
  161.0 7.1 %copy-start.2 = (bf16[2,128,1024]{2,1,0:T(8,128)(2,1)S(1)}, bf16[2,128,1024]{2,1,0:T(8,128)(2,1)}, u32[]{:S(2)}) copy-start(bf16[2,128,1024]{2,1,0:T(8,128)(2,1)} %param.15) | copy-start | bytes 1572868
  161.0 7.3 %copy-start.1 = (bf16[2,128,1024]{2,1,0:T(8,128)(2,1)S(1)}, bf16[2,128,1024]{2,1,0:T(8,128)(2,1)}, u32[]{:S(2)}) copy-start(bf16[2,128,1024]{2,1,0:T(8,128)(2,1)} %param.13) | copy-start | bytes 1572868
  162.5 10.2 %collective-permute-start.8 = (bf16[16,32,2048]{2,1,0:T(8,128)(2,1)}, bf16[16,32,2048]{2,1,0:T(8,128)(2,1)}, u32[]{:S(2)}, u32[]{:S(2)}) collective-permute-start(bf16[16,32,2048]{2,1,0:T(8,128)(2,1)} %fusion.4), channel_id=1, source_target_pairs={{0,1},{1,0},{2,3},{3,2},{4,5},{5,4},{6,7},{7,6},{8,9},{9,8},{10,11... | collective-permute-start | bytes 6291464 | tf_op jit(solution)/shard_map/ppermute | solution.py:8
  165.0 13.4 %collective-permute-start.10 = (bf16[128,1024]{1,0:T(8,128)(2,1)S(1)}, bf16[128,1024]{1,0:T(8,128)(2,1)S(1)}, u32[]{:S(2)}, u32[]{:S(2)}) collective-permute-start(bf16[128,1024]{1,0:T(8,128)(2,1)S(1)} %bitcast_select_fusion.6), channel_id=1, source_target_pairs={{0,16},{16,32},{32,48},{48,64},{64,80},{80,96},{96,112},{112,128},... | collective-permute-start | bytes 786440 | tf_op jit(solution)/shard_map/ppermute | solution.py:13
  168.1 15.9 %collective-permute-start.11 = (bf16[128,1024]{1,0:T(8,128)(2,1)S(1)}, bf16[128,1024]{1,0:T(8,128)(2,1)S(1)}, u32[]{:S(2)}, u32[]{:S(2)}) collective-permute-start(bf16[128,1024]{1,0:T(8,128)(2,1)S(1)} %bitcast_select_fusion.3), channel_id=1, source_target_pairs={{0,16},{16,32},{32,48},{48,64},{64,80},{80,96},{96,112},{112,128},... | collective-permute-start | bytes 786440 | tf_op jit(solution)/shard_map/ppermute | solution.py:13
  168.3 21.2 %collective-permute-start.9 = (bf16[128,1024]{1,0:T(8,128)(2,1)S(1)}, bf16[128,1024]{1,0:T(8,128)(2,1)S(1)}, u32[]{:S(2)}, u32[]{:S(2)}) collective-permute-start(bf16[128,1024]{1,0:T(8,128)(2,1)S(1)} %bitcast_select_fusion.9), channel_id=1, source_target_pairs={{0,16},{16,32},{32,48},{48,64},{64,80},{80,96},{96,112},{112,128},... | collective-permute-start | bytes 786440 | tf_op jit(solution)/shard_map/ppermute | solution.py:13
  189.5 7.9 %copy-start.4 = (bf16[2,16,32,2048]{3,2,1,0:T(8,128)(2,1)S(1)}, bf16[2,16,32,2048]{3,2,1,0:T(8,128)(2,1)}, u32[]{:S(2)}) copy-start(bf16[2,16,32,2048]{3,2,1,0:T(8,128)(2,1)} %pad_maximum_fusion) | copy-start | bytes 12582916
  221.3 4.2 %collective-permute-start.14 = (bf16[16,32,2048]{2,1,0:T(8,128)(2,1)S(1)}, bf16[16,32,2048]{2,1,0:T(8,128)(2,1)S(1)}, u32[]{:S(2)}, u32[]{:S(2)}) collective-permute-start(bf16[16,32,2048]{2,1,0:T(8,128)(2,1)S(1)} %bitcast.175), channel_id=1, source_target_pairs={{0,1},{1,0},{2,3},{3,2},{4,5},{5,4},{6,7},{7,6},{8,9},{9,8},{10,11... | collective-permute-start | bytes 6291464 | tf_op jit(solution)/shard_map/ppermute | solution.py:8
  227.7 4.9 %copy-start.6 = (f32[64,8]{0,1:T(8,128)S(1)}, f32[64,8]{0,1:T(8,128)}, u32[]{:S(2)}) copy-start(f32[64,8]{0,1:T(8,128)} %param.9) | copy-start | bytes 6148
  227.7 104.6 %all-to-all-start = ((bf16[16,2,32,2048]{3,2,1,0:T(8,128)(2,1)}), bf16[16,2,32,2048]{3,2,1,0:T(8,128)(2,1)}, u32[]{:S(2)}, u32[]{:S(2)}) async-start(bf16[16,2,32,2048]{3,2,1,0:T(8,128)(2,1)} %maximum_select_fusion), calls=%async_computation | async-start | bytes 8388608 | tf_op jit(solution)/shard_map/all_to_all | solution.py:129
Sparse Core Ops, SparseCore 0:
  52.5 124.0 all-gather.1

commit v13 on v11

--- a/solution.py
+++ b/solution.py
@@ -75,11 +75,23 @@
     ext = jnp.concatenate([tokens, side], axis=1)
     pair = jnp.stack([ext, partner_2(ext, "dp", 0)], axis=0)
     pair = jnp.where(row_id % 2 == 1, pair[::-1], pair)
+    base_slot = 2 * row_id
+    second_old = lax.dynamic_index_in_dim(old_place, base_slot + 1, 0, keepdims=False)
+    second_new = lax.dynamic_index_in_dim(new_place, base_slot + 1, 0, keepdims=False)
+    second_moved = second_new != second_old
+    leave_gate = jnp.where(second_moved, w_gate[1], w_gate[0])
+    leave_up = jnp.where(second_moved, w_up[1], w_up[0])
+    leave_down = jnp.where(second_moved, w_down[1], w_down[0])
+    arrive_gate, arrive_up, arrive_down = passed_along((leave_gate, leave_up, leave_down), "dp", 1)
     z_count = n_rows // 2
     ahead = [pair]
     behind = [pair]
     for hop in range(1, z_count // 2 + 1):
         ahead.append(passed_along(ahead[-1], "dp", -2))
+        if hop == 2:
+            ahead[-1], arrive_gate, arrive_up, arrive_down = lax.optimization_barrier(
+                (ahead[-1], arrive_gate, arrive_up, arrive_down)
+            )
         if hop < z_count // 2:
             behind.append(passed_along(behind[-1], "dp", 2))
     by_offset = jnp.stack(ahead + behind[:0:-1], axis=0)
@@ -134,14 +146,6 @@
     moe_output = jnp.dot(
         combine, returned.reshape(places, model_width), preferred_element_type=jnp.float32
     ).astype(jnp.bfloat16)
-    base_slot = 2 * row_id
-    second_old = lax.dynamic_index_in_dim(old_place, base_slot + 1, 0, keepdims=False)
-    second_new = lax.dynamic_index_in_dim(new_place, base_slot + 1, 0, keepdims=False)
-    second_moved = second_new != second_old
-    leave_gate = jnp.where(second_moved, w_gate[1], w_gate[0])
-    leave_up = jnp.where(second_moved, w_up[1], w_up[0])
-    leave_down = jnp.where(second_moved, w_down[1], w_down[0])
-    arrive_gate, arrive_up, arrive_down = passed_along((leave_gate, leave_up, leave_down), "dp", 1)
     new_gate = jnp.stack(
         [
             jnp.where(second_moved, w_gate[0], arrive_gate),

time: 353 us -> 335 us (0.949)
  waiting for transfers between devices: 204 us -> 193 us
  starting transfers between devices: 39.8 us -> 30.6 us
    ppermute x10, waiting for transfers between devices: 140 us -> 40.5 us  [passed_along(): return lax.ppermute(x, axis, [(i, (i + by) % size) for i in range(size)])]
    all_to_all x1, waiting for transfers between devices: 0.01 us -> 94.9 us  [local(): lax.all_to_all(pair_halves(upper_half, result[0], returned_other), 'dp',...]
    ppermute x10, starting transfers between devices: 25 us -> 15.9 us  [passed_along(): return lax.ppermute(x, axis, [(i, (i + by) % size) for i in range(size)])]
    ppermute x5, waiting for transfers between devices: 53.5 us -> 49.8 us  [partner_2(): lax.ppermute(x, axis, [(i, i ^ 1 << apart) for i in range(lax.axis_size(a...]
  transfers between devices with their start and end apart: 17 -> 17, of which waited for: 13 -> 12; matrix products, arithmetic and copies ran while one was open for 14% -> 16% of each run, Pallas kernels for 0% -> 0%
where the time goes in v13:
time: 335 us
  waiting for transfers between devices  193 us (58%)
  local copies, waits for them, and re-layouts  40.7 us (12%)
  matrix products  31.3 us (9%)
  starting transfers between devices  30.6 us (9%)
  other arithmetic  23.8 us (7%)
  between operations  15.6 us (5%)
    all_to_all x1, waiting for transfers between devices, local(): lax.all_to_all(pair_halves(upper_half, result[0], returned_other), 'dp',...  94.9 us
    ppermute x5, waiting for transfers between devices, partner_2(): lax.ppermute(x, axis, [(i, i ^ 1 << apart) for i in range(lax.axis_size(a...  49.8 us
    ppermute x10, waiting for transfers between devices, passed_along(): return lax.ppermute(x, axis, [(i, (i + by) % size) for i in range(size)])  40.5 us
    ppermute x10, starting transfers between devices, passed_along(): return lax.ppermute(x, axis, [(i, (i + by) % size) for i in range(size)])  15.9 us
    dot_general x1, matrix products, local(): lax.dot_general(hidden, full_down, (((1,), (1,)), ((), ())), preferred_el...  15.2 us
    dynamic_slice x2, local copies, waits for them, and re-layouts, local(): jnp.roll(by_offset, row_id // 2, axis=0).reshape(n_rows, tok_count, -1)  14 us
    unnamed x32, local copies, waits for them, and re-layouts  12 us
    all_to_all x1, starting transfers between devices, local(): lax.all_to_all(pair_halves(upper_half, result[0], returned_other), 'dp',...  9.72 us
  transfers between devices with their start and end apart: 17, of which 12 were waited for; matrix products, arithmetic and copies ran while one was open for 16% of the time, Pallas kernels for 0%

profile of v13, /device:TPU:8, one launch (start us, length us, event | category | flops | bytes accessed | tf_op | source)
XLA Modules:
  0.0 334.7 jit_solution(5548127430802929631)
XLA Ops:
  7.2 2.7 fusion.21
  10.0 1.5 collective-permute-start.12
  11.5 34.9 %collective-permute-done.12 = bf16[2,3,128,1024]{3,2,1,0:T(8,128)(2,1)S(1)} collective-permute-done((bf16[2,3,128,1024]{3,2,1,0:T(8,128)(2,1)}, bf16[2,3,128,1024]{3,2,1,0:T(8,128)(2,1)S(1)}, u32[]{:S(2)}, u32[]{:S(2)}) %collective-permute-start.12) | collective-permute-done | bytes 1572896 | tf_op jit(solution)/shard_map/ppermute | solution.py:8
  47.1 3.4 %collective-permute-done.13 = bf16[2,3,128,1024]{3,2,0,1:T(8,128)(2,1)S(1)} collective-permute-done((bf16[2,3,128,1024]{3,2,0,1:T(8,128)(2,1)S(1)}, bf16[2,3,128,1024]{3,2,0,1:T(8,128)(2,1)S(1)}, u32[]{:S(2)}, u32[]{:S(2)}) %collective-permute-start.13) | collective-permute-done | bytes 1572896 | tf_op jit(solution)/shard_map/ppermute | solution.py:8
  50.5 1.9 maximum_select_fusion.2
  53.0 1.2 reduce-window.14
  54.9 3.1 collective-permute-start
  61.7 3.5 %collective-permute-done = bf16[64,2176]{1,0:T(8,128)(2,1)S(1)} collective-permute-done((bf16[64,2176]{1,0:T(8,128)(2,1)S(1)}, bf16[64,2176]{1,0:T(8,128)(2,1)S(1)}, u32[]{:S(2)}, u32[]{:S(2)}) %collective-permute-start) | collective-permute-done | bytes 278560 | tf_op jit(solution)/shard_map/ppermute | solution.py:8
  65.2 0.9 bitcast_dynamic-update-slice_fusion.14
  66.2 5.9 %collective-permute-start.1 = (bf16[2,64,2176]{2,1,0:T(8,128)(2,1)S(1)}, bf16[2,64,2176]{2,1,0:T(8,128)(2,1)S(1)}, u32[]{:S(2)}, u32[]{:S(2)}) collective-permute-start(bf16[2,64,2176]{2,1,0:T(8,128)(2,1)S(1)} %get-tuple-element.13), channel_id=1, source_target_pairs={{0,224},{16,240},{32,0},{48,16},{64,32},{80,48},{96,64},{112,80},{... | collective-permute-start | bytes 1671176 | tf_op jit(solution)/shard_map/ppermute | solution.py:13
  72.8 3.8 %collective-permute-start.4 = (bf16[128,1024]{1,0:T(8,128)(2,1)}, bf16[128,1024]{1,0:T(8,128)(2,1)}, u32[]{:S(2)}, u32[]{:S(2)}) collective-permute-start(bf16[128,1024]{1,0:T(8,128)(2,1)} %bitcast_select_fusion.6), channel_id=1, source_target_pairs={{0,16},{16,32},{32,48},{48,64},{64,80},{80,96},{96,112},{112,128},... | collective-permute-start | bytes 786440 | tf_op jit(solution)/shard_map/ppermute | solution.py:13
  77.3 6.0 %collective-permute-done.1 = bf16[2,64,2176]{2,1,0:T(8,128)(2,1)S(1)} collective-permute-done((bf16[2,64,2176]{2,1,0:T(8,128)(2,1)S(1)}, bf16[2,64,2176]{2,1,0:T(8,128)(2,1)S(1)}, u32[]{:S(2)}, u32[]{:S(2)}) %collective-permute-start.1) | collective-permute-done | bytes 557088 | tf_op jit(solution)/shard_map/ppermute | solution.py:13
  83.4 3.7 %collective-permute-start.2 = (bf16[2,64,2176]{2,1,0:T(8,128)(2,1)S(1)}, bf16[2,64,2176]{2,1,0:T(8,128)(2,1)S(1)}, u32[]{:S(2)}, u32[]{:S(2)}) collective-permute-start(bf16[2,64,2176]{2,1,0:T(8,128)(2,1)S(1)} %collective-permute-done.1), channel_id=1, source_target_pairs={{0,224},{16,240},{32,0},{48,16},{64,32},{80,48},{96,64},{112,80},{... | collective-permute-start | bytes 1671176 | tf_op jit(solution)/shard_map/ppermute | solution.py:13
  87.1 0.9 bitcast_dynamic-update-slice_fusion.12
  87.9 9.9 %collective-permute-done.4 = bf16[128,1024]{1,0:T(8,128)(2,1)} collective-permute-done((bf16[128,1024]{1,0:T(8,128)(2,1)}, bf16[128,1024]{1,0:T(8,128)(2,1)}, u32[]{:S(2)}, u32[]{:S(2)}) %collective-permute-start.4) | collective-permute-done | bytes 262176 | tf_op jit(solution)/shard_map/ppermute | solution.py:13
  97.8 5.6 %collective-permute-done.5 = bf16[128,1024]{1,0:T(8,128)(2,1)} collective-permute-done((bf16[128,1024]{1,0:T(8,128)(2,1)}, bf16[128,1024]{1,0:T(8,128)(2,1)}, u32[]{:S(2)}, u32[]{:S(2)}) %collective-permute-start.5) | collective-permute-done | bytes 262176 | tf_op jit(solution)/shard_map/ppermute | solution.py:13
  103.4 2.0 collective-permute-start.10
  105.5 0.9 bitcast_dynamic-update-slice_fusion.10
  106.3 10.3 %collective-permute-done.6 = bf16[2,64,2176]{2,1,0:T(8,128)(2,1)S(1)} collective-permute-done((bf16[2,64,2176]{2,1,0:T(8,128)(2,1)S(1)}, bf16[2,64,2176]{2,1,0:T(8,128)(2,1)S(1)}, u32[]{:S(2)}, u32[]{:S(2)}) %collective-permute-start.6) | collective-permute-done | bytes 557088 | tf_op jit(solution)/shard_map/ppermute | solution.py:13
  117.4 8.7 %collective-permute-done.7 = bf16[2,64,2176]{2,1,0:T(8,128)(2,1)S(1)} collective-permute-done((bf16[2,64,2176]{2,1,0:T(8,128)(2,1)S(1)}, bf16[2,64,2176]{2,1,0:T(8,128)(2,1)S(1)}, u32[]{:S(2)}, u32[]{:S(2)}) %collective-permute-start.7) | collective-permute-done | bytes 557088 | tf_op jit(solution)/shard_map/ppermute | solution.py:13
  126.1 0.8 bitcast_dynamic-update-slice_fusion.6
  127.0 0.9 bitcast_dynamic-update-slice_fusion.4
  127.9 0.9 bitcast_dynamic-update-slice_fusion.2
  128.7 0.9 bitcast_dynamic-update-slice_fusion
  129.6 0.9 bitcast_dynamic-update-slice_fusion.15
  130.4 0.9 bitcast_dynamic-update-slice_fusion.13
  131.3 0.9 bitcast_dynamic-update-slice_fusion.11
  133.0 0.9 bitcast_dynamic-update-slice_fusion.7
  134.7 0.9 bitcast_dynamic-update-slice_fusion.3
  135.6 0.9 bitcast_dynamic-update-slice_fusion.1
  136.4 4.7 %constant_dynamic-slice_fusion = bf16[8,2,64,2176]{3,2,1,0:T(8,128)(2,1)} fusion(bf16[16,2,64,2176]{3,2,1,0:T(8,128)(2,1)} %bitcast_dynamic-update-slice_fusion.1, s32[]{:T(128)S(6)} %select_n.180), kind=kLoop, calls=%fused_computation.82 | loop fusion | bytes 8912900 | tf_op jit(solution)/shard_map/jit(_roll_dynamic)/dynamic_slice | solution.py:98
  141.2 9.3 %copy.90 = bf16[8,2,64,2176]{2,3,1,0:T(8,128)(2,1)} copy(bf16[8,2,64,2176]{3,2,1,0:T(8,128)(2,1)} %constant_dynamic-slice_fusion) | data formatting | bytes 8912896 | tf_op jit(solution)/shard_map/jit(_roll_dynamic)/dynamic_slice | solution.py:98
  151.5 2.3 reduce-window.16
  154.9 1.0 fusion.2
  155.9 6.4 %fusion.3 = bf16[16,2,32,2048]{3,2,1,0:T(8,128)(2,1)S(1)} fusion(pred[16,64,2,32]{1,3,2,0:T(8,128)(4,1)S(1)} %fusion.2, bf16[16,64,2176]{1,2,0:T(8,128)(2,1)} %bitcast.160), kind=kOutput, calls=%fused_computation.9 | convolution fusion | flops 270532608 | bytes 12648448 | tf_op jit(solution)/shard_map/stcr,std->scrd/dot_general | solution.py:111
  162.9 3.9 %collective-permute-done.11 = bf16[16,32,2048]{2,1,0:T(8,128)(2,1)S(1)} collective-permute-done((bf16[16,32,2048]{2,1,0:T(8,128)(2,1)S(1)}, bf16[16,32,2048]{2,1,0:T(8,128)(2,1)S(1)}, u32[]{:S(2)}, u32[]{:S(2)}) %collective-permute-start.11) | collective-permute-done | bytes 2097184 | tf_op jit(solution)/shard_map/ppermute | solution.py:8
  166.8 2.3 pad_maximum_fusion
  169.1 7.6 %all-gather.2.cloned.1.call-done = bf16[4,2,2,3,128,1024]{5,4,2,0,1,3:T(8,128)(2,1)} async-done(((bf16[1,2,2,3,128,1024]{5,4,2,0,1,3:T(8,128)(2,1)}), bf16[4,2,2,3,128,1024]{5,4,2,0,1,3:T(8,128)(2,1)}) %all-gather.2.cloned.1.call-update) | async-done | bytes 12582928 | tf_op jit(solution)/shard_map/all_gather | solution.py:57
  176.7 7.8 %fusion.22 = (bf16[1,2,4,2,128,1024]{5,4,3,2,1,0:T(8,128)(2,1)}, bf16[1,2,4,2,128,1024]{5,4,3,2,1,0:T(8,128)(2,1)}, bf16[1,2,4,2,128,1024]{5,4,3,2,1,0:T(8,128)(2,1)S(1)}) fusion(bf16[3,2,4,2,128,1024]{5,4,3,2,1,0:T(8,128)(2,1)} %bitcast.161), kind=kLoop, calls=%fused_computation.85 | loop fusion | bytes 25165824 | tf_op jit(solution)/shard_map/slice | solution.py:59
  184.5 6.0 %fusion.25 = f32[1024,1024]{1,0:T(8,128)} fusion(bf16[1024,2048]{1,0:T(8,128)(2,1)S(1)} %bitcast.167, bf16[2048,1024]{1,0:T(8,128)(2,1)S(1)} %bitcast.170), kind=kOutput, calls=%fused_computation.88 | convolution fusion | flops 4294967296 | bytes 12582912 | tf_op jit(solution)/shard_map/dot_general | solution.py:122
  190.6 15.2 %convolution_convert_fusion = bf16[1024,2048]{1,0:T(8,128)(2,1)} fusion(bf16[2048,1024]{1,0:T(8,128)(2,1)} %bitcast.169, f32[1024,1024]{1,0:T(8,128)} %fusion.25, bf16[1024,2048]{1,0:T(8,128)(2,1)} %bitcast.166, bf16[2048,1024]{1,0:T(8,128)(2,1)} %bitcast.168), kind=kOutput, calls=%fused_computation.10 | convolution fusion | flops 8598323200 | bytes 20971520 | tf_op jit(solution)/shard_map/dot_general | solution.py:125
  205.7 2.7 fusion.23
  208.5 4.1 %collective-permute-done.14 = bf16[16,32,2048]{2,1,0:T(8,128)(2,1)S(1)} collective-permute-done((bf16[16,32,2048]{2,1,0:T(8,128)(2,1)S(1)}, bf16[16,32,2048]{2,1,0:T(8,128)(2,1)S(1)}, u32[]{:S(2)}, u32[]{:S(2)}) %collective-permute-start.14) | collective-permute-done | bytes 2097184 | tf_op jit(solution)/shard_map/ppermute | solution.py:8
  212.7 2.2 maximum_select_fusion
  214.8 9.7 %all-to-all-start = ((bf16[16,2,32,2048]{3,2,1,0:T(8,128)(2,1)}), bf16[16,2,32,2048]{3,2,1,0:T(8,128)(2,1)}, u32[]{:S(2)}, u32[]{:S(2)}) async-start(bf16[16,2,32,2048]{3,2,1,0:T(8,128)(2,1)} %maximum_select_fusion), calls=%async_computation | async-start | bytes 8388608 | tf_op jit(solution)/shard_map/all_to_all | solution.py:130
  225.5 1.1 fusion.8
  229.2 94.9 %all-to-all-done = bf16[16,2,32,2048]{3,2,1,0:T(8,128)(2,1)} async-done(((bf16[16,2,32,2048]{3,2,1,0:T(8,128)(2,1)}), bf16[16,2,32,2048]{3,2,1,0:T(8,128)(2,1)}, u32[]{:S(2)}, u32[]{:S(2)}) %all-to-all-start) | async-done | bytes 4194336 | tf_op jit(solution)/shard_map/all_to_all | solution.py:130
  324.2 3.7 %convolution_convert_fusion.1 = bf16[64,2048]{1,0:T(8,128)(2,1)} fusion(bf16[64,1024]{1,0:T(8,128)(2,1)S(1)} %fusion.7, bf16[1024,2048]{1,0:T(8,128)(2,1)} %bitcast.49), kind=kOutput, calls=%fused_computation.13 | convolution fusion | flops 268566528 | bytes 4587520 | tf_op jit(solution)/shard_map/dot_general | solution.py:146
  (87 shorter events, 14.8 us)
Async XLA Ops:
  7.2 169.5 %all-gather.2.cloned.1.call-start = ((), (), s32[]{:S(2)}) async-start(), calls=%async_computation.1 | async-start | bytes 15728640 | tf_op jit(solution)/shard_map/all_gather | solution.py:57
  10.0 36.3 %collective-permute-start.12 = (bf16[2,3,128,1024]{3,2,1,0:T(8,128)(2,1)}, bf16[2,3,128,1024]{3,2,1,0:T(8,128)(2,1)S(1)}, u32[]{:S(2)}, u32[]{:S(2)}) collective-permute-start(bf16[2,3,128,1024]{3,2,1,0:T(8,128)(2,1)} %get-tuple-element.22), channel_id=1, source_target_pairs={{0,8},{1,9},{2,10},{3,11},{4,12},{5,13},{6,14},{7,15},{8,0},{9,1},... | collective-permute-start | bytes 4718600 | tf_op jit(solution)/shard_map/ppermute | solution.py:8
  47.0 3.5 %collective-permute-start.13 = (bf16[2,3,128,1024]{3,2,0,1:T(8,128)(2,1)S(1)}, bf16[2,3,128,1024]{3,2,0,1:T(8,128)(2,1)S(1)}, u32[]{:S(2)}, u32[]{:S(2)}) collective-permute-start(bf16[2,3,128,1024]{3,2,0,1:T(8,128)(2,1)S(1)} %get-tuple-element.20), channel_id=1, source_target_pairs={{0,1},{1,0},{2,3},{3,2},{4,5},{5,4},{6,7},{7,6},{8,9},{9,8},{10,11... | collective-permute-start | bytes 4718600 | tf_op jit(solution)/shard_map/ppermute | solution.py:8
  50.5 2.0 copy-start.7
  50.5 2.1 copy-start.6
  50.5 4.3 %copy-start.4 = (bf16[64,2048]{1,0:T(8,128)(2,1)S(1)}, bf16[64,2048]{1,0:T(8,128)(2,1)}, u32[]{:S(2)}) copy-start(bf16[64,2048]{1,0:T(8,128)(2,1)} %param.8) | copy-start | bytes 786436
  50.5 8.1 %copy-start.8 = (s32[32]{0:T(128)S(1)}, s32[32]{0:T(128)}, u32[]{:S(2)}) copy-start(s32[32]{0:T(128)} %param.12) | copy-start | bytes 388
  50.5 10.0 %copy-start = (bf16[2,128,1024]{2,1,0:T(8,128)(2,1)S(1)}, bf16[2,128,1024]{2,1,0:T(8,128)(2,1)}, u32[]{:S(2)}) copy-start(bf16[2,128,1024]{2,1,0:T(8,128)(2,1)} %param.13) | copy-start | bytes 1572868
  52.4 19.6 %copy-start.2 = (bf16[2,128,1024]{2,1,0:T(8,128)(2,1)S(1)}, bf16[2,128,1024]{2,1,0:T(8,128)(2,1)}, u32[]{:S(2)}) copy-start(bf16[2,128,1024]{2,1,0:T(8,128)(2,1)} %param.14) | copy-start | bytes 1572868
  52.4 24.2 %copy-start.1 = (bf16[2,128,1024]{2,1,0:T(8,128)(2,1)S(1)}, bf16[2,128,1024]{2,1,0:T(8,128)(2,1)}, u32[]{:S(2)}) copy-start(bf16[2,128,1024]{2,1,0:T(8,128)(2,1)} %param.15) | copy-start | bytes 1572868
  54.9 10.3 %collective-permute-start = (bf16[64,2176]{1,0:T(8,128)(2,1)S(1)}, bf16[64,2176]{1,0:T(8,128)(2,1)S(1)}, u32[]{:S(2)}, u32[]{:S(2)}) collective-permute-start(bf16[64,2176]{1,0:T(8,128)(2,1)S(1)} %concatenate.22), channel_id=1, source_target_pairs={{0,16},{16,0},{32,48},{48,32},{64,80},{80,64},{96,112},{112,96},{1... | collective-permute-start | bytes 835592 | tf_op jit(solution)/shard_map/ppermute | solution.py:8
  61.2 26.7 %collective-permute-start.3 = (bf16[128,1024]{1,0:T(8,128)(2,1)}, bf16[128,1024]{1,0:T(8,128)(2,1)S(1)}, u32[]{:S(2)}, u32[]{:S(2)}) collective-permute-start(bf16[128,1024]{1,0:T(8,128)(2,1)} %bitcast_select_fusion.9), channel_id=1, source_target_pairs={{0,16},{16,32},{32,48},{48,64},{64,80},{80,96},{96,112},{112,128},... | collective-permute-start | bytes 786440 | tf_op jit(solution)/shard_map/ppermute | solution.py:13
  66.2 17.2 %collective-permute-start.1 = (bf16[2,64,2176]{2,1,0:T(8,128)(2,1)S(1)}, bf16[2,64,2176]{2,1,0:T(8,128)(2,1)S(1)}, u32[]{:S(2)}, u32[]{:S(2)}) collective-permute-start(bf16[2,64,2176]{2,1,0:T(8,128)(2,1)S(1)} %get-tuple-element.13), channel_id=1, source_target_pairs={{0,224},{16,240},{32,0},{48,16},{64,32},{80,48},{96,64},{112,80},{... | collective-permute-start | bytes 1671176 | tf_op jit(solution)/shard_map/ppermute | solution.py:13
  72.0 15.0 %collective-permute-start.8 = (bf16[2,64,2176]{2,1,0:T(8,128)(2,1)S(1)}, bf16[2,64,2176]{2,1,0:T(8,128)(2,1)S(1)}, u32[]{:S(2)}, u32[]{:S(2)}) collective-permute-start(bf16[2,64,2176]{2,1,0:T(8,128)(2,1)S(1)} %get-tuple-element.13), channel_id=1, source_target_pairs={{0,32},{16,48},{32,64},{48,80},{64,96},{80,112},{96,128},{112,144}... | collective-permute-start | bytes 1671176 | tf_op jit(solution)/shard_map/ppermute | solution.py:13
  72.8 25.0 %collective-permute-start.4 = (bf16[128,1024]{1,0:T(8,128)(2,1)}, bf16[128,1024]{1,0:T(8,128)(2,1)}, u32[]{:S(2)}, u32[]{:S(2)}) collective-permute-start(bf16[128,1024]{1,0:T(8,128)(2,1)} %bitcast_select_fusion.6), channel_id=1, source_target_pairs={{0,16},{16,32},{32,48},{48,64},{64,80},{80,96},{96,112},{112,128},... | collective-permute-start | bytes 786440 | tf_op jit(solution)/shard_map/ppermute | solution.py:13
  77.3 26.1 %collective-permute-start.5 = (bf16[128,1024]{1,0:T(8,128)(2,1)}, bf16[128,1024]{1,0:T(8,128)(2,1)}, u32[]{:S(2)}, u32[]{:S(2)}) collective-permute-start(bf16[128,1024]{1,0:T(8,128)(2,1)} %bitcast_select_fusion.3), channel_id=1, source_target_pairs={{0,16},{16,32},{32,48},{48,64},{64,80},{80,96},{96,112},{112,128},... | collective-permute-start | bytes 786440 | tf_op jit(solution)/shard_map/ppermute | solution.py:13
  83.4 20.1 %collective-permute-start.2 = (bf16[2,64,2176]{2,1,0:T(8,128)(2,1)S(1)}, bf16[2,64,2176]{2,1,0:T(8,128)(2,1)S(1)}, u32[]{:S(2)}, u32[]{:S(2)}) collective-permute-start(bf16[2,64,2176]{2,1,0:T(8,128)(2,1)S(1)} %collective-permute-done.1), channel_id=1, source_target_pairs={{0,224},{16,240},{32,0},{48,16},{64,32},{80,48},{96,64},{112,80},{... | collective-permute-start | bytes 1671176 | tf_op jit(solution)/shard_map/ppermute | solution.py:13
  87.1 16.4 %collective-permute-start.9 = (bf16[2,64,2176]{2,1,0:T(8,128)(2,1)S(1)}, bf16[2,64,2176]{2,1,0:T(8,128)(2,1)S(1)}, u32[]{:S(2)}, u32[]{:S(2)}) collective-permute-start(bf16[2,64,2176]{2,1,0:T(8,128)(2,1)S(1)} %collective-permute-done.8), channel_id=1, source_target_pairs={{0,32},{16,48},{32,64},{48,80},{64,96},{80,112},{96,128},{112,144}... | collective-permute-start | bytes 1671176 | tf_op jit(solution)/shard_map/ppermute | solution.py:13
  103.4 13.2 %collective-permute-start.6 = (bf16[2,64,2176]{2,1,0:T(8,128)(2,1)S(1)}, bf16[2,64,2176]{2,1,0:T(8,128)(2,1)S(1)}, u32[]{:S(2)}, u32[]{:S(2)}) collective-permute-start(bf16[2,64,2176]{2,1,0:T(8,128)(2,1)S(1)} %collective-permute-done.2), channel_id=1, source_target_pairs={{0,224},{16,240},{32,0},{48,16},{64,32},{80,48},{96,64},{112,80},{... | collective-permute-start | bytes 1671176 | tf_op jit(solution)/shard_map/ppermute | solution.py:13
  103.4 23.6 %collective-permute-start.10 = (bf16[2,64,2176]{2,1,0:T(8,128)(2,1)S(1)}, bf16[2,64,2176]{2,1,0:T(8,128)(2,1)S(1)}, u32[]{:S(2)}, u32[]{:S(2)}) collective-permute-start(bf16[2,64,2176]{2,1,0:T(8,128)(2,1)S(1)} %collective-permute-done.9), channel_id=1, source_target_pairs={{0,32},{16,48},{32,64},{48,80},{64,96},{80,112},{96,128},{112,144}... | collective-permute-start | bytes 1671176 | tf_op jit(solution)/shard_map/ppermute | solution.py:13
  116.6 9.5 %collective-permute-start.7 = (bf16[2,64,2176]{2,1,0:T(8,128)(2,1)S(1)}, bf16[2,64,2176]{2,1,0:T(8,128)(2,1)S(1)}, u32[]{:S(2)}, u32[]{:S(2)}) collective-permute-start(bf16[2,64,2176]{2,1,0:T(8,128)(2,1)S(1)} %collective-permute-done.6), channel_id=1, source_target_pairs={{0,224},{16,240},{32,0},{48,16},{64,32},{80,48},{96,64},{112,80},{... | collective-permute-start | bytes 1671176 | tf_op jit(solution)/shard_map/ppermute | solution.py:13
  162.5 4.2 %collective-permute-start.11 = (bf16[16,32,2048]{2,1,0:T(8,128)(2,1)S(1)}, bf16[16,32,2048]{2,1,0:T(8,128)(2,1)S(1)}, u32[]{:S(2)}, u32[]{:S(2)}) collective-permute-start(bf16[16,32,2048]{2,1,0:T(8,128)(2,1)S(1)} %fusion.4), channel_id=1, source_target_pairs={{0,1},{1,0},{2,3},{3,2},{4,5},{5,4},{6,7},{7,6},{8,9},{9,8},{10,11... | collective-permute-start | bytes 6291464 | tf_op jit(solution)/shard_map/ppermute | solution.py:8
  176.7 7.8 %copy-start.3 = (bf16[2,16,32,2048]{3,2,1,0:T(8,128)(2,1)S(1)}, bf16[2,16,32,2048]{3,2,1,0:T(8,128)(2,1)}, u32[]{:S(2)}) copy-start(bf16[2,16,32,2048]{3,2,1,0:T(8,128)(2,1)} %pad_maximum_fusion) | copy-start | bytes 12582916
  208.4 4.2 %collective-permute-start.14 = (bf16[16,32,2048]{2,1,0:T(8,128)(2,1)S(1)}, bf16[16,32,2048]{2,1,0:T(8,128)(2,1)S(1)}, u32[]{:S(2)}, u32[]{:S(2)}) collective-permute-start(bf16[16,32,2048]{2,1,0:T(8,128)(2,1)S(1)} %bitcast.176), channel_id=1, source_target_pairs={{0,1},{1,0},{2,3},{3,2},{4,5},{5,4},{6,7},{7,6},{8,9},{9,8},{10,11... | collective-permute-start | bytes 6291464 | tf_op jit(solution)/shard_map/ppermute | solution.py:8
  214.8 9.8 %copy-start.5 = (f32[64,8]{0,1:T(8,128)S(1)}, f32[64,8]{0,1:T(8,128)}, u32[]{:S(2)}) copy-start(f32[64,8]{0,1:T(8,128)} %param.9) | copy-start | bytes 6148
  214.8 109.3 %all-to-all-start = ((bf16[16,2,32,2048]{3,2,1,0:T(8,128)(2,1)}), bf16[16,2,32,2048]{3,2,1,0:T(8,128)(2,1)}, u32[]{:S(2)}, u32[]{:S(2)}) async-start(bf16[16,2,32,2048]{3,2,1,0:T(8,128)(2,1)} %maximum_select_fusion), calls=%async_computation | async-start | bytes 8388608 | tf_op jit(solution)/shard_map/all_to_all | solution.py:130
Sparse Core Ops, SparseCore 0:
  52.6 124.0 all-gather.1

commit v14 on v13

--- a/solution.py
+++ b/solution.py
@@ -54,8 +54,9 @@
         core == 0, jnp.stack([kept, received], axis=1), jnp.stack([received, kept], axis=1)
     )
     groups = [list(range(g % 2 + (g // 2) * half_count, (g // 2 + 1) * half_count, 2)) for g in range(4)]
-    ring = lax.all_gather(block, "shard", axis=0, tiled=False, axis_index_groups=groups)
-    full = jnp.transpose(ring, (3, 1, 0, 2, 4, 5)).reshape(3, model_width, -1)
+    block = jnp.transpose(block, (2, 0, 1, 3, 4))
+    ring = lax.all_gather(block, "shard", axis=1, tiled=False, axis_index_groups=groups)
+    full = ring.reshape(3, model_width, -1)
     full_gate, full_up, full_down = full[0], full[1], full[2]
     slot_index = jnp.arange(slot_count, dtype=jnp.int32)
     owner_slot = jnp.sum(
@@ -118,13 +119,15 @@
     other_rows = jnp.where(upper_half, arrived[:, 0], arrived[:, 1])
     partner = partner_2(other_rows, "shard", 0)
     work_rows = jnp.stack([own_rows, partner], axis=0)
-    flat_rows = work_rows.reshape(-1, model_width)
+    flat_rows = work_rows.reshape(-1, 2, 4, 2, model_width // 16)
+    flat_rows = jnp.transpose(flat_rows, (0, 2, 1, 3, 4)).reshape(-1, model_width)
     gate_part = jnp.dot(flat_rows, full_gate, preferred_element_type=jnp.float32)
     up_part = jnp.dot(flat_rows, full_up, preferred_element_type=jnp.float32)
     hidden = (jax.nn.silu(gate_part) * up_part).astype(jnp.bfloat16)
     result = lax.dot_general(
         hidden, full_down, (((1,), (1,)), ((), ())), preferred_element_type=jnp.float32
     ).astype(jnp.bfloat16)
+    result = jnp.transpose(result.reshape(-1, 4, 2, 2, model_width // 16), (0, 2, 1, 3, 4))
     result = result.reshape(2, n_rows, capacity, model_width)
     returned_other = partner_2(result[1], "shard", 0)
     returned = lax.all_to_all(

time: 335 us -> 367 us (1.096)
  local copies, waits for them, and re-layouts: 40.7 us -> 82.8 us
  waiting for transfers between devices: 193 us -> 185 us
    reshape x0 -> x4, local copies, waits for them, and re-layouts: none -> 31.7 us  [the longest x2 18.8 us: local(): flat_rows = work_rows.reshape(-1, 2, 4, 2, model_width // 16)]
    all_gather x1, waiting for transfers between devices: 7.63 us -> 0.01 us  [local(): lax.all_gather(block, 'shard', axis=1, tiled=False, axis_index_groups=gro...]
    squeeze x0 -> x1, local copies, waits for them, and re-layouts: none -> 4.47 us  [local(): returned_other = partner_2(result[1], 'shard', 0)]
    unnamed x32 -> x46, local copies, waits for them, and re-layouts: 12 us -> 12 us
  transfers between devices with their start and end apart: 17 -> 17, of which waited for: 12 -> 11; matrix products, arithmetic and copies ran while one was open for 16% -> 20% of each run, Pallas kernels for 0% -> 0%
where the time goes in v14:
time: 367 us; the launch traced here: 366 us
  waiting for transfers between devices  185 us (50%)
  local copies, waits for them, and re-layouts  82.8 us (23%)
  matrix products  31.8 us (9%)
  starting transfers between devices  27.8 us (8%)
  other arithmetic  23.5 us (6%)
  between operations  15.7 us (4%)
    all_to_all x1, waiting for transfers between devices, local(): lax.all_to_all(pair_halves(upper_half, result[0], returned_other), 'dp',...  95.9 us
    ppermute x5, waiting for transfers between devices, partner_2(): lax.ppermute(x, axis, [(i, i ^ 1 << apart) for i in range(lax.axis_size(a...  47 us
    ppermute x10, waiting for transfers between devices, passed_along(): return lax.ppermute(x, axis, [(i, (i + by) % size) for i in range(size)])  41.6 us
    reshape x2, local copies, waits for them, and re-layouts, local(): flat_rows = work_rows.reshape(-1, 2, 4, 2, model_width // 16)  18.8 us
    ppermute x10, starting transfers between devices, passed_along(): return lax.ppermute(x, axis, [(i, (i + by) % size) for i in range(size)])  16.1 us
    dot_general x1, matrix products, local(): lax.dot_general(hidden, full_down, (((1,), (1,)), ((), ())), preferred_el...  15.5 us
    dynamic_slice x2, local copies, waits for them, and re-layouts, local(): jnp.roll(by_offset, row_id // 2, axis=0).reshape(n_rows, tok_count, -1)  13.9 us
    reshape x2, local copies, waits for them, and re-layouts, local(): result.reshape(-1, 4, 2, 2, model_width // 16)  12.8 us
  transfers between devices with their start and end apart: 17, of which 11 were waited for; matrix products, arithmetic and copies ran while one was open for 20% of the time, Pallas kernels for 0%

profile of v14, /device:TPU:8, one launch (start us, length us, event | category | flops | bytes accessed | tf_op | source)
XLA Modules:
  0.0 366.0 jit_solution(15411622770704543474)
XLA Ops:
  7.2 2.7 fusion.22
  9.9 1.5 collective-permute-start.12
  11.4 34.9 %collective-permute-done.12 = bf16[2,3,128,1024]{3,2,1,0:T(8,128)(2,1)S(1)} collective-permute-done((bf16[2,3,128,1024]{3,2,1,0:T(8,128)(2,1)}, bf16[2,3,128,1024]{3,2,1,0:T(8,128)(2,1)S(1)}, u32[]{:S(2)}, u32[]{:S(2)}) %collective-permute-start.12) | collective-permute-done | bytes 1572896 | tf_op jit(solution)/shard_map/ppermute | solution.py:8
  47.2 3.2 collective-permute-done.13
  50.5 1.9 fusion.4
  52.9 1.2 reduce-window.14
  54.8 3.1 collective-permute-start
  61.6 3.5 collective-permute-done
  65.2 0.9 bitcast_dynamic-update-slice_fusion.14
  66.1 5.9 %collective-permute-start.1 = (bf16[2,64,2176]{2,1,0:T(8,128)(2,1)S(1)}, bf16[2,64,2176]{2,1,0:T(8,128)(2,1)S(1)}, u32[]{:S(2)}, u32[]{:S(2)}) collective-permute-start(bf16[2,64,2176]{2,1,0:T(8,128)(2,1)S(1)} %get-tuple-element.13), channel_id=1, source_target_pairs={{0,224},{16,240},{32,0},{48,16},{64,32},{80,48},{96,64},{112,80},{... | collective-permute-start | bytes 1671176 | tf_op jit(solution)/shard_map/ppermute | solution.py:13
  72.0 3.9 %collective-permute-start.4 = (bf16[128,1024]{1,0:T(8,128)(2,1)S(1)}, bf16[128,1024]{1,0:T(8,128)(2,1)S(1)}, u32[]{:S(2)}, u32[]{:S(2)}) collective-permute-start(bf16[128,1024]{1,0:T(8,128)(2,1)S(1)} %bitcast_select_fusion.7), channel_id=1, source_target_pairs={{0,16},{16,32},{32,48},{48,64},{64,80},{80,96},{96,112},{112,128},... | collective-permute-start | bytes 786440 | tf_op jit(solution)/shard_map/ppermute | solution.py:13
  76.1 7.2 %collective-permute-done.1 = bf16[2,64,2176]{2,1,0:T(8,128)(2,1)S(1)} collective-permute-done((bf16[2,64,2176]{2,1,0:T(8,128)(2,1)S(1)}, bf16[2,64,2176]{2,1,0:T(8,128)(2,1)S(1)}, u32[]{:S(2)}, u32[]{:S(2)}) %collective-permute-start.1) | collective-permute-done | bytes 557088 | tf_op jit(solution)/shard_map/ppermute | solution.py:13
  83.3 3.7 %collective-permute-start.2 = (bf16[2,64,2176]{2,1,0:T(8,128)(2,1)S(1)}, bf16[2,64,2176]{2,1,0:T(8,128)(2,1)S(1)}, u32[]{:S(2)}, u32[]{:S(2)}) collective-permute-start(bf16[2,64,2176]{2,1,0:T(8,128)(2,1)S(1)} %collective-permute-done.1), channel_id=1, source_target_pairs={{0,224},{16,240},{32,0},{48,16},{64,32},{80,48},{96,64},{112,80},{... | collective-permute-start | bytes 1671176 | tf_op jit(solution)/shard_map/ppermute | solution.py:13
  87.0 0.9 bitcast_dynamic-update-slice_fusion.12
  87.9 9.8 %collective-permute-done.4 = bf16[128,1024]{1,0:T(8,128)(2,1)S(1)} collective-permute-done((bf16[128,1024]{1,0:T(8,128)(2,1)S(1)}, bf16[128,1024]{1,0:T(8,128)(2,1)S(1)}, u32[]{:S(2)}, u32[]{:S(2)}) %collective-permute-start.4) | collective-permute-done | bytes 262176 | tf_op jit(solution)/shard_map/ppermute | solution.py:13
  97.6 5.6 %collective-permute-done.5 = bf16[128,1024]{1,0:T(8,128)(2,1)S(1)} collective-permute-done((bf16[128,1024]{1,0:T(8,128)(2,1)S(1)}, bf16[128,1024]{1,0:T(8,128)(2,1)S(1)}, u32[]{:S(2)}, u32[]{:S(2)}) %collective-permute-start.5) | collective-permute-done | bytes 262176 | tf_op jit(solution)/shard_map/ppermute | solution.py:13
  103.3 2.0 collective-permute-start.10
  106.1 10.3 %collective-permute-done.6 = bf16[2,64,2176]{2,1,0:T(8,128)(2,1)S(1)} collective-permute-done((bf16[2,64,2176]{2,1,0:T(8,128)(2,1)S(1)}, bf16[2,64,2176]{2,1,0:T(8,128)(2,1)S(1)}, u32[]{:S(2)}, u32[]{:S(2)}) %collective-permute-start.6) | collective-permute-done | bytes 557088 | tf_op jit(solution)/shard_map/ppermute | solution.py:13
  116.4 0.9 bitcast_dynamic-update-slice_fusion.8
  117.3 8.7 %collective-permute-done.7 = bf16[2,64,2176]{2,1,0:T(8,128)(2,1)S(1)} collective-permute-done((bf16[2,64,2176]{2,1,0:T(8,128)(2,1)S(1)}, bf16[2,64,2176]{2,1,0:T(8,128)(2,1)S(1)}, u32[]{:S(2)}, u32[]{:S(2)}) %collective-permute-start.7) | collective-permute-done | bytes 557088 | tf_op jit(solution)/shard_map/ppermute | solution.py:13
  126.8 0.9 bitcast_dynamic-update-slice_fusion.4
  130.2 0.9 bitcast_dynamic-update-slice_fusion.13
  131.1 0.9 bitcast_dynamic-update-slice_fusion.11
  132.8 0.9 bitcast_dynamic-update-slice_fusion.7
  135.3 0.9 bitcast_dynamic-update-slice_fusion.1
  136.2 4.7 %constant_dynamic-slice_fusion = bf16[8,2,64,2176]{3,2,1,0:T(8,128)(2,1)} fusion(bf16[16,2,64,2176]{3,2,1,0:T(8,128)(2,1)} %bitcast_dynamic-update-slice_fusion.1, s32[]{:T(128)S(6)} %select_n.173), kind=kLoop, calls=%fused_computation.84 | loop fusion | bytes 8912900 | tf_op jit(solution)/shard_map/jit(_roll_dynamic)/dynamic_slice | solution.py:99
  140.9 9.2 %copy.123 = bf16[8,2,64,2176]{2,3,1,0:T(8,128)(2,1)} copy(bf16[8,2,64,2176]{3,2,1,0:T(8,128)(2,1)} %constant_dynamic-slice_fusion) | data formatting | bytes 8912896 | tf_op jit(solution)/shard_map/jit(_roll_dynamic)/dynamic_slice | solution.py:99
  151.2 2.3 reduce-window.16
  154.5 1.0 fusion.2
  155.5 6.4 %fusion.3 = bf16[16,2,32,2048]{3,2,1,0:T(8,128)(2,1)S(1)} fusion(pred[16,64,2,32]{1,3,2,0:T(8,128)(4,1)S(1)} %fusion.2, bf16[16,64,2176]{1,2,0:T(8,128)(2,1)} %bitcast.167), kind=kOutput, calls=%fused_computation.10 | convolution fusion | flops 270532608 | bytes 12648448 | tf_op jit(solution)/shard_map/stcr,std->scrd/dot_general | solution.py:112
  162.5 3.9 %collective-permute-done.11 = bf16[16,32,2048]{2,1,0:T(8,128)(2,1)S(1)} collective-permute-done((bf16[16,32,2048]{2,1,0:T(8,128)(2,1)S(1)}, bf16[16,32,2048]{2,1,0:T(8,128)(2,1)S(1)}, u32[]{:S(2)}, u32[]{:S(2)}) %collective-permute-start.11) | collective-permute-done | bytes 2097184 | tf_op jit(solution)/shard_map/ppermute | solution.py:8
  166.4 2.3 pad_maximum_fusion
  168.7 7.7 %reshape.120 = bf16[1024,2,4,2,128]{4,3,2,1,0:T(2,128)(2,1)} reshape(bf16[2,16,32,2048]{3,2,1,0:T(8,128)(2,1)} %pad_maximum_fusion) | data formatting | bytes 8388608 | tf_op jit(solution)/shard_map/reshape | solution.py:122
  176.4 11.2 %copy.138 = bf16[1024,2,4,2,128]{0,4,3,1,2:T(8,128)(2,1)} copy(bf16[1024,2,4,2,128]{4,3,2,1,0:T(2,128)(2,1)} %reshape.120) | data formatting | bytes 8388608 | tf_op jit(solution)/shard_map/reshape | solution.py:122
  187.6 7.9 %fusion.23 = (bf16[1,8,2,128,1024]{4,3,2,1,0:T(8,128)(2,1)}, bf16[1,8,2,128,1024]{4,3,2,1,0:T(8,128)(2,1)S(1)}, bf16[1,8,2,128,1024]{4,3,2,1,0:T(8,128)(2,1)}) fusion(bf16[3,8,2,128,1024]{4,3,2,1,0:T(8,128)(2,1)} %all-gather.3.cloned.1.call-done), kind=kLoop, calls=%fused_computation.87 | loop fusion | bytes 25165824 | tf_op jit(solution)/shard_map/slice | solution.py:60
  195.4 6.1 %fusion.26 = f32[1024,1024]{1,0:T(8,128)} fusion(bf16[1024,2048]{0,1:T(8,128)(2,1)S(1)} %bitcast.173, bf16[2048,1024]{1,0:T(8,128)(2,1)S(1)} %bitcast.176), kind=kOutput, calls=%fused_computation.90 | convolution fusion | flops 4294967296 | bytes 12582912 | tf_op jit(solution)/shard_map/dot_general | solution.py:124
  201.5 15.5 %convolution_convert_fusion = bf16[1024,2048]{1,0:T(8,128)(2,1)} fusion(bf16[2048,1024]{1,0:T(8,128)(2,1)} %bitcast.175, f32[1024,1024]{1,0:T(8,128)} %fusion.26, bf16[1024,2048]{0,1:T(8,128)(2,1)} %bitcast.172, bf16[2048,1024]{1,0:T(8,128)(2,1)} %bitcast.174), kind=kOutput, calls=%fused_computation.11 | convolution fusion | flops 8598323200 | bytes 20971520 | tf_op jit(solution)/shard_map/dot_general | solution.py:127
  217.0 7.8 %reshape.122 = bf16[1024,4,2,2,128]{4,3,2,1,0:T(2,128)(2,1)} reshape(bf16[1024,2048]{1,0:T(8,128)(2,1)} %convolution_convert_fusion) | data formatting | bytes 8388608 | tf_op jit(solution)/shard_map/reshape | solution.py:130
  224.8 5.1 %copy.153 = bf16[1024,4,2,2,128]{4,3,1,2,0:T(2,128)(2,1)S(1)} copy(bf16[1024,4,2,2,128]{4,3,2,1,0:T(2,128)(2,1)} %reshape.122) | data formatting | bytes 8388608 | tf_op jit(solution)/shard_map/reshape | solution.py:130
  229.9 3.8 %fusion.24 = (bf16[512,2,4,2,128]{4,3,2,1,0:T(2,128)(2,1)}, bf16[512,2,4,2,128]{4,3,2,1,0:T(2,128)(2,1)S(1)}) fusion(bf16[1024,2,4,2,128]{4,3,2,1,0:T(2,128)(2,1)S(1)} %bitcast.168), kind=kLoop, calls=%fused_computation.88 | loop fusion | bytes 8388608 | tf_op jit(solution)/shard_map/slice | solution.py:132
  233.7 4.5 %squeeze.56 = bf16[16,32,2048]{2,1,0:T(8,128)(2,1)} reshape(bf16[512,2,4,2,128]{4,3,2,1,0:T(2,128)(2,1)} %get-tuple-element.17) | data formatting | bytes 4194304 | tf_op jit(solution)/shard_map/squeeze | solution.py:132
  238.3 2.8 stack_squeeze.4
  241.1 1.6 collective-permute-done.14
  242.6 4.2 %maximum_select_fusion = bf16[16,2,32,2048]{3,2,0,1:T(8,128)(2,1)S(1)} fusion(bf16[16,1,32,2048]{3,2,0,1:T(8,128)(2,1)} %stack_squeeze.4, bf16[16,1,32,2048]{3,2,0,1:T(8,128)(2,1)} %bitcast.49, pred[]{:T(512)S(6)} %eq.161), kind=kLoop, calls=%fused_computation.3 | loop fusion | flops 6291456 | bytes 8388609 | tf_op jit(solution)/shard_map/jit(_where)/select_n | solution.py:26
  246.9 2.3 copy.143
  249.2 6.7 %all-to-all-start = ((bf16[16,2,32,2048]{3,2,1,0:T(8,128)(2,1)}), bf16[16,2,32,2048]{3,2,1,0:T(8,128)(2,1)}, u32[]{:S(2)}, u32[]{:S(2)}) async-start(bf16[16,2,32,2048]{3,2,1,0:T(8,128)(2,1)} %copy.143), calls=%async_computation | async-start | bytes 8388608 | tf_op jit(solution)/shard_map/all_to_all | solution.py:133
  259.6 95.9 %all-to-all-done = bf16[16,2,32,2048]{3,2,1,0:T(8,128)(2,1)} async-done(((bf16[16,2,32,2048]{3,2,1,0:T(8,128)(2,1)}), bf16[16,2,32,2048]{3,2,1,0:T(8,128)(2,1)}, u32[]{:S(2)}, u32[]{:S(2)}) %all-to-all-start) | async-done | bytes 4194336 | tf_op jit(solution)/shard_map/all_to_all | solution.py:133
  355.4 3.7 %convolution_convert_fusion.1 = bf16[64,2048]{1,0:T(8,128)(2,1)} fusion(bf16[64,1024]{1,0:T(8,128)(2,1)S(1)} %fusion.8, bf16[1024,2048]{1,0:T(8,128)(2,1)} %bitcast.50), kind=kOutput, calls=%fused_computation.16 | convolution fusion | flops 268566528 | bytes 4587520 | tf_op jit(solution)/shard_map/dot_general | solution.py:149
  (109 shorter events, 18.0 us)
Async XLA Ops:
  7.2 180.4 %all-gather.3.cloned.1.call-start = ((), (), s32[]{:S(2)}) async-start(), calls=%async_computation.1 | async-start | bytes 15728640 | tf_op jit(solution)/shard_map/all_gather | solution.py:58
  9.9 36.3 %collective-permute-start.12 = (bf16[2,3,128,1024]{3,2,1,0:T(8,128)(2,1)}, bf16[2,3,128,1024]{3,2,1,0:T(8,128)(2,1)S(1)}, u32[]{:S(2)}, u32[]{:S(2)}) collective-permute-start(bf16[2,3,128,1024]{3,2,1,0:T(8,128)(2,1)} %get-tuple-element.20), channel_id=1, source_target_pairs={{0,8},{1,9},{2,10},{3,11},{4,12},{5,13},{6,14},{7,15},{8,0},{9,1},... | collective-permute-start | bytes 4718600 | tf_op jit(solution)/shard_map/ppermute | solution.py:8
  46.9 3.5 collective-permute-start.13
  50.4 1.9 copy-start.14
  50.4 2.0 copy-start.13
  50.4 4.3 %copy-start.7 = (bf16[64,2048]{1,0:T(8,128)(2,1)S(1)}, bf16[64,2048]{1,0:T(8,128)(2,1)}, u32[]{:S(2)}) copy-start(bf16[64,2048]{1,0:T(8,128)(2,1)} %param.8) | copy-start | bytes 786436
  50.4 8.1 %copy-start.15 = (s32[32]{0:T(128)S(1)}, s32[32]{0:T(128)}, u32[]{:S(2)}) copy-start(s32[32]{0:T(128)} %param.12) | copy-start | bytes 388
  50.4 9.9 %copy-start = (bf16[2,128,1024]{2,1,0:T(8,128)(2,1)S(1)}, bf16[2,128,1024]{2,1,0:T(8,128)(2,1)}, u32[]{:S(2)}) copy-start(bf16[2,128,1024]{2,1,0:T(8,128)(2,1)} %param.13) | copy-start | bytes 1572868
  52.3 19.6 %copy-start.4 = (bf16[2,128,1024]{2,1,0:T(8,128)(2,1)S(1)}, bf16[2,128,1024]{2,1,0:T(8,128)(2,1)}, u32[]{:S(2)}) copy-start(bf16[2,128,1024]{2,1,0:T(8,128)(2,1)} %param.14) | copy-start | bytes 1572868
  52.3 23.6 %copy-start.2 = (bf16[2,128,1024]{2,1,0:T(8,128)(2,1)S(1)}, bf16[2,128,1024]{2,1,0:T(8,128)(2,1)}, u32[]{:S(2)}) copy-start(bf16[2,128,1024]{2,1,0:T(8,128)(2,1)} %param.15) | copy-start | bytes 1572868
  54.8 10.3 %collective-permute-start = (bf16[64,2176]{1,0:T(8,128)(2,1)S(1)}, bf16[64,2176]{1,0:T(8,128)(2,1)S(1)}, u32[]{:S(2)}, u32[]{:S(2)}) collective-permute-start(bf16[64,2176]{1,0:T(8,128)(2,1)S(1)} %concatenate.8), channel_id=1, source_target_pairs={{0,16},{16,0},{32,48},{48,32},{64,80},{80,64},{96,112},{112,96},{1... | collective-permute-start | bytes 835592 | tf_op jit(solution)/shard_map/ppermute | solution.py:8
  61.1 26.7 %collective-permute-start.3 = (bf16[128,1024]{1,0:T(8,128)(2,1)}, bf16[128,1024]{1,0:T(8,128)(2,1)S(1)}, u32[]{:S(2)}, u32[]{:S(2)}) collective-permute-start(bf16[128,1024]{1,0:T(8,128)(2,1)} %bitcast_select_fusion.10), channel_id=1, source_target_pairs={{0,16},{16,32},{32,48},{48,64},{64,80},{80,96},{96,112},{112,128},... | collective-permute-start | bytes 786440 | tf_op jit(solution)/shard_map/ppermute | solution.py:13
  66.1 17.2 %collective-permute-start.1 = (bf16[2,64,2176]{2,1,0:T(8,128)(2,1)S(1)}, bf16[2,64,2176]{2,1,0:T(8,128)(2,1)S(1)}, u32[]{:S(2)}, u32[]{:S(2)}) collective-permute-start(bf16[2,64,2176]{2,1,0:T(8,128)(2,1)S(1)} %get-tuple-element.13), channel_id=1, source_target_pairs={{0,224},{16,240},{32,0},{48,16},{64,32},{80,48},{96,64},{112,80},{... | collective-permute-start | bytes 1671176 | tf_op jit(solution)/shard_map/ppermute | solution.py:13
  71.9 15.0 %collective-permute-start.8 = (bf16[2,64,2176]{2,1,0:T(8,128)(2,1)S(1)}, bf16[2,64,2176]{2,1,0:T(8,128)(2,1)S(1)}, u32[]{:S(2)}, u32[]{:S(2)}) collective-permute-start(bf16[2,64,2176]{2,1,0:T(8,128)(2,1)S(1)} %get-tuple-element.13), channel_id=1, source_target_pairs={{0,32},{16,48},{32,64},{48,80},{64,96},{80,112},{96,128},{112,144}... | collective-permute-start | bytes 1671176 | tf_op jit(solution)/shard_map/ppermute | solution.py:13
  72.0 25.6 %collective-permute-start.4 = (bf16[128,1024]{1,0:T(8,128)(2,1)S(1)}, bf16[128,1024]{1,0:T(8,128)(2,1)S(1)}, u32[]{:S(2)}, u32[]{:S(2)}) collective-permute-start(bf16[128,1024]{1,0:T(8,128)(2,1)S(1)} %bitcast_select_fusion.7), channel_id=1, source_target_pairs={{0,16},{16,32},{32,48},{48,64},{64,80},{80,96},{96,112},{112,128},... | collective-permute-start | bytes 786440 | tf_op jit(solution)/shard_map/ppermute | solution.py:13
  75.9 27.3 %collective-permute-start.5 = (bf16[128,1024]{1,0:T(8,128)(2,1)S(1)}, bf16[128,1024]{1,0:T(8,128)(2,1)S(1)}, u32[]{:S(2)}, u32[]{:S(2)}) collective-permute-start(bf16[128,1024]{1,0:T(8,128)(2,1)S(1)} %bitcast_select_fusion.4), channel_id=1, source_target_pairs={{0,16},{16,32},{32,48},{48,64},{64,80},{80,96},{96,112},{112,128},... | collective-permute-start | bytes 786440 | tf_op jit(solution)/shard_map/ppermute | solution.py:13
  83.3 19.9 %collective-permute-start.2 = (bf16[2,64,2176]{2,1,0:T(8,128)(2,1)S(1)}, bf16[2,64,2176]{2,1,0:T(8,128)(2,1)S(1)}, u32[]{:S(2)}, u32[]{:S(2)}) collective-permute-start(bf16[2,64,2176]{2,1,0:T(8,128)(2,1)S(1)} %collective-permute-done.1), channel_id=1, source_target_pairs={{0,224},{16,240},{32,0},{48,16},{64,32},{80,48},{96,64},{112,80},{... | collective-permute-start | bytes 1671176 | tf_op jit(solution)/shard_map/ppermute | solution.py:13
  87.0 16.3 %collective-permute-start.9 = (bf16[2,64,2176]{2,1,0:T(8,128)(2,1)S(1)}, bf16[2,64,2176]{2,1,0:T(8,128)(2,1)S(1)}, u32[]{:S(2)}, u32[]{:S(2)}) collective-permute-start(bf16[2,64,2176]{2,1,0:T(8,128)(2,1)S(1)} %collective-permute-done.8), channel_id=1, source_target_pairs={{0,32},{16,48},{32,64},{48,80},{64,96},{80,112},{96,128},{112,144}... | collective-permute-start | bytes 1671176 | tf_op jit(solution)/shard_map/ppermute | solution.py:13
  97.6 33.5 %copy-start.8 = (bf16[128,1024]{1,0:T(8,128)(2,1)}, bf16[128,1024]{1,0:T(8,128)(2,1)S(1)}, u32[]{:S(2)}) copy-start(bf16[128,1024]{1,0:T(8,128)(2,1)S(1)} %collective-permute-done.4) | copy-start | bytes 786436
  103.2 27.8 %copy-start.10 = (bf16[128,1024]{1,0:T(8,128)(2,1)}, bf16[128,1024]{1,0:T(8,128)(2,1)S(1)}, u32[]{:S(2)}) copy-start(bf16[128,1024]{1,0:T(8,128)(2,1)S(1)} %collective-permute-done.5) | copy-start | bytes 786436
  103.2 13.2 %collective-permute-start.6 = (bf16[2,64,2176]{2,1,0:T(8,128)(2,1)S(1)}, bf16[2,64,2176]{2,1,0:T(8,128)(2,1)S(1)}, u32[]{:S(2)}, u32[]{:S(2)}) collective-permute-start(bf16[2,64,2176]{2,1,0:T(8,128)(2,1)S(1)} %collective-permute-done.2), channel_id=1, source_target_pairs={{0,224},{16,240},{32,0},{48,16},{64,32},{80,48},{96,64},{112,80},{... | collective-permute-start | bytes 1671176 | tf_op jit(solution)/shard_map/ppermute | solution.py:13
  103.3 23.5 %collective-permute-start.10 = (bf16[2,64,2176]{2,1,0:T(8,128)(2,1)S(1)}, bf16[2,64,2176]{2,1,0:T(8,128)(2,1)S(1)}, u32[]{:S(2)}, u32[]{:S(2)}) collective-permute-start(bf16[2,64,2176]{2,1,0:T(8,128)(2,1)S(1)} %collective-permute-done.9), channel_id=1, source_target_pairs={{0,32},{16,48},{32,64},{48,80},{64,96},{80,112},{96,128},{112,144}... | collective-permute-start | bytes 1671176 | tf_op jit(solution)/shard_map/ppermute | solution.py:13
  116.4 9.5 %collective-permute-start.7 = (bf16[2,64,2176]{2,1,0:T(8,128)(2,1)S(1)}, bf16[2,64,2176]{2,1,0:T(8,128)(2,1)S(1)}, u32[]{:S(2)}, u32[]{:S(2)}) collective-permute-start(bf16[2,64,2176]{2,1,0:T(8,128)(2,1)S(1)} %collective-permute-done.6), channel_id=1, source_target_pairs={{0,224},{16,240},{32,0},{48,16},{64,32},{80,48},{96,64},{112,80},{... | collective-permute-start | bytes 1671176 | tf_op jit(solution)/shard_map/ppermute | solution.py:13
  162.2 4.2 %collective-permute-start.11 = (bf16[16,32,2048]{2,1,0:T(8,128)(2,1)S(1)}, bf16[16,32,2048]{2,1,0:T(8,128)(2,1)S(1)}, u32[]{:S(2)}, u32[]{:S(2)}) collective-permute-start(bf16[16,32,2048]{2,1,0:T(8,128)(2,1)S(1)} %fusion.5), channel_id=1, source_target_pairs={{0,1},{1,0},{2,3},{3,2},{4,5},{5,4},{6,7},{7,6},{8,9},{9,8},{10,11... | collective-permute-start | bytes 6291464 | tf_op jit(solution)/shard_map/ppermute | solution.py:8
  187.6 7.9 %copy-start.6 = (bf16[1024,2,4,2,128]{0,4,3,1,2:T(8,128)(2,1)S(1)}, bf16[1024,2,4,2,128]{0,4,3,1,2:T(8,128)(2,1)}, u32[]{:S(2)}) copy-start(bf16[1024,2,4,2,128]{0,4,3,1,2:T(8,128)(2,1)} %copy.138) | copy-start | bytes 12582916
  238.1 4.5 %collective-permute-start.14 = (bf16[16,32,2048]{2,1,0:T(8,128)(2,1)}, bf16[16,32,2048]{2,1,0:T(8,128)(2,1)}, u32[]{:S(2)}, u32[]{:S(2)}) collective-permute-start(bf16[16,32,2048]{2,1,0:T(8,128)(2,1)} %squeeze.56), channel_id=1, source_target_pairs={{0,1},{1,0},{2,3},{3,2},{4,5},{5,4},{6,7},{7,6},{8,9},{9,8},{10,11... | collective-permute-start | bytes 6291464 | tf_op jit(solution)/shard_map/ppermute | solution.py:8
  249.1 6.8 %copy-start.12 = (f32[64,8]{0,1:T(8,128)S(1)}, f32[64,8]{0,1:T(8,128)}, u32[]{:S(2)}) copy-start(f32[64,8]{0,1:T(8,128)} %param.9) | copy-start | bytes 6148
  249.1 7.7 %copy-start.3 = (bf16[2,128,1024]{2,1,0:T(8,128)(2,1)S(1)}, bf16[2,128,1024]{2,1,0:T(8,128)(2,1)}, u32[]{:S(2)}) copy-start(bf16[2,128,1024]{2,1,0:T(8,128)(2,1)} %param.15) | copy-start | bytes 1572868
  249.1 7.7 %copy-start.5 = (bf16[2,128,1024]{2,1,0:T(8,128)(2,1)S(1)}, bf16[2,128,1024]{2,1,0:T(8,128)(2,1)}, u32[]{:S(2)}) copy-start(bf16[2,128,1024]{2,1,0:T(8,128)(2,1)} %param.14) | copy-start | bytes 1572868
  249.1 7.7 %copy-start.9 = (bf16[128,1024]{1,0:T(8,128)(2,1)S(1)}, bf16[128,1024]{1,0:T(8,128)(2,1)}, u32[]{:S(2)}) copy-start(bf16[128,1024]{1,0:T(8,128)(2,1)} %copy-done.8) | copy-start | bytes 786436
  249.1 7.7 %copy-start.11 = (bf16[128,1024]{1,0:T(8,128)(2,1)S(1)}, bf16[128,1024]{1,0:T(8,128)(2,1)}, u32[]{:S(2)}) copy-start(bf16[128,1024]{1,0:T(8,128)(2,1)} %copy-done.10) | copy-start | bytes 786436
  249.2 106.3 %all-to-all-start = ((bf16[16,2,32,2048]{3,2,1,0:T(8,128)(2,1)}), bf16[16,2,32,2048]{3,2,1,0:T(8,128)(2,1)}, u32[]{:S(2)}, u32[]{:S(2)}) async-start(bf16[16,2,32,2048]{3,2,1,0:T(8,128)(2,1)} %copy.143), calls=%async_computation | async-start | bytes 8388608 | tf_op jit(solution)/shard_map/all_to_all | solution.py:133
  255.9 2.8 copy-start.1
Sparse Core Ops, SparseCore 0:
  52.5 124.0 all-gather.2

commit v15 on v13

--- a/solution.py
+++ b/solution.py
@@ -43,7 +43,7 @@
     capacity = max(2, 2 * tok_count * top_count // slot_count)
     places = slot_count * capacity
     core = column % 2
-    own = jnp.stack([w_gate, w_up, w_down], axis=1)
+    own = jnp.stack([w_gate, w_up], axis=1)
     across = partner_2(own, "shard", n_shard.bit_length() - 2)
     first_plane = column < half_count
     by_plane = jnp.where(first_plane, jnp.stack([own, across]), jnp.stack([across, own]))
@@ -55,8 +55,20 @@
     )
     groups = [list(range(g % 2 + (g // 2) * half_count, (g // 2 + 1) * half_count, 2)) for g in range(4)]
     ring = lax.all_gather(block, "shard", axis=0, tiled=False, axis_index_groups=groups)
-    full = jnp.transpose(ring, (3, 1, 0, 2, 4, 5)).reshape(3, model_width, -1)
-    full_gate, full_up, full_down = full[0], full[1], full[2]
+    full = jnp.transpose(ring, (3, 1, 0, 2, 4, 5)).reshape(2, model_width, -1)
+    full_gate, full_up = full[0], full[1]
+    down_kept = jnp.where(core == 0, w_down[0], w_down[1])
+    down_received = partner_2(jnp.where(core == 0, w_down[1], w_down[0]), "shard", 0)
+    down_block = jnp.where(
+        core == 0,
+        jnp.stack([down_kept, down_received]),
+        jnp.stack([down_received, down_kept]),
+    )
+    down_plane = lax.all_gather(down_block, "shard", axis=0, tiled=False, axis_index_groups=groups)
+    down_other = partner_2(down_plane, "shard", n_shard.bit_length() - 2)
+    full_down = jnp.where(
+        first_plane, jnp.stack([down_plane, down_other]), jnp.stack([down_other, down_plane])
+    ).reshape(model_width, -1)
     slot_index = jnp.arange(slot_count, dtype=jnp.int32)
     owner_slot = jnp.sum(
         jnp.where(old_place[None, :] == slot_index[:, None], slot_index[None, :], 0), axis=1

time: 335 us -> 376 us (1.12)
  local copies, waits for them, and re-layouts: 40.7 us -> 57.8 us
  waiting for transfers between devices: 193 us -> 208 us
  other arithmetic: 23.8 us -> 34.2 us
    unnamed x32 -> x36, local copies, waits for them, and re-layouts: 12 us -> 28.3 us
    ppermute x10, waiting for transfers between devices: 40.5 us -> 53.8 us  [passed_along(): return lax.ppermute(x, axis, [(i, (i + by) % size) for i in range(size)])]
    ppermute x5 -> x7, waiting for transfers between devices: 49.8 us -> 58.3 us  [partner_2(): lax.ppermute(x, axis, [(i, i ^ 1 << apart) for i in range(lax.axis_size(a...]
    all_gather x1, waiting for transfers between devices: 7.63 us -> 0.01 us  [local(): lax.all_gather(block, 'shard', axis=0, tiled=False, axis_index_groups=gro...]
    all_to_all x1, starting transfers between devices: 9.72 us -> 4.68 us  [local(): lax.all_to_all(pair_halves(upper_half, result[0], returned_other), 'dp',...]
  transfers between devices with their start and end apart: 17 -> 20, of which waited for: 12 -> 13; matrix products, arithmetic and copies ran while one was open for 16% -> 21% of each run, Pallas kernels for 0% -> 0%
where the time goes in v15:
time: 376 us; the launch traced here: 374 us
  waiting for transfers between devices  208 us (55%)
  local copies, waits for them, and re-layouts  57.8 us (15%)
  other arithmetic  34.2 us (9%)
  matrix products  31.4 us (8%)
  starting transfers between devices  27.6 us (7%)
  between operations  15.7 us (4%)
    all_to_all x1, waiting for transfers between devices, local(): lax.all_to_all(pair_halves(upper_half, result[0], returned_other), 'dp',...  95.6 us
    ppermute x7, waiting for transfers between devices, partner_2(): lax.ppermute(x, axis, [(i, i ^ 1 << apart) for i in range(lax.axis_size(a...  58.3 us
    ppermute x10, waiting for transfers between devices, passed_along(): return lax.ppermute(x, axis, [(i, (i + by) % size) for i in range(size)])  53.8 us
    unnamed x36, local copies, waits for them, and re-layouts  28.3 us
    ppermute x10, starting transfers between devices, passed_along(): return lax.ppermute(x, axis, [(i, (i + by) % size) for i in range(size)])  17.2 us
    dot_general x1, matrix products, local(): lax.dot_general(hidden, full_down, (((1,), (1,)), ((), ())), preferred_el...  15.1 us
    dynamic_slice x2, local copies, waits for them, and re-layouts, local(): jnp.roll(by_offset, row_id // 2, axis=0).reshape(n_rows, tok_count, -1)  14 us
  transfers between devices with their start and end apart: 20, of which 13 were waited for; matrix products, arithmetic and copies ran while one was open for 21% of the time, Pallas kernels for 0%

profile of v15, /device:TPU:8, one launch (start us, length us, event | category | flops | bytes accessed | tf_op | source)
XLA Modules:
  0.0 374.5 jit_solution(1833186640101348683)
XLA Ops:
  12.1 3.1 collective-permute-start
  15.2 6.9 %collective-permute-done = bf16[64,2176]{1,0:T(8,128)(2,1)S(1)} collective-permute-done((bf16[64,2176]{1,0:T(8,128)(2,1)S(1)}, bf16[64,2176]{1,0:T(8,128)(2,1)S(1)}, u32[]{:S(2)}, u32[]{:S(2)}) %collective-permute-start) | collective-permute-done | bytes 278560 | tf_op jit(solution)/shard_map/ppermute | solution.py:8
  23.0 5.9 %collective-permute-start.1 = (bf16[2,64,2176]{2,1,0:T(8,128)(2,1)S(1)}, bf16[2,64,2176]{2,1,0:T(8,128)(2,1)S(1)}, u32[]{:S(2)}, u32[]{:S(2)}) collective-permute-start(bf16[2,64,2176]{2,1,0:T(8,128)(2,1)S(1)} %get-tuple-element.13), channel_id=1, source_target_pairs={{0,224},{16,240},{32,0},{48,16},{64,32},{80,48},{96,64},{112,80},{... | collective-permute-start | bytes 1671176 | tf_op jit(solution)/shard_map/ppermute | solution.py:13
  32.7 3.1 collective-permute-start.3
  35.8 4.1 %collective-permute-done.1 = bf16[2,64,2176]{2,1,0:T(8,128)(2,1)S(1)} collective-permute-done((bf16[2,64,2176]{2,1,0:T(8,128)(2,1)S(1)}, bf16[2,64,2176]{2,1,0:T(8,128)(2,1)S(1)}, u32[]{:S(2)}, u32[]{:S(2)}) %collective-permute-start.1) | collective-permute-done | bytes 557088 | tf_op jit(solution)/shard_map/ppermute | solution.py:13
  39.9 3.7 collective-permute-start.2
  44.3 3.0 collective-permute-start.4
  48.1 9.1 %collective-permute-done.4 = bf16[128,1024]{1,0:T(8,128)(2,1)} collective-permute-done((bf16[128,1024]{1,0:T(8,128)(2,1)}, bf16[128,1024]{1,0:T(8,128)(2,1)}, u32[]{:S(2)}, u32[]{:S(2)}) %collective-permute-start.4) | collective-permute-done | bytes 262176 | tf_op jit(solution)/shard_map/ppermute | solution.py:13
  57.2 3.0 collective-permute-done.5
  60.8 1.7 fusion.8
  65.9 15.0 %collective-permute-done.8 = bf16[2,64,2176]{2,1,0:T(8,128)(2,1)} collective-permute-done((bf16[2,64,2176]{2,1,0:T(8,128)(2,1)S(1)}, bf16[2,64,2176]{2,1,0:T(8,128)(2,1)}, u32[]{:S(2)}, u32[]{:S(2)}) %collective-permute-start.8) | collective-permute-done | bytes 557088 | tf_op jit(solution)/shard_map/ppermute | solution.py:13
  80.9 1.9 bitcast_dynamic-update-slice_fusion.12
  82.8 6.7 %collective-permute-done.12 = bf16[2,2,128,1024]{3,2,1,0:T(8,128)(2,1)} collective-permute-done((bf16[2,2,128,1024]{3,2,1,0:T(8,128)(2,1)}, bf16[2,2,128,1024]{3,2,1,0:T(8,128)(2,1)}, u32[]{:S(2)}, u32[]{:S(2)}) %collective-permute-start.12) | collective-permute-done | bytes 1048608 | tf_op jit(solution)/shard_map/ppermute | solution.py:8
  89.6 1.9 maximum_select_fusion.2
  91.8 1.9 bitcast_dynamic-update-slice_fusion.10
  93.7 2.7 collective-permute-done.9
  96.4 10.6 %collective-permute-done.6 = bf16[2,64,2176]{2,1,0:T(8,128)(2,1)} collective-permute-done((bf16[2,64,2176]{2,1,0:T(8,128)(2,1)}, bf16[2,64,2176]{2,1,0:T(8,128)(2,1)}, u32[]{:S(2)}, u32[]{:S(2)}) %collective-permute-start.6) | collective-permute-done | bytes 557088 | tf_op jit(solution)/shard_map/ppermute | solution.py:13
  108.5 2.0 bitcast_dynamic-update-slice_fusion.8
  110.5 1.7 maximum_select_fusion.3
  112.2 9.4 %collective-permute-done.7 = bf16[2,64,2176]{2,1,0:T(8,128)(2,1)} collective-permute-done((bf16[2,64,2176]{2,1,0:T(8,128)(2,1)}, bf16[2,64,2176]{2,1,0:T(8,128)(2,1)}, u32[]{:S(2)}, u32[]{:S(2)}) %collective-permute-start.7) | collective-permute-done | bytes 557088 | tf_op jit(solution)/shard_map/ppermute | solution.py:13
  121.5 2.0 bitcast_dynamic-update-slice_fusion.6
  123.5 1.9 bitcast_dynamic-update-slice_fusion.4
  125.5 1.9 bitcast_dynamic-update-slice_fusion.2
  127.4 1.9 bitcast_dynamic-update-slice_fusion
  131.0 1.9 bitcast_dynamic-update-slice_fusion.11
  132.9 1.9 bitcast_dynamic-update-slice_fusion.9
  134.8 1.9 bitcast_dynamic-update-slice_fusion.7
  136.8 1.9 bitcast_dynamic-update-slice_fusion.5
  138.6 2.0 bitcast_dynamic-update-slice_fusion.3
  140.6 1.9 bitcast_dynamic-update-slice_fusion.1
  142.5 4.7 %constant_dynamic-slice_fusion = bf16[8,2,64,2176]{3,2,1,0:T(8,128)(2,1)} fusion(bf16[16,2,64,2176]{3,2,1,0:T(8,128)(2,1)} %bitcast_dynamic-update-slice_fusion.1, s32[]{:T(128)S(6)} %select_n.220), kind=kLoop, calls=%fused_computation.86 | loop fusion | bytes 8912900 | tf_op jit(solution)/shard_map/jit(_roll_dynamic)/dynamic_slice | solution.py:110
  147.2 9.3 %copy.108 = bf16[8,2,64,2176]{2,3,1,0:T(8,128)(2,1)} copy(bf16[8,2,64,2176]{3,2,1,0:T(8,128)(2,1)} %constant_dynamic-slice_fusion) | data formatting | bytes 8912896 | tf_op jit(solution)/shard_map/jit(_roll_dynamic)/dynamic_slice | solution.py:110
  157.6 2.3 reduce-window.16
  161.9 6.5 %fusion.3 = bf16[16,2,32,2048]{3,2,1,0:T(8,128)(2,1)S(1)} fusion(pred[16,64,2,32]{1,3,2,0:T(8,128)(4,1)S(1)} %fusion.2, bf16[16,64,2176]{1,2,0:T(8,128)(2,1)} %bitcast.166), kind=kOutput, calls=%fused_computation.10 | convolution fusion | flops 270532608 | bytes 12648448 | tf_op jit(solution)/shard_map/stcr,std->scrd/dot_general | solution.py:123
  168.4 2.0 copy-done
  173.0 2.5 fusion.5
  176.4 4.1 %pad_maximum_fusion = bf16[2,16,32,2048]{3,2,1,0:T(8,128)(2,1)} fusion(bf16[1,16,32,2048]{3,2,1,0:T(8,128)(2,1)} %bitcast.30, bf16[1,16,32,2048]{3,2,1,0:T(8,128)(2,1)S(1)} %fusion.5), kind=kLoop, calls=%fused_computation.2 | loop fusion | flops 2097152 | bytes 8388608 | tf_op jit(solution)/shard_map/stack | solution.py:132
  180.5 39.7 %collective-permute-done.15 = bf16[4,2,128,1024]{3,2,1,0:T(8,128)(2,1)S(1)} collective-permute-done((bf16[4,2,128,1024]{3,2,1,0:T(8,128)(2,1)}, bf16[4,2,128,1024]{3,2,1,0:T(8,128)(2,1)S(1)}, u32[]{:S(2)}, u32[]{:S(2)}) %collective-permute-start.15) | collective-permute-done | bytes 2097184 | tf_op jit(solution)/shard_map/ppermute | solution.py:8
  220.2 2.4 maximum_select_fusion
  222.5 5.4 %fusion.22 = (bf16[1,2,4,2,128,1024]{5,4,3,2,1,0:T(8,128)(2,1)}, bf16[1,2,4,2,128,1024]{5,4,3,2,1,0:T(8,128)(2,1)S(1)}) fusion(bf16[2,2,4,2,128,1024]{5,4,3,2,1,0:T(8,128)(2,1)} %bitcast.167), kind=kLoop, calls=%fused_computation.89 | loop fusion | bytes 16777216 | tf_op jit(solution)/shard_map/slice | solution.py:59
  228.7 6.0 %fusion.25 = f32[1024,1024]{1,0:T(8,128)} fusion(bf16[1024,2048]{1,0:T(8,128)(2,1)S(1)} %bitcast.172, bf16[2048,1024]{1,0:T(8,128)(2,1)S(1)} %bitcast.175), kind=kOutput, calls=%fused_computation.92 | convolution fusion | flops 4294967296 | bytes 12582912 | tf_op jit(solution)/shard_map/dot_general | solution.py:134
  234.7 15.1 %convolution_convert_fusion = bf16[1024,2048]{1,0:T(8,128)(2,1)} fusion(bf16[2048,1024]{1,0:T(8,128)(2,1)} %bitcast.173, f32[1024,1024]{1,0:T(8,128)} %fusion.25, bf16[1024,2048]{1,0:T(8,128)(2,1)} %bitcast.171, bf16[2048,1024]{1,0:T(8,128)(2,1)} %bitcast.174), kind=kOutput, calls=%fused_computation.11 | convolution fusion | flops 8598323200 | bytes 20971520 | tf_op jit(solution)/shard_map/dot_general | solution.py:137
  249.8 2.7 fusion.23
  252.7 4.1 %collective-permute-done.16 = bf16[16,32,2048]{2,1,0:T(8,128)(2,1)S(1)} collective-permute-done((bf16[16,32,2048]{2,1,0:T(8,128)(2,1)S(1)}, bf16[16,32,2048]{2,1,0:T(8,128)(2,1)S(1)}, u32[]{:S(2)}, u32[]{:S(2)}) %collective-permute-start.16) | collective-permute-done | bytes 2097184 | tf_op jit(solution)/shard_map/ppermute | solution.py:8
  256.8 2.2 maximum_select_fusion.1
  259.0 4.7 %all-to-all-start = ((bf16[16,2,32,2048]{3,2,1,0:T(8,128)(2,1)}), bf16[16,2,32,2048]{3,2,1,0:T(8,128)(2,1)}, u32[]{:S(2)}, u32[]{:S(2)}) async-start(bf16[16,2,32,2048]{3,2,1,0:T(8,128)(2,1)} %maximum_select_fusion.1), calls=%async_computation | async-start | bytes 8388608 | tf_op jit(solution)/shard_map/all_to_all | solution.py:142
  268.3 95.6 %all-to-all-done = bf16[16,2,32,2048]{3,2,1,0:T(8,128)(2,1)} async-done(((bf16[16,2,32,2048]{3,2,1,0:T(8,128)(2,1)}), bf16[16,2,32,2048]{3,2,1,0:T(8,128)(2,1)}, u32[]{:S(2)}, u32[]{:S(2)}) %all-to-all-start) | async-done | bytes 4194336 | tf_op jit(solution)/shard_map/all_to_all | solution.py:142
  363.9 3.7 convolution_convert_fusion.1
  (101 shorter events, 29.4 us)
Async XLA Ops:
  7.2 25.5 %copy-start.3 = (bf16[2,128,1024]{2,1,0:T(8,128)(2,1)S(1)}, bf16[2,128,1024]{2,1,0:T(8,128)(2,1)}, u32[]{:S(2)}) copy-start(bf16[2,128,1024]{2,1,0:T(8,128)(2,1)} %param.13) | copy-start | bytes 1572868
  7.2 36.4 %copy-start.2 = (bf16[2,128,1024]{2,1,0:T(8,128)(2,1)S(1)}, bf16[2,128,1024]{2,1,0:T(8,128)(2,1)}, u32[]{:S(2)}) copy-start(bf16[2,128,1024]{2,1,0:T(8,128)(2,1)} %param.14) | copy-start | bytes 1572868
  7.2 40.2 %copy-start.1 = (bf16[2,128,1024]{2,1,0:T(8,128)(2,1)S(1)}, bf16[2,128,1024]{2,1,0:T(8,128)(2,1)}, u32[]{:S(2)}) copy-start(bf16[2,128,1024]{2,1,0:T(8,128)(2,1)} %param.15) | copy-start | bytes 1572868
  7.2 164.7 %all-gather.5.cloned.1.call-start = ((), (), s32[]{:S(2)}) async-start(), calls=%async_computation.2 | async-start | bytes 2621440 | tf_op jit(solution)/shard_map/all_gather | solution.py:67
  12.1 10.0 %collective-permute-start = (bf16[64,2176]{1,0:T(8,128)(2,1)S(1)}, bf16[64,2176]{1,0:T(8,128)(2,1)S(1)}, u32[]{:S(2)}, u32[]{:S(2)}) collective-permute-start(bf16[64,2176]{1,0:T(8,128)(2,1)S(1)} %concatenate.36), channel_id=1, source_target_pairs={{0,16},{16,0},{32,48},{48,32},{64,80},{80,64},{96,112},{112,96},{1... | collective-permute-start | bytes 835592 | tf_op jit(solution)/shard_map/ppermute | solution.py:8
  23.0 16.9 %collective-permute-start.1 = (bf16[2,64,2176]{2,1,0:T(8,128)(2,1)S(1)}, bf16[2,64,2176]{2,1,0:T(8,128)(2,1)S(1)}, u32[]{:S(2)}, u32[]{:S(2)}) collective-permute-start(bf16[2,64,2176]{2,1,0:T(8,128)(2,1)S(1)} %get-tuple-element.13), channel_id=1, source_target_pairs={{0,224},{16,240},{32,0},{48,16},{64,32},{80,48},{96,64},{112,80},{... | collective-permute-start | bytes 1671176 | tf_op jit(solution)/shard_map/ppermute | solution.py:13
  32.7 15.4 %collective-permute-start.3 = (bf16[128,1024]{1,0:T(8,128)(2,1)S(1)}, bf16[128,1024]{1,0:T(8,128)(2,1)}, u32[]{:S(2)}, u32[]{:S(2)}) collective-permute-start(bf16[128,1024]{1,0:T(8,128)(2,1)S(1)} %bitcast_select_fusion.10), channel_id=1, source_target_pairs={{0,16},{16,32},{32,48},{48,64},{64,80},{80,96},{96,112},{112,128},... | collective-permute-start | bytes 786440 | tf_op jit(solution)/shard_map/ppermute | solution.py:13
  39.9 22.7 %copy-start.5 = (bf16[2,64,2176]{2,1,0:T(8,128)(2,1)}, bf16[2,64,2176]{2,1,0:T(8,128)(2,1)S(1)}, u32[]{:S(2)}) copy-start(bf16[2,64,2176]{2,1,0:T(8,128)(2,1)S(1)} %collective-permute-done.1) | copy-start | bytes 1671172
  39.9 20.9 %collective-permute-start.2 = (bf16[2,64,2176]{2,1,0:T(8,128)(2,1)S(1)}, bf16[2,64,2176]{2,1,0:T(8,128)(2,1)}, u32[]{:S(2)}, u32[]{:S(2)}) collective-permute-start(bf16[2,64,2176]{2,1,0:T(8,128)(2,1)S(1)} %collective-permute-done.1), channel_id=1, source_target_pairs={{0,224},{16,240},{32,0},{48,16},{64,32},{80,48},{96,64},{112,80},{... | collective-permute-start | bytes 1671176 | tf_op jit(solution)/shard_map/ppermute | solution.py:13
  44.3 12.8 %collective-permute-start.4 = (bf16[128,1024]{1,0:T(8,128)(2,1)}, bf16[128,1024]{1,0:T(8,128)(2,1)}, u32[]{:S(2)}, u32[]{:S(2)}) collective-permute-start(bf16[128,1024]{1,0:T(8,128)(2,1)} %bitcast_select_fusion.7), channel_id=1, source_target_pairs={{0,16},{16,32},{32,48},{48,64},{64,80},{80,96},{96,112},{112,128},... | collective-permute-start | bytes 786440 | tf_op jit(solution)/shard_map/ppermute | solution.py:13
  48.1 12.1 %collective-permute-start.5 = (bf16[128,1024]{1,0:T(8,128)(2,1)}, bf16[128,1024]{1,0:T(8,128)(2,1)S(1)}, u32[]{:S(2)}, u32[]{:S(2)}) collective-permute-start(bf16[128,1024]{1,0:T(8,128)(2,1)} %bitcast_select_fusion.4), channel_id=1, source_target_pairs={{0,16},{16,32},{32,48},{48,64},{64,80},{80,96},{96,112},{112,128},... | collective-permute-start | bytes 786440 | tf_op jit(solution)/shard_map/ppermute | solution.py:13
  60.1 0.7 copy-start.9
  62.6 2.3 collective-permute-start.14
  63.7 25.9 %collective-permute-start.12 = (bf16[2,2,128,1024]{3,2,1,0:T(8,128)(2,1)}, bf16[2,2,128,1024]{3,2,1,0:T(8,128)(2,1)}, u32[]{:S(2)}, u32[]{:S(2)}) collective-permute-start(bf16[2,2,128,1024]{3,2,1,0:T(8,128)(2,1)} %get-tuple-element.21), channel_id=1, source_target_pairs={{0,8},{1,9},{2,10},{3,11},{4,12},{5,13},{6,14},{7,15},{8,0},{9,1},... | collective-permute-start | bytes 3145736 | tf_op jit(solution)/shard_map/ppermute | solution.py:8
  64.9 16.1 %collective-permute-start.8 = (bf16[2,64,2176]{2,1,0:T(8,128)(2,1)S(1)}, bf16[2,64,2176]{2,1,0:T(8,128)(2,1)}, u32[]{:S(2)}, u32[]{:S(2)}) collective-permute-start(bf16[2,64,2176]{2,1,0:T(8,128)(2,1)S(1)} %get-tuple-element.13), channel_id=1, source_target_pairs={{0,32},{16,48},{32,64},{48,80},{64,96},{80,112},{96,128},{112,144}... | collective-permute-start | bytes 1671176 | tf_op jit(solution)/shard_map/ppermute | solution.py:13
  65.8 156.7 %all-gather.3.cloned.1.call-start = ((), (), s32[]{:S(2)}) async-start(), calls=%async_computation.1 | async-start | bytes 10485760 | tf_op jit(solution)/shard_map/all_gather | solution.py:57
  80.9 15.5 %collective-permute-start.9 = (bf16[2,64,2176]{2,1,0:T(8,128)(2,1)}, bf16[2,64,2176]{2,1,0:T(8,128)(2,1)}, u32[]{:S(2)}, u32[]{:S(2)}) collective-permute-start(bf16[2,64,2176]{2,1,0:T(8,128)(2,1)} %collective-permute-done.8), channel_id=1, source_target_pairs={{0,32},{16,48},{32,64},{48,80},{64,96},{80,112},{96,128},{112,144}... | collective-permute-start | bytes 1671176 | tf_op jit(solution)/shard_map/ppermute | solution.py:13
  91.6 18.9 %collective-permute-start.13 = (bf16[2,2,128,1024]{3,2,0,1:T(8,128)(2,1)S(1)}, bf16[2,2,128,1024]{3,2,0,1:T(8,128)(2,1)S(1)}, u32[]{:S(2)}, u32[]{:S(2)}) collective-permute-start(bf16[2,2,128,1024]{3,2,0,1:T(8,128)(2,1)S(1)} %get-tuple-element.19), channel_id=1, source_target_pairs={{0,1},{1,0},{2,3},{3,2},{4,5},{5,4},{6,7},{7,6},{8,9},{9,8},{10,11... | collective-permute-start | bytes 3145736 | tf_op jit(solution)/shard_map/ppermute | solution.py:8
  91.7 15.4 %collective-permute-start.6 = (bf16[2,64,2176]{2,1,0:T(8,128)(2,1)}, bf16[2,64,2176]{2,1,0:T(8,128)(2,1)}, u32[]{:S(2)}, u32[]{:S(2)}) collective-permute-start(bf16[2,64,2176]{2,1,0:T(8,128)(2,1)} %collective-permute-done.2), channel_id=1, source_target_pairs={{0,224},{16,240},{32,0},{48,16},{64,32},{80,48},{96,64},{112,80},{... | collective-permute-start | bytes 1671176 | tf_op jit(solution)/shard_map/ppermute | solution.py:13
  96.4 27.1 %collective-permute-start.10 = (bf16[2,64,2176]{2,1,0:T(8,128)(2,1)}, bf16[2,64,2176]{2,1,0:T(8,128)(2,1)}, u32[]{:S(2)}, u32[]{:S(2)}) collective-permute-start(bf16[2,64,2176]{2,1,0:T(8,128)(2,1)} %collective-permute-done.9), channel_id=1, source_target_pairs={{0,32},{16,48},{32,64},{48,80},{64,96},{80,112},{96,128},{112,144}... | collective-permute-start | bytes 1671176 | tf_op jit(solution)/shard_map/ppermute | solution.py:13
  107.0 14.5 %collective-permute-start.7 = (bf16[2,64,2176]{2,1,0:T(8,128)(2,1)}, bf16[2,64,2176]{2,1,0:T(8,128)(2,1)}, u32[]{:S(2)}, u32[]{:S(2)}) collective-permute-start(bf16[2,64,2176]{2,1,0:T(8,128)(2,1)} %collective-permute-done.6), channel_id=1, source_target_pairs={{0,224},{16,240},{32,0},{48,16},{64,32},{80,48},{96,64},{112,80},{... | collective-permute-start | bytes 1671176 | tf_op jit(solution)/shard_map/ppermute | solution.py:13
  112.1 18.0 %copy-start.6 = (bf16[2,64,2176]{2,1,0:T(8,128)(2,1)S(1)}, bf16[2,64,2176]{2,1,0:T(8,128)(2,1)}, u32[]{:S(2)}) copy-start(bf16[2,64,2176]{2,1,0:T(8,128)(2,1)} %copy-done.5) | copy-start | bytes 1671172
  168.4 2.0 copy-start
  171.9 4.5 %collective-permute-start.11 = (bf16[16,32,2048]{2,1,0:T(8,128)(2,1)}, bf16[16,32,2048]{2,1,0:T(8,128)(2,1)}, u32[]{:S(2)}, u32[]{:S(2)}) collective-permute-start(bf16[16,32,2048]{2,1,0:T(8,128)(2,1)} %fusion.4), channel_id=1, source_target_pairs={{0,1},{1,0},{2,3},{3,2},{4,5},{5,4},{6,7},{7,6},{8,9},{9,8},{10,11... | collective-permute-start | bytes 6291464 | tf_op jit(solution)/shard_map/ppermute | solution.py:8
  171.9 48.3 %collective-permute-start.15 = (bf16[4,2,128,1024]{3,2,1,0:T(8,128)(2,1)}, bf16[4,2,128,1024]{3,2,1,0:T(8,128)(2,1)S(1)}, u32[]{:S(2)}, u32[]{:S(2)}) collective-permute-start(bf16[4,2,128,1024]{3,2,1,0:T(8,128)(2,1)} %all-gather.5.cloned.1.call-done), channel_id=1, source_target_pairs={{0,8},{1,9},{2,10},{3,11},{4,12},{5,13},{6,14},{7,15},{8,0},{9,1},... | collective-permute-start | bytes 6291464 | tf_op jit(solution)/shard_map/ppermute | solution.py:8
  176.4 43.8 %copy-start.7 = (bf16[4,2,128,1024]{3,2,1,0:T(8,128)(2,1)S(1)}, bf16[4,2,128,1024]{3,2,1,0:T(8,128)(2,1)}, u32[]{:S(2)}) copy-start(bf16[4,2,128,1024]{3,2,1,0:T(8,128)(2,1)} %all-gather.5.cloned.1.call-done) | copy-start | bytes 6291460
  222.5 6.2 %copy-start.4 = (bf16[2,16,32,2048]{3,2,1,0:T(8,128)(2,1)S(1)}, bf16[2,16,32,2048]{3,2,1,0:T(8,128)(2,1)}, u32[]{:S(2)}) copy-start(bf16[2,16,32,2048]{3,2,1,0:T(8,128)(2,1)} %pad_maximum_fusion) | copy-start | bytes 12582916
  252.6 4.2 %collective-permute-start.16 = (bf16[16,32,2048]{2,1,0:T(8,128)(2,1)S(1)}, bf16[16,32,2048]{2,1,0:T(8,128)(2,1)S(1)}, u32[]{:S(2)}, u32[]{:S(2)}) collective-permute-start(bf16[16,32,2048]{2,1,0:T(8,128)(2,1)S(1)} %bitcast.182), channel_id=1, source_target_pairs={{0,1},{1,0},{2,3},{3,2},{4,5},{5,4},{6,7},{7,6},{8,9},{9,8},{10,11... | collective-permute-start | bytes 6291464 | tf_op jit(solution)/shard_map/ppermute | solution.py:8
  259.0 4.8 %copy-start.10 = (f32[64,8]{0,1:T(8,128)S(1)}, f32[64,8]{0,1:T(8,128)}, u32[]{:S(2)}) copy-start(f32[64,8]{0,1:T(8,128)} %param.9) | copy-start | bytes 6148
  259.0 104.9 %all-to-all-start = ((bf16[16,2,32,2048]{3,2,1,0:T(8,128)(2,1)}), bf16[16,2,32,2048]{3,2,1,0:T(8,128)(2,1)}, u32[]{:S(2)}, u32[]{:S(2)}) async-start(bf16[16,2,32,2048]{3,2,1,0:T(8,128)(2,1)} %maximum_select_fusion.1), calls=%async_computation | async-start | bytes 8388608 | tf_op jit(solution)/shard_map/all_to_all | solution.py:142
  263.7 3.8 %copy-start.8 = (bf16[1,128,1024]{2,1,0:T(8,128)(2,1)S(1)}, bf16[1,128,1024]{2,1,0:T(8,128)(2,1)}, u32[]{:S(2)}) copy-start(bf16[1,128,1024]{2,1,0:T(8,128)(2,1)} %get-tuple-element.23) | copy-start | bytes 786436
Sparse Core Ops, SparseCore 0:
  65.9 29.1 all-gather.4
  112.3 81.3 all-gather.2

commit v16 on v13

--- a/solution.py
+++ b/solution.py
@@ -54,9 +54,12 @@
         core == 0, jnp.stack([kept, received], axis=1), jnp.stack([received, kept], axis=1)
     )
     groups = [list(range(g % 2 + (g // 2) * half_count, (g // 2 + 1) * half_count, 2)) for g in range(4)]
-    ring = lax.all_gather(block, "shard", axis=0, tiled=False, axis_index_groups=groups)
-    full = jnp.transpose(ring, (3, 1, 0, 2, 4, 5)).reshape(3, model_width, -1)
-    full_gate, full_up, full_down = full[0], full[1], full[2]
+    ring = lax.all_gather(block[:, :, :2], "shard", axis=0, tiled=False, axis_index_groups=groups)
+    full = jnp.transpose(ring, (3, 1, 0, 2, 4, 5)).reshape(2, model_width, -1)
+    full_gate, full_up = full[0], full[1]
+    down_block, full_gate, full_up = lax.optimization_barrier((block[:, :, 2], full_gate, full_up))
+    ring = lax.all_gather(down_block, "shard", axis=0, tiled=False, axis_index_groups=groups)
+    full_down = jnp.transpose(ring, (1, 0, 2, 3, 4)).reshape(model_width, -1)
     slot_index = jnp.arange(slot_count, dtype=jnp.int32)
     owner_slot = jnp.sum(
         jnp.where(old_place[None, :] == slot_index[:, None], slot_index[None, :], 0), axis=1

time: 335 us -> 359 us (1.072)
  local copies, waits for them, and re-layouts: 40.7 us -> 59.7 us
  other arithmetic: 23.8 us -> 31.1 us
  waiting for transfers between devices: 193 us -> 189 us
    unnamed x32 -> x34, local copies, waits for them, and re-layouts: 12 us -> 20.7 us
    transpose x0 -> x1, local copies, waits for them, and re-layouts: none -> 4.75 us  [local(): full_down = jnp.transpose(ring, (1, 0, 2, 3, 4)).reshape(model_width, -1)]
    slice x2 -> x5, local copies, waits for them, and re-layouts: 8.07 us -> 10.6 us  [the longest x3 8.76 us: local(): full_gate, full_up = (full[0], full[1])]
    all_gather x1 -> x2, waiting for transfers between devices: 7.63 us -> 9.76 us  [the longest x1 9.03 us: local(): lax.all_gather(down_block, 'shard', axis=0, tiled=False, axis_index_group...]
  transfers between devices with their start and end apart: 17 -> 18, of which waited for: 12 -> 13; matrix products, arithmetic and copies ran while one was open for 16% -> 19% of each run, Pallas kernels for 0% -> 0%
where the time goes in v16:
time: 359 us; the launch traced here: 358 us
  waiting for transfers between devices  189 us (53%)
  local copies, waits for them, and re-layouts  59.7 us (17%)
  matrix products  31.4 us (9%)
  other arithmetic  31.1 us (9%)
  starting transfers between devices  30.8 us (9%)
  between operations  15.6 us (4%)
    all_to_all x1, waiting for transfers between devices, local(): lax.all_to_all(pair_halves(upper_half, result[0], returned_other), 'dp',...  93.9 us
    ppermute x5, waiting for transfers between devices, partner_2(): lax.ppermute(x, axis, [(i, i ^ 1 << apart) for i in range(lax.axis_size(a...  47.2 us
    ppermute x10, waiting for transfers between devices, passed_along(): return lax.ppermute(x, axis, [(i, (i + by) % size) for i in range(size)])  38.1 us
    unnamed x34, local copies, waits for them, and re-layouts  20.7 us
    ppermute x10, starting transfers between devices, passed_along(): return lax.ppermute(x, axis, [(i, (i + by) % size) for i in range(size)])  16 us
    dot_general x1, matrix products, local(): lax.dot_general(hidden, full_down, (((1,), (1,)), ((), ())), preferred_el...  15.2 us
    dynamic_slice x2, local copies, waits for them, and re-layouts, local(): jnp.roll(by_offset, row_id // 2, axis=0).reshape(n_rows, tok_count, -1)  13.9 us
    all_to_all x1, starting transfers between devices, local(): lax.all_to_all(pair_halves(upper_half, result[0], returned_other), 'dp',...  9.71 us
  transfers between devices with their start and end apart: 18, of which 13 were waited for; matrix products, arithmetic and copies ran while one was open for 19% of the time, Pallas kernels for 0%

profile of v16, /device:TPU:8, one launch (start us, length us, event | category | flops | bytes accessed | tf_op | source)
XLA Modules:
  0.0 357.6 jit_solution(4717599859157991466)
XLA Ops:
  7.2 2.7 fusion.21
  9.9 1.5 collective-permute-start.12
  11.4 34.6 %collective-permute-done.12 = bf16[2,3,128,1024]{3,2,1,0:T(8,128)(2,1)S(1)} collective-permute-done((bf16[2,3,128,1024]{3,2,1,0:T(8,128)(2,1)S(1)}, bf16[2,3,128,1024]{3,2,1,0:T(8,128)(2,1)S(1)}, u32[]{:S(2)}, u32[]{:S(2)}) %collective-permute-start.12) | collective-permute-done | bytes 1572896 | tf_op jit(solution)/shard_map/ppermute | solution.py:8
  46.1 1.2 copy-done.5
  47.2 3.4 maximum_select_fusion.1
  50.6 1.3 select_bitcast_fusion
  52.5 1.2 reduce-window.14
  53.8 1.9 collective-permute-done.13
  55.7 2.4 maximum_select_fusion.2
  58.1 1.6 slice.112
  61.5 3.1 collective-permute-start
  67.1 1.8 bitcast_select_fusion.10
  69.4 2.5 collective-permute-done
  74.1 5.9 %collective-permute-start.1 = (bf16[2,64,2176]{2,1,0:T(8,128)(2,1)}, bf16[2,64,2176]{2,1,0:T(8,128)(2,1)}, u32[]{:S(2)}, u32[]{:S(2)}) collective-permute-start(bf16[2,64,2176]{2,1,0:T(8,128)(2,1)} %get-tuple-element.19), channel_id=1, source_target_pairs={{0,224},{16,240},{32,0},{48,16},{64,32},{80,48},{96,64},{112,80},{... | collective-permute-start | bytes 1671176 | tf_op jit(solution)/shard_map/ppermute | solution.py:13
  81.1 3.9 %collective-permute-start.4 = (bf16[128,1024]{1,0:T(8,128)(2,1)S(1)}, bf16[128,1024]{1,0:T(8,128)(2,1)}, u32[]{:S(2)}, u32[]{:S(2)}) collective-permute-start(bf16[128,1024]{1,0:T(8,128)(2,1)S(1)} %bitcast_select_fusion.7), channel_id=1, source_target_pairs={{0,16},{16,32},{32,48},{48,64},{64,80},{80,96},{96,112},{112,128},... | collective-permute-start | bytes 786440 | tf_op jit(solution)/shard_map/ppermute | solution.py:13
  85.0 1.8 bitcast_select_fusion.4
  86.7 4.9 %collective-permute-done.1 = bf16[2,64,2176]{2,1,0:T(8,128)(2,1)} collective-permute-done((bf16[2,64,2176]{2,1,0:T(8,128)(2,1)}, bf16[2,64,2176]{2,1,0:T(8,128)(2,1)}, u32[]{:S(2)}, u32[]{:S(2)}) %collective-permute-start.1) | collective-permute-done | bytes 557088 | tf_op jit(solution)/shard_map/ppermute | solution.py:13
  91.6 3.7 %collective-permute-start.2 = (bf16[2,64,2176]{2,1,0:T(8,128)(2,1)}, bf16[2,64,2176]{2,1,0:T(8,128)(2,1)S(1)}, u32[]{:S(2)}, u32[]{:S(2)}) collective-permute-start(bf16[2,64,2176]{2,1,0:T(8,128)(2,1)} %collective-permute-done.1), channel_id=1, source_target_pairs={{0,224},{16,240},{32,0},{48,16},{64,32},{80,48},{96,64},{112,80},{... | collective-permute-start | bytes 1671176 | tf_op jit(solution)/shard_map/ppermute | solution.py:13
  95.3 1.9 bitcast_dynamic-update-slice_fusion.12
  97.2 8.7 %collective-permute-done.4 = bf16[128,1024]{1,0:T(8,128)(2,1)} collective-permute-done((bf16[128,1024]{1,0:T(8,128)(2,1)S(1)}, bf16[128,1024]{1,0:T(8,128)(2,1)}, u32[]{:S(2)}, u32[]{:S(2)}) %collective-permute-start.4) | collective-permute-done | bytes 262176 | tf_op jit(solution)/shard_map/ppermute | solution.py:13
  105.9 5.6 %collective-permute-done.5 = bf16[128,1024]{1,0:T(8,128)(2,1)} collective-permute-done((bf16[128,1024]{1,0:T(8,128)(2,1)}, bf16[128,1024]{1,0:T(8,128)(2,1)}, u32[]{:S(2)}, u32[]{:S(2)}) %collective-permute-start.5) | collective-permute-done | bytes 262176 | tf_op jit(solution)/shard_map/ppermute | solution.py:13
  111.6 2.0 collective-permute-start.10
  114.5 10.2 %collective-permute-done.6 = bf16[2,64,2176]{2,1,0:T(8,128)(2,1)S(1)} collective-permute-done((bf16[2,64,2176]{2,1,0:T(8,128)(2,1)S(1)}, bf16[2,64,2176]{2,1,0:T(8,128)(2,1)S(1)}, u32[]{:S(2)}, u32[]{:S(2)}) %collective-permute-start.6) | collective-permute-done | bytes 557088 | tf_op jit(solution)/shard_map/ppermute | solution.py:13
  125.5 8.7 %collective-permute-done.7 = bf16[2,64,2176]{2,1,0:T(8,128)(2,1)S(1)} collective-permute-done((bf16[2,64,2176]{2,1,0:T(8,128)(2,1)S(1)}, bf16[2,64,2176]{2,1,0:T(8,128)(2,1)S(1)}, u32[]{:S(2)}, u32[]{:S(2)}) %collective-permute-start.7) | collective-permute-done | bytes 557088 | tf_op jit(solution)/shard_map/ppermute | solution.py:13
  136.8 1.9 bitcast_dynamic-update-slice_fusion
  138.7 1.9 bitcast_dynamic-update-slice_fusion.15
  140.6 1.9 bitcast_dynamic-update-slice_fusion.13
  148.5 3.9 %fusion.22 = (bf16[1,2,4,2,128,1024]{5,4,0,3,1,2:T(8,128)(2,1)S(1)}, bf16[1,2,4,2,128,1024]{5,4,0,3,1,2:T(8,128)(2,1)S(1)}) fusion(bf16[2,2,4,2,128,1024]{5,4,0,3,1,2:T(8,128)(2,1)} %bitcast.172), kind=kLoop, calls=%fused_computation.86 | loop fusion | bytes 16777216 | tf_op jit(solution)/shard_map/slice | solution.py:59
  152.4 2.4 copy.148
  154.9 2.4 copy.149
  157.3 1.9 bitcast_dynamic-update-slice_fusion.1
  159.2 4.7 %constant_dynamic-slice_fusion = bf16[8,2,64,2176]{3,2,1,0:T(8,128)(2,1)} fusion(bf16[16,2,64,2176]{3,2,1,0:T(8,128)(2,1)} %bitcast_dynamic-update-slice_fusion.1, s32[]{:T(128)S(6)} %select_n.173), kind=kLoop, calls=%fused_computation.83 | loop fusion | bytes 8912900 | tf_op jit(solution)/shard_map/jit(_roll_dynamic)/dynamic_slice | solution.py:101
  164.0 9.2 %copy.130 = bf16[8,2,64,2176]{2,3,1,0:T(8,128)(2,1)} copy(bf16[8,2,64,2176]{3,2,1,0:T(8,128)(2,1)} %constant_dynamic-slice_fusion) | data formatting | bytes 8912896 | tf_op jit(solution)/shard_map/jit(_roll_dynamic)/dynamic_slice | solution.py:101
  174.3 2.3 reduce-window.16
  178.6 6.5 %fusion.3 = bf16[16,2,32,2048]{3,2,1,0:T(8,128)(2,1)S(1)} fusion(pred[16,64,2,32]{1,3,2,0:T(8,128)(4,1)S(1)} %fusion.2, bf16[16,64,2176]{1,2,0:T(8,128)(2,1)} %bitcast.171), kind=kOutput, calls=%fused_computation.9 | convolution fusion | flops 270532608 | bytes 12648448 | tf_op jit(solution)/shard_map/stcr,std->scrd/dot_general | solution.py:114
  185.9 3.9 %collective-permute-done.11 = bf16[16,32,2048]{2,1,0:T(8,128)(2,1)S(1)} collective-permute-done((bf16[16,32,2048]{2,1,0:T(8,128)(2,1)S(1)}, bf16[16,32,2048]{2,1,0:T(8,128)(2,1)S(1)}, u32[]{:S(2)}, u32[]{:S(2)}) %collective-permute-start.11) | collective-permute-done | bytes 2097184 | tf_op jit(solution)/shard_map/ppermute | solution.py:8
  190.2 2.1 copy-done.4
  192.4 1.2 copy-done.3
  193.6 6.0 %fusion.25 = f32[1024,1024]{1,0:T(8,128)} fusion(bf16[1024,2048]{1,0:T(8,128)(2,1)S(1)} %bitcast.180, bf16[2048,1024]{1,0:T(8,128)(2,1)S(1)} %bitcast.178), kind=kOutput, calls=%fused_computation.89 | convolution fusion | flops 4294967296 | bytes 12582912 | tf_op jit(solution)/shard_map/dot_general | solution.py:125
  199.6 9.0 %all-gather.7.cloned.1.call-done = bf16[8,2,128,1024]{3,2,1,0:T(8,128)(2,1)} async-done(((bf16[2,2,128,1024]{3,2,1,0:T(8,128)(2,1)}), bf16[8,2,128,1024]{3,2,1,0:T(8,128)(2,1)}) %all-gather.7.cloned.1.call-update) | async-done | bytes 4194320 | tf_op jit(solution)/shard_map/all_gather | solution.py:61
  208.6 4.8 %copy.150 = bf16[2,4,2,128,1024]{4,3,2,1,0:T(8,128)(2,1)} copy(bf16[2,4,2,128,1024]{4,3,2,0,1:T(8,128)(2,1)} %bitcast.179) | data formatting | bytes 8388608 | tf_op jit(solution)/shard_map/transpose | solution.py:62
  213.4 15.2 %convolution_convert_fusion = bf16[1024,2048]{1,0:T(8,128)(2,1)} fusion(bf16[2048,1024]{1,0:T(8,128)(2,1)} %bitcast.182, f32[1024,1024]{1,0:T(8,128)} %fusion.25, bf16[1024,2048]{1,0:T(8,128)(2,1)} %bitcast.181, bf16[2048,1024]{1,0:T(8,128)(2,1)} %bitcast.177), kind=kOutput, calls=%fused_computation.10 | convolution fusion | flops 8598323200 | bytes 20971520 | tf_op jit(solution)/shard_map/dot_general | solution.py:128
  228.6 2.7 fusion.23
  231.4 4.1 %collective-permute-done.14 = bf16[16,32,2048]{2,1,0:T(8,128)(2,1)S(1)} collective-permute-done((bf16[16,32,2048]{2,1,0:T(8,128)(2,1)S(1)}, bf16[16,32,2048]{2,1,0:T(8,128)(2,1)S(1)}, u32[]{:S(2)}, u32[]{:S(2)}) %collective-permute-start.14) | collective-permute-done | bytes 2097184 | tf_op jit(solution)/shard_map/ppermute | solution.py:8
  235.6 2.2 maximum_select_fusion
  237.7 9.7 %all-to-all-start = ((bf16[16,2,32,2048]{3,2,1,0:T(8,128)(2,1)}), bf16[16,2,32,2048]{3,2,1,0:T(8,128)(2,1)}, u32[]{:S(2)}, u32[]{:S(2)}) async-start(bf16[16,2,32,2048]{3,2,1,0:T(8,128)(2,1)} %maximum_select_fusion), calls=%async_computation | async-start | bytes 8388608 | tf_op jit(solution)/shard_map/all_to_all | solution.py:133
  253.1 93.9 %all-to-all-done = bf16[16,2,32,2048]{3,2,1,0:T(8,128)(2,1)} async-done(((bf16[16,2,32,2048]{3,2,1,0:T(8,128)(2,1)}), bf16[16,2,32,2048]{3,2,1,0:T(8,128)(2,1)}, u32[]{:S(2)}, u32[]{:S(2)}) %all-to-all-start) | async-done | bytes 4194336 | tf_op jit(solution)/shard_map/all_to_all | solution.py:133
  347.0 3.7 %convolution_convert_fusion.1 = bf16[64,2048]{1,0:T(8,128)(2,1)} fusion(bf16[64,1024]{1,0:T(8,128)(2,1)S(1)} %fusion.7, bf16[1024,2048]{1,0:T(8,128)(2,1)} %bitcast.56), kind=kOutput, calls=%fused_computation.14 | convolution fusion | flops 268566528 | bytes 4587520 | tf_op jit(solution)/shard_map/dot_general | solution.py:149
  (98 shorter events, 27.7 us)
Async XLA Ops:
  7.2 141.3 %all-gather.5.cloned.1.call-start = ((), (), s32[]{:S(2)}) async-start(), calls=%async_computation.1 | async-start | bytes 10485760 | tf_op jit(solution)/shard_map/all_gather | solution.py:57
  9.9 36.1 %collective-permute-start.12 = (bf16[2,3,128,1024]{3,2,1,0:T(8,128)(2,1)S(1)}, bf16[2,3,128,1024]{3,2,1,0:T(8,128)(2,1)S(1)}, u32[]{:S(2)}, u32[]{:S(2)}) collective-permute-start(bf16[2,3,128,1024]{3,2,1,0:T(8,128)(2,1)S(1)} %get-tuple-element.25), channel_id=1, source_target_pairs={{0,8},{1,9},{2,10},{3,11},{4,12},{5,13},{6,14},{7,15},{8,0},{9,1},... | collective-permute-start | bytes 4718600 | tf_op jit(solution)/shard_map/ppermute | solution.py:8
  46.1 1.2 copy-start.5
  47.2 4.7 %copy-start.8 = (s32[32]{0:T(128)S(1)}, s32[32]{0:T(128)}, u32[]{:S(2)}) copy-start(s32[32]{0:T(128)} %param.11) | copy-start | bytes 388
  47.2 4.8 %copy-start.7 = (s32[64,8]{0,1:T(8,128)S(1)}, s32[64,8]{0,1:T(8,128)}, u32[]{:S(2)}) copy-start(s32[64,8]{0,1:T(8,128)} %param.10) | copy-start | bytes 6148
  51.9 3.8 %collective-permute-start.13 = (bf16[2,3,128,1024]{3,2,1,0:T(8,128)(2,1)}, bf16[2,3,128,1024]{3,2,1,0:T(8,128)(2,1)}, u32[]{:S(2)}, u32[]{:S(2)}) collective-permute-start(bf16[2,3,128,1024]{3,2,1,0:T(8,128)(2,1)} %select_bitcast_fusion), channel_id=1, source_target_pairs={{0,1},{1,0},{2,3},{3,2},{4,5},{5,4},{6,7},{7,6},{8,9},{9,8},{10,11... | collective-permute-start | bytes 4718600 | tf_op jit(solution)/shard_map/ppermute | solution.py:8
  58.1 7.1 %copy-start.9 = (s32[32]{0:T(128)S(1)}, s32[32]{0:T(128)}, u32[]{:S(2)}) copy-start(s32[32]{0:T(128)} %param.12) | copy-start | bytes 388
  59.8 148.9 %all-gather.7.cloned.1.call-start = ((), (), s32[]{:S(2)}) async-start(), calls=%async_computation.2 | async-start | bytes 5242880 | tf_op jit(solution)/shard_map/all_gather | solution.py:61
  61.5 10.4 %collective-permute-start = (bf16[64,2176]{1,0:T(8,128)(2,1)S(1)}, bf16[64,2176]{1,0:T(8,128)(2,1)}, u32[]{:S(2)}, u32[]{:S(2)}) collective-permute-start(bf16[64,2176]{1,0:T(8,128)(2,1)S(1)} %concatenate.8), channel_id=1, source_target_pairs={{0,16},{16,0},{32,48},{48,32},{64,80},{80,64},{96,112},{112,96},{1... | collective-permute-start | bytes 835592 | tf_op jit(solution)/shard_map/ppermute | solution.py:8
  68.9 28.4 %collective-permute-start.3 = (bf16[128,1024]{1,0:T(8,128)(2,1)}, bf16[128,1024]{1,0:T(8,128)(2,1)}, u32[]{:S(2)}, u32[]{:S(2)}) collective-permute-start(bf16[128,1024]{1,0:T(8,128)(2,1)} %bitcast_select_fusion.10), channel_id=1, source_target_pairs={{0,16},{16,32},{32,48},{48,64},{64,80},{80,96},{96,112},{112,128},... | collective-permute-start | bytes 786440 | tf_op jit(solution)/shard_map/ppermute | solution.py:13
  74.1 17.6 %collective-permute-start.1 = (bf16[2,64,2176]{2,1,0:T(8,128)(2,1)}, bf16[2,64,2176]{2,1,0:T(8,128)(2,1)}, u32[]{:S(2)}, u32[]{:S(2)}) collective-permute-start(bf16[2,64,2176]{2,1,0:T(8,128)(2,1)} %get-tuple-element.19), channel_id=1, source_target_pairs={{0,224},{16,240},{32,0},{48,16},{64,32},{80,48},{96,64},{112,80},{... | collective-permute-start | bytes 1671176 | tf_op jit(solution)/shard_map/ppermute | solution.py:13
  80.0 15.4 %collective-permute-start.8 = (bf16[2,64,2176]{2,1,0:T(8,128)(2,1)}, bf16[2,64,2176]{2,1,0:T(8,128)(2,1)}, u32[]{:S(2)}, u32[]{:S(2)}) collective-permute-start(bf16[2,64,2176]{2,1,0:T(8,128)(2,1)} %get-tuple-element.19), channel_id=1, source_target_pairs={{0,32},{16,48},{32,64},{48,80},{64,96},{80,112},{96,128},{112,144}... | collective-permute-start | bytes 1671176 | tf_op jit(solution)/shard_map/ppermute | solution.py:13
  81.1 24.9 %collective-permute-start.4 = (bf16[128,1024]{1,0:T(8,128)(2,1)S(1)}, bf16[128,1024]{1,0:T(8,128)(2,1)}, u32[]{:S(2)}, u32[]{:S(2)}) collective-permute-start(bf16[128,1024]{1,0:T(8,128)(2,1)S(1)} %bitcast_select_fusion.7), channel_id=1, source_target_pairs={{0,16},{16,32},{32,48},{48,64},{64,80},{80,96},{96,112},{112,128},... | collective-permute-start | bytes 786440 | tf_op jit(solution)/shard_map/ppermute | solution.py:13
  86.7 24.8 %collective-permute-start.5 = (bf16[128,1024]{1,0:T(8,128)(2,1)}, bf16[128,1024]{1,0:T(8,128)(2,1)}, u32[]{:S(2)}, u32[]{:S(2)}) collective-permute-start(bf16[128,1024]{1,0:T(8,128)(2,1)} %bitcast_select_fusion.4), channel_id=1, source_target_pairs={{0,16},{16,32},{32,48},{48,64},{64,80},{80,96},{96,112},{112,128},... | collective-permute-start | bytes 786440 | tf_op jit(solution)/shard_map/ppermute | solution.py:13
  91.6 19.9 %collective-permute-start.2 = (bf16[2,64,2176]{2,1,0:T(8,128)(2,1)}, bf16[2,64,2176]{2,1,0:T(8,128)(2,1)S(1)}, u32[]{:S(2)}, u32[]{:S(2)}) collective-permute-start(bf16[2,64,2176]{2,1,0:T(8,128)(2,1)} %collective-permute-done.1), channel_id=1, source_target_pairs={{0,224},{16,240},{32,0},{48,16},{64,32},{80,48},{96,64},{112,80},{... | collective-permute-start | bytes 1671176 | tf_op jit(solution)/shard_map/ppermute | solution.py:13
  95.3 16.2 %collective-permute-start.9 = (bf16[2,64,2176]{2,1,0:T(8,128)(2,1)}, bf16[2,64,2176]{2,1,0:T(8,128)(2,1)S(1)}, u32[]{:S(2)}, u32[]{:S(2)}) collective-permute-start(bf16[2,64,2176]{2,1,0:T(8,128)(2,1)} %collective-permute-done.8), channel_id=1, source_target_pairs={{0,32},{16,48},{32,64},{48,80},{64,96},{80,112},{96,128},{112,144}... | collective-permute-start | bytes 1671176 | tf_op jit(solution)/shard_map/ppermute | solution.py:13
  111.5 13.1 %collective-permute-start.6 = (bf16[2,64,2176]{2,1,0:T(8,128)(2,1)S(1)}, bf16[2,64,2176]{2,1,0:T(8,128)(2,1)S(1)}, u32[]{:S(2)}, u32[]{:S(2)}) collective-permute-start(bf16[2,64,2176]{2,1,0:T(8,128)(2,1)S(1)} %collective-permute-done.2), channel_id=1, source_target_pairs={{0,224},{16,240},{32,0},{48,16},{64,32},{80,48},{96,64},{112,80},{... | collective-permute-start | bytes 1671176 | tf_op jit(solution)/shard_map/ppermute | solution.py:13
  111.6 23.5 %collective-permute-start.10 = (bf16[2,64,2176]{2,1,0:T(8,128)(2,1)S(1)}, bf16[2,64,2176]{2,1,0:T(8,128)(2,1)S(1)}, u32[]{:S(2)}, u32[]{:S(2)}) collective-permute-start(bf16[2,64,2176]{2,1,0:T(8,128)(2,1)S(1)} %collective-permute-done.9), channel_id=1, source_target_pairs={{0,32},{16,48},{32,64},{48,80},{64,96},{80,112},{96,128},{112,144}... | collective-permute-start | bytes 1671176 | tf_op jit(solution)/shard_map/ppermute | solution.py:13
  124.7 9.5 %collective-permute-start.7 = (bf16[2,64,2176]{2,1,0:T(8,128)(2,1)S(1)}, bf16[2,64,2176]{2,1,0:T(8,128)(2,1)S(1)}, u32[]{:S(2)}, u32[]{:S(2)}) collective-permute-start(bf16[2,64,2176]{2,1,0:T(8,128)(2,1)S(1)} %collective-permute-done.6), channel_id=1, source_target_pairs={{0,224},{16,240},{32,0},{48,16},{64,32},{80,48},{96,64},{112,80},{... | collective-permute-start | bytes 1671176 | tf_op jit(solution)/shard_map/ppermute | solution.py:13
  185.4 4.5 %collective-permute-start.11 = (bf16[16,32,2048]{2,1,0:T(8,128)(2,1)S(1)}, bf16[16,32,2048]{2,1,0:T(8,128)(2,1)S(1)}, u32[]{:S(2)}, u32[]{:S(2)}) collective-permute-start(bf16[16,32,2048]{2,1,0:T(8,128)(2,1)S(1)} %fusion.4), channel_id=1, source_target_pairs={{0,1},{1,0},{2,3},{3,2},{4,5},{5,4},{6,7},{7,6},{8,9},{9,8},{10,11... | collective-permute-start | bytes 6291464 | tf_op jit(solution)/shard_map/ppermute | solution.py:8
  189.8 3.7 %copy-start.3 = (bf16[1,2,4,2,128,1024]{5,4,3,2,1,0:T(8,128)(2,1)S(1)}, bf16[1,2,4,2,128,1024]{5,4,3,2,1,0:T(8,128)(2,1)}, u32[]{:S(2)}) copy-start(bf16[1,2,4,2,128,1024]{5,4,3,2,1,0:T(8,128)(2,1)} %copy.148) | copy-start | bytes 12582916
  190.2 2.1 copy-start.4
  231.3 4.2 %collective-permute-start.14 = (bf16[16,32,2048]{2,1,0:T(8,128)(2,1)S(1)}, bf16[16,32,2048]{2,1,0:T(8,128)(2,1)S(1)}, u32[]{:S(2)}, u32[]{:S(2)}) collective-permute-start(bf16[16,32,2048]{2,1,0:T(8,128)(2,1)S(1)} %bitcast.188), channel_id=1, source_target_pairs={{0,1},{1,0},{2,3},{3,2},{4,5},{5,4},{6,7},{7,6},{8,9},{9,8},{10,11... | collective-permute-start | bytes 6291464 | tf_op jit(solution)/shard_map/ppermute | solution.py:8
  237.7 9.8 %copy-start.6 = (f32[64,8]{0,1:T(8,128)S(1)}, f32[64,8]{0,1:T(8,128)}, u32[]{:S(2)}) copy-start(f32[64,8]{0,1:T(8,128)} %param.9) | copy-start | bytes 6148
  237.7 10.7 %copy-start.1 = (bf16[2,128,1024]{2,1,0:T(8,128)(2,1)S(1)}, bf16[2,128,1024]{2,1,0:T(8,128)(2,1)}, u32[]{:S(2)}) copy-start(bf16[2,128,1024]{2,1,0:T(8,128)(2,1)} %param.15) | copy-start | bytes 1572868
  237.7 10.7 %copy-start.2 = (bf16[2,128,1024]{2,1,0:T(8,128)(2,1)S(1)}, bf16[2,128,1024]{2,1,0:T(8,128)(2,1)}, u32[]{:S(2)}) copy-start(bf16[2,128,1024]{2,1,0:T(8,128)(2,1)} %param.14) | copy-start | bytes 1572868
  237.7 109.3 %all-to-all-start = ((bf16[16,2,32,2048]{3,2,1,0:T(8,128)(2,1)}), bf16[16,2,32,2048]{3,2,1,0:T(8,128)(2,1)}, u32[]{:S(2)}, u32[]{:S(2)}) async-start(bf16[16,2,32,2048]{3,2,1,0:T(8,128)(2,1)} %maximum_select_fusion), calls=%async_computation | async-start | bytes 8388608 | tf_op jit(solution)/shard_map/all_to_all | solution.py:133
  247.5 3.8 %copy-start = (bf16[2,128,1024]{2,1,0:T(8,128)(2,1)S(1)}, bf16[2,128,1024]{2,1,0:T(8,128)(2,1)}, u32[]{:S(2)}) copy-start(bf16[2,128,1024]{2,1,0:T(8,128)(2,1)} %param.13) | copy-start | bytes 1572868
Sparse Core Ops, SparseCore 0:
  59.9 88.5 all-gather.4
  157.4 51.1 all-gather.6

commit v17 on v13

--- a/solution.py
+++ b/solution.py
@@ -53,8 +53,18 @@
     block = jnp.where(
         core == 0, jnp.stack([kept, received], axis=1), jnp.stack([received, kept], axis=1)
     )
-    groups = [list(range(g % 2 + (g // 2) * half_count, (g // 2 + 1) * half_count, 2)) for g in range(4)]
-    ring = lax.all_gather(block, "shard", axis=0, tiled=False, axis_index_groups=groups)
+    def along_y(x, dy):
+        pairs = [
+            (i, i - i % half_count + ((i % half_count // 2 + dy) % 4) * 2 + i % 2)
+            for i in range(n_shard)
+        ]
+        return lax.ppermute(x, "shard", pairs)
+
+    from_next = along_y(block, -1)
+    from_prev = along_y(block, 1)
+    opposite = jnp.stack([along_y(from_next[0], -1), along_y(from_prev[1], 1)])
+    by_offset = jnp.stack([block, from_next, opposite, from_prev])
+    ring = jnp.roll(by_offset, (column % half_count) // 2, axis=0)
     full = jnp.transpose(ring, (3, 1, 0, 2, 4, 5)).reshape(3, model_width, -1)
     full_gate, full_up, full_down = full[0], full[1], full[2]
     slot_index = jnp.arange(slot_count, dtype=jnp.int32)

time: 335 us -> 388 us (1.16)
  starting transfers between devices: 30.6 us -> 50.9 us
  local copies, waits for them, and re-layouts: 40.7 us -> 60.4 us
  between operations: 15.6 us -> 2.58 us
  waiting for transfers between devices: 193 us -> 204 us
  other arithmetic: 23.8 us -> 34.7 us
    ppermute x0 -> x4, waiting for transfers between devices: none -> 54.8 us  [along_y(): return lax.ppermute(x, 'shard', pairs)]
    ppermute x5, waiting for transfers between devices: 49.8 us -> 4.16 us  [partner_2(): lax.ppermute(x, axis, [(i, i ^ 1 << apart) for i in range(lax.axis_size(a...]
    ppermute x10, starting transfers between devices: 15.9 us -> 27.8 us  [passed_along(): return lax.ppermute(x, axis, [(i, (i + by) % size) for i in range(size)])]
    ppermute x10, waiting for transfers between devices: 40.5 us -> 49.2 us  [passed_along(): return lax.ppermute(x, axis, [(i, (i + by) % size) for i in range(size)])]
    unnamed x1 -> x5, other arithmetic: 0.93 us -> 8.82 us
    all_gather x1 -> x0, waiting for transfers between devices: 7.63 us -> none  [local(): lax.all_gather(block, 'shard', axis=0, tiled=False, axis_index_groups=gro...]
    unnamed x32 -> x71, local copies, waits for them, and re-layouts: 12 us -> 18.5 us
    transpose x0 -> x1, local copies, waits for them, and re-layouts: none -> 6.29 us  [local(): full = jnp.transpose(ring, (3, 1, 0, 2, 4, 5)).reshape(3, model_width, -1)]
  transfers between devices with their start and end apart: 17 -> 20, of which waited for: 12 -> 10; matrix products, arithmetic and copies ran while one was open for 16% -> 15% of each run, Pallas kernels for 0% -> 0%
where the time goes in v17:
time: 388 us; the launch traced here: 384 us
  waiting for transfers between devices  204 us (53%)
  local copies, waits for them, and re-layouts  60.4 us (16%)
  starting transfers between devices  50.9 us (13%)
  other arithmetic  34.7 us (9%)
  matrix products  31.4 us (8%)
    all_to_all x1, waiting for transfers between devices, local(): lax.all_to_all(pair_halves(upper_half, result[0], returned_other), 'dp',...  95.9 us
    ppermute x4, waiting for transfers between devices, along_y(): return lax.ppermute(x, 'shard', pairs)  54.8 us
    ppermute x10, waiting for transfers between devices, passed_along(): return lax.ppermute(x, axis, [(i, (i + by) % size) for i in range(size)])  49.2 us
    ppermute x10, starting transfers between devices, passed_along(): return lax.ppermute(x, axis, [(i, (i + by) % size) for i in range(size)])  27.8 us
    unnamed x71, local copies, waits for them, and re-layouts  18.5 us
    dot_general x1, matrix products, local(): lax.dot_general(hidden, full_down, (((1,), (1,)), ((), ())), preferred_el...  15.2 us
    all_to_all x1, starting transfers between devices, local(): lax.all_to_all(pair_halves(upper_half, result[0], returned_other), 'dp',...  13.7 us
    dynamic_slice x2, local copies, waits for them, and re-layouts, local(): jnp.roll(by_offset, row_id // 2, axis=0).reshape(n_rows, tok_count, -1)  11.7 us
  transfers between devices with their start and end apart: 20, of which 10 were waited for; matrix products, arithmetic and copies ran while one was open for 15% of the time, Pallas kernels for 0%

profile of v17, /device:TPU:8, one launch (start us, length us, event | category | flops | bytes accessed | tf_op | source)
XLA Modules:
  0.0 384.1 jit_solution(17594328084886052206)
XLA Ops:
  5.5 3.1 collective-permute-start
  8.6 3.3 fusion.21
  14.9 2.1 collective-permute-start.3
  18.0 5.9 %collective-permute-start.1 = (bf16[2,64,2176]{2,1,0:T(8,128)(2,1)S(1)}, bf16[2,64,2176]{2,1,0:T(8,128)(2,1)S(1)}, u32[]{:S(2)}, u32[]{:S(2)}) collective-permute-start(bf16[2,64,2176]{2,1,0:T(8,128)(2,1)S(1)} %get-tuple-element.13), channel_id=1, source_target_pairs={{0,224},{16,240},{32,0},{48,16},{64,32},{80,48},{96,64},{112,80},{... | collective-permute-start | bytes 1671176 | tf_op jit(solution)/shard_map/ppermute | solution.py:13
  23.9 2.7 collective-permute-start.4
  26.7 28.3 %collective-permute-done.3 = bf16[128,1024]{1,0:T(8,128)(2,1)S(1)} collective-permute-done((bf16[128,1024]{1,0:T(8,128)(2,1)S(1)}, bf16[128,1024]{1,0:T(8,128)(2,1)S(1)}, u32[]{:S(2)}, u32[]{:S(2)}) %collective-permute-start.3) | collective-permute-done | bytes 262176 | tf_op jit(solution)/shard_map/ppermute | solution.py:13
  55.0 4.0 %collective-permute-start.5 = (bf16[128,1024]{1,0:T(8,128)(2,1)S(1)}, bf16[128,1024]{1,0:T(8,128)(2,1)S(1)}, u32[]{:S(2)}, u32[]{:S(2)}) collective-permute-start(bf16[128,1024]{1,0:T(8,128)(2,1)S(1)} %bitcast_select_fusion.4), channel_id=1, source_target_pairs={{0,16},{16,32},{32,48},{48,64},{64,80},{80,96},{96,112},{112,128},... | collective-permute-start | bytes 786440 | tf_op jit(solution)/shard_map/ppermute | solution.py:13
  59.0 5.9 %collective-permute-start.2 = (bf16[2,64,2176]{2,1,0:T(8,128)(2,1)S(1)}, bf16[2,64,2176]{2,1,0:T(8,128)(2,1)S(1)}, u32[]{:S(2)}, u32[]{:S(2)}) collective-permute-start(bf16[2,64,2176]{2,1,0:T(8,128)(2,1)S(1)} %collective-permute-done.1), channel_id=1, source_target_pairs={{0,224},{16,240},{32,0},{48,16},{64,32},{80,48},{96,64},{112,80},{... | collective-permute-start | bytes 1671176 | tf_op jit(solution)/shard_map/ppermute | solution.py:13
  65.7 5.7 %collective-permute-done.5 = bf16[128,1024]{1,0:T(8,128)(2,1)S(1)} collective-permute-done((bf16[128,1024]{1,0:T(8,128)(2,1)S(1)}, bf16[128,1024]{1,0:T(8,128)(2,1)S(1)}, u32[]{:S(2)}, u32[]{:S(2)}) %collective-permute-start.5) | collective-permute-done | bytes 262176 | tf_op jit(solution)/shard_map/ppermute | solution.py:13
  71.5 2.9 collective-permute-done.2
  74.4 3.7 collective-permute-start.6
  79.0 3.4 maximum_select_fusion.1
  82.9 3.8 collective-permute-done.6
  86.8 3.7 collective-permute-start.7
  90.5 8.5 %collective-permute-done.7 = bf16[2,64,2176]{2,1,0:T(8,128)(2,1)S(1)} collective-permute-done((bf16[2,64,2176]{2,1,0:T(8,128)(2,1)S(1)}, bf16[2,64,2176]{2,1,0:T(8,128)(2,1)S(1)}, u32[]{:S(2)}, u32[]{:S(2)}) %collective-permute-start.7) | collective-permute-done | bytes 557088 | tf_op jit(solution)/shard_map/ppermute | solution.py:13
  101.0 1.9 maximum_select_fusion.3
  103.3 3.9 %copy.142 = bf16[2,2,3,128,1024]{4,3,1,0,2:T(8,128)(2,1)} copy(bf16[2,2,3,128,1024]{4,3,1,2,0:T(8,128)(2,1)} %maximum_select_fusion.3) | data formatting | bytes 6291456 | tf_op jit(solution)/shard_map/jit(_where)/select_n | solution.py:53
  107.1 1.6 collective-permute-start.16
  108.7 2.5 constant_dynamic-slice_fusion
  111.2 9.2 %copy.124 = bf16[8,2,64,2176]{2,3,1,0:T(8,128)(2,1)} copy(bf16[8,2,64,2176]{3,2,1,0:T(8,128)(2,1)} %constant_dynamic-slice_fusion) | data formatting | bytes 8912896 | tf_op jit(solution)/shard_map/jit(_roll_dynamic)/dynamic_slice | solution.py:108
  121.6 2.3 reduce-window.16
  127.6 6.4 %fusion.3 = bf16[16,2,32,2048]{3,2,1,0:T(8,128)(2,1)S(1)} fusion(pred[16,64,2,32]{1,3,2,0:T(8,128)(4,1)S(1)} %fusion.2, bf16[16,64,2176]{1,2,0:T(8,128)(2,1)} %bitcast.192), kind=kOutput, calls=%fused_computation.10 | convolution fusion | flops 270532608 | bytes 12648448 | tf_op jit(solution)/shard_map/stcr,std->scrd/dot_general | solution.py:121
  134.1 1.9 copy-done
  136.0 1.6 fusion.4
  137.8 36.3 %collective-permute-done.16 = bf16[2,2,3,128,1024]{4,3,1,0,2:T(8,128)(2,1)} collective-permute-done((bf16[2,2,3,128,1024]{4,3,1,0,2:T(8,128)(2,1)}, bf16[2,2,3,128,1024]{4,3,1,0,2:T(8,128)(2,1)}, u32[]{:S(2)}, u32[]{:S(2)}) %collective-permute-start.16) | collective-permute-done | bytes 3145760 | tf_op jit(solution)/shard_map/ppermute | solution.py:61
  174.0 1.5 slice_bitcast_fusion.4
  176.9 1.5 slice_bitcast_fusion.5
  178.5 2.1 collective-permute-start.15
  180.8 2.1 copy_dynamic-update-slice_fusion.4
  182.9 2.0 pad_maximum_fusion
  184.9 5.3 %copy_dynamic-update-slice_fusion.2 = bf16[8,2,2,3,128,1024]{5,4,2,0,1,3:T(8,128)(2,1)} fusion(bf16[8,2,2,3,128,1024]{5,4,2,0,1,3:T(8,128)(2,1)} %copy_dynamic-update-slice_fusion.4, bf16[2,2,3,128,1024]{4,3,1,2,0:T(8,128)(2,1)} %collective-permute-done.14), kind=kLoop, calls=%fused_computation.21 | loop fusion | bytes 6291456
  190.1 17.4 %collective-permute-done.17 = bf16[2,3,128,1024]{3,2,0,1:T(8,128)(2,1)S(1)} collective-permute-done((bf16[2,3,128,1024]{3,2,0,1:T(8,128)(2,1)S(1)}, bf16[2,3,128,1024]{3,2,0,1:T(8,128)(2,1)S(1)}, u32[]{:S(2)}, u32[]{:S(2)}) %collective-permute-start.17) | collective-permute-done | bytes 1572896 | tf_op jit(solution)/shard_map/ppermute | solution.py:61
  208.7 1.9 copy_dynamic-update-slice_fusion
  210.6 3.8 bitcast_dynamic-update-slice_fusion
  214.4 2.0 copy_dynamic-update-slice_fusion.5
  216.4 3.8 copy_dynamic-update-slice_fusion.3
  220.2 1.9 copy_dynamic-update-slice_fusion.1
  222.1 3.9 %bitcast_dynamic-update-slice_fusion.1 = bf16[8,2,2,3,128,1024]{5,4,2,0,1,3:T(8,128)(2,1)} fusion(bf16[8,2,2,3,128,1024]{5,4,2,0,1,3:T(8,128)(2,1)} %copy_dynamic-update-slice_fusion.1, bf16[2,2,3,128,1024]{4,3,1,0,2:T(8,128)(2,1)} %collective-permute-done.16), kind=kLoop, calls=%fused_computation.17 | loop fusion | bytes 6291456 | tf_op jit(solution)/shard_map/jit(_roll_dynamic)/concatenate | solution.py:67
  226.0 6.3 %dynamic-slice_bitcast_fusion = bf16[3,2,4,2,128,1024]{5,4,3,2,1,0:T(8,128)(2,1)S(1)} fusion(bf16[8,2,2,3,128,1024]{5,4,2,0,1,3:T(8,128)(2,1)} %bitcast_dynamic-update-slice_fusion.1, s32[]{:T(128)S(6)} %select_n.219), kind=kLoop, calls=%fused_computation | loop fusion | bytes 25165828 | tf_op jit(solution)/shard_map/transpose | solution.py:68
  232.3 4.4 %fusion.22 = (bf16[1,2,4,2,128,1024]{5,4,3,2,1,0:T(8,128)(2,1)}, bf16[1,2,4,2,128,1024]{5,4,3,2,1,0:T(8,128)(2,1)}, bf16[1,2,4,2,128,1024]{5,4,3,2,1,0:T(8,128)(2,1)S(1)}) fusion(bf16[3,2,4,2,128,1024]{5,4,3,2,1,0:T(8,128)(2,1)S(1)} %dynamic-slice_bitcast_fusion), kind=kLoop, calls=%fused_computation.98 | loop fusion | bytes 25165824 | tf_op jit(solution)/shard_map/slice | solution.py:69
  236.7 6.1 %fusion.25 = f32[1024,1024]{1,0:T(8,128)} fusion(bf16[1024,2048]{1,0:T(8,128)(2,1)S(1)} %bitcast.204, bf16[2048,1024]{1,0:T(8,128)(2,1)S(1)} %bitcast.208), kind=kOutput, calls=%fused_computation.101 | convolution fusion | flops 4294967296 | bytes 12582912 | tf_op jit(solution)/shard_map/dot_general | solution.py:132
  242.7 15.2 %convolution_convert_fusion = bf16[1024,2048]{1,0:T(8,128)(2,1)} fusion(bf16[2048,1024]{1,0:T(8,128)(2,1)} %bitcast.207, f32[1024,1024]{1,0:T(8,128)} %fusion.25, bf16[1024,2048]{1,0:T(8,128)(2,1)} %bitcast.205, bf16[2048,1024]{1,0:T(8,128)(2,1)} %bitcast.206), kind=kOutput, calls=%fused_computation.11 | convolution fusion | flops 8598323200 | bytes 20971520 | tf_op jit(solution)/shard_map/dot_general | solution.py:135
  257.9 2.7 fusion.23
  260.7 4.1 %collective-permute-done.18 = bf16[16,32,2048]{2,1,0:T(8,128)(2,1)S(1)} collective-permute-done((bf16[16,32,2048]{2,1,0:T(8,128)(2,1)S(1)}, bf16[16,32,2048]{2,1,0:T(8,128)(2,1)S(1)}, u32[]{:S(2)}, u32[]{:S(2)}) %collective-permute-start.18) | collective-permute-done | bytes 2097184 | tf_op jit(solution)/shard_map/ppermute | solution.py:8
  264.9 2.2 maximum_select_fusion
  267.1 13.7 %all-to-all-start = ((bf16[16,2,32,2048]{3,2,1,0:T(8,128)(2,1)}), bf16[16,2,32,2048]{3,2,1,0:T(8,128)(2,1)}, u32[]{:S(2)}, u32[]{:S(2)}) async-start(bf16[16,2,32,2048]{3,2,1,0:T(8,128)(2,1)} %maximum_select_fusion), calls=%async_computation | async-start | bytes 8388608 | tf_op jit(solution)/shard_map/all_to_all | solution.py:140
  284.5 95.9 %all-to-all-done = bf16[16,2,32,2048]{3,2,1,0:T(8,128)(2,1)} async-done(((bf16[16,2,32,2048]{3,2,1,0:T(8,128)(2,1)}), bf16[16,2,32,2048]{3,2,1,0:T(8,128)(2,1)}, u32[]{:S(2)}, u32[]{:S(2)}) %all-to-all-start) | async-done | bytes 4194336 | tf_op jit(solution)/shard_map/all_to_all | solution.py:140
  380.4 3.7 convolution_convert_fusion.1
  (142 shorter events, 23.7 us)
Async XLA Ops:
  0.6 11.8 %copy-start.25 = (s32[32]{0:T(128)S(1)}, s32[32]{0:T(128)}, u32[]{:S(2)}) copy-start(s32[32]{0:T(128)} %param.11) | copy-start | bytes 388
  0.6 14.3 %copy-start.4 = (bf16[2,128,1024]{2,1,0:T(8,128)(2,1)S(1)}, bf16[2,128,1024]{2,1,0:T(8,128)(2,1)}, u32[]{:S(2)}) copy-start(bf16[2,128,1024]{2,1,0:T(8,128)(2,1)} %param.13) | copy-start | bytes 1572868
  0.7 12.4 %copy-start.26 = (s32[32]{0:T(128)S(1)}, s32[32]{0:T(128)}, u32[]{:S(2)}) copy-start(s32[32]{0:T(128)} %param.12) | copy-start | bytes 388
  5.4 18.4 %copy-start.8 = (bf16[2,128,1024]{2,1,0:T(8,128)(2,1)S(1)}, bf16[2,128,1024]{2,1,0:T(8,128)(2,1)}, u32[]{:S(2)}) copy-start(bf16[2,128,1024]{2,1,0:T(8,128)(2,1)} %param.14) | copy-start | bytes 1572868
  5.5 11.6 %collective-permute-start = (bf16[64,2176]{1,0:T(8,128)(2,1)S(1)}, bf16[64,2176]{1,0:T(8,128)(2,1)S(1)}, u32[]{:S(2)}, u32[]{:S(2)}) collective-permute-start(bf16[64,2176]{1,0:T(8,128)(2,1)S(1)} %concatenate.27), channel_id=1, source_target_pairs={{0,16},{16,0},{32,48},{48,32},{64,80},{80,64},{96,112},{112,96},{1... | collective-permute-start | bytes 835592 | tf_op jit(solution)/shard_map/ppermute | solution.py:8
  8.6 18.0 %copy-start.6 = (bf16[2,128,1024]{2,1,0:T(8,128)(2,1)S(1)}, bf16[2,128,1024]{2,1,0:T(8,128)(2,1)}, u32[]{:S(2)}) copy-start(bf16[2,128,1024]{2,1,0:T(8,128)(2,1)} %param.15) | copy-start | bytes 1572868
  11.8 67.1 %collective-permute-start.12 = (bf16[2,3,128,1024]{3,2,1,0:T(8,128)(2,1)}, bf16[2,3,128,1024]{3,2,1,0:T(8,128)(2,1)}, u32[]{:S(2)}, u32[]{:S(2)}) collective-permute-start(bf16[2,3,128,1024]{3,2,1,0:T(8,128)(2,1)} %get-tuple-element.20), channel_id=1, source_target_pairs={{0,8},{1,9},{2,10},{3,11},{4,12},{5,13},{6,14},{7,15},{8,0},{9,1},... | collective-permute-start | bytes 4718600 | tf_op jit(solution)/shard_map/ppermute | solution.py:8
  14.9 40.0 %collective-permute-start.3 = (bf16[128,1024]{1,0:T(8,128)(2,1)S(1)}, bf16[128,1024]{1,0:T(8,128)(2,1)S(1)}, u32[]{:S(2)}, u32[]{:S(2)}) collective-permute-start(bf16[128,1024]{1,0:T(8,128)(2,1)S(1)} %bitcast_select_fusion.10), channel_id=1, source_target_pairs={{0,16},{16,32},{32,48},{48,64},{64,80},{80,96},{96,112},{112,128},... | collective-permute-start | bytes 786440 | tf_op jit(solution)/shard_map/ppermute | solution.py:13
  18.0 60.9 %copy-start.12 = (bf16[2,64,2176]{2,1,0:T(8,128)(2,1)}, bf16[2,64,2176]{2,1,0:T(8,128)(2,1)S(1)}, u32[]{:S(2)}) copy-start(bf16[2,64,2176]{2,1,0:T(8,128)(2,1)S(1)} %get-tuple-element.13) | copy-start | bytes 1671172
  18.0 40.9 %collective-permute-start.1 = (bf16[2,64,2176]{2,1,0:T(8,128)(2,1)S(1)}, bf16[2,64,2176]{2,1,0:T(8,128)(2,1)S(1)}, u32[]{:S(2)}, u32[]{:S(2)}) collective-permute-start(bf16[2,64,2176]{2,1,0:T(8,128)(2,1)S(1)} %get-tuple-element.13), channel_id=1, source_target_pairs={{0,224},{16,240},{32,0},{48,16},{64,32},{80,48},{96,64},{112,80},{... | collective-permute-start | bytes 1671176 | tf_op jit(solution)/shard_map/ppermute | solution.py:13
  23.9 40.9 %collective-permute-start.8 = (bf16[2,64,2176]{2,1,0:T(8,128)(2,1)S(1)}, bf16[2,64,2176]{2,1,0:T(8,128)(2,1)S(1)}, u32[]{:S(2)}, u32[]{:S(2)}) collective-permute-start(bf16[2,64,2176]{2,1,0:T(8,128)(2,1)S(1)} %get-tuple-element.13), channel_id=1, source_target_pairs={{0,32},{16,48},{32,64},{48,80},{64,96},{80,112},{96,128},{112,144}... | collective-permute-start | bytes 1671176 | tf_op jit(solution)/shard_map/ppermute | solution.py:13
  23.9 41.8 %collective-permute-start.4 = (bf16[128,1024]{1,0:T(8,128)(2,1)S(1)}, bf16[128,1024]{1,0:T(8,128)(2,1)S(1)}, u32[]{:S(2)}, u32[]{:S(2)}) collective-permute-start(bf16[128,1024]{1,0:T(8,128)(2,1)S(1)} %bitcast_select_fusion.7), channel_id=1, source_target_pairs={{0,16},{16,32},{32,48},{48,64},{64,80},{80,96},{96,112},{112,128},... | collective-permute-start | bytes 786440 | tf_op jit(solution)/shard_map/ppermute | solution.py:13
  55.0 24.0 %copy-start.18 = (bf16[128,1024]{1,0:T(8,128)(2,1)}, bf16[128,1024]{1,0:T(8,128)(2,1)S(1)}, u32[]{:S(2)}) copy-start(bf16[128,1024]{1,0:T(8,128)(2,1)S(1)} %collective-permute-done.3) | copy-start | bytes 786436
  55.0 16.5 %collective-permute-start.5 = (bf16[128,1024]{1,0:T(8,128)(2,1)S(1)}, bf16[128,1024]{1,0:T(8,128)(2,1)S(1)}, u32[]{:S(2)}, u32[]{:S(2)}) collective-permute-start(bf16[128,1024]{1,0:T(8,128)(2,1)S(1)} %bitcast_select_fusion.4), channel_id=1, source_target_pairs={{0,16},{16,32},{32,48},{48,64},{64,80},{80,96},{96,112},{112,128},... | collective-permute-start | bytes 786440 | tf_op jit(solution)/shard_map/ppermute | solution.py:13
  58.9 20.0 %copy-start.16 = (bf16[2,64,2176]{2,1,0:T(8,128)(2,1)}, bf16[2,64,2176]{2,1,0:T(8,128)(2,1)S(1)}, u32[]{:S(2)}) copy-start(bf16[2,64,2176]{2,1,0:T(8,128)(2,1)S(1)} %collective-permute-done.1) | copy-start | bytes 1671172
  59.0 15.4 %collective-permute-start.2 = (bf16[2,64,2176]{2,1,0:T(8,128)(2,1)S(1)}, bf16[2,64,2176]{2,1,0:T(8,128)(2,1)S(1)}, u32[]{:S(2)}, u32[]{:S(2)}) collective-permute-start(bf16[2,64,2176]{2,1,0:T(8,128)(2,1)S(1)} %collective-permute-done.1), channel_id=1, source_target_pairs={{0,224},{16,240},{32,0},{48,16},{64,32},{80,48},{96,64},{112,80},{... | collective-permute-start | bytes 1671176 | tf_op jit(solution)/shard_map/ppermute | solution.py:13
  64.8 14.2 %copy-start.14 = (bf16[2,64,2176]{2,1,0:T(8,128)(2,1)}, bf16[2,64,2176]{2,1,0:T(8,128)(2,1)S(1)}, u32[]{:S(2)}) copy-start(bf16[2,64,2176]{2,1,0:T(8,128)(2,1)S(1)} %collective-permute-done.8) | copy-start | bytes 1671172
  64.8 13.3 %collective-permute-start.9 = (bf16[2,64,2176]{2,1,0:T(8,128)(2,1)S(1)}, bf16[2,64,2176]{2,1,0:T(8,128)(2,1)S(1)}, u32[]{:S(2)}, u32[]{:S(2)}) collective-permute-start(bf16[2,64,2176]{2,1,0:T(8,128)(2,1)S(1)} %collective-permute-done.8), channel_id=1, source_target_pairs={{0,32},{16,48},{32,64},{48,80},{64,96},{80,112},{96,128},{112,144}... | collective-permute-start | bytes 1671176 | tf_op jit(solution)/shard_map/ppermute | solution.py:13
  65.7 13.2 %copy-start.20 = (bf16[128,1024]{1,0:T(8,128)(2,1)}, bf16[128,1024]{1,0:T(8,128)(2,1)S(1)}, u32[]{:S(2)}) copy-start(bf16[128,1024]{1,0:T(8,128)(2,1)S(1)} %collective-permute-done.4) | copy-start | bytes 786436
  71.5 7.5 %copy-start.22 = (bf16[128,1024]{1,0:T(8,128)(2,1)}, bf16[128,1024]{1,0:T(8,128)(2,1)S(1)}, u32[]{:S(2)}) copy-start(bf16[128,1024]{1,0:T(8,128)(2,1)S(1)} %collective-permute-done.5) | copy-start | bytes 786436
  74.4 12.4 %collective-permute-start.6 = (bf16[2,64,2176]{2,1,0:T(8,128)(2,1)S(1)}, bf16[2,64,2176]{2,1,0:T(8,128)(2,1)S(1)}, u32[]{:S(2)}, u32[]{:S(2)}) collective-permute-start(bf16[2,64,2176]{2,1,0:T(8,128)(2,1)S(1)} %collective-permute-done.2), channel_id=1, source_target_pairs={{0,224},{16,240},{32,0},{48,16},{64,32},{80,48},{96,64},{112,80},{... | collective-permute-start | bytes 1671176 | tf_op jit(solution)/shard_map/ppermute | solution.py:13
  78.1 20.9 %collective-permute-start.10 = (bf16[2,64,2176]{2,1,0:T(8,128)(2,1)S(1)}, bf16[2,64,2176]{2,1,0:T(8,128)(2,1)S(1)}, u32[]{:S(2)}, u32[]{:S(2)}) collective-permute-start(bf16[2,64,2176]{2,1,0:T(8,128)(2,1)S(1)} %collective-permute-done.9), channel_id=1, source_target_pairs={{0,32},{16,48},{32,64},{48,80},{64,96},{80,112},{96,128},{112,144}... | collective-permute-start | bytes 1671176 | tf_op jit(solution)/shard_map/ppermute | solution.py:13
  82.4 8.0 %copy-start.11 = (bf16[16,2,64,2176]{3,2,1,0:T(8,128)(2,1)S(1)}, bf16[16,2,64,2176]{3,2,1,0:T(8,128)(2,1)}, u32[]{:S(2)}) copy-start(bf16[16,2,64,2176]{3,2,1,0:T(8,128)(2,1)} %bitcast_dynamic-update-slice_fusion.12) | copy-start | bytes 26738692
  82.6 16.5 %copy-start.15 = (bf16[2,64,2176]{2,1,0:T(8,128)(2,1)S(1)}, bf16[2,64,2176]{2,1,0:T(8,128)(2,1)}, u32[]{:S(2)}) copy-start(bf16[2,64,2176]{2,1,0:T(8,128)(2,1)} %copy-done.14) | copy-start | bytes 1671172
  82.6 16.6 %copy-start.13 = (bf16[2,64,2176]{2,1,0:T(8,128)(2,1)S(1)}, bf16[2,64,2176]{2,1,0:T(8,128)(2,1)}, u32[]{:S(2)}) copy-start(bf16[2,64,2176]{2,1,0:T(8,128)(2,1)} %copy-done.12) | copy-start | bytes 1671172
  82.6 17.1 %collective-permute-start.13 = (bf16[2,3,128,1024]{3,2,1,0:T(8,128)(2,1)S(1)}, bf16[2,3,128,1024]{3,2,1,0:T(8,128)(2,1)S(1)}, u32[]{:S(2)}, u32[]{:S(2)}) collective-permute-start(bf16[2,3,128,1024]{3,2,1,0:T(8,128)(2,1)S(1)} %select_bitcast_fusion), channel_id=1, source_target_pairs={{0,1},{1,0},{2,3},{3,2},{4,5},{5,4},{6,7},{7,6},{8,9},{9,8},{10,11... | collective-permute-start | bytes 4718600 | tf_op jit(solution)/shard_map/ppermute | solution.py:8
  82.9 16.4 %copy-start.17 = (bf16[2,64,2176]{2,1,0:T(8,128)(2,1)S(1)}, bf16[2,64,2176]{2,1,0:T(8,128)(2,1)}, u32[]{:S(2)}) copy-start(bf16[2,64,2176]{2,1,0:T(8,128)(2,1)} %copy-done.16) | copy-start | bytes 1671172
  86.8 12.2 %collective-permute-start.7 = (bf16[2,64,2176]{2,1,0:T(8,128)(2,1)S(1)}, bf16[2,64,2176]{2,1,0:T(8,128)(2,1)S(1)}, u32[]{:S(2)}, u32[]{:S(2)}) collective-permute-start(bf16[2,64,2176]{2,1,0:T(8,128)(2,1)S(1)} %collective-permute-done.6), channel_id=1, source_target_pairs={{0,224},{16,240},{32,0},{48,16},{64,32},{80,48},{96,64},{112,80},{... | collective-permute-start | bytes 1671176 | tf_op jit(solution)/shard_map/ppermute | solution.py:13
  99.8 1.2 copy-start.2
  102.8 74.1 %collective-permute-start.14 = (bf16[2,2,3,128,1024]{4,3,1,2,0:T(8,128)(2,1)}, bf16[2,2,3,128,1024]{4,3,1,2,0:T(8,128)(2,1)}, u32[]{:S(2)}, u32[]{:S(2)}) collective-permute-start(bf16[2,2,3,128,1024]{4,3,1,2,0:T(8,128)(2,1)} %maximum_select_fusion.3), channel_id=1, source_target_pairs={{0,6},{1,7},{2,0},{3,1},{4,2},{5,3},{6,4},{7,5},{8,14},{9,15},{10,... | collective-permute-start | bytes 9437192 | tf_op jit(solution)/shard_map/ppermute | solution.py:61
  107.1 66.9 %collective-permute-start.16 = (bf16[2,2,3,128,1024]{4,3,1,0,2:T(8,128)(2,1)}, bf16[2,2,3,128,1024]{4,3,1,0,2:T(8,128)(2,1)}, u32[]{:S(2)}, u32[]{:S(2)}) collective-permute-start(bf16[2,2,3,128,1024]{4,3,1,0,2:T(8,128)(2,1)} %copy.142), channel_id=1, source_target_pairs={{0,2},{1,3},{2,4},{3,5},{4,6},{5,7},{6,0},{7,1},{8,10},{9,11},{10,... | collective-permute-start | bytes 9437192 | tf_op jit(solution)/shard_map/ppermute | solution.py:61
  134.0 1.9 copy-start
  137.6 45.3 %collective-permute-start.11 = (bf16[16,32,2048]{2,1,0:T(8,128)(2,1)}, bf16[16,32,2048]{2,1,0:T(8,128)(2,1)}, u32[]{:S(2)}, u32[]{:S(2)}) collective-permute-start(bf16[16,32,2048]{2,1,0:T(8,128)(2,1)} %fusion.4), channel_id=1, source_target_pairs={{0,1},{1,0},{2,3},{3,2},{4,5},{5,4},{6,7},{7,6},{8,9},{9,8},{10,11... | collective-permute-start | bytes 6291464 | tf_op jit(solution)/shard_map/ppermute | solution.py:8
  137.8 42.8 %copy-start.1 = (bf16[16,2,32,2048]{3,2,1,0:T(8,128)(2,1)S(1)}, bf16[16,2,32,2048]{3,2,1,0:T(8,128)(2,1)}, u32[]{:S(2)}) copy-start(bf16[16,2,32,2048]{3,2,1,0:T(8,128)(2,1)} %copy-done) | copy-start | bytes 12582916
  175.6 5.2 %copy-start.3 = (bf16[2,3,128,1024]{3,2,1,0:T(8,128)(2,1)S(1)}, bf16[2,3,128,1024]{3,2,1,0:T(8,128)(2,1)}, u32[]{:S(2)}) copy-start(bf16[2,3,128,1024]{3,2,1,0:T(8,128)(2,1)} %copy-done.2) | copy-start | bytes 4718596
  175.6 32.0 %collective-permute-start.17 = (bf16[2,3,128,1024]{3,2,0,1:T(8,128)(2,1)S(1)}, bf16[2,3,128,1024]{3,2,0,1:T(8,128)(2,1)S(1)}, u32[]{:S(2)}, u32[]{:S(2)}) collective-permute-start(bf16[2,3,128,1024]{3,2,0,1:T(8,128)(2,1)S(1)} %slice_bitcast_fusion.4), channel_id=1, source_target_pairs={{0,2},{1,3},{2,4},{3,5},{4,6},{5,7},{6,0},{7,1},{8,10},{9,11},{10,... | collective-permute-start | bytes 4718600 | tf_op jit(solution)/shard_map/ppermute | solution.py:61
  178.5 30.2 %collective-permute-start.15 = (bf16[2,3,128,1024]{3,2,0,1:T(8,128)(2,1)S(1)}, bf16[2,3,128,1024]{3,2,0,1:T(8,128)(2,1)S(1)}, u32[]{:S(2)}, u32[]{:S(2)}) collective-permute-start(bf16[2,3,128,1024]{3,2,0,1:T(8,128)(2,1)S(1)} %slice_bitcast_fusion.5), channel_id=1, source_target_pairs={{0,6},{1,7},{2,0},{3,1},{4,2},{5,3},{6,4},{7,5},{8,14},{9,15},{10,... | collective-permute-start | bytes 4718600 | tf_op jit(solution)/shard_map/ppermute | solution.py:61
  184.8 51.8 %copy-start.10 = (bf16[2,16,32,2048]{3,2,1,0:T(8,128)(2,1)}, bf16[2,16,32,2048]{3,2,1,0:T(8,128)(2,1)S(1)}, u32[]{:S(2)}) copy-start(bf16[2,16,32,2048]{3,2,1,0:T(8,128)(2,1)S(1)} %pad_maximum_fusion) | copy-start | bytes 12582916
  260.6 4.2 %collective-permute-start.18 = (bf16[16,32,2048]{2,1,0:T(8,128)(2,1)S(1)}, bf16[16,32,2048]{2,1,0:T(8,128)(2,1)S(1)}, u32[]{:S(2)}, u32[]{:S(2)}) collective-permute-start(bf16[16,32,2048]{2,1,0:T(8,128)(2,1)S(1)} %bitcast.213), channel_id=1, source_target_pairs={{0,1},{1,0},{2,3},{3,2},{4,5},{5,4},{6,7},{7,6},{8,9},{9,8},{10,11... | collective-permute-start | bytes 6291464 | tf_op jit(solution)/shard_map/ppermute | solution.py:8
  267.1 13.8 %copy-start.24 = (f32[64,8]{0,1:T(8,128)S(1)}, f32[64,8]{0,1:T(8,128)}, u32[]{:S(2)}) copy-start(f32[64,8]{0,1:T(8,128)} %param.9) | copy-start | bytes 6148
  267.1 14.7 %copy-start.5 = (bf16[2,128,1024]{2,1,0:T(8,128)(2,1)S(1)}, bf16[2,128,1024]{2,1,0:T(8,128)(2,1)}, u32[]{:S(2)}) copy-start(bf16[2,128,1024]{2,1,0:T(8,128)(2,1)} %param.13) | copy-start | bytes 1572868
  267.1 14.7 %copy-start.19 = (bf16[128,1024]{1,0:T(8,128)(2,1)S(1)}, bf16[128,1024]{1,0:T(8,128)(2,1)}, u32[]{:S(2)}) copy-start(bf16[128,1024]{1,0:T(8,128)(2,1)} %copy-done.18) | copy-start | bytes 786436
  267.1 15.6 %copy-start.7 = (bf16[2,128,1024]{2,1,0:T(8,128)(2,1)S(1)}, bf16[2,128,1024]{2,1,0:T(8,128)(2,1)}, u32[]{:S(2)}) copy-start(bf16[2,128,1024]{2,1,0:T(8,128)(2,1)} %param.15) | copy-start | bytes 1572868
  267.1 15.6 %copy-start.9 = (bf16[2,128,1024]{2,1,0:T(8,128)(2,1)S(1)}, bf16[2,128,1024]{2,1,0:T(8,128)(2,1)}, u32[]{:S(2)}) copy-start(bf16[2,128,1024]{2,1,0:T(8,128)(2,1)} %param.14) | copy-start | bytes 1572868
  267.1 15.6 %copy-start.21 = (bf16[128,1024]{1,0:T(8,128)(2,1)S(1)}, bf16[128,1024]{1,0:T(8,128)(2,1)}, u32[]{:S(2)}) copy-start(bf16[128,1024]{1,0:T(8,128)(2,1)} %copy-done.20) | copy-start | bytes 786436
  267.1 15.6 %copy-start.23 = (bf16[128,1024]{1,0:T(8,128)(2,1)S(1)}, bf16[128,1024]{1,0:T(8,128)(2,1)}, u32[]{:S(2)}) copy-start(bf16[128,1024]{1,0:T(8,128)(2,1)} %copy-done.22) | copy-start | bytes 786436
  267.1 113.2 %all-to-all-start = ((bf16[16,2,32,2048]{3,2,1,0:T(8,128)(2,1)}), bf16[16,2,32,2048]{3,2,1,0:T(8,128)(2,1)}, u32[]{:S(2)}, u32[]{:S(2)}) async-start(bf16[16,2,32,2048]{3,2,1,0:T(8,128)(2,1)} %maximum_select_fusion), calls=%async_computation | async-start | bytes 8388608 | tf_op jit(solution)/shard_map/all_to_all | solution.py:140

commit v18 on v13

--- a/solution.py
+++ b/solution.py
@@ -88,7 +88,7 @@
     behind = [pair]
     for hop in range(1, z_count // 2 + 1):
         ahead.append(passed_along(ahead[-1], "dp", -2))
-        if hop == 2:
+        if hop == 1:
             ahead[-1], arrive_gate, arrive_up, arrive_down = lax.optimization_barrier(
                 (ahead[-1], arrive_gate, arrive_up, arrive_down)
             )

time: 335 us -> 336 us (level)
    ppermute x10, waiting for transfers between devices: 40.5 us -> 50.8 us  [passed_along(): return lax.ppermute(x, axis, [(i, (i + by) % size) for i in range(size)])]
    all_gather x1, waiting for transfers between devices: 7.63 us -> 0.01 us  [local(): lax.all_gather(block, 'shard', axis=0, tiled=False, axis_index_groups=gro...]
  transfers between devices with their start and end apart: 17 -> 17, of which waited for: 12 -> 11; matrix products, arithmetic and copies ran while one was open for 16% -> 16% of each run, Pallas kernels for 0% -> 0%
where the time goes in v18:
time: 336 us; the launch traced here: 335 us
  waiting for transfers between devices  195 us (58%)
  local copies, waits for them, and re-layouts  40.6 us (12%)
  matrix products  31.3 us (9%)
  starting transfers between devices  28.8 us (9%)
  other arithmetic  23.8 us (7%)
  between operations  15.6 us (5%)
    all_to_all x1, waiting for transfers between devices, local(): lax.all_to_all(pair_halves(upper_half, result[0], returned_other), 'dp',...  94.9 us
    ppermute x10, waiting for transfers between devices, passed_along(): return lax.ppermute(x, axis, [(i, (i + by) % size) for i in range(size)])  50.8 us
    ppermute x5, waiting for transfers between devices, partner_2(): lax.ppermute(x, axis, [(i, i ^ 1 << apart) for i in range(lax.axis_size(a...  49.7 us
    ppermute x10, starting transfers between devices, passed_along(): return lax.ppermute(x, axis, [(i, (i + by) % size) for i in range(size)])  15.8 us
    dot_general x1, matrix products, local(): lax.dot_general(hidden, full_down, (((1,), (1,)), ((), ())), preferred_el...  15.2 us
    dynamic_slice x2, local copies, waits for them, and re-layouts, local(): jnp.roll(by_offset, row_id // 2, axis=0).reshape(n_rows, tok_count, -1)  13.9 us
    unnamed x32, local copies, waits for them, and re-layouts  12 us
    all_to_all x1, starting transfers between devices, local(): lax.all_to_all(pair_halves(upper_half, result[0], returned_other), 'dp',...  7.93 us
  transfers between devices with their start and end apart: 17, of which 11 were waited for; matrix products, arithmetic and copies ran while one was open for 16% of the time, Pallas kernels for 0%

profile of v18, /device:TPU:8, one launch (start us, length us, event | category | flops | bytes accessed | tf_op | source)
XLA Modules:
  0.0 335.4 jit_solution(8447448232629769168)
XLA Ops:
  7.2 2.7 fusion.21
  10.0 1.5 collective-permute-start.12
  11.5 34.9 %collective-permute-done.12 = bf16[2,3,128,1024]{3,2,1,0:T(8,128)(2,1)S(1)} collective-permute-done((bf16[2,3,128,1024]{3,2,1,0:T(8,128)(2,1)}, bf16[2,3,128,1024]{3,2,1,0:T(8,128)(2,1)S(1)}, u32[]{:S(2)}, u32[]{:S(2)}) %collective-permute-start.12) | collective-permute-done | bytes 1572896 | tf_op jit(solution)/shard_map/ppermute | solution.py:8
  47.1 3.4 %collective-permute-done.13 = bf16[2,3,128,1024]{3,2,0,1:T(8,128)(2,1)S(1)} collective-permute-done((bf16[2,3,128,1024]{3,2,0,1:T(8,128)(2,1)S(1)}, bf16[2,3,128,1024]{3,2,0,1:T(8,128)(2,1)S(1)}, u32[]{:S(2)}, u32[]{:S(2)}) %collective-permute-start.13) | collective-permute-done | bytes 1572896 | tf_op jit(solution)/shard_map/ppermute | solution.py:8
  50.5 1.9 maximum_select_fusion.2
  53.0 1.2 reduce-window.14
  54.9 3.1 collective-permute-start
  61.7 3.5 %collective-permute-done = bf16[64,2176]{1,0:T(8,128)(2,1)S(1)} collective-permute-done((bf16[64,2176]{1,0:T(8,128)(2,1)S(1)}, bf16[64,2176]{1,0:T(8,128)(2,1)S(1)}, u32[]{:S(2)}, u32[]{:S(2)}) %collective-permute-start) | collective-permute-done | bytes 278560 | tf_op jit(solution)/shard_map/ppermute | solution.py:8
  65.2 0.9 bitcast_dynamic-update-slice_fusion.14
  66.2 5.9 %collective-permute-start.1 = (bf16[2,64,2176]{2,1,0:T(8,128)(2,1)S(1)}, bf16[2,64,2176]{2,1,0:T(8,128)(2,1)S(1)}, u32[]{:S(2)}, u32[]{:S(2)}) collective-permute-start(bf16[2,64,2176]{2,1,0:T(8,128)(2,1)S(1)} %get-tuple-element.13), channel_id=1, source_target_pairs={{0,224},{16,240},{32,0},{48,16},{64,32},{80,48},{96,64},{112,80},{... | collective-permute-start | bytes 1671176 | tf_op jit(solution)/shard_map/ppermute | solution.py:13
  72.8 3.8 %collective-permute-start.3 = (bf16[128,1024]{1,0:T(8,128)(2,1)}, bf16[128,1024]{1,0:T(8,128)(2,1)}, u32[]{:S(2)}, u32[]{:S(2)}) collective-permute-start(bf16[128,1024]{1,0:T(8,128)(2,1)} %bitcast_select_fusion.6), channel_id=1, source_target_pairs={{0,16},{16,32},{32,48},{48,64},{64,80},{80,96},{96,112},{112,128},... | collective-permute-start | bytes 786440 | tf_op jit(solution)/shard_map/ppermute | solution.py:13
  77.4 20.4 %collective-permute-done.3 = bf16[128,1024]{1,0:T(8,128)(2,1)} collective-permute-done((bf16[128,1024]{1,0:T(8,128)(2,1)}, bf16[128,1024]{1,0:T(8,128)(2,1)}, u32[]{:S(2)}, u32[]{:S(2)}) %collective-permute-start.3) | collective-permute-done | bytes 262176 | tf_op jit(solution)/shard_map/ppermute | solution.py:13
  97.8 2.8 collective-permute-done.4
  101.1 1.5 collective-permute-start.9
  102.6 0.9 bitcast_dynamic-update-slice_fusion.12
  103.5 9.8 %collective-permute-done.5 = bf16[2,64,2176]{2,1,0:T(8,128)(2,1)S(1)} collective-permute-done((bf16[2,64,2176]{2,1,0:T(8,128)(2,1)S(1)}, bf16[2,64,2176]{2,1,0:T(8,128)(2,1)S(1)}, u32[]{:S(2)}, u32[]{:S(2)}) %collective-permute-start.5) | collective-permute-done | bytes 557088 | tf_op jit(solution)/shard_map/ppermute | solution.py:13
  113.3 1.4 collective-permute-start.6
  115.3 0.9 bitcast_dynamic-update-slice_fusion.10
  116.2 9.8 %collective-permute-done.6 = bf16[2,64,2176]{2,1,0:T(8,128)(2,1)S(1)} collective-permute-done((bf16[2,64,2176]{2,1,0:T(8,128)(2,1)S(1)}, bf16[2,64,2176]{2,1,0:T(8,128)(2,1)S(1)}, u32[]{:S(2)}, u32[]{:S(2)}) %collective-permute-start.6) | collective-permute-done | bytes 557088 | tf_op jit(solution)/shard_map/ppermute | solution.py:13
  126.0 1.5 collective-permute-start.7
  128.3 7.9 %collective-permute-done.7 = bf16[2,64,2176]{2,1,0:T(8,128)(2,1)S(1)} collective-permute-done((bf16[2,64,2176]{2,1,0:T(8,128)(2,1)S(1)}, bf16[2,64,2176]{2,1,0:T(8,128)(2,1)S(1)}, u32[]{:S(2)}, u32[]{:S(2)}) %collective-permute-start.7) | collective-permute-done | bytes 557088 | tf_op jit(solution)/shard_map/ppermute | solution.py:13
  136.3 0.8 bitcast_dynamic-update-slice_fusion.6
  137.1 0.9 bitcast_dynamic-update-slice_fusion.4
  138.0 0.9 bitcast_dynamic-update-slice_fusion.2
  138.9 0.9 bitcast_dynamic-update-slice_fusion
  139.7 0.9 bitcast_dynamic-update-slice_fusion.15
  140.6 0.9 bitcast_dynamic-update-slice_fusion.13
  141.4 0.9 bitcast_dynamic-update-slice_fusion.11
  143.1 0.9 bitcast_dynamic-update-slice_fusion.7
  144.9 0.9 bitcast_dynamic-update-slice_fusion.3
  145.7 0.9 bitcast_dynamic-update-slice_fusion.1
  146.6 4.7 %constant_dynamic-slice_fusion = bf16[8,2,64,2176]{3,2,1,0:T(8,128)(2,1)} fusion(bf16[16,2,64,2176]{3,2,1,0:T(8,128)(2,1)} %bitcast_dynamic-update-slice_fusion.1, s32[]{:T(128)S(6)} %select_n.180), kind=kLoop, calls=%fused_computation.82 | loop fusion | bytes 8912900 | tf_op jit(solution)/shard_map/jit(_roll_dynamic)/dynamic_slice | solution.py:98
  151.3 9.2 %copy.90 = bf16[8,2,64,2176]{2,3,1,0:T(8,128)(2,1)} copy(bf16[8,2,64,2176]{3,2,1,0:T(8,128)(2,1)} %constant_dynamic-slice_fusion) | data formatting | bytes 8912896 | tf_op jit(solution)/shard_map/jit(_roll_dynamic)/dynamic_slice | solution.py:98
  161.6 2.3 reduce-window.16
  164.9 1.0 fusion.2
  165.9 6.4 %fusion.3 = bf16[16,2,32,2048]{3,2,1,0:T(8,128)(2,1)S(1)} fusion(pred[16,64,2,32]{1,3,2,0:T(8,128)(4,1)S(1)} %fusion.2, bf16[16,64,2176]{1,2,0:T(8,128)(2,1)} %bitcast.160), kind=kOutput, calls=%fused_computation.9 | convolution fusion | flops 270532608 | bytes 12648448 | tf_op jit(solution)/shard_map/stcr,std->scrd/dot_general | solution.py:111
  172.9 3.9 %collective-permute-done.11 = bf16[16,32,2048]{2,1,0:T(8,128)(2,1)S(1)} collective-permute-done((bf16[16,32,2048]{2,1,0:T(8,128)(2,1)S(1)}, bf16[16,32,2048]{2,1,0:T(8,128)(2,1)S(1)}, u32[]{:S(2)}, u32[]{:S(2)}) %collective-permute-start.11) | collective-permute-done | bytes 2097184 | tf_op jit(solution)/shard_map/ppermute | solution.py:8
  176.8 2.3 pad_maximum_fusion
  179.1 7.8 %fusion.22 = (bf16[1,2,4,2,128,1024]{5,4,3,2,1,0:T(8,128)(2,1)}, bf16[1,2,4,2,128,1024]{5,4,3,2,1,0:T(8,128)(2,1)}, bf16[1,2,4,2,128,1024]{5,4,3,2,1,0:T(8,128)(2,1)S(1)}) fusion(bf16[3,2,4,2,128,1024]{5,4,3,2,1,0:T(8,128)(2,1)} %bitcast.161), kind=kLoop, calls=%fused_computation.85 | loop fusion | bytes 25165824 | tf_op jit(solution)/shard_map/slice | solution.py:59
  187.0 6.0 %fusion.25 = f32[1024,1024]{1,0:T(8,128)} fusion(bf16[1024,2048]{1,0:T(8,128)(2,1)S(1)} %bitcast.167, bf16[2048,1024]{1,0:T(8,128)(2,1)S(1)} %bitcast.170), kind=kOutput, calls=%fused_computation.88 | convolution fusion | flops 4294967296 | bytes 12582912 | tf_op jit(solution)/shard_map/dot_general | solution.py:122
  193.0 15.2 %convolution_convert_fusion = bf16[1024,2048]{1,0:T(8,128)(2,1)} fusion(bf16[2048,1024]{1,0:T(8,128)(2,1)} %bitcast.169, f32[1024,1024]{1,0:T(8,128)} %fusion.25, bf16[1024,2048]{1,0:T(8,128)(2,1)} %bitcast.166, bf16[2048,1024]{1,0:T(8,128)(2,1)} %bitcast.168), kind=kOutput, calls=%fused_computation.10 | convolution fusion | flops 8598323200 | bytes 20971520 | tf_op jit(solution)/shard_map/dot_general | solution.py:125
  208.1 2.7 fusion.23
  211.1 4.0 %collective-permute-done.14 = bf16[16,32,2048]{2,1,0:T(8,128)(2,1)S(1)} collective-permute-done((bf16[16,32,2048]{2,1,0:T(8,128)(2,1)S(1)}, bf16[16,32,2048]{2,1,0:T(8,128)(2,1)S(1)}, u32[]{:S(2)}, u32[]{:S(2)}) %collective-permute-start.14) | collective-permute-done | bytes 2097184 | tf_op jit(solution)/shard_map/ppermute | solution.py:8
  215.1 2.2 maximum_select_fusion
  217.3 7.9 %all-to-all-start = ((bf16[16,2,32,2048]{3,2,1,0:T(8,128)(2,1)}), bf16[16,2,32,2048]{3,2,1,0:T(8,128)(2,1)}, u32[]{:S(2)}, u32[]{:S(2)}) async-start(bf16[16,2,32,2048]{3,2,1,0:T(8,128)(2,1)} %maximum_select_fusion), calls=%async_computation | async-start | bytes 8388608 | tf_op jit(solution)/shard_map/all_to_all | solution.py:130
  226.2 1.1 fusion.8
  229.9 94.9 %all-to-all-done = bf16[16,2,32,2048]{3,2,1,0:T(8,128)(2,1)} async-done(((bf16[16,2,32,2048]{3,2,1,0:T(8,128)(2,1)}), bf16[16,2,32,2048]{3,2,1,0:T(8,128)(2,1)}, u32[]{:S(2)}, u32[]{:S(2)}) %all-to-all-start) | async-done | bytes 4194336 | tf_op jit(solution)/shard_map/all_to_all | solution.py:130
  324.8 3.7 %convolution_convert_fusion.1 = bf16[64,2048]{1,0:T(8,128)(2,1)} fusion(bf16[64,1024]{1,0:T(8,128)(2,1)S(1)} %fusion.7, bf16[1024,2048]{1,0:T(8,128)(2,1)} %bitcast.49), kind=kOutput, calls=%fused_computation.13 | convolution fusion | flops 268566528 | bytes 4587520 | tf_op jit(solution)/shard_map/dot_general | solution.py:146
  (87 shorter events, 16.0 us)
Async XLA Ops:
  7.2 172.0 %all-gather.2.cloned.1.call-start = ((), (), s32[]{:S(2)}) async-start(), calls=%async_computation.1 | async-start | bytes 15728640 | tf_op jit(solution)/shard_map/all_gather | solution.py:57
  10.0 36.3 %collective-permute-start.12 = (bf16[2,3,128,1024]{3,2,1,0:T(8,128)(2,1)}, bf16[2,3,128,1024]{3,2,1,0:T(8,128)(2,1)S(1)}, u32[]{:S(2)}, u32[]{:S(2)}) collective-permute-start(bf16[2,3,128,1024]{3,2,1,0:T(8,128)(2,1)} %get-tuple-element.22), channel_id=1, source_target_pairs={{0,8},{1,9},{2,10},{3,11},{4,12},{5,13},{6,14},{7,15},{8,0},{9,1},... | collective-permute-start | bytes 4718600 | tf_op jit(solution)/shard_map/ppermute | solution.py:8
  47.0 3.5 %collective-permute-start.13 = (bf16[2,3,128,1024]{3,2,0,1:T(8,128)(2,1)S(1)}, bf16[2,3,128,1024]{3,2,0,1:T(8,128)(2,1)S(1)}, u32[]{:S(2)}, u32[]{:S(2)}) collective-permute-start(bf16[2,3,128,1024]{3,2,0,1:T(8,128)(2,1)S(1)} %get-tuple-element.20), channel_id=1, source_target_pairs={{0,1},{1,0},{2,3},{3,2},{4,5},{5,4},{6,7},{7,6},{8,9},{9,8},{10,11... | collective-permute-start | bytes 4718600 | tf_op jit(solution)/shard_map/ppermute | solution.py:8
  50.5 2.0 copy-start.7
  50.5 2.1 copy-start.6
  50.5 4.3 %copy-start.4 = (bf16[64,2048]{1,0:T(8,128)(2,1)S(1)}, bf16[64,2048]{1,0:T(8,128)(2,1)}, u32[]{:S(2)}) copy-start(bf16[64,2048]{1,0:T(8,128)(2,1)} %param.8) | copy-start | bytes 786436
  50.5 8.1 %copy-start.8 = (s32[32]{0:T(128)S(1)}, s32[32]{0:T(128)}, u32[]{:S(2)}) copy-start(s32[32]{0:T(128)} %param.12) | copy-start | bytes 388
  50.5 10.0 %copy-start = (bf16[2,128,1024]{2,1,0:T(8,128)(2,1)S(1)}, bf16[2,128,1024]{2,1,0:T(8,128)(2,1)}, u32[]{:S(2)}) copy-start(bf16[2,128,1024]{2,1,0:T(8,128)(2,1)} %param.13) | copy-start | bytes 1572868
  52.4 19.6 %copy-start.2 = (bf16[2,128,1024]{2,1,0:T(8,128)(2,1)S(1)}, bf16[2,128,1024]{2,1,0:T(8,128)(2,1)}, u32[]{:S(2)}) copy-start(bf16[2,128,1024]{2,1,0:T(8,128)(2,1)} %param.14) | copy-start | bytes 1572868
  52.4 24.2 %copy-start.1 = (bf16[2,128,1024]{2,1,0:T(8,128)(2,1)S(1)}, bf16[2,128,1024]{2,1,0:T(8,128)(2,1)}, u32[]{:S(2)}) copy-start(bf16[2,128,1024]{2,1,0:T(8,128)(2,1)} %param.15) | copy-start | bytes 1572868
  54.9 10.3 %collective-permute-start = (bf16[64,2176]{1,0:T(8,128)(2,1)S(1)}, bf16[64,2176]{1,0:T(8,128)(2,1)S(1)}, u32[]{:S(2)}, u32[]{:S(2)}) collective-permute-start(bf16[64,2176]{1,0:T(8,128)(2,1)S(1)} %concatenate.22), channel_id=1, source_target_pairs={{0,16},{16,0},{32,48},{48,32},{64,80},{80,64},{96,112},{112,96},{1... | collective-permute-start | bytes 835592 | tf_op jit(solution)/shard_map/ppermute | solution.py:8
  61.2 16.1 %collective-permute-start.2 = (bf16[128,1024]{1,0:T(8,128)(2,1)}, bf16[128,1024]{1,0:T(8,128)(2,1)S(1)}, u32[]{:S(2)}, u32[]{:S(2)}) collective-permute-start(bf16[128,1024]{1,0:T(8,128)(2,1)} %bitcast_select_fusion.9), channel_id=1, source_target_pairs={{0,16},{16,32},{32,48},{48,64},{64,80},{80,96},{96,112},{112,128},... | collective-permute-start | bytes 786440 | tf_op jit(solution)/shard_map/ppermute | solution.py:13
  66.2 34.4 %collective-permute-start.1 = (bf16[2,64,2176]{2,1,0:T(8,128)(2,1)S(1)}, bf16[2,64,2176]{2,1,0:T(8,128)(2,1)S(1)}, u32[]{:S(2)}, u32[]{:S(2)}) collective-permute-start(bf16[2,64,2176]{2,1,0:T(8,128)(2,1)S(1)} %get-tuple-element.13), channel_id=1, source_target_pairs={{0,224},{16,240},{32,0},{48,16},{64,32},{80,48},{96,64},{112,80},{... | collective-permute-start | bytes 1671176 | tf_op jit(solution)/shard_map/ppermute | solution.py:13
  72.0 29.0 %collective-permute-start.8 = (bf16[2,64,2176]{2,1,0:T(8,128)(2,1)S(1)}, bf16[2,64,2176]{2,1,0:T(8,128)(2,1)S(1)}, u32[]{:S(2)}, u32[]{:S(2)}) collective-permute-start(bf16[2,64,2176]{2,1,0:T(8,128)(2,1)S(1)} %get-tuple-element.13), channel_id=1, source_target_pairs={{0,32},{16,48},{32,64},{48,80},{64,96},{80,112},{96,128},{112,144}... | collective-permute-start | bytes 1671176 | tf_op jit(solution)/shard_map/ppermute | solution.py:13
  72.8 25.0 %collective-permute-start.3 = (bf16[128,1024]{1,0:T(8,128)(2,1)}, bf16[128,1024]{1,0:T(8,128)(2,1)}, u32[]{:S(2)}, u32[]{:S(2)}) collective-permute-start(bf16[128,1024]{1,0:T(8,128)(2,1)} %bitcast_select_fusion.6), channel_id=1, source_target_pairs={{0,16},{16,32},{32,48},{48,64},{64,80},{80,96},{96,112},{112,128},... | collective-permute-start | bytes 786440 | tf_op jit(solution)/shard_map/ppermute | solution.py:13
  77.3 23.2 %collective-permute-start.4 = (bf16[128,1024]{1,0:T(8,128)(2,1)}, bf16[128,1024]{1,0:T(8,128)(2,1)}, u32[]{:S(2)}, u32[]{:S(2)}) collective-permute-start(bf16[128,1024]{1,0:T(8,128)(2,1)} %bitcast_select_fusion.3), channel_id=1, source_target_pairs={{0,16},{16,32},{32,48},{48,64},{64,80},{80,96},{96,112},{112,128},... | collective-permute-start | bytes 786440 | tf_op jit(solution)/shard_map/ppermute | solution.py:13
  100.6 12.7 %collective-permute-start.5 = (bf16[2,64,2176]{2,1,0:T(8,128)(2,1)S(1)}, bf16[2,64,2176]{2,1,0:T(8,128)(2,1)S(1)}, u32[]{:S(2)}, u32[]{:S(2)}) collective-permute-start(bf16[2,64,2176]{2,1,0:T(8,128)(2,1)S(1)} %collective-permute-done.1), channel_id=1, source_target_pairs={{0,224},{16,240},{32,0},{48,16},{64,32},{80,48},{96,64},{112,80},{... | collective-permute-start | bytes 1671176 | tf_op jit(solution)/shard_map/ppermute | solution.py:13
  101.1 13.6 %collective-permute-start.9 = (bf16[2,64,2176]{2,1,0:T(8,128)(2,1)S(1)}, bf16[2,64,2176]{2,1,0:T(8,128)(2,1)S(1)}, u32[]{:S(2)}, u32[]{:S(2)}) collective-permute-start(bf16[2,64,2176]{2,1,0:T(8,128)(2,1)S(1)} %collective-permute-done.8), channel_id=1, source_target_pairs={{0,32},{16,48},{32,64},{48,80},{64,96},{80,112},{96,128},{112,144}... | collective-permute-start | bytes 1671176 | tf_op jit(solution)/shard_map/ppermute | solution.py:13
  113.3 12.7 %collective-permute-start.6 = (bf16[2,64,2176]{2,1,0:T(8,128)(2,1)S(1)}, bf16[2,64,2176]{2,1,0:T(8,128)(2,1)S(1)}, u32[]{:S(2)}, u32[]{:S(2)}) collective-permute-start(bf16[2,64,2176]{2,1,0:T(8,128)(2,1)S(1)} %collective-permute-done.5), channel_id=1, source_target_pairs={{0,224},{16,240},{32,0},{48,16},{64,32},{80,48},{96,64},{112,80},{... | collective-permute-start | bytes 1671176 | tf_op jit(solution)/shard_map/ppermute | solution.py:13
  114.7 22.4 %collective-permute-start.10 = (bf16[2,64,2176]{2,1,0:T(8,128)(2,1)S(1)}, bf16[2,64,2176]{2,1,0:T(8,128)(2,1)S(1)}, u32[]{:S(2)}, u32[]{:S(2)}) collective-permute-start(bf16[2,64,2176]{2,1,0:T(8,128)(2,1)S(1)} %collective-permute-done.9), channel_id=1, source_target_pairs={{0,32},{16,48},{32,64},{48,80},{64,96},{80,112},{96,128},{112,144}... | collective-permute-start | bytes 1671176 | tf_op jit(solution)/shard_map/ppermute | solution.py:13
  126.0 10.3 %collective-permute-start.7 = (bf16[2,64,2176]{2,1,0:T(8,128)(2,1)S(1)}, bf16[2,64,2176]{2,1,0:T(8,128)(2,1)S(1)}, u32[]{:S(2)}, u32[]{:S(2)}) collective-permute-start(bf16[2,64,2176]{2,1,0:T(8,128)(2,1)S(1)} %collective-permute-done.6), channel_id=1, source_target_pairs={{0,224},{16,240},{32,0},{48,16},{64,32},{80,48},{96,64},{112,80},{... | collective-permute-start | bytes 1671176 | tf_op jit(solution)/shard_map/ppermute | solution.py:13
  172.6 4.2 %collective-permute-start.11 = (bf16[16,32,2048]{2,1,0:T(8,128)(2,1)S(1)}, bf16[16,32,2048]{2,1,0:T(8,128)(2,1)S(1)}, u32[]{:S(2)}, u32[]{:S(2)}) collective-permute-start(bf16[16,32,2048]{2,1,0:T(8,128)(2,1)S(1)} %fusion.4), channel_id=1, source_target_pairs={{0,1},{1,0},{2,3},{3,2},{4,5},{5,4},{6,7},{7,6},{8,9},{9,8},{10,11... | collective-permute-start | bytes 6291464 | tf_op jit(solution)/shard_map/ppermute | solution.py:8
  179.1 7.9 %copy-start.3 = (bf16[2,16,32,2048]{3,2,1,0:T(8,128)(2,1)S(1)}, bf16[2,16,32,2048]{3,2,1,0:T(8,128)(2,1)}, u32[]{:S(2)}) copy-start(bf16[2,16,32,2048]{3,2,1,0:T(8,128)(2,1)} %pad_maximum_fusion) | copy-start | bytes 12582916
  210.9 4.2 %collective-permute-start.14 = (bf16[16,32,2048]{2,1,0:T(8,128)(2,1)S(1)}, bf16[16,32,2048]{2,1,0:T(8,128)(2,1)S(1)}, u32[]{:S(2)}, u32[]{:S(2)}) collective-permute-start(bf16[16,32,2048]{2,1,0:T(8,128)(2,1)S(1)} %bitcast.176), channel_id=1, source_target_pairs={{0,1},{1,0},{2,3},{3,2},{4,5},{5,4},{6,7},{7,6},{8,9},{9,8},{10,11... | collective-permute-start | bytes 6291464 | tf_op jit(solution)/shard_map/ppermute | solution.py:8
  217.3 8.0 %copy-start.5 = (f32[64,8]{0,1:T(8,128)S(1)}, f32[64,8]{0,1:T(8,128)}, u32[]{:S(2)}) copy-start(f32[64,8]{0,1:T(8,128)} %param.9) | copy-start | bytes 6148
  217.3 107.5 %all-to-all-start = ((bf16[16,2,32,2048]{3,2,1,0:T(8,128)(2,1)}), bf16[16,2,32,2048]{3,2,1,0:T(8,128)(2,1)}, u32[]{:S(2)}, u32[]{:S(2)}) async-start(bf16[16,2,32,2048]{3,2,1,0:T(8,128)(2,1)} %maximum_select_fusion), calls=%async_computation | async-start | bytes 8388608 | tf_op jit(solution)/shard_map/all_to_all | solution.py:130
Sparse Core Ops, SparseCore 0:
  52.6 124.0 all-gather.1

commit v19 on v18

--- a/solution.py
+++ b/solution.py
@@ -88,7 +88,7 @@
     behind = [pair]
     for hop in range(1, z_count // 2 + 1):
         ahead.append(passed_along(ahead[-1], "dp", -2))
-        if hop == 1:
+        if hop == 3:
             ahead[-1], arrive_gate, arrive_up, arrive_down = lax.optimization_barrier(
                 (ahead[-1], arrive_gate, arrive_up, arrive_down)
             )

time: 336 us -> 335 us (level)
  waiting for transfers between devices: 195 us -> 187 us
  starting transfers between devices: 28.8 us -> 35.9 us
    ppermute x10, waiting for transfers between devices: 50.8 us -> 32.1 us  [passed_along(): return lax.ppermute(x, axis, [(i, (i + by) % size) for i in range(size)])]
    all_gather x1, waiting for transfers between devices: 0.01 us -> 10.6 us  [local(): lax.all_gather(block, 'shard', axis=0, tiled=False, axis_index_groups=gro...]
    ppermute x10, starting transfers between devices: 15.8 us -> 21.3 us  [passed_along(): return lax.ppermute(x, axis, [(i, (i + by) % size) for i in range(size)])]
  transfers between devices with their start and end apart: 17 -> 17, of which waited for: 11 -> 12; matrix products, arithmetic and copies ran while one was open for 16% -> 16% of each run, Pallas kernels for 0% -> 0%
where the time goes in v19:
time: 335 us
  waiting for transfers between devices  187 us (56%)
  local copies, waits for them, and re-layouts  40.6 us (12%)
  starting transfers between devices  35.9 us (11%)
  matrix products  31.3 us (9%)
  other arithmetic  23.8 us (7%)
  between operations  15.6 us (5%)
    all_to_all x1, waiting for transfers between devices, local(): lax.all_to_all(pair_halves(upper_half, result[0], returned_other), 'dp',...  94.9 us
    ppermute x5, waiting for transfers between devices, partner_2(): lax.ppermute(x, axis, [(i, i ^ 1 << apart) for i in range(lax.axis_size(a...  49.8 us
    ppermute x10, waiting for transfers between devices, passed_along(): return lax.ppermute(x, axis, [(i, (i + by) % size) for i in range(size)])  32.1 us
    ppermute x10, starting transfers between devices, passed_along(): return lax.ppermute(x, axis, [(i, (i + by) % size) for i in range(size)])  21.3 us
    dot_general x1, matrix products, local(): lax.dot_general(hidden, full_down, (((1,), (1,)), ((), ())), preferred_el...  15.2 us
    dynamic_slice x2, local copies, waits for them, and re-layouts, local(): jnp.roll(by_offset, row_id // 2, axis=0).reshape(n_rows, tok_count, -1)  14 us
    unnamed x32, local copies, waits for them, and re-layouts  12 us
    all_gather x1, waiting for transfers between devices, local(): lax.all_gather(block, 'shard', axis=0, tiled=False, axis_index_groups=gro...  10.6 us
  transfers between devices with their start and end apart: 17, of which 12 were waited for; matrix products, arithmetic and copies ran while one was open for 16% of the time, Pallas kernels for 0%

profile of v19, /device:TPU:8, one launch (start us, length us, event | category | flops | bytes accessed | tf_op | source)
XLA Modules:
  0.0 334.7 jit_solution(15724550340738523701)
XLA Ops:
  7.2 2.7 fusion.21
  10.0 1.5 collective-permute-start.12
  11.5 34.9 %collective-permute-done.12 = bf16[2,3,128,1024]{3,2,1,0:T(8,128)(2,1)S(1)} collective-permute-done((bf16[2,3,128,1024]{3,2,1,0:T(8,128)(2,1)}, bf16[2,3,128,1024]{3,2,1,0:T(8,128)(2,1)S(1)}, u32[]{:S(2)}, u32[]{:S(2)}) %collective-permute-start.12) | collective-permute-done | bytes 1572896 | tf_op jit(solution)/shard_map/ppermute | solution.py:8
  47.1 3.4 %collective-permute-done.13 = bf16[2,3,128,1024]{3,2,0,1:T(8,128)(2,1)S(1)} collective-permute-done((bf16[2,3,128,1024]{3,2,0,1:T(8,128)(2,1)S(1)}, bf16[2,3,128,1024]{3,2,0,1:T(8,128)(2,1)S(1)}, u32[]{:S(2)}, u32[]{:S(2)}) %collective-permute-start.13) | collective-permute-done | bytes 1572896 | tf_op jit(solution)/shard_map/ppermute | solution.py:8
  50.5 1.9 maximum_select_fusion.2
  53.0 1.2 reduce-window.14
  54.9 3.1 collective-permute-start
  61.7 3.5 %collective-permute-done = bf16[64,2176]{1,0:T(8,128)(2,1)S(1)} collective-permute-done((bf16[64,2176]{1,0:T(8,128)(2,1)S(1)}, bf16[64,2176]{1,0:T(8,128)(2,1)S(1)}, u32[]{:S(2)}, u32[]{:S(2)}) %collective-permute-start) | collective-permute-done | bytes 278560 | tf_op jit(solution)/shard_map/ppermute | solution.py:8
  65.2 0.9 bitcast_dynamic-update-slice_fusion.14
  66.2 5.9 %collective-permute-start.1 = (bf16[2,64,2176]{2,1,0:T(8,128)(2,1)S(1)}, bf16[2,64,2176]{2,1,0:T(8,128)(2,1)S(1)}, u32[]{:S(2)}, u32[]{:S(2)}) collective-permute-start(bf16[2,64,2176]{2,1,0:T(8,128)(2,1)S(1)} %get-tuple-element.13), channel_id=1, source_target_pairs={{0,224},{16,240},{32,0},{48,16},{64,32},{80,48},{96,64},{112,80},{... | collective-permute-start | bytes 1671176 | tf_op jit(solution)/shard_map/ppermute | solution.py:13
  72.8 3.8 %collective-permute-start.5 = (bf16[128,1024]{1,0:T(8,128)(2,1)}, bf16[128,1024]{1,0:T(8,128)(2,1)}, u32[]{:S(2)}, u32[]{:S(2)}) collective-permute-start(bf16[128,1024]{1,0:T(8,128)(2,1)} %bitcast_select_fusion.6), channel_id=1, source_target_pairs={{0,16},{16,32},{32,48},{48,64},{64,80},{80,96},{96,112},{112,128},... | collective-permute-start | bytes 786440 | tf_op jit(solution)/shard_map/ppermute | solution.py:13
  77.3 6.0 %collective-permute-done.1 = bf16[2,64,2176]{2,1,0:T(8,128)(2,1)S(1)} collective-permute-done((bf16[2,64,2176]{2,1,0:T(8,128)(2,1)S(1)}, bf16[2,64,2176]{2,1,0:T(8,128)(2,1)S(1)}, u32[]{:S(2)}, u32[]{:S(2)}) %collective-permute-start.1) | collective-permute-done | bytes 557088 | tf_op jit(solution)/shard_map/ppermute | solution.py:13
  83.4 3.7 %collective-permute-start.2 = (bf16[2,64,2176]{2,1,0:T(8,128)(2,1)S(1)}, bf16[2,64,2176]{2,1,0:T(8,128)(2,1)S(1)}, u32[]{:S(2)}, u32[]{:S(2)}) collective-permute-start(bf16[2,64,2176]{2,1,0:T(8,128)(2,1)S(1)} %collective-permute-done.1), channel_id=1, source_target_pairs={{0,224},{16,240},{32,0},{48,16},{64,32},{80,48},{96,64},{112,80},{... | collective-permute-start | bytes 1671176 | tf_op jit(solution)/shard_map/ppermute | solution.py:13
  87.1 0.9 bitcast_dynamic-update-slice_fusion.12
  87.9 9.5 %collective-permute-done.2 = bf16[2,64,2176]{2,1,0:T(8,128)(2,1)S(1)} collective-permute-done((bf16[2,64,2176]{2,1,0:T(8,128)(2,1)S(1)}, bf16[2,64,2176]{2,1,0:T(8,128)(2,1)S(1)}, u32[]{:S(2)}, u32[]{:S(2)}) %collective-permute-start.2) | collective-permute-done | bytes 557088 | tf_op jit(solution)/shard_map/ppermute | solution.py:13
  97.5 3.7 %collective-permute-start.3 = (bf16[2,64,2176]{2,1,0:T(8,128)(2,1)S(1)}, bf16[2,64,2176]{2,1,0:T(8,128)(2,1)S(1)}, u32[]{:S(2)}, u32[]{:S(2)}) collective-permute-start(bf16[2,64,2176]{2,1,0:T(8,128)(2,1)S(1)} %collective-permute-done.2), channel_id=1, source_target_pairs={{0,224},{16,240},{32,0},{48,16},{64,32},{80,48},{96,64},{112,80},{... | collective-permute-start | bytes 1671176 | tf_op jit(solution)/shard_map/ppermute | solution.py:13
  101.2 0.9 bitcast_dynamic-update-slice_fusion.10
  102.1 1.4 collective-permute-done.6
  103.4 7.4 %collective-permute-done.3 = bf16[2,64,2176]{2,1,0:T(8,128)(2,1)S(1)} collective-permute-done((bf16[2,64,2176]{2,1,0:T(8,128)(2,1)S(1)}, bf16[2,64,2176]{2,1,0:T(8,128)(2,1)S(1)}, u32[]{:S(2)}, u32[]{:S(2)}) %collective-permute-start.3) | collective-permute-done | bytes 557088 | tf_op jit(solution)/shard_map/ppermute | solution.py:13
  110.8 3.7 %collective-permute-start.7 = (bf16[2,64,2176]{2,1,0:T(8,128)(2,1)S(1)}, bf16[2,64,2176]{2,1,0:T(8,128)(2,1)S(1)}, u32[]{:S(2)}, u32[]{:S(2)}) collective-permute-start(bf16[2,64,2176]{2,1,0:T(8,128)(2,1)S(1)} %collective-permute-done.3), channel_id=1, source_target_pairs={{0,224},{16,240},{32,0},{48,16},{64,32},{80,48},{96,64},{112,80},{... | collective-permute-start | bytes 1671176 | tf_op jit(solution)/shard_map/ppermute | solution.py:13
  115.3 7.8 %collective-permute-done.7 = bf16[2,64,2176]{2,1,0:T(8,128)(2,1)S(1)} collective-permute-done((bf16[2,64,2176]{2,1,0:T(8,128)(2,1)S(1)}, bf16[2,64,2176]{2,1,0:T(8,128)(2,1)S(1)}, u32[]{:S(2)}, u32[]{:S(2)}) %collective-permute-start.7) | collective-permute-done | bytes 557088 | tf_op jit(solution)/shard_map/ppermute | solution.py:13
  124.0 0.9 bitcast_dynamic-update-slice_fusion.4
  124.9 0.9 bitcast_dynamic-update-slice_fusion.2
  125.7 0.9 bitcast_dynamic-update-slice_fusion
  126.6 0.9 bitcast_dynamic-update-slice_fusion.15
  127.5 0.9 bitcast_dynamic-update-slice_fusion.13
  128.3 0.9 bitcast_dynamic-update-slice_fusion.11
  130.0 0.9 bitcast_dynamic-update-slice_fusion.7
  131.7 0.9 bitcast_dynamic-update-slice_fusion.3
  132.6 0.9 bitcast_dynamic-update-slice_fusion.1
  133.4 4.7 %constant_dynamic-slice_fusion = bf16[8,2,64,2176]{3,2,1,0:T(8,128)(2,1)} fusion(bf16[16,2,64,2176]{3,2,1,0:T(8,128)(2,1)} %bitcast_dynamic-update-slice_fusion.1, s32[]{:T(128)S(6)} %select_n.180), kind=kLoop, calls=%fused_computation.82 | loop fusion | bytes 8912900 | tf_op jit(solution)/shard_map/jit(_roll_dynamic)/dynamic_slice | solution.py:98
  138.2 9.3 %copy.90 = bf16[8,2,64,2176]{2,3,1,0:T(8,128)(2,1)} copy(bf16[8,2,64,2176]{3,2,1,0:T(8,128)(2,1)} %constant_dynamic-slice_fusion) | data formatting | bytes 8912896 | tf_op jit(solution)/shard_map/jit(_roll_dynamic)/dynamic_slice | solution.py:98
  148.5 2.3 reduce-window.16
  151.9 1.0 fusion.2
  152.9 6.4 %fusion.3 = bf16[16,2,32,2048]{3,2,1,0:T(8,128)(2,1)S(1)} fusion(pred[16,64,2,32]{1,3,2,0:T(8,128)(4,1)S(1)} %fusion.2, bf16[16,64,2176]{1,2,0:T(8,128)(2,1)} %bitcast.160), kind=kOutput, calls=%fused_computation.9 | convolution fusion | flops 270532608 | bytes 12648448 | tf_op jit(solution)/shard_map/stcr,std->scrd/dot_general | solution.py:111
  159.8 3.9 %collective-permute-done.11 = bf16[16,32,2048]{2,1,0:T(8,128)(2,1)S(1)} collective-permute-done((bf16[16,32,2048]{2,1,0:T(8,128)(2,1)S(1)}, bf16[16,32,2048]{2,1,0:T(8,128)(2,1)S(1)}, u32[]{:S(2)}, u32[]{:S(2)}) %collective-permute-start.11) | collective-permute-done | bytes 2097184 | tf_op jit(solution)/shard_map/ppermute | solution.py:8
  163.8 2.3 pad_maximum_fusion
  166.1 10.6 %all-gather.2.cloned.1.call-done = bf16[4,2,2,3,128,1024]{5,4,2,0,1,3:T(8,128)(2,1)} async-done(((bf16[1,2,2,3,128,1024]{5,4,2,0,1,3:T(8,128)(2,1)}), bf16[4,2,2,3,128,1024]{5,4,2,0,1,3:T(8,128)(2,1)}) %all-gather.2.cloned.1.call-update) | async-done | bytes 12582928 | tf_op jit(solution)/shard_map/all_gather | solution.py:57
  176.7 7.8 %fusion.22 = (bf16[1,2,4,2,128,1024]{5,4,3,2,1,0:T(8,128)(2,1)}, bf16[1,2,4,2,128,1024]{5,4,3,2,1,0:T(8,128)(2,1)}, bf16[1,2,4,2,128,1024]{5,4,3,2,1,0:T(8,128)(2,1)S(1)}) fusion(bf16[3,2,4,2,128,1024]{5,4,3,2,1,0:T(8,128)(2,1)} %bitcast.161), kind=kLoop, calls=%fused_computation.85 | loop fusion | bytes 25165824 | tf_op jit(solution)/shard_map/slice | solution.py:59
  184.5 6.0 %fusion.25 = f32[1024,1024]{1,0:T(8,128)} fusion(bf16[1024,2048]{1,0:T(8,128)(2,1)S(1)} %bitcast.167, bf16[2048,1024]{1,0:T(8,128)(2,1)S(1)} %bitcast.170), kind=kOutput, calls=%fused_computation.88 | convolution fusion | flops 4294967296 | bytes 12582912 | tf_op jit(solution)/shard_map/dot_general | solution.py:122
  190.6 15.2 %convolution_convert_fusion = bf16[1024,2048]{1,0:T(8,128)(2,1)} fusion(bf16[2048,1024]{1,0:T(8,128)(2,1)} %bitcast.169, f32[1024,1024]{1,0:T(8,128)} %fusion.25, bf16[1024,2048]{1,0:T(8,128)(2,1)} %bitcast.166, bf16[2048,1024]{1,0:T(8,128)(2,1)} %bitcast.168), kind=kOutput, calls=%fused_computation.10 | convolution fusion | flops 8598323200 | bytes 20971520 | tf_op jit(solution)/shard_map/dot_general | solution.py:125
  205.7 2.7 fusion.23
  208.5 4.1 %collective-permute-done.14 = bf16[16,32,2048]{2,1,0:T(8,128)(2,1)S(1)} collective-permute-done((bf16[16,32,2048]{2,1,0:T(8,128)(2,1)S(1)}, bf16[16,32,2048]{2,1,0:T(8,128)(2,1)S(1)}, u32[]{:S(2)}, u32[]{:S(2)}) %collective-permute-start.14) | collective-permute-done | bytes 2097184 | tf_op jit(solution)/shard_map/ppermute | solution.py:8
  212.7 2.2 maximum_select_fusion
  214.8 9.7 %all-to-all-start = ((bf16[16,2,32,2048]{3,2,1,0:T(8,128)(2,1)}), bf16[16,2,32,2048]{3,2,1,0:T(8,128)(2,1)}, u32[]{:S(2)}, u32[]{:S(2)}) async-start(bf16[16,2,32,2048]{3,2,1,0:T(8,128)(2,1)} %maximum_select_fusion), calls=%async_computation | async-start | bytes 8388608 | tf_op jit(solution)/shard_map/all_to_all | solution.py:130
  225.5 1.1 fusion.8
  229.2 94.9 %all-to-all-done = bf16[16,2,32,2048]{3,2,1,0:T(8,128)(2,1)} async-done(((bf16[16,2,32,2048]{3,2,1,0:T(8,128)(2,1)}), bf16[16,2,32,2048]{3,2,1,0:T(8,128)(2,1)}, u32[]{:S(2)}, u32[]{:S(2)}) %all-to-all-start) | async-done | bytes 4194336 | tf_op jit(solution)/shard_map/all_to_all | solution.py:130
  324.2 3.7 %convolution_convert_fusion.1 = bf16[64,2048]{1,0:T(8,128)(2,1)} fusion(bf16[64,1024]{1,0:T(8,128)(2,1)S(1)} %fusion.7, bf16[1024,2048]{1,0:T(8,128)(2,1)} %bitcast.49), kind=kOutput, calls=%fused_computation.13 | convolution fusion | flops 268566528 | bytes 4587520 | tf_op jit(solution)/shard_map/dot_general | solution.py:146
  (87 shorter events, 15.7 us)
Async XLA Ops:
  7.2 169.5 %all-gather.2.cloned.1.call-start = ((), (), s32[]{:S(2)}) async-start(), calls=%async_computation.1 | async-start | bytes 15728640 | tf_op jit(solution)/shard_map/all_gather | solution.py:57
  10.0 36.3 %collective-permute-start.12 = (bf16[2,3,128,1024]{3,2,1,0:T(8,128)(2,1)}, bf16[2,3,128,1024]{3,2,1,0:T(8,128)(2,1)S(1)}, u32[]{:S(2)}, u32[]{:S(2)}) collective-permute-start(bf16[2,3,128,1024]{3,2,1,0:T(8,128)(2,1)} %get-tuple-element.22), channel_id=1, source_target_pairs={{0,8},{1,9},{2,10},{3,11},{4,12},{5,13},{6,14},{7,15},{8,0},{9,1},... | collective-permute-start | bytes 4718600 | tf_op jit(solution)/shard_map/ppermute | solution.py:8
  47.0 3.5 %collective-permute-start.13 = (bf16[2,3,128,1024]{3,2,0,1:T(8,128)(2,1)S(1)}, bf16[2,3,128,1024]{3,2,0,1:T(8,128)(2,1)S(1)}, u32[]{:S(2)}, u32[]{:S(2)}) collective-permute-start(bf16[2,3,128,1024]{3,2,0,1:T(8,128)(2,1)S(1)} %get-tuple-element.20), channel_id=1, source_target_pairs={{0,1},{1,0},{2,3},{3,2},{4,5},{5,4},{6,7},{7,6},{8,9},{9,8},{10,11... | collective-permute-start | bytes 4718600 | tf_op jit(solution)/shard_map/ppermute | solution.py:8
  50.5 2.0 copy-start.7
  50.5 2.1 copy-start.6
  50.5 4.3 %copy-start.4 = (bf16[64,2048]{1,0:T(8,128)(2,1)S(1)}, bf16[64,2048]{1,0:T(8,128)(2,1)}, u32[]{:S(2)}) copy-start(bf16[64,2048]{1,0:T(8,128)(2,1)} %param.8) | copy-start | bytes 786436
  50.5 8.1 %copy-start.8 = (s32[32]{0:T(128)S(1)}, s32[32]{0:T(128)}, u32[]{:S(2)}) copy-start(s32[32]{0:T(128)} %param.12) | copy-start | bytes 388
  50.5 10.0 %copy-start = (bf16[2,128,1024]{2,1,0:T(8,128)(2,1)S(1)}, bf16[2,128,1024]{2,1,0:T(8,128)(2,1)}, u32[]{:S(2)}) copy-start(bf16[2,128,1024]{2,1,0:T(8,128)(2,1)} %param.13) | copy-start | bytes 1572868
  52.4 19.6 %copy-start.2 = (bf16[2,128,1024]{2,1,0:T(8,128)(2,1)S(1)}, bf16[2,128,1024]{2,1,0:T(8,128)(2,1)}, u32[]{:S(2)}) copy-start(bf16[2,128,1024]{2,1,0:T(8,128)(2,1)} %param.14) | copy-start | bytes 1572868
  52.4 24.2 %copy-start.1 = (bf16[2,128,1024]{2,1,0:T(8,128)(2,1)S(1)}, bf16[2,128,1024]{2,1,0:T(8,128)(2,1)}, u32[]{:S(2)}) copy-start(bf16[2,128,1024]{2,1,0:T(8,128)(2,1)} %param.15) | copy-start | bytes 1572868
  54.9 10.3 %collective-permute-start = (bf16[64,2176]{1,0:T(8,128)(2,1)S(1)}, bf16[64,2176]{1,0:T(8,128)(2,1)S(1)}, u32[]{:S(2)}, u32[]{:S(2)}) collective-permute-start(bf16[64,2176]{1,0:T(8,128)(2,1)S(1)} %concatenate.22), channel_id=1, source_target_pairs={{0,16},{16,0},{32,48},{48,32},{64,80},{80,64},{96,112},{112,96},{1... | collective-permute-start | bytes 835592 | tf_op jit(solution)/shard_map/ppermute | solution.py:8
  61.2 40.8 %collective-permute-start.4 = (bf16[128,1024]{1,0:T(8,128)(2,1)}, bf16[128,1024]{1,0:T(8,128)(2,1)S(1)}, u32[]{:S(2)}, u32[]{:S(2)}) collective-permute-start(bf16[128,1024]{1,0:T(8,128)(2,1)} %bitcast_select_fusion.9), channel_id=1, source_target_pairs={{0,16},{16,32},{32,48},{48,64},{64,80},{80,96},{96,112},{112,128},... | collective-permute-start | bytes 786440 | tf_op jit(solution)/shard_map/ppermute | solution.py:13
  66.2 17.2 %collective-permute-start.1 = (bf16[2,64,2176]{2,1,0:T(8,128)(2,1)S(1)}, bf16[2,64,2176]{2,1,0:T(8,128)(2,1)S(1)}, u32[]{:S(2)}, u32[]{:S(2)}) collective-permute-start(bf16[2,64,2176]{2,1,0:T(8,128)(2,1)S(1)} %get-tuple-element.13), channel_id=1, source_target_pairs={{0,224},{16,240},{32,0},{48,16},{64,32},{80,48},{96,64},{112,80},{... | collective-permute-start | bytes 1671176 | tf_op jit(solution)/shard_map/ppermute | solution.py:13
  72.0 15.0 %collective-permute-start.8 = (bf16[2,64,2176]{2,1,0:T(8,128)(2,1)S(1)}, bf16[2,64,2176]{2,1,0:T(8,128)(2,1)S(1)}, u32[]{:S(2)}, u32[]{:S(2)}) collective-permute-start(bf16[2,64,2176]{2,1,0:T(8,128)(2,1)S(1)} %get-tuple-element.13), channel_id=1, source_target_pairs={{0,32},{16,48},{32,64},{48,80},{64,96},{80,112},{96,128},{112,144}... | collective-permute-start | bytes 1671176 | tf_op jit(solution)/shard_map/ppermute | solution.py:13
  72.8 29.3 %collective-permute-start.5 = (bf16[128,1024]{1,0:T(8,128)(2,1)}, bf16[128,1024]{1,0:T(8,128)(2,1)}, u32[]{:S(2)}, u32[]{:S(2)}) collective-permute-start(bf16[128,1024]{1,0:T(8,128)(2,1)} %bitcast_select_fusion.6), channel_id=1, source_target_pairs={{0,16},{16,32},{32,48},{48,64},{64,80},{80,96},{96,112},{112,128},... | collective-permute-start | bytes 786440 | tf_op jit(solution)/shard_map/ppermute | solution.py:13
  77.3 26.1 %collective-permute-start.6 = (bf16[128,1024]{1,0:T(8,128)(2,1)}, bf16[128,1024]{1,0:T(8,128)(2,1)}, u32[]{:S(2)}, u32[]{:S(2)}) collective-permute-start(bf16[128,1024]{1,0:T(8,128)(2,1)} %bitcast_select_fusion.3), channel_id=1, source_target_pairs={{0,16},{16,32},{32,48},{48,64},{64,80},{80,96},{96,112},{112,128},... | collective-permute-start | bytes 786440 | tf_op jit(solution)/shard_map/ppermute | solution.py:13
  83.4 14.1 %collective-permute-start.2 = (bf16[2,64,2176]{2,1,0:T(8,128)(2,1)S(1)}, bf16[2,64,2176]{2,1,0:T(8,128)(2,1)S(1)}, u32[]{:S(2)}, u32[]{:S(2)}) collective-permute-start(bf16[2,64,2176]{2,1,0:T(8,128)(2,1)S(1)} %collective-permute-done.1), channel_id=1, source_target_pairs={{0,224},{16,240},{32,0},{48,16},{64,32},{80,48},{96,64},{112,80},{... | collective-permute-start | bytes 1671176 | tf_op jit(solution)/shard_map/ppermute | solution.py:13
  87.1 15.0 %collective-permute-start.9 = (bf16[2,64,2176]{2,1,0:T(8,128)(2,1)S(1)}, bf16[2,64,2176]{2,1,0:T(8,128)(2,1)S(1)}, u32[]{:S(2)}, u32[]{:S(2)}) collective-permute-start(bf16[2,64,2176]{2,1,0:T(8,128)(2,1)S(1)} %collective-permute-done.8), channel_id=1, source_target_pairs={{0,32},{16,48},{32,64},{48,80},{64,96},{80,112},{96,128},{112,144}... | collective-permute-start | bytes 1671176 | tf_op jit(solution)/shard_map/ppermute | solution.py:13
  97.5 13.3 %collective-permute-start.3 = (bf16[2,64,2176]{2,1,0:T(8,128)(2,1)S(1)}, bf16[2,64,2176]{2,1,0:T(8,128)(2,1)S(1)}, u32[]{:S(2)}, u32[]{:S(2)}) collective-permute-start(bf16[2,64,2176]{2,1,0:T(8,128)(2,1)S(1)} %collective-permute-done.2), channel_id=1, source_target_pairs={{0,224},{16,240},{32,0},{48,16},{64,32},{80,48},{96,64},{112,80},{... | collective-permute-start | bytes 1671176 | tf_op jit(solution)/shard_map/ppermute | solution.py:13
  102.0 22.0 %collective-permute-start.10 = (bf16[2,64,2176]{2,1,0:T(8,128)(2,1)S(1)}, bf16[2,64,2176]{2,1,0:T(8,128)(2,1)S(1)}, u32[]{:S(2)}, u32[]{:S(2)}) collective-permute-start(bf16[2,64,2176]{2,1,0:T(8,128)(2,1)S(1)} %collective-permute-done.9), channel_id=1, source_target_pairs={{0,32},{16,48},{32,64},{48,80},{64,96},{80,112},{96,128},{112,144}... | collective-permute-start | bytes 1671176 | tf_op jit(solution)/shard_map/ppermute | solution.py:13
  110.8 12.4 %collective-permute-start.7 = (bf16[2,64,2176]{2,1,0:T(8,128)(2,1)S(1)}, bf16[2,64,2176]{2,1,0:T(8,128)(2,1)S(1)}, u32[]{:S(2)}, u32[]{:S(2)}) collective-permute-start(bf16[2,64,2176]{2,1,0:T(8,128)(2,1)S(1)} %collective-permute-done.3), channel_id=1, source_target_pairs={{0,224},{16,240},{32,0},{48,16},{64,32},{80,48},{96,64},{112,80},{... | collective-permute-start | bytes 1671176 | tf_op jit(solution)/shard_map/ppermute | solution.py:13
  159.5 4.2 %collective-permute-start.11 = (bf16[16,32,2048]{2,1,0:T(8,128)(2,1)S(1)}, bf16[16,32,2048]{2,1,0:T(8,128)(2,1)S(1)}, u32[]{:S(2)}, u32[]{:S(2)}) collective-permute-start(bf16[16,32,2048]{2,1,0:T(8,128)(2,1)S(1)} %fusion.4), channel_id=1, source_target_pairs={{0,1},{1,0},{2,3},{3,2},{4,5},{5,4},{6,7},{7,6},{8,9},{9,8},{10,11... | collective-permute-start | bytes 6291464 | tf_op jit(solution)/shard_map/ppermute | solution.py:8
  176.7 7.8 %copy-start.3 = (bf16[2,16,32,2048]{3,2,1,0:T(8,128)(2,1)S(1)}, bf16[2,16,32,2048]{3,2,1,0:T(8,128)(2,1)}, u32[]{:S(2)}) copy-start(bf16[2,16,32,2048]{3,2,1,0:T(8,128)(2,1)} %pad_maximum_fusion) | copy-start | bytes 12582916
  208.4 4.2 %collective-permute-start.14 = (bf16[16,32,2048]{2,1,0:T(8,128)(2,1)S(1)}, bf16[16,32,2048]{2,1,0:T(8,128)(2,1)S(1)}, u32[]{:S(2)}, u32[]{:S(2)}) collective-permute-start(bf16[16,32,2048]{2,1,0:T(8,128)(2,1)S(1)} %bitcast.176), channel_id=1, source_target_pairs={{0,1},{1,0},{2,3},{3,2},{4,5},{5,4},{6,7},{7,6},{8,9},{9,8},{10,11... | collective-permute-start | bytes 6291464 | tf_op jit(solution)/shard_map/ppermute | solution.py:8
  214.8 9.8 %copy-start.5 = (f32[64,8]{0,1:T(8,128)S(1)}, f32[64,8]{0,1:T(8,128)}, u32[]{:S(2)}) copy-start(f32[64,8]{0,1:T(8,128)} %param.9) | copy-start | bytes 6148
  214.8 109.3 %all-to-all-start = ((bf16[16,2,32,2048]{3,2,1,0:T(8,128)(2,1)}), bf16[16,2,32,2048]{3,2,1,0:T(8,128)(2,1)}, u32[]{:S(2)}, u32[]{:S(2)}) async-start(bf16[16,2,32,2048]{3,2,1,0:T(8,128)(2,1)} %maximum_select_fusion), calls=%async_computation | async-start | bytes 8388608 | tf_op jit(solution)/shard_map/all_to_all | solution.py:130
Sparse Core Ops, SparseCore 0:
  52.6 124.0 all-gather.1
